TPU v7x, 256 devices: a whole 4x4x8 slice. The times are simulated.
256 devices in a mesh: mem: 16 (over z_hi, x), tensor: 16 (over y, z_lo, core).
Axes of the slice: x: 4, y: 4, z: 8 (z_hi: 4, z_lo: 2; z = z_hi * 2 + z_lo), core: 2. Of those that a mesh axis runs over, the one named last changes fastest.
Arguments:
- queries: bfloat16 [4096, 6144], P('mem', 'tensor'), may hold values from -180 to 180
- local_keys: bfloat16 [4096, 6144], P('mem', 'tensor'), may hold values from -6 to 6
- local_values: bfloat16 [4096, 6144], P('mem', 'tensor'), may hold values from -6 to 6
- segments: int32 [4096], P('mem'), may hold values from 0 to 15, never falling along the last dimension, each value on 1 to 512 neighbouring positions
- memory_keys: bfloat16 [8192, 6144], P('mem', 'tensor'), may hold values from -6 to 6
- memory_values: bfloat16 [8192, 6144], P('mem', 'tensor'), may hold values from -6 to 6
- retrieved: int32 [32, 8], P('mem'), may hold values from 0 to 63, as said below
- block_slot: int32 [64], replicated, may hold values from 0 to 63, as said below
- gate_bias: float32 [48], P('tensor'), may hold values from -4 to 4
- out_weight: bfloat16 [6144, 6144], P('tensor'), may hold values from -0.078125 to 0.078125
- cotangent: bfloat16 [4096, 6144], P('mem', 'tensor'), may hold values from -1.5 to 1.5
Outputs:
- attention: bfloat16 [4096, 6144], P('mem', 'tensor')
- attention_grad: bfloat16 [4096, 6144], P('mem', 'tensor')
- weight_grad: float32 [6144, 6144], P('tensor', 'mem')
Inputs may be any that keep to these rules, and one draw needn't show every extreme that they name: `retrieved`: within a row the 8 ids are distinct and stored in distinct memory shards (shard of id b: block_slot[b] // 4). The 2 consecutive rows of one data group name at most 2 distinct ids stored in any one shard; in every draw every data group names at least one shard twice. `block_slot`: each value once; memory block b is row block block_slot[b] of memory_keys and memory_values. `segments`: segment ids never fall along the rows; a segment has 1 to 512 rows.
All inputs are finite; a program needn't handle non-finite values.
Results may differ from a plain program's by a relative error of at most 0.015.
Values may be sent and summed in bfloat16 or wider, within the bound.
No kernel may reach another device: no remote copies, remote signals or barrier semaphores. Data moves between devices by JAX's collectives and lax.ppermute only.
A program may use at most 64 MiB of HBM per device.

v0:
```python
import jax
import jax.numpy as jnp
from jax import lax
from jax.sharding import PartitionSpec as P

CAP = 2


masked_score = -1e30


def rounded_probs(scores):
    row_max = jnp.max(scores, axis=-1, keepdims=True)
    weights = jnp.exp(scores - row_max)
    totals = jnp.sum(weights, axis=-1, keepdims=True)
    return (weights / totals).astype(jnp.bfloat16)


def local_attention(queries, local_keys, local_values, segments, head_count):
    row_count, full_width = queries.shape
    head_width = full_width // head_count
    block_rows = min(row_count, 512)
    key_heads = local_keys.reshape(row_count, head_count, head_width)
    value_heads = local_values.reshape(row_count, head_count, head_width)
    positions = jnp.arange(row_count, dtype=jnp.int32)

    def one_block(offset):
        query_rows = queries.reshape(block_rows, head_count, head_width)
        row_positions = offset + jnp.arange(block_rows, dtype=jnp.int32)
        scores = jnp.einsum(
            "qhd,khd->hqk", query_rows, key_heads, preferred_element_type=jnp.float32
        ) * head_width ** (-0.5)
        allowed = (positions[None, :] <= row_positions[:, None]) & (
            segments[None, :] == segments[:, None]
        )
        scores = jnp.where(allowed[None, :, :], scores, masked_score)
        weights = rounded_probs(scores)
        return jnp.einsum("hqk,khd->qhd", weights, value_heads, preferred_element_type=jnp.float32)

    offsets = jnp.arange(row_count // block_rows, dtype=jnp.int32) * block_rows
    return lax.map(one_block, offsets).reshape(row_count, head_count, head_width)


def memory_attention(query_blocks, chosen_keys, chosen_values, head_count):
    block_total, block_len, full_width = query_blocks.shape
    head_width = full_width // head_count
    key_len = chosen_keys.shape[1]
    group_size = min(block_total, 4)

    def one_group(inputs):
        group_queries, group_keys, group_values = inputs
        query_heads = group_queries.reshape(group_size, block_len, head_count, head_width)
        key_heads = group_keys.reshape(group_size, key_len, head_count, head_width)
        value_heads = group_values.reshape(group_size, key_len, head_count, head_width)
        scores = jnp.einsum(
            "bqhd,bkhd->bhqk", query_heads, key_heads, preferred_element_type=jnp.float32
        ) * head_width ** (-0.5)
        weights = rounded_probs(scores)
        return jnp.einsum(
            "bhqk,bkhd->bqhd", weights, value_heads, preferred_element_type=jnp.float32
        )

    def grouped(stacked):
        return stacked.reshape(block_total // group_size, group_size, stacked.shape[1], full_width)

    result = lax.map(
        one_group, (grouped(query_blocks), grouped(chosen_keys), grouped(chosen_values))
    )
    return result.reshape(block_total * block_len, head_count, head_width)


def plan_requests(storage, group_count, shard_blocks, capacity):
    all_cells = jnp.arange(group_count * shard_blocks, dtype=jnp.int32)
    present = jnp.any(storage.reshape(-1)[:, None] == all_cells[None, :], axis=0)
    present = present.astype(jnp.int32).reshape(group_count, shard_blocks)
    slot_rank = jnp.cumsum(present, axis=1) - present
    slot_ids = jnp.arange(capacity, dtype=jnp.int32)
    chosen = present[:, :, None] * (slot_rank[:, :, None] == slot_ids[None, None, :]).astype(
        jnp.int32
    )
    local_ids = jnp.arange(shard_blocks, dtype=jnp.int32)
    requests = jnp.sum(chosen * local_ids[None, :, None], axis=1)
    owners = storage // shard_blocks
    position = owners * capacity + slot_rank.reshape(-1)[storage]
    return (requests, position)


def per_device(
    queries,
    local_keys,
    local_values,
    segments,
    memory_keys,
    memory_values,
    retrieved,
    block_slot,
    gate_bias,
    out_weight,
    cotangent,
):
    head_count = gate_bias.shape[0]
    row_count, full_width = queries.shape
    query_blocks = retrieved.shape[0]
    block_len = row_count // query_blocks
    top_count = retrieved.shape[1]
    storage = block_slot[retrieved]
    shard_blocks = memory_keys.shape[0] // block_len
    group_count = lax.axis_size("mem")
    requests, position = plan_requests(storage, group_count, shard_blocks, CAP)
    asked_slots = lax.all_to_all(requests, "mem", split_axis=0, concat_axis=0, tiled=True)
    key_blocks = memory_keys.reshape(shard_blocks, block_len, full_width)
    value_blocks = memory_values.reshape(shard_blocks, block_len, full_width)
    sent_keys = key_blocks[asked_slots].reshape(group_count, CAP * block_len, full_width)
    sent_values = value_blocks[asked_slots].reshape(group_count, CAP * block_len, full_width)
    fetched_keys, fetched_values = (
        lax.all_to_all(sent_keys, "mem", split_axis=0, concat_axis=0, tiled=True),
        lax.all_to_all(sent_values, "mem", split_axis=0, concat_axis=0, tiled=True),
    )
    buffer_keys = fetched_keys.reshape(group_count * CAP, block_len, full_width)
    buffer_values = fetched_values.reshape(group_count * CAP, block_len, full_width)
    chosen_keys = buffer_keys[position].reshape(query_blocks, top_count * block_len, full_width)
    chosen_values = buffer_values[position].reshape(query_blocks, top_count * block_len, full_width)
    local_out = local_attention(queries, local_keys, local_values, segments, head_count)
    memory_out = memory_attention(
        queries.reshape(query_blocks, block_len, full_width), chosen_keys, chosen_values, head_count
    )
    gate_weight = jax.nn.sigmoid(gate_bias)[None, :, None]
    attention = (
        (gate_weight * memory_out + (1.0 - gate_weight) * local_out)
        .reshape(row_count, full_width)
        .astype(jnp.bfloat16)
    )
    grad_sum = jnp.einsum(
        "tc,dc->td",
        lax.all_gather(cotangent, "tensor", axis=1, tiled=True),
        out_weight,
        preferred_element_type=jnp.float32,
    )
    partial_value = jnp.einsum(
        "td,tc->dc",
        attention,
        lax.all_gather(cotangent, "tensor", axis=1, tiled=True),
        preferred_element_type=jnp.float32,
    )
    weight_grad = lax.psum_scatter(
        partial_value.astype(jnp.bfloat16), "mem", scatter_dimension=1, tiled=True
    ).astype(jnp.float32)
    return (attention, grad_sum.astype(jnp.bfloat16), weight_grad)


def solution(mesh):
    return jax.shard_map(
        per_device,
        mesh=mesh,
        in_specs=(
            P("mem", "tensor"),
            P("mem", "tensor"),
            P("mem", "tensor"),
            P("mem"),
            P("mem", "tensor"),
            P("mem", "tensor"),
            P("mem", None),
            P(),
            P("tensor"),
            P("tensor", None),
            P("mem", "tensor"),
        ),
        out_specs=(P("mem", "tensor"), P("mem", "tensor"), P("tensor", "mem")),
        check_vma=False,
    )
```

profile of v0, /device:TPU:1, one launch (start us, length us, event | category | flops | bytes accessed | tf_op | source)
XLA Modules:
  0.0 338.0 jit_solution(4169536046799865004)
XLA Ops:
  7.2 0.0 copy-start
  7.2 0.7 compare_select_fusion.2
  7.9 0.1 reshape.260
  8.0 1.3 gather_fusion
  9.3 0.1 fusion.27
  9.4 0.4 copy-done.5
  9.8 0.6 copy-done.6
  10.4 0.1 reshape.257
  10.5 0.1 copy.71
  10.6 0.2 reduce_window_sum.13
  10.7 0.1 copy.70
  10.8 0.1 copy.72
  10.9 20.2 %all_to_all.22 = s32[16,1,2]{2,1,0:T(1,128)S(1)} all-to-all(s32[16,1,2]{2,1,0:T(1,128)S(1)} %copy.72), channel_id=1, replica_groups=mesh['mem'=16,'tensor'=16] {'mem'}, dimensions={0} | all-to-all | bytes 256 | tf_op jit(solution)/shard_map/all_to_all | solution.py:110
  31.1 0.1 copy.73
  31.2 0.1 copy.74
  31.3 0.1 reshape.268
  31.4 2.7 gather_fusion.4
  34.1 4.6 %all-to-all-start.2 = ((bf16[16,256,384]{2,1,0:T(8,128)(2,1)}), bf16[16,256,384]{2,1,0:T(8,128)(2,1)}, u32[]{:S(2)}, u32[]{:S(2)}) async-start(bf16[16,256,384]{2,1,0:T(8,128)(2,1)} %bitcast.75), calls=%async_computation.2 | async-start | bytes 6291456 | tf_op jit(solution)/shard_map/all_to_all | solution.py:116
  38.7 0.0 copy-done.1
  38.7 2.7 gather_fusion.1
  41.4 67.4 %all-to-all-done.2 = bf16[16,256,384]{2,1,0:T(8,128)(2,1)} async-done(((bf16[16,256,384]{2,1,0:T(8,128)(2,1)}), bf16[16,256,384]{2,1,0:T(8,128)(2,1)}, u32[]{:S(2)}, u32[]{:S(2)}) %all-to-all-start.2) | async-done | bytes 3145760 | tf_op jit(solution)/shard_map/all_to_all | solution.py:116
  108.8 9.4 %all-to-all-start.1 = ((bf16[16,256,384]{2,1,0:T(8,128)(2,1)}), bf16[16,256,384]{2,1,0:T(8,128)(2,1)S(1)}, u32[]{:S(2)}, u32[]{:S(2)}) async-start(bf16[16,256,384]{2,1,0:T(8,128)(2,1)} %bitcast.74), calls=%async_computation.1 | async-start | bytes 6291456 | tf_op jit(solution)/shard_map/all_to_all | solution.py:117
  118.2 0.0 all-gather.2.cloned.1.call-start
  118.3 0.7 all-gather.2.cloned.1.call-update
  119.0 0.0 reduce-scatter.4.cloned.1.call-start
  119.0 0.6 reduce_window_sum.14
  119.6 0.7 gather.24
  120.3 1.7 reshape.322
  122.0 1.7 copy.83
  123.8 0.7 reshape.276
  124.4 0.7 pad_clamp_fusion.1
  125.1 0.7 convert_subtract_fusion
  125.8 1.2 gather_fusion.2
  127.0 0.7 gather.26
  127.7 0.1 reshape.284
  127.8 1.7 copy.87
  129.5 1.8 copy.84
  131.3 0.7 fusion.21
  132.0 1.5 fusion.36
  133.5 0.7 broadcast_subtract_fusion
  134.2 0.1 broadcast_bitcast_fusion
  134.3 2.2 fusion.14
  136.5 2.5 fusion.20
  139.0 3.8 %gather_fusion.5 = bf16[16,128,384]{2,1,0:T(8,128)(2,1)} fusion(bf16[32,128,384]{2,1,0:T(8,128)(2,1)} %bitcast.8, s32[1024]{0:T(1024)S(1)} %pad_clamp_fusion), kind=kCustom, calls=%fused_computation.5 | custom fusion | bytes 3145792 | tf_op jit(solution)/shard_map/gather | solution.py:121
  142.8 5.1 %reshape.321 = bf16[2,1024,3,128]{3,2,1,0:T(4,128)(2,1)} reshape(bf16[16,128,384]{2,1,0:T(8,128)(2,1)} %gather_fusion.5) | data formatting | bytes 3145728 | tf_op jit(solution)/shard_map/while/body/eval_jaxpr/reshape | solution.py:53
  148.0 58.4 %all-to-all-done.1 = bf16[16,256,384]{2,1,0:T(8,128)(2,1)S(1)} async-done(((bf16[16,256,384]{2,1,0:T(8,128)(2,1)}), bf16[16,256,384]{2,1,0:T(8,128)(2,1)S(1)}, u32[]{:S(2)}, u32[]{:S(2)}) %all-to-all-start.1) | async-done | bytes 3145760 | tf_op jit(solution)/shard_map/all_to_all | solution.py:117
  206.4 1.9 gather_fusion.3
  208.2 5.1 %reshape.320 = bf16[2,1024,3,128]{3,2,1,0:T(4,128)(2,1)} reshape(bf16[16,128,384]{2,1,0:T(8,128)(2,1)} %gather_fusion.3) | data formatting | bytes 3145728 | tf_op jit(solution)/shard_map/while/body/eval_jaxpr/reshape | solution.py:54
  213.4 2.2 fusion.7
  215.6 0.8 fusion.35
  216.4 3.9 %fusion.15 = f32[2,128,3,128]{1,3,2,0:T(8,128)} fusion(f32[2,3,128]{2,1,0:T(4,128)S(1)} %fusion.35, bf16[2,1024,3,128]{3,2,1,0:T(4,128)(2,1)} %reshape.320, f32[2,3,1024,128]{3,2,1,0:T(8,128)S(1)} %fusion.7), kind=kOutput, calls=%fused_computation.24 | convolution fusion | flops 205260544 | bytes 5114880 | tf_op jit(solution)/shard_map/while/body/eval_jaxpr/bhqk,bkhd->bqhd/dot_general | solution.py:59
  220.3 1.3 copy.82
  221.6 1.2 fusion.19
  222.8 0.0 copy-start.3
  222.8 0.0 all-gather.2.cloned.1.call-done
  222.8 5.5 %convolution_convert_fusion = bf16[384,6144]{1,0:T(8,128)(2,1)} fusion(bf16[256,384]{0,1:T(8,128)(2,1)S(1)} %fusion.19, bf16[256,6144]{1,0:T(8,128)(2,1)} %all-gather.2.cloned.1.call-done), kind=kOutput, calls=%fused_computation.8 | convolution fusion | flops 1210318848 | bytes 8060928 | tf_op jit(solution)/shard_map/td,tc->dc/dot_general | solution.py:139
  228.3 6.6 %copy.100 = bf16[384,6144]{0,1:T(8,128)(2,1)} copy(bf16[384,6144]{1,0:T(8,128)(2,1)} %convolution_convert_fusion) | data formatting | bytes 9437184
  234.9 0.0 reduce-scatter.4.cloned.1.call-update
  235.0 1.9 copy-done.2
  236.8 4.8 %convolution_convert_fusion.1 = bf16[256,384]{1,0:T(8,128)(2,1)} fusion(bf16[256,6144]{1,0:T(8,128)(2,1)S(1)} %copy-done.2, bf16[384,6144]{1,0:T(8,128)(2,1)} %param.20), kind=kOutput, calls=%fused_computation.25 | convolution fusion | flops 1208057856 | bytes 8060928 | tf_op jit(solution)/shard_map/tc,dc->td/dot_general | solution.py:133
  241.7 1.7 copy.89
  243.4 85.7 %reduce-scatter.4.cloned.1.call-done = bf16[384,384]{1,0:T(8,128)(2,1)} async-done(((bf16[6144,384]{1,0:T(8,128)(2,1)}), bf16[384,384]{1,0:T(8,128)(2,1)}) %reduce-scatter.4.cloned.1.call-update) | async-done | bytes 294928
  329.1 1.2 copy.101
  330.3 0.9 convert_element_type.46
  (17 shorter events, 0.1 us)
Async XLA Ops:
  7.2 24.2 %copy-start = (bf16[512,384]{1,0:T(8,128)(2,1)S(1)}, bf16[512,384]{1,0:T(8,128)(2,1)}, u32[]{:S(2)}) copy-start(bf16[512,384]{1,0:T(8,128)(2,1)} %param.15) | copy-start | bytes 1179652
  9.3 0.5 copy-start.5
  9.8 0.6 copy-start.6
  34.1 4.6 %copy-start.1 = (bf16[512,384]{1,0:T(8,128)(2,1)S(1)}, bf16[512,384]{1,0:T(8,128)(2,1)}, u32[]{:S(2)}) copy-start(bf16[512,384]{1,0:T(8,128)(2,1)} %param.16) | copy-start | bytes 1179652
  34.1 74.7 %all-to-all-start.2 = ((bf16[16,256,384]{2,1,0:T(8,128)(2,1)}), bf16[16,256,384]{2,1,0:T(8,128)(2,1)}, u32[]{:S(2)}, u32[]{:S(2)}) async-start(bf16[16,256,384]{2,1,0:T(8,128)(2,1)} %bitcast.75), calls=%async_computation.2 | async-start | bytes 6291456 | tf_op jit(solution)/shard_map/all_to_all | solution.py:116
  108.8 22.5 %copy-start.4 = (s32[256]{0:T(256)S(1)}, s32[256]{0:T(256)}, u32[]{:S(2)}) copy-start(s32[256]{0:T(256)} %param.14) | copy-start | bytes 3076
  108.8 97.5 %all-to-all-start.1 = ((bf16[16,256,384]{2,1,0:T(8,128)(2,1)}), bf16[16,256,384]{2,1,0:T(8,128)(2,1)S(1)}, u32[]{:S(2)}, u32[]{:S(2)}) async-start(bf16[16,256,384]{2,1,0:T(8,128)(2,1)} %bitcast.74), calls=%async_computation.1 | async-start | bytes 6291456 | tf_op jit(solution)/shard_map/all_to_all | solution.py:117
  118.2 104.6 %all-gather.2.cloned.1.call-start = ((), (), s32[]{:S(2)}) async-start(), calls=%async_computation.4 | async-start | bytes 3342336 | tf_op jit(solution)/shard_map/all_gather | solution.py:135
  119.0 210.2 %reduce-scatter.4.cloned.1.call-start = ((), (), s32[]{:S(2)}) async-start(), calls=%async_computation.5 | async-start | bytes 5013504
  222.8 5.5 %copy-start.3 = (bf16[256,384]{0,1:T(8,128)(2,1)}, bf16[256,384]{0,1:T(8,128)(2,1)S(1)}, u32[]{:S(2)}) copy-start(bf16[256,384]{0,1:T(8,128)(2,1)S(1)} %fusion.19) | copy-start | bytes 589828
  234.9 1.9 copy-start.2
Sparse Core Ops, SparseCore 0:
  120.9 72.7 all-gather.1
  235.1 93.9 reduce-scatter.3
where the time goes:
time: 339 us; the launch traced here: 338 us
  waiting for transfers between devices  212 us (63%)
  local copies, waits for them, and re-layouts  48 us (14%)
  matrix products  22.6 us (7%)
  blocking collectives  20.2 us (6%)
  between operations  14.2 us (4%)
  starting transfers between devices  14.1 us (4%)
  other arithmetic  6.66 us (2%)
    unnamed x3, waiting for transfers between devices  86.4 us
    all_to_all x1, waiting for transfers between devices, per_device(): lax.all_to_all(sent_keys, 'mem', split_axis=0, concat_axis=0, tiled=True)  67.4 us
    all_to_all x1, waiting for transfers between devices, per_device(): lax.all_to_all(sent_values, 'mem', split_axis=0, concat_axis=0, tiled=True)  58.4 us
    all_to_all x1, blocking collectives, per_device(): lax.all_to_all(requests, 'mem', split_axis=0, concat_axis=0, tiled=True)  20.2 us
    unnamed x20, local copies, waits for them, and re-layouts  17.6 us
    all_to_all x1, starting transfers between devices, per_device(): lax.all_to_all(sent_values, 'mem', split_axis=0, concat_axis=0, tiled=True)  9.41 us
  transfers between devices with their start and end apart: 4, of which 3 were waited for; matrix products, arithmetic and copies ran while one was open for 16% of the time, Pallas kernels for 0%

commit v1 on v0

v1 whole, which is shorter than its diff:
```python
import jax
import jax.numpy as jnp
from jax import lax
from jax.experimental import pallas as pl
from jax.experimental.pallas import tpu as pltpu
from jax.sharding import PartitionSpec as P

HEAD = 128
BLOCK = 128
SLOTS = 4
NX = 4
NZ = 4
NY = 4
LOG2E = 1.4426950408889634
SCALE2 = HEAD**-0.5 * LOG2E
NEG = -1e30
EXTRA = 16

VM = pl.BlockSpec(memory_space=pltpu.VMEM)
SM = pl.BlockSpec(memory_space=pltpu.SMEM)


def dot_nt(a, b):
    return lax.dot_general(a, b, (((1,), (1,)), ((), ())), preferred_element_type=jnp.float32)


def dot_nn(a, b):
    return lax.dot_general(a, b, (((1,), (0,)), ((), ())), preferred_element_type=jnp.float32)


def shift_x(value, k):
    pairs = [(z * NX + x, z * NX + (x + k) % NX) for z in range(NZ) for x in range(NX)]
    return lax.ppermute(value, "mem", pairs)


def shift_z(value, k):
    pairs = [(z * NX + x, (z + k) % NZ * NX + x) for z in range(NZ) for x in range(NX)]
    return lax.ppermute(value, "mem", pairs)


def shift_y(value, k):
    pairs = [(y * 4 + r, (y + k) % NY * 4 + r) for y in range(NY) for r in range(4)]
    return lax.ppermute(value, "tensor", pairs)


def flip_tensor(value, bit):
    return lax.ppermute(value, "tensor", [(t, t ^ bit) for t in range(16)])


def swap_zy(value):
    pairs = []
    for z in range(NZ):
        for x in range(NX):
            for y in range(NY):
                for r in range(4):
                    pairs.append(((z * NX + x) * 16 + y * 4 + r, (y * NX + x) * 16 + z * 4 + r))
    return lax.ppermute(value, ("mem", "tensor"), pairs)


def local_kernel(gate_ref, seg_ref, q_ref, k_ref, v_ref, out_ref):
    rows = q_ref.shape[0]
    heads = q_ref.shape[1] // HEAD
    seg_cols = jnp.broadcast_to(seg_ref[...].astype(jnp.float32), (rows, rows))
    seg_rows = seg_cols.T
    row_ids = lax.broadcasted_iota(jnp.int32, (rows, rows), 0)
    col_ids = lax.broadcasted_iota(jnp.int32, (rows, rows), 1)
    allowed = (col_ids <= row_ids) & (seg_cols == seg_rows)
    for h in range(heads):
        cols = pl.ds(h * HEAD, HEAD)
        scores = jnp.where(allowed, dot_nt(q_ref[:, cols], k_ref[:, cols]) * SCALE2, NEG)
        top = jnp.max(scores, axis=1, keepdims=True)
        weights = jnp.exp2(scores - top)
        total = jnp.sum(weights, axis=1, keepdims=True)
        out = dot_nn(weights.astype(jnp.bfloat16), v_ref[:, cols])
        out_ref[:, cols] = out * ((1.0 - gate_ref[h]) / total)


def memory_kernel(sel_ref, *refs):
    q_refs, k_refs, v_refs, out_refs = refs[0:4], refs[4:8], refs[8:12], refs[12:16]
    heads = k_refs[0].shape[1] // HEAD
    lane = lax.broadcasted_iota(jnp.int32, (BLOCK, BLOCK), 1)
    for j in range(NZ):
        q_ref, out_ref = q_refs[j], out_refs[j]

        for b in range(2):
            row = b * BLOCK
            stat = jnp.zeros((BLOCK, BLOCK), jnp.float32)
            starts, biases = [], []
            for i in range(NX):
                slot = sel_ref[(2 * j + b) * NX + i]
                starts.append(pl.multiple_of(jnp.maximum(slot, 0) * BLOCK, BLOCK))
                biases.append(jnp.where(slot >= 0, 0.0, NEG))
            for h in range(heads):
                cols = pl.ds(h * HEAD, HEAD)
                query = q_ref[pl.ds(row, BLOCK), cols]
                scores = [
                    dot_nt(query, k_refs[i][pl.ds(starts[i], BLOCK), cols]) * SCALE2 + biases[i]
                    for i in range(NX)
                ]
                peak = jnp.maximum(
                    jnp.maximum(scores[0], scores[1]), jnp.maximum(scores[2], scores[3])
                )
                top = jnp.max(peak, axis=1, keepdims=True)
                weights = [jnp.exp2(s - top) for s in scores]
                total = jnp.sum(
                    (weights[0] + weights[1]) + (weights[2] + weights[3]), axis=1, keepdims=True
                )
                acc = None
                for i in range(NX):
                    part = dot_nn(
                        weights[i].astype(jnp.bfloat16), v_refs[i][pl.ds(starts[i], BLOCK), cols]
                    )
                    acc = part if acc is None else acc + part
                out_ref[pl.ds(row, BLOCK), cols] = (acc / total).astype(jnp.bfloat16)
                stat = jnp.where(lane == h, top + jnp.log2(total), stat)
            stat = stat.T[0:8]
            high = stat.astype(jnp.bfloat16)
            rest = stat - high.astype(jnp.float32)
            mid = rest.astype(jnp.bfloat16)
            low = rest - mid.astype(jnp.float32)
            packed = jnp.concatenate(
                [
                    high[0:4].astype(jnp.float32),
                    mid[0:4].astype(jnp.float32),
                    low[0:4],
                    jnp.zeros((4, BLOCK), jnp.float32),
                ],
                axis=0,
            )
            out_ref[2 * BLOCK : 2 * BLOCK + EXTRA, pl.ds(row, BLOCK)] = packed.astype(jnp.bfloat16)
        out_ref[2 * BLOCK : 2 * BLOCK + EXTRA, 2 * BLOCK :] = jnp.zeros(
            (EXTRA, out_ref.shape[1] - 2 * BLOCK), jnp.bfloat16
        )


def merge_kernel(gate_ref, local_ref, p0, p1, p2, p3, att_ref, att_t_ref):
    parts = (p0, p1, p2, p3)
    heads = local_ref.shape[1] // HEAD
    for b in range(2):
        rows = pl.ds(b * BLOCK, BLOCK)
        logs = []
        for p in parts:
            s = p[2 * BLOCK : 2 * BLOCK + EXTRA, rows].astype(jnp.float32)
            logs.append((s[0:4] + s[4:8]) + s[8:12])
        top = jnp.maximum(jnp.maximum(logs[0], logs[1]), jnp.maximum(logs[2], logs[3]))
        shares = [jnp.exp2(s - top) for s in logs]
        total = (shares[0] + shares[1]) + (shares[2] + shares[3])
        shares = [s / total for s in shares]
        table = jnp.concatenate(shares + [jnp.zeros((BLOCK - 16, BLOCK), jnp.float32)], axis=0).T
        for h in range(heads):
            cols = pl.ds(h * HEAD, HEAD)
            acc = None
            for n, p in enumerate(parts):
                term = p[rows, cols].astype(jnp.float32) * table[:, 4 * n + h : 4 * n + h + 1]
                acc = term if acc is None else acc + term
            out = gate_ref[h] * acc + local_ref[rows, cols]
            att_ref[rows, cols] = out.astype(jnp.bfloat16)
            att_t_ref[cols, rows] = out.T.astype(jnp.bfloat16)


def grad_kernel(ids_ref, *refs):
    own, other, w_ref, out_ref, acc_ref = refs[0:4], refs[4:8], refs[8], refs[9], refs[10]
    step = pl.program_id(0)
    zl, c = ids_ref[4], ids_ref[5]
    width = own[0].shape[1]
    rows = out_ref.shape[0]

    @pl.when(step == 0)
    def _():
        acc_ref[...] = jnp.zeros_like(acc_ref)

    for k in range(NY):

        @pl.when(step == k)
        def _(k=k):
            acc = acc_ref[...]
            for w, arrays in enumerate((own, other)):
                for s in range(2):
                    place = (zl ^ s) * 2 + (c ^ w)
                    cols = pl.ds(pl.multiple_of(place * width, 128), width)
                    acc = acc + dot_nt(arrays[k][s * rows : (s + 1) * rows, :], w_ref[:, cols])
            acc_ref[...] = acc

    @pl.when(step == NY - 1)
    def _():
        out_ref[...] = acc_ref[...].astype(jnp.bfloat16)


def weight_kernel(ids_ref, *refs):
    atts, own, other = refs[0:4], refs[4:8], refs[8:12]
    outs, att_scr = refs[12:16], refs[16]
    z, x, y, zl, c = ids_ref[0], ids_ref[1], ids_ref[2], ids_ref[4], ids_ref[5]
    rows = att_scr.shape[2]
    for j in range(NZ):
        att_scr[(z - j) & 3] = atts[j][...]
    for w, arrays in enumerate((own, other)):
        for s in range(2):
            acc = None
            for k in range(NY):
                block = arrays[k][(2 + s) * rows : (3 + s) * rows, :]
                part = dot_nn(att_scr[(y - k) & 3], block)
                acc = part if acc is None else acc + part
            target = (((zl ^ s) * 2 + (c ^ w)) - x) & 3

            for n in range(NX):

                @pl.when(target == n)
                def _(n=n, acc=acc):
                    outs[n][...] = acc.astype(outs[n].dtype)


def per_device(
    queries,
    local_keys,
    local_values,
    segments,
    memory_keys,
    memory_values,
    retrieved,
    block_slot,
    gate_bias,
    out_weight,
    cotangent,
):
    rows, width = queries.shape
    heads = width // HEAD
    mem, ten = lax.axis_index("mem"), lax.axis_index("tensor")
    z, x = mem // NX, mem % NX
    y, zl, c = ten // 4, (ten // 2) % 2, ten % 2
    ids = jnp.stack([z, x, y, jnp.zeros_like(z), zl, c]).astype(jnp.int32)
    gate = jax.nn.sigmoid(gate_bias)
    params = pltpu.CompilerParams(vmem_limit_bytes=48 << 20)

    names = jnp.arange(block_slot.shape[0], dtype=jnp.int32)
    storage = jnp.sum(
        jnp.where(retrieved.reshape(-1)[:, None] == names[None, :], block_slot[None, :], 0), axis=1
    )
    extra = jnp.zeros((EXTRA, width), jnp.bfloat16)
    extra = extra.at[0, 0 : storage.shape[0]].set(storage.astype(jnp.bfloat16))
    q_pack = jnp.concatenate([queries, extra], axis=0)

    k1, v3 = shift_x(memory_keys, 1), shift_x(memory_values, -1)
    k3, v1 = shift_x(memory_keys, -1), shift_x(memory_values, 1)
    k2, v2 = shift_x(k1, 1), shift_x(v3, -1)
    q_all = [q_pack] + [shift_z(q_pack, j) for j in (1, 2, 3)]

    stored = jnp.stack([q[rows, 0:16].astype(jnp.int32) for q in q_all]).reshape(8, 8)
    shards = z * NX + (x - jnp.arange(NX, dtype=jnp.int32)) % NX
    hit = (stored // SLOTS)[:, None, :] == shards[None, :, None]
    sel = (jnp.sum(jnp.where(hit, (stored % SLOTS)[:, None, :] + 1, 0), axis=2) - 1).reshape(-1)

    both = jnp.concatenate([cotangent, swap_zy(cotangent)], axis=0)
    pair = flip_tensor(both, 2)
    quad = jnp.concatenate([both[:rows], pair[:rows], both[rows:], pair[rows:]], axis=0)
    own = [quad] + [shift_y(quad, k) for k in (1, 2, 3)]
    other = [flip_tensor(a, 1) for a in own]

    local_out = pl.pallas_call(
        local_kernel,
        out_shape=jax.ShapeDtypeStruct((rows, width), jnp.float32),
        in_specs=[SM] + [VM] * 4,
        out_specs=VM,
        compiler_params=params,
        name="local_attention",
    )(gate, segments.reshape(1, rows), queries, local_keys, local_values)

    parts = pl.pallas_call(
        memory_kernel,
        out_shape=[jax.ShapeDtypeStruct((rows + EXTRA, width), jnp.bfloat16)] * 4,
        in_specs=[SM] + [VM] * 12,
        out_specs=[VM] * 4,
        compiler_params=params,
        name="memory_attention",
    )(sel, *q_all, memory_keys, k1, k2, k3, memory_values, v1, v2, v3)

    back = [parts[0]] + [shift_z(parts[j], -j) for j in (1, 2, 3)]
    attention, att_t = pl.pallas_call(
        merge_kernel,
        out_shape=[
            jax.ShapeDtypeStruct((rows, width), jnp.bfloat16),
            jax.ShapeDtypeStruct((width, rows), jnp.bfloat16),
        ],
        in_specs=[SM] + [VM] * 5,
        out_specs=[VM] * 2,
        compiler_params=params,
        name="merge",
    )(gate, local_out, *back)

    attention_grad = pl.pallas_call(
        grad_kernel,
        out_shape=jax.ShapeDtypeStruct((rows, width), jnp.bfloat16),
        grid_spec=pltpu.PrefetchScalarGridSpec(
            num_scalar_prefetch=1,
            grid=(NY,),
            in_specs=[pl.BlockSpec((4 * rows, width), lambda g, ids: (0, 0))] * 8
            + [pl.BlockSpec((width, 4 * width), lambda g, ids: (0, (ids[2] - g) & 3))],
            out_specs=pl.BlockSpec((rows, width), lambda g, ids: (0, 0)),
            scratch_shapes=[pltpu.VMEM((rows, width), jnp.float32)],
        ),
        compiler_params=params,
        name="attention_grad",
    )(ids, *own, *other, out_weight)

    att_all = [att_t] + [shift_z(att_t, j) for j in (1, 2, 3)]
    mine, *sent = pl.pallas_call(
        weight_kernel,
        out_shape=[jax.ShapeDtypeStruct((width, width), jnp.float32)]
        + [jax.ShapeDtypeStruct((width, width), jnp.bfloat16)] * 3,
        in_specs=[SM] + [VM] * 12,
        out_specs=[VM] * 4,
        scratch_shapes=[pltpu.VMEM((NZ, width, rows), jnp.bfloat16)],
        compiler_params=params,
        name="weight_partials",
    )(ids, *att_all, *own, *other)
    got = [shift_x(sent[n - 1], n) for n in (1, 2, 3)]
    weight_grad = (mine + got[0].astype(jnp.float32)) + (
        got[1].astype(jnp.float32) + got[2].astype(jnp.float32)
    )
    return (attention, attention_grad, weight_grad)


def solution(mesh):
    return jax.shard_map(
        per_device,
        mesh=mesh,
        in_specs=(
            P("mem", "tensor"),
            P("mem", "tensor"),
            P("mem", "tensor"),
            P("mem"),
            P("mem", "tensor"),
            P("mem", "tensor"),
            P("mem", None),
            P(),
            P("tensor"),
            P("tensor", None),
            P("mem", "tensor"),
        ),
        out_specs=(P("mem", "tensor"), P("mem", "tensor"), P("tensor", "mem")),
        check_vma=False,
    )
```

time: 339 us -> 180 us (0.53)
  waiting for transfers between devices: 212 us -> 76.4 us
  starting transfers between devices: 14.1 us -> 64.2 us
  local copies, waits for them, and re-layouts: 48 us -> 7.55 us
  Pallas kernels: 0 us -> 24.1 us
  matrix products: 22.6 us -> 0 us
  blocking collectives: 20.2 us -> 0 us
  between operations: 14.2 us -> 0.82 us
    all_to_all x2 -> x0, waiting for transfers between devices: 126 us -> none  [the longest x1 67.4 us: per_device(): lax.all_to_all(sent_keys, 'mem', split_axis=0, concat_axis=0, tiled=True)]
    unnamed x3 -> x0, waiting for transfers between devices: 86.4 us -> none
    ppermute x0 -> x27, waiting for transfers between devices: none -> 76.4 us  [the longest x9 59.7 us: shift_z(): return lax.ppermute(value, 'mem', pairs)]
    ppermute x0 -> x27, starting transfers between devices: none -> 64.2 us  [the longest x9 28.5 us: shift_z(): return lax.ppermute(value, 'mem', pairs)]
    pallas_call x0 -> x5, Pallas kernels: none -> 24.1 us  [the longest x1 9.47 us: per_device(): pl.pallas_call(memory_kernel, out_shape=[jax.ShapeDtypeStruct((rows + EXT...]
    dot_general x6 -> x0, matrix products: 21.1 us -> none  [the longest x1 5.49 us: per_device(): jnp.einsum('td,tc->dc', attention, lax.all_gather(cotangent, 'tensor', ax...]
    all_to_all x1 -> x0, blocking collectives: 20.2 us -> none  [per_device(): lax.all_to_all(requests, 'mem', split_axis=0, concat_axis=0, tiled=True)]
    gather x8 -> x0, local copies, waits for them, and re-layouts: 15 us -> none  [the longest x1 3.83 us: per_device(): buffer_keys[position]]
  transfers between devices with their start and end apart: 4 -> 27, of which waited for: 3 -> 11; matrix products, arithmetic and copies ran while one was open for 16% -> 2% of each run, Pallas kernels for 0% -> 11%
where the time goes in v1:
time: 180 us; the launch traced here: 177 us
  waiting for transfers between devices  76.4 us (42%)
  starting transfers between devices  64.2 us (36%)
  Pallas kernels  24.1 us (13%)
  local copies, waits for them, and re-layouts  7.55 us (4%)
  other arithmetic  4.05 us (2%)
    ppermute x9, waiting for transfers between devices, shift_z(): return lax.ppermute(value, 'mem', pairs)  59.7 us
    ppermute x9, starting transfers between devices, shift_z(): return lax.ppermute(value, 'mem', pairs)  28.5 us
    ppermute x9, waiting for transfers between devices, shift_x(): return lax.ppermute(value, 'mem', pairs)  16.6 us
    ppermute x5, starting transfers between devices, flip_tensor(): return lax.ppermute(value, 'tensor', [(t, t ^ bit) for t in range(16)])  14.4 us
    ppermute x9, starting transfers between devices, shift_x(): return lax.ppermute(value, 'mem', pairs)  12.1 us
    pallas_call x1, Pallas kernels, per_device(): pl.pallas_call(memory_kernel, out_shape=[jax.ShapeDtypeStruct((rows + EXT...  9.47 us
    ppermute x3, starting transfers between devices, shift_y(): return lax.ppermute(value, 'tensor', pairs)  7.48 us
    pallas_call x1, Pallas kernels, per_device(): pl.pallas_call(grad_kernel, out_shape=jax.ShapeDtypeStruct((rows, width),...  6.86 us
  transfers between devices with their start and end apart: 27, of which 11 were waited for; matrix products, arithmetic and copies ran while one was open for 2% of the time, Pallas kernels for 11%

profile of v1, /device:TPU:1, one launch (start us, length us, event | category | flops | bytes accessed | tf_op | source)
XLA Modules:
  0.0 177.1 jit_solution(16133017682772089075)
XLA Ops:
  0.6 0.0 copy-start.14
  0.6 1.7 collective-permute-start.12
  2.4 0.8 eq.36
  3.1 0.8 select_reduce_fusion.1
  4.0 1.0 pad_maximum_fusion.1
  4.9 2.6 %collective-permute-start.13 = (bf16[512,384]{1,0:T(8,128)(2,1)S(1)}, bf16[512,384]{1,0:T(8,128)(2,1)S(1)}, u32[]{:S(2)}, u32[]{:S(2)}) collective-permute-start(bf16[512,384]{1,0:T(8,128)(2,1)S(1)} %pad_maximum_fusion.1), channel_id=1, source_target_pairs={{0,2},{1,3},{2,0},{3,1},{4,6},{5,7},{6,4},{7,5},{8,10},{9,11},{10,... | collective-permute-start | bytes 1179656 | tf_op jit(solution)/shard_map/ppermute | solution.py:47
  7.5 0.9 fusion.1.refs_0_
  8.4 19.0 %collective-permute-start = (bf16[272,384]{1,0:T(8,128)(2,1)S(1)}, bf16[272,384]{1,0:T(8,128)(2,1)S(1)}, u32[]{:S(2)}, u32[]{:S(2)}) collective-permute-start(bf16[272,384]{1,0:T(8,128)(2,1)S(1)} %fusion.1.refs_0_), channel_id=1, source_target_pairs={{0,64},{16,80},{32,96},{48,112},{64,128},{80,144},{96,160},{112,17... | collective-permute-start | bytes 626696 | tf_op jit(solution)/shard_map/ppermute | solution.py:38
  27.4 5.5 %collective-permute-start.1 = (bf16[272,384]{1,0:T(8,128)(2,1)S(1)}, bf16[272,384]{1,0:T(8,128)(2,1)S(1)}, u32[]{:S(2)}, u32[]{:S(2)}) collective-permute-start(bf16[272,384]{1,0:T(8,128)(2,1)S(1)} %fusion.1.refs_0_), channel_id=1, source_target_pairs={{0,128},{16,144},{32,160},{48,176},{64,192},{80,208},{96,224},{112... | collective-permute-start | bytes 626696 | tf_op jit(solution)/shard_map/ppermute | solution.py:38
  32.9 0.0 collective-permute-start.2
  32.9 1.2 collective-permute-start.3
  34.1 17.6 %collective-permute-done.refs_1_ = bf16[272,384]{1,0:T(8,128)(2,1)S(1)} collective-permute-done((bf16[272,384]{1,0:T(8,128)(2,1)S(1)}, bf16[272,384]{1,0:T(8,128)(2,1)S(1)}, u32[]{:S(2)}, u32[]{:S(2)}) %collective-permute-start) | collective-permute-done | bytes 208928 | tf_op jit(solution)/shard_map/ppermute | solution.py:38
  51.7 2.5 %collective-permute-start.7 = (bf16[512,384]{1,0:T(8,128)(2,1)}, bf16[512,384]{1,0:T(8,128)(2,1)}, u32[]{:S(2)}, u32[]{:S(2)}) collective-permute-start(bf16[512,384]{1,0:T(8,128)(2,1)} %refs_8_.2), channel_id=1, source_target_pairs={{0,48},{16,0},{32,16},{48,32},{64,112},{80,64},{96,80},{112,96},{1... | collective-permute-start | bytes 1179656 | tf_op jit(solution)/shard_map/ppermute | solution.py:33
  54.2 0.0 collective-permute-done.1.refs_2_
  54.2 0.6 collective-permute-start.5
  54.9 0.0 collective-permute-done.2.refs_3_
  54.9 0.9 collective-permute-start.6
  55.9 0.1 pad_maximum_fusion.refs_0_.refs_4_
  56.0 5.0 %collective-permute-start.14 = (bf16[1024,384]{1,0:T(8,128)(2,1)S(1)}, bf16[1024,384]{1,0:T(8,128)(2,1)S(1)}, u32[]{:S(2)}, u32[]{:S(2)}) collective-permute-start(bf16[1024,384]{1,0:T(8,128)(2,1)S(1)} %pad_maximum_fusion.refs_0_.refs_4_), channel_id=1, source_target_pairs={{0,4},{1,5},{2,6},{3,7},{4,8},{5,9},{6,10},{7,11},{8,12},{9,13},{1... | collective-permute-start | bytes 2359304 | tf_op jit(solution)/shard_map/ppermute | solution.py:43
  61.0 1.0 collective-permute-start.15
  61.9 1.5 collective-permute-start.16
  63.5 0.1 reshape.132
  63.5 5.1 %collective-permute-done.5.refs_7_ = bf16[512,384]{1,0:T(8,128)(2,1)} collective-permute-done((bf16[512,384]{1,0:T(8,128)(2,1)}, bf16[512,384]{1,0:T(8,128)(2,1)}, u32[]{:S(2)}, u32[]{:S(2)}) %collective-permute-start.5) | collective-permute-done | bytes 393248 | tf_op jit(solution)/shard_map/ppermute | solution.py:33
  68.6 0.9 collective-permute-start.4
  69.6 2.5 %collective-permute-start.8 = (bf16[512,384]{1,0:T(8,128)(2,1)}, bf16[512,384]{1,0:T(8,128)(2,1)}, u32[]{:S(2)}, u32[]{:S(2)}) collective-permute-start(bf16[512,384]{1,0:T(8,128)(2,1)} %collective-permute-done.7.refs_11_), channel_id=1, source_target_pairs={{0,48},{16,0},{32,16},{48,32},{64,112},{80,64},{96,80},{112,96},{1... | collective-permute-start | bytes 1179656 | tf_op jit(solution)/shard_map/ppermute | solution.py:33
  72.1 0.2 select_reduce_fusion
  72.3 0.1 copy.14
  72.4 0.1 sub.37.sel_ref
  72.5 5.7 %collective-permute-done.4.refs_6_ = bf16[512,384]{1,0:T(8,128)(2,1)} collective-permute-done((bf16[512,384]{1,0:T(8,128)(2,1)}, bf16[512,384]{1,0:T(8,128)(2,1)}, u32[]{:S(2)}, u32[]{:S(2)}) %collective-permute-start.4) | collective-permute-done | bytes 393248 | tf_op jit(solution)/shard_map/ppermute | solution.py:33
  78.2 0.0 collective-permute-done.8.refs_10_
  78.2 1.0 copy-done.1
  79.2 1.0 copy-done.2
  80.2 0.9 copy-done.4
  81.1 0.9 copy-done.6
  82.0 0.9 copy-done.8
  83.0 9.5 %memory_attention.1 = (bf16[272,384]{1,0:T(8,128)(2,1)S(1)}, bf16[272,384]{1,0:T(8,128)(2,1)S(1)}, bf16[272,384]{1,0:T(8,128)(2,1)S(1)}, bf16[272,384]{1,0:T(8,128)(2,1)S(1)}) custom-call(s32[32]{0:T(128)S(1)} %sub.37.sel_ref, bf16[272,384]{1,0:T(8,128)(2,1)S(1)} %fusion.1.refs_0_, bf16[272,384]{1,0:T(8,128)(2,1)S(1)} %copy-done.4, ...), custom_call_target="tpu_custom_call" | custom-call | tf_op jit(solution)/shard_map/memory_attention/pallas_call | solution.py:267
  92.4 0.4 collective-permute-start.10
  92.8 1.3 collective-permute-start.11
  94.1 9.8 %collective-permute-done.10.p2 = bf16[272,384]{1,0:T(8,128)(2,1)S(1)} collective-permute-done((bf16[272,384]{1,0:T(8,128)(2,1)S(1)}, bf16[272,384]{1,0:T(8,128)(2,1)S(1)}, u32[]{:S(2)}, u32[]{:S(2)}) %collective-permute-start.10) | collective-permute-done | bytes 208928 | tf_op jit(solution)/shard_map/ppermute | solution.py:38
  103.9 8.6 %collective-permute-start.17 = (bf16[1024,384]{1,0:T(8,128)(2,1)S(1)}, bf16[1024,384]{1,0:T(8,128)(2,1)}, u32[]{:S(2)}, u32[]{:S(2)}) collective-permute-start(bf16[1024,384]{1,0:T(8,128)(2,1)S(1)} %pad_maximum_fusion.refs_0_.refs_4_), channel_id=1, source_target_pairs={{0,1},{1,0},{2,3},{3,2},{4,5},{5,4},{6,7},{7,6},{8,9},{9,8},{10,11... | collective-permute-start | bytes 2359304 | tf_op jit(solution)/shard_map/ppermute | solution.py:47
  112.5 0.3 collective-permute-done.11.p3
  112.8 2.8 %collective-permute-start.18 = (bf16[1024,384]{1,0:T(8,128)(2,1)S(1)}, bf16[1024,384]{1,0:T(8,128)(2,1)}, u32[]{:S(2)}, u32[]{:S(2)}) collective-permute-start(bf16[1024,384]{1,0:T(8,128)(2,1)S(1)} %collective-permute-done.14.refs_1_.refs_5_), channel_id=1, source_target_pairs={{0,1},{1,0},{2,3},{3,2},{4,5},{5,4},{6,7},{7,6},{8,9},{9,8},{10,11... | collective-permute-start | bytes 2359304 | tf_op jit(solution)/shard_map/ppermute | solution.py:47
  115.6 0.1 collective-permute-start.19
  115.7 0.4 collective-permute-start.20
  116.2 1.4 local_attention.1.local_ref
  117.5 0.9 collective-permute-done.9.p1
  118.4 2.1 %merge.1 = (bf16[256,384]{1,0:T(8,128)(2,1)}, bf16[384,256]{1,0:T(8,128)(2,1)S(1)}) custom-call(f32[3]{0:T(128)S(1)} %add_divide_fusion.gate_ref, f32[256,384]{1,0:T(8,128)S(1)} %local_attention.1.local_ref, bf16[272,384]{1,0:T(8,128)(2,1)S(1)} %get-tuple-element.25.p0, bf16[272,384]{1,0:T(8,128)(2,1)S(1)} %collective-permute-done.9.p1, ...), custom_call_target="tpu_custom_call" | custom-call | tf_op jit(solution)/shard_map/merge/pallas_call | solution.py:277
  120.5 0.7 collective-permute-start.21
  121.2 6.5 %collective-permute-done.21.refs_1_ = bf16[384,256]{1,0:T(8,128)(2,1)S(1)} collective-permute-done((bf16[384,256]{1,0:T(8,128)(2,1)S(1)}, bf16[384,256]{1,0:T(8,128)(2,1)S(1)}, u32[]{:S(2)}, u32[]{:S(2)}) %collective-permute-start.21) | collective-permute-done | bytes 196640 | tf_op jit(solution)/shard_map/ppermute | solution.py:38
  127.7 1.7 collective-permute-start.22
  129.3 13.9 %collective-permute-done.22.refs_2_ = bf16[384,256]{1,0:T(8,128)(2,1)S(1)} collective-permute-done((bf16[384,256]{1,0:T(8,128)(2,1)S(1)}, bf16[384,256]{1,0:T(8,128)(2,1)S(1)}, u32[]{:S(2)}, u32[]{:S(2)}) %collective-permute-start.22) | collective-permute-done | bytes 196640 | tf_op jit(solution)/shard_map/ppermute | solution.py:38
  143.2 0.7 copy-done.9
  143.9 0.0 collective-permute-start.23
  143.9 0.1 stack.32.ids_ref
  144.0 10.8 %collective-permute-done.23.refs_3_ = bf16[384,256]{1,0:T(8,128)(2,1)} collective-permute-done((bf16[384,256]{1,0:T(8,128)(2,1)S(1)}, bf16[384,256]{1,0:T(8,128)(2,1)}, u32[]{:S(2)}, u32[]{:S(2)}) %collective-permute-start.23) | collective-permute-done | bytes 196640 | tf_op jit(solution)/shard_map/ppermute | solution.py:38
  154.8 0.0 copy-start.10
  154.8 0.9 copy-done.10
  155.7 4.4 %weight_partials.1 = (f32[384,384]{1,0:T(8,128)S(1)}, bf16[384,384]{1,0:T(8,128)(2,1)S(1)}, bf16[384,384]{1,0:T(8,128)(2,1)S(1)}, bf16[384,384]{1,0:T(8,128)(2,1)S(1)}) custom-call(s32[6]{0:T(128)S(1)} %stack.32.ids_ref, bf16[384,256]{1,0:T(8,128)(2,1)S(1)} %get-tuple-element.30.refs_0_, bf16[384,256]{1,0:T(8,128)(2,1)S(1)} %collective-permute-done.21.refs_1_, ...), custom_call_target="tpu_custom_call" | custom-call | tf_op jit(solution)/shard_map/weight_partials/pallas_call | solution.py:305
  160.1 0.9 collective-permute-start.24
  161.0 2.5 %collective-permute-start.26 = (bf16[384,384]{1,0:T(8,128)(2,1)S(1)}, bf16[384,384]{1,0:T(8,128)(2,1)S(1)}, u32[]{:S(2)}, u32[]{:S(2)}) collective-permute-start(bf16[384,384]{1,0:T(8,128)(2,1)S(1)} %get-tuple-element.34), channel_id=1, source_target_pairs={{0,48},{16,0},{32,16},{48,32},{64,112},{80,64},{96,80},{112,96},{1... | collective-permute-start | bytes 884744 | tf_op jit(solution)/shard_map/ppermute | solution.py:33
  163.5 6.9 %attention_grad.1 = bf16[256,384]{1,0:T(8,128)(2,1)} custom-call(s32[6]{0:T(128)S(1)} %stack.32.ids_ref, bf16[1024,384]{1,0:T(8,128)(2,1)S(1)} %pad_maximum_fusion.refs_0_.refs_4_, bf16[1024,384]{1,0:T(8,128)(2,1)S(1)} %collective-permute-done.14.refs_1_.refs_5_, bf16[1024,384]{1,0:T(8,128)(2,1)S(1)} %collective-permute-done.15.refs_2_.refs_6_, ...), custom_call_target="tpu_custom_call" | custom-call | tf_op jit(solution)/shard_map/attention_grad/pallas_call | solution.py:289
  170.4 4.9 %collective-permute-done.24 = bf16[384,384]{1,0:T(8,128)(2,1)S(1)} collective-permute-done((bf16[384,384]{1,0:T(8,128)(2,1)S(1)}, bf16[384,384]{1,0:T(8,128)(2,1)S(1)}, u32[]{:S(2)}, u32[]{:S(2)}) %collective-permute-start.24) | collective-permute-done | bytes 294944 | tf_op jit(solution)/shard_map/ppermute | solution.py:33
  175.3 0.9 collective-permute-done.26
  176.2 0.9 add_add_fusion
  (48 shorter events, 0.2 us)
Async XLA Ops:
  0.6 55.2 %copy-start.14 = (bf16[256,384]{1,0:T(8,128)(2,1)S(1)}, bf16[256,384]{1,0:T(8,128)(2,1)}, u32[]{:S(2)}) copy-start(bf16[256,384]{1,0:T(8,128)(2,1)} %param.23) | copy-start | bytes 589828
  0.6 3.3 %collective-permute-start.12 = (bf16[256,384]{1,0:T(8,128)(2,1)}, bf16[256,384]{1,0:T(8,128)(2,1)S(1)}, u32[]{:S(2)}, u32[]{:S(2)}) collective-permute-start(bf16[256,384]{1,0:T(8,128)(2,1)} %param.23), channel_id=1, source_target_pairs={{0,0},{1,1},{2,2},{3,3},{4,64},{5,65},{6,66},{7,67},{8,128},{9,129... | collective-permute-start | bytes 589832 | tf_op jit(solution)/shard_map/ppermute | solution.py:57
  4.9 50.9 %collective-permute-start.13 = (bf16[512,384]{1,0:T(8,128)(2,1)S(1)}, bf16[512,384]{1,0:T(8,128)(2,1)S(1)}, u32[]{:S(2)}, u32[]{:S(2)}) collective-permute-start(bf16[512,384]{1,0:T(8,128)(2,1)S(1)} %pad_maximum_fusion.1), channel_id=1, source_target_pairs={{0,2},{1,3},{2,0},{3,1},{4,6},{5,7},{6,4},{7,5},{8,10},{9,11},{10,... | collective-permute-start | bytes 1179656 | tf_op jit(solution)/shard_map/ppermute | solution.py:47
  8.4 43.3 %collective-permute-start = (bf16[272,384]{1,0:T(8,128)(2,1)S(1)}, bf16[272,384]{1,0:T(8,128)(2,1)S(1)}, u32[]{:S(2)}, u32[]{:S(2)}) collective-permute-start(bf16[272,384]{1,0:T(8,128)(2,1)S(1)} %fusion.1.refs_0_), channel_id=1, source_target_pairs={{0,64},{16,80},{32,96},{48,112},{64,128},{80,144},{96,160},{112,17... | collective-permute-start | bytes 626696 | tf_op jit(solution)/shard_map/ppermute | solution.py:38
  27.4 26.8 %collective-permute-start.1 = (bf16[272,384]{1,0:T(8,128)(2,1)S(1)}, bf16[272,384]{1,0:T(8,128)(2,1)S(1)}, u32[]{:S(2)}, u32[]{:S(2)}) collective-permute-start(bf16[272,384]{1,0:T(8,128)(2,1)S(1)} %fusion.1.refs_0_), channel_id=1, source_target_pairs={{0,128},{16,144},{32,160},{48,176},{64,192},{80,208},{96,224},{112... | collective-permute-start | bytes 626696 | tf_op jit(solution)/shard_map/ppermute | solution.py:38
  32.9 22.0 %collective-permute-start.2 = (bf16[272,384]{1,0:T(8,128)(2,1)S(1)}, bf16[272,384]{1,0:T(8,128)(2,1)S(1)}, u32[]{:S(2)}, u32[]{:S(2)}) collective-permute-start(bf16[272,384]{1,0:T(8,128)(2,1)S(1)} %fusion.1.refs_0_), channel_id=1, source_target_pairs={{0,192},{16,208},{32,224},{48,240},{64,0},{80,16},{96,32},{112,48}... | collective-permute-start | bytes 626696 | tf_op jit(solution)/shard_map/ppermute | solution.py:38
  32.9 28.0 %collective-permute-start.3 = (bf16[512,384]{1,0:T(8,128)(2,1)}, bf16[512,384]{1,0:T(8,128)(2,1)}, u32[]{:S(2)}, u32[]{:S(2)}) collective-permute-start(bf16[512,384]{1,0:T(8,128)(2,1)} %refs_4_.1), channel_id=1, source_target_pairs={{0,16},{16,32},{32,48},{48,0},{64,80},{80,96},{96,112},{112,64},{1... | collective-permute-start | bytes 1179656 | tf_op jit(solution)/shard_map/ppermute | solution.py:33
  51.7 4.1 %copy-start.3 = (bf16[272,384]{1,0:T(8,128)(2,1)}, bf16[272,384]{1,0:T(8,128)(2,1)S(1)}, u32[]{:S(2)}) copy-start(bf16[272,384]{1,0:T(8,128)(2,1)S(1)} %collective-permute-done.refs_1_) | copy-start | bytes 626692
  51.7 10.2 %collective-permute-start.7 = (bf16[512,384]{1,0:T(8,128)(2,1)}, bf16[512,384]{1,0:T(8,128)(2,1)}, u32[]{:S(2)}, u32[]{:S(2)}) collective-permute-start(bf16[512,384]{1,0:T(8,128)(2,1)} %refs_8_.2), channel_id=1, source_target_pairs={{0,48},{16,0},{32,16},{48,32},{64,112},{80,64},{96,80},{112,96},{1... | collective-permute-start | bytes 1179656 | tf_op jit(solution)/shard_map/ppermute | solution.py:33
  54.2 1.6 copy-start.5
  54.2 14.4 %collective-permute-start.5 = (bf16[512,384]{1,0:T(8,128)(2,1)}, bf16[512,384]{1,0:T(8,128)(2,1)}, u32[]{:S(2)}, u32[]{:S(2)}) collective-permute-start(bf16[512,384]{1,0:T(8,128)(2,1)} %refs_4_.1), channel_id=1, source_target_pairs={{0,48},{16,0},{32,16},{48,32},{64,112},{80,64},{96,80},{112,96},{1... | collective-permute-start | bytes 1179656 | tf_op jit(solution)/shard_map/ppermute | solution.py:33
  54.9 1.0 copy-start.7
  54.9 14.7 %collective-permute-start.6 = (bf16[512,384]{1,0:T(8,128)(2,1)}, bf16[512,384]{1,0:T(8,128)(2,1)}, u32[]{:S(2)}, u32[]{:S(2)}) collective-permute-start(bf16[512,384]{1,0:T(8,128)(2,1)} %refs_8_.2), channel_id=1, source_target_pairs={{0,16},{16,32},{32,48},{48,0},{64,80},{80,96},{96,112},{112,64},{1... | collective-permute-start | bytes 1179656 | tf_op jit(solution)/shard_map/ppermute | solution.py:33
  56.0 56.9 %collective-permute-start.14 = (bf16[1024,384]{1,0:T(8,128)(2,1)S(1)}, bf16[1024,384]{1,0:T(8,128)(2,1)S(1)}, u32[]{:S(2)}, u32[]{:S(2)}) collective-permute-start(bf16[1024,384]{1,0:T(8,128)(2,1)S(1)} %pad_maximum_fusion.refs_0_.refs_4_), channel_id=1, source_target_pairs={{0,4},{1,5},{2,6},{3,7},{4,8},{5,9},{6,10},{7,11},{8,12},{9,13},{1... | collective-permute-start | bytes 2359304 | tf_op jit(solution)/shard_map/ppermute | solution.py:43
  61.0 54.7 %collective-permute-start.15 = (bf16[1024,384]{1,0:T(8,128)(2,1)S(1)}, bf16[1024,384]{1,0:T(8,128)(2,1)S(1)}, u32[]{:S(2)}, u32[]{:S(2)}) collective-permute-start(bf16[1024,384]{1,0:T(8,128)(2,1)S(1)} %pad_maximum_fusion.refs_0_.refs_4_), channel_id=1, source_target_pairs={{0,8},{1,9},{2,10},{3,11},{4,12},{5,13},{6,14},{7,15},{8,0},{9,1},... | collective-permute-start | bytes 2359304 | tf_op jit(solution)/shard_map/ppermute | solution.py:43
  61.9 53.8 %collective-permute-start.16 = (bf16[1024,384]{1,0:T(8,128)(2,1)S(1)}, bf16[1024,384]{1,0:T(8,128)(2,1)S(1)}, u32[]{:S(2)}, u32[]{:S(2)}) collective-permute-start(bf16[1024,384]{1,0:T(8,128)(2,1)S(1)} %pad_maximum_fusion.refs_0_.refs_4_), channel_id=1, source_target_pairs={{0,12},{1,13},{2,14},{3,15},{4,0},{5,1},{6,2},{7,3},{8,4},{9,5},{1... | collective-permute-start | bytes 2359304 | tf_op jit(solution)/shard_map/ppermute | solution.py:43
  68.6 9.5 %collective-permute-start.4 = (bf16[512,384]{1,0:T(8,128)(2,1)}, bf16[512,384]{1,0:T(8,128)(2,1)}, u32[]{:S(2)}, u32[]{:S(2)}) collective-permute-start(bf16[512,384]{1,0:T(8,128)(2,1)} %collective-permute-done.3.refs_5_), channel_id=1, source_target_pairs={{0,16},{16,32},{32,48},{48,0},{64,80},{80,96},{96,112},{112,64},{1... | collective-permute-start | bytes 1179656 | tf_op jit(solution)/shard_map/ppermute | solution.py:33
  69.6 8.6 %collective-permute-start.8 = (bf16[512,384]{1,0:T(8,128)(2,1)}, bf16[512,384]{1,0:T(8,128)(2,1)}, u32[]{:S(2)}, u32[]{:S(2)}) collective-permute-start(bf16[512,384]{1,0:T(8,128)(2,1)} %collective-permute-done.7.refs_11_), channel_id=1, source_target_pairs={{0,48},{16,0},{32,16},{48,32},{64,112},{80,64},{96,80},{112,96},{1... | collective-permute-start | bytes 1179656 | tf_op jit(solution)/shard_map/ppermute | solution.py:33
  72.4 43.7 %copy-start.15 = (f32[3]{0:T(128)S(1)}, f32[3]{0:T(128)}, u32[]{:S(2)}) copy-start(f32[3]{0:T(128)} %param.21) | copy-start | bytes 40
  72.4 43.8 %copy-start.13 = (s32[256]{0:T(256)S(1)}, s32[256]{0:T(256)}, u32[]{:S(2)}) copy-start(s32[256]{0:T(256)} %param.16) | copy-start | bytes 3076
  72.5 43.7 %copy-start = (bf16[256,384]{1,0:T(8,128)(2,1)S(1)}, bf16[256,384]{1,0:T(8,128)(2,1)}, u32[]{:S(2)}) copy-start(bf16[256,384]{1,0:T(8,128)(2,1)} %q_ref.1) | copy-start | bytes 589828
  78.2 1.0 copy-start.1
  79.2 1.0 copy-start.2
  80.2 0.9 copy-start.4
  81.1 0.9 copy-start.6
  82.0 0.9 copy-start.8
  83.0 33.2 %copy-start.11 = (bf16[256,384]{1,0:T(8,128)(2,1)S(1)}, bf16[256,384]{1,0:T(8,128)(2,1)}, u32[]{:S(2)}) copy-start(bf16[256,384]{1,0:T(8,128)(2,1)} %k_ref.1) | copy-start | bytes 589828
  83.0 33.2 %copy-start.12 = (bf16[256,384]{1,0:T(8,128)(2,1)S(1)}, bf16[256,384]{1,0:T(8,128)(2,1)}, u32[]{:S(2)}) copy-start(bf16[256,384]{1,0:T(8,128)(2,1)} %v_ref.1) | copy-start | bytes 589828
  92.4 11.5 %collective-permute-start.10 = (bf16[272,384]{1,0:T(8,128)(2,1)S(1)}, bf16[272,384]{1,0:T(8,128)(2,1)S(1)}, u32[]{:S(2)}, u32[]{:S(2)}) collective-permute-start(bf16[272,384]{1,0:T(8,128)(2,1)S(1)} %get-tuple-element.27), channel_id=1, source_target_pairs={{0,128},{16,144},{32,160},{48,176},{64,192},{80,208},{96,224},{112... | collective-permute-start | bytes 626696 | tf_op jit(solution)/shard_map/ppermute | solution.py:38
  92.8 20.0 %collective-permute-start.11 = (bf16[272,384]{1,0:T(8,128)(2,1)S(1)}, bf16[272,384]{1,0:T(8,128)(2,1)S(1)}, u32[]{:S(2)}, u32[]{:S(2)}) collective-permute-start(bf16[272,384]{1,0:T(8,128)(2,1)S(1)} %get-tuple-element.28), channel_id=1, source_target_pairs={{0,64},{16,80},{32,96},{48,112},{64,128},{80,144},{96,160},{112,17... | collective-permute-start | bytes 626696 | tf_op jit(solution)/shard_map/ppermute | solution.py:38
  103.9 50.9 %collective-permute-start.17 = (bf16[1024,384]{1,0:T(8,128)(2,1)S(1)}, bf16[1024,384]{1,0:T(8,128)(2,1)}, u32[]{:S(2)}, u32[]{:S(2)}) collective-permute-start(bf16[1024,384]{1,0:T(8,128)(2,1)S(1)} %pad_maximum_fusion.refs_0_.refs_4_), channel_id=1, source_target_pairs={{0,1},{1,0},{2,3},{3,2},{4,5},{5,4},{6,7},{7,6},{8,9},{9,8},{10,11... | collective-permute-start | bytes 2359304 | tf_op jit(solution)/shard_map/ppermute | solution.py:47
  112.8 5.6 %collective-permute-start.9 = (bf16[272,384]{1,0:T(8,128)(2,1)S(1)}, bf16[272,384]{1,0:T(8,128)(2,1)S(1)}, u32[]{:S(2)}, u32[]{:S(2)}) collective-permute-start(bf16[272,384]{1,0:T(8,128)(2,1)S(1)} %get-tuple-element.26), channel_id=1, source_target_pairs={{0,192},{16,208},{32,224},{48,240},{64,0},{80,16},{96,32},{112,48}... | collective-permute-start | bytes 626696 | tf_op jit(solution)/shard_map/ppermute | solution.py:38
  112.8 42.0 %collective-permute-start.18 = (bf16[1024,384]{1,0:T(8,128)(2,1)S(1)}, bf16[1024,384]{1,0:T(8,128)(2,1)}, u32[]{:S(2)}, u32[]{:S(2)}) collective-permute-start(bf16[1024,384]{1,0:T(8,128)(2,1)S(1)} %collective-permute-done.14.refs_1_.refs_5_), channel_id=1, source_target_pairs={{0,1},{1,0},{2,3},{3,2},{4,5},{5,4},{6,7},{7,6},{8,9},{9,8},{10,11... | collective-permute-start | bytes 2359304 | tf_op jit(solution)/shard_map/ppermute | solution.py:47
  115.6 39.2 %collective-permute-start.19 = (bf16[1024,384]{1,0:T(8,128)(2,1)S(1)}, bf16[1024,384]{1,0:T(8,128)(2,1)}, u32[]{:S(2)}, u32[]{:S(2)}) collective-permute-start(bf16[1024,384]{1,0:T(8,128)(2,1)S(1)} %collective-permute-done.15.refs_2_.refs_6_), channel_id=1, source_target_pairs={{0,1},{1,0},{2,3},{3,2},{4,5},{5,4},{6,7},{7,6},{8,9},{9,8},{10,11... | collective-permute-start | bytes 2359304 | tf_op jit(solution)/shard_map/ppermute | solution.py:47
  115.7 39.1 %collective-permute-start.20 = (bf16[1024,384]{1,0:T(8,128)(2,1)S(1)}, bf16[1024,384]{1,0:T(8,128)(2,1)}, u32[]{:S(2)}, u32[]{:S(2)}) collective-permute-start(bf16[1024,384]{1,0:T(8,128)(2,1)S(1)} %collective-permute-done.16.refs_3_.refs_7_), channel_id=1, source_target_pairs={{0,1},{1,0},{2,3},{3,2},{4,5},{5,4},{6,7},{7,6},{8,9},{9,8},{10,11... | collective-permute-start | bytes 2359304 | tf_op jit(solution)/shard_map/ppermute | solution.py:47
  120.5 7.2 %collective-permute-start.21 = (bf16[384,256]{1,0:T(8,128)(2,1)S(1)}, bf16[384,256]{1,0:T(8,128)(2,1)S(1)}, u32[]{:S(2)}, u32[]{:S(2)}) collective-permute-start(bf16[384,256]{1,0:T(8,128)(2,1)S(1)} %get-tuple-element.30.refs_0_), channel_id=1, source_target_pairs={{0,64},{16,80},{32,96},{48,112},{64,128},{80,144},{96,160},{112,17... | collective-permute-start | bytes 589832 | tf_op jit(solution)/shard_map/ppermute | solution.py:38
  127.7 15.5 %collective-permute-start.22 = (bf16[384,256]{1,0:T(8,128)(2,1)S(1)}, bf16[384,256]{1,0:T(8,128)(2,1)S(1)}, u32[]{:S(2)}, u32[]{:S(2)}) collective-permute-start(bf16[384,256]{1,0:T(8,128)(2,1)S(1)} %get-tuple-element.30.refs_0_), channel_id=1, source_target_pairs={{0,128},{16,144},{32,160},{48,176},{64,192},{80,208},{96,224},{112... | collective-permute-start | bytes 589832 | tf_op jit(solution)/shard_map/ppermute | solution.py:38
  143.2 0.7 copy-start.9
  143.9 10.9 %collective-permute-start.23 = (bf16[384,256]{1,0:T(8,128)(2,1)S(1)}, bf16[384,256]{1,0:T(8,128)(2,1)}, u32[]{:S(2)}, u32[]{:S(2)}) collective-permute-start(bf16[384,256]{1,0:T(8,128)(2,1)S(1)} %get-tuple-element.30.refs_0_), channel_id=1, source_target_pairs={{0,192},{16,208},{32,224},{48,240},{64,0},{80,16},{96,32},{112,48}... | collective-permute-start | bytes 589832 | tf_op jit(solution)/shard_map/ppermute | solution.py:38
  154.8 0.9 copy-start.10
  160.1 15.2 %collective-permute-start.24 = (bf16[384,384]{1,0:T(8,128)(2,1)S(1)}, bf16[384,384]{1,0:T(8,128)(2,1)S(1)}, u32[]{:S(2)}, u32[]{:S(2)}) collective-permute-start(bf16[384,384]{1,0:T(8,128)(2,1)S(1)} %get-tuple-element.32), channel_id=1, source_target_pairs={{0,16},{16,32},{32,48},{48,0},{64,80},{80,96},{96,112},{112,64},{1... | collective-permute-start | bytes 884744 | tf_op jit(solution)/shard_map/ppermute | solution.py:33
  161.0 14.2 %collective-permute-start.25 = (bf16[384,384]{1,0:T(8,128)(2,1)S(1)}, bf16[384,384]{1,0:T(8,128)(2,1)S(1)}, u32[]{:S(2)}, u32[]{:S(2)}) collective-permute-start(bf16[384,384]{1,0:T(8,128)(2,1)S(1)} %get-tuple-element.33), channel_id=1, source_target_pairs={{0,32},{16,48},{32,0},{48,16},{64,96},{80,112},{96,64},{112,80},{1... | collective-permute-start | bytes 884744 | tf_op jit(solution)/shard_map/ppermute | solution.py:33
  161.0 15.2 %collective-permute-start.26 = (bf16[384,384]{1,0:T(8,128)(2,1)S(1)}, bf16[384,384]{1,0:T(8,128)(2,1)S(1)}, u32[]{:S(2)}, u32[]{:S(2)}) collective-permute-start(bf16[384,384]{1,0:T(8,128)(2,1)S(1)} %get-tuple-element.34), channel_id=1, source_target_pairs={{0,48},{16,0},{32,16},{48,32},{64,112},{80,64},{96,80},{112,96},{1... | collective-permute-start | bytes 884744 | tf_op jit(solution)/shard_map/ppermute | solution.py:33

commit v2 on v1

--- a/solution.py
+++ b/solution.py
@@ -18,6 +18,19 @@
 
 VM = pl.BlockSpec(memory_space=pltpu.VMEM)
 SM = pl.BlockSpec(memory_space=pltpu.SMEM)
+HB = pl.BlockSpec(memory_space=pltpu.HBM)
+
+
+def in_hbm(values):
+    return [pltpu.with_memory_space_constraint(v, pltpu.HBM) for v in values]
+
+
+def together(*values):
+    return lax.optimization_barrier(values)
+
+
+def after(value, *deps):
+    return lax.optimization_barrier((value, *deps))[0]
 
 
 def dot_nt(a, b):
@@ -33,9 +46,11 @@
     return lax.ppermute(value, "mem", pairs)
 
 
-def shift_z(value, k):
-    pairs = [(z * NX + x, (z + k) % NZ * NX + x) for z in range(NZ) for x in range(NX)]
-    return lax.ppermute(value, "mem", pairs)
+def exchange_z(value):
+    groups = [[z * NX + x for z in range(NZ)] for x in range(NX)]
+    return lax.all_to_all(
+        value, "mem", split_axis=0, concat_axis=0, axis_index_groups=groups, tiled=True
+    )
 
 
 def shift_y(value, k):
@@ -76,11 +91,22 @@
 
 
 def memory_kernel(sel_ref, *refs):
-    q_refs, k_refs, v_refs, out_refs = refs[0:4], refs[4:8], refs[8:12], refs[12:16]
-    heads = k_refs[0].shape[1] // HEAD
+    sources, result_ref = refs[0:9], refs[9]
+    q_buf, k_buf, v_buf, sems = refs[10:14]
+    targets = [q_buf] + [buf.at[n] for buf in (k_buf, v_buf) for n in range(4)]
+    copies = [
+        pltpu.make_async_copy(src, dst, sems.at[n])
+        for n, (src, dst) in enumerate(zip(sources, targets))
+    ]
+    for copy in copies:
+        copy.start()
+    for copy in copies:
+        copy.wait()
+    q_refs, k_refs, v_refs = [[buf.at[n] for n in range(4)] for buf in (q_buf, k_buf, v_buf)]
+    heads = k_buf.shape[2] // HEAD
     lane = lax.broadcasted_iota(jnp.int32, (BLOCK, BLOCK), 1)
     for j in range(NZ):
-        q_ref, out_ref = q_refs[j], out_refs[j]
+        q_ref, out_ref = q_refs[j], result_ref.at[j]
 
         for b in range(2):
             row = b * BLOCK
@@ -89,28 +115,22 @@
             for i in range(NX):
                 slot = sel_ref[(2 * j + b) * NX + i]
                 starts.append(pl.multiple_of(jnp.maximum(slot, 0) * BLOCK, BLOCK))
-                biases.append(jnp.where(slot >= 0, 0.0, NEG))
+                biases.append(
+                    jnp.full((1, BLOCK), jnp.where(slot >= 0, 0.0, NEG), jnp.float32)
+                )
+            bias = jnp.concatenate(biases, axis=1)
             for h in range(heads):
                 cols = pl.ds(h * HEAD, HEAD)
                 query = q_ref[pl.ds(row, BLOCK), cols]
-                scores = [
-                    dot_nt(query, k_refs[i][pl.ds(starts[i], BLOCK), cols]) * SCALE2 + biases[i]
-                    for i in range(NX)
-                ]
-                peak = jnp.maximum(
-                    jnp.maximum(scores[0], scores[1]), jnp.maximum(scores[2], scores[3])
+                keys = jnp.concatenate([k_refs[i][pl.ds(starts[i], BLOCK), cols] for i in range(NX)])
+                values = jnp.concatenate(
+                    [v_refs[i][pl.ds(starts[i], BLOCK), cols] for i in range(NX)]
                 )
-                top = jnp.max(peak, axis=1, keepdims=True)
-                weights = [jnp.exp2(s - top) for s in scores]
-                total = jnp.sum(
-                    (weights[0] + weights[1]) + (weights[2] + weights[3]), axis=1, keepdims=True
-                )
-                acc = None
-                for i in range(NX):
-                    part = dot_nn(
-                        weights[i].astype(jnp.bfloat16), v_refs[i][pl.ds(starts[i], BLOCK), cols]
-                    )
-                    acc = part if acc is None else acc + part
+                scores = dot_nt(query, keys) * SCALE2 + bias
+                top = jnp.max(scores, axis=1, keepdims=True)
+                weights = jnp.exp2(scores - top)
+                total = jnp.sum(weights, axis=1, keepdims=True)
+                acc = dot_nn(weights.astype(jnp.bfloat16), values)
                 out_ref[pl.ds(row, BLOCK), cols] = (acc / total).astype(jnp.bfloat16)
                 stat = jnp.where(lane == h, top + jnp.log2(total), stat)
             stat = stat.T[0:8]
@@ -133,8 +153,8 @@
         )
 
 
-def merge_kernel(gate_ref, local_ref, p0, p1, p2, p3, att_ref, att_t_ref):
-    parts = (p0, p1, p2, p3)
+def merge_kernel(gate_ref, local_ref, back_ref, att_ref, att_t_ref):
+    parts = [back_ref.at[n] for n in range(NZ)]
     heads = local_ref.shape[1] // HEAD
     for b in range(2):
         rows = pl.ds(b * BLOCK, BLOCK)
@@ -155,7 +175,9 @@
                 acc = term if acc is None else acc + term
             out = gate_ref[h] * acc + local_ref[rows, cols]
             att_ref[rows, cols] = out.astype(jnp.bfloat16)
-            att_t_ref[cols, rows] = out.T.astype(jnp.bfloat16)
+            flipped = out.T.astype(jnp.bfloat16)
+            for n in range(NZ):
+                att_t_ref[n, cols, rows] = flipped
 
 
 def grad_kernel(ids_ref, *refs):
@@ -187,19 +209,31 @@
 
 
 def weight_kernel(ids_ref, *refs):
-    atts, own, other = refs[0:4], refs[4:8], refs[8:12]
-    outs, att_scr = refs[12:16], refs[16]
-    z, x, y, zl, c = ids_ref[0], ids_ref[1], ids_ref[2], ids_ref[4], ids_ref[5]
-    rows = att_scr.shape[2]
-    for j in range(NZ):
-        att_scr[(z - j) & 3] = atts[j][...]
+    att_ref, own, other = refs[0], refs[1:5], refs[5:9]
+    outs, att_scr, cot_buf, sems = refs[9:13], refs[13], refs[14], refs[15]
+    x, y, zl, c = ids_ref[1], ids_ref[2], ids_ref[4], ids_ref[5]
+    rows = att_ref.shape[2]
+    copies = []
     for w, arrays in enumerate((own, other)):
         for s in range(2):
-            acc = None
             for k in range(NY):
-                block = arrays[k][(2 + s) * rows : (3 + s) * rows, :]
-                part = dot_nn(att_scr[(y - k) & 3], block)
-                acc = part if acc is None else acc + part
+                n = (2 * w + s) * NY + k
+                copies.append(
+                    pltpu.make_async_copy(
+                        arrays[k].at[pl.ds((2 + s) * rows, rows)],
+                        cot_buf.at[2 * w + s, pl.ds(k * rows, rows)],
+                        sems.at[n],
+                    )
+                )
+                copies[-1].start()
+    for j in range(NZ):
+        place = ((y - j) & 3) * rows
+        att_scr[:, pl.ds(pl.multiple_of(place, 128), rows)] = att_ref[j]
+    for w in range(2):
+        for s in range(2):
+            for copy in copies[(2 * w + s) * NY : (2 * w + s + 1) * NY]:
+                copy.wait()
+            acc = dot_nn(att_scr[...], cot_buf[2 * w + s])
             target = (((zl ^ s) * 2 + (c ^ w)) - x) & 3
 
             for n in range(NX):
@@ -229,7 +263,7 @@
     y, zl, c = ten // 4, (ten // 2) % 2, ten % 2
     ids = jnp.stack([z, x, y, jnp.zeros_like(z), zl, c]).astype(jnp.int32)
     gate = jax.nn.sigmoid(gate_bias)
-    params = pltpu.CompilerParams(vmem_limit_bytes=48 << 20)
+    params = pltpu.CompilerParams(vmem_limit_bytes=16 << 20)
 
     names = jnp.arange(block_slot.shape[0], dtype=jnp.int32)
     storage = jnp.sum(
@@ -239,21 +273,22 @@
     extra = extra.at[0, 0 : storage.shape[0]].set(storage.astype(jnp.bfloat16))
     q_pack = jnp.concatenate([queries, extra], axis=0)
 
-    k1, v3 = shift_x(memory_keys, 1), shift_x(memory_values, -1)
-    k3, v1 = shift_x(memory_keys, -1), shift_x(memory_values, 1)
-    k2, v2 = shift_x(k1, 1), shift_x(v3, -1)
-    q_all = [q_pack] + [shift_z(q_pack, j) for j in (1, 2, 3)]
-
-    stored = jnp.stack([q[rows, 0:16].astype(jnp.int32) for q in q_all]).reshape(8, 8)
+    q_all = exchange_z(jnp.broadcast_to(q_pack[None], (NZ, *q_pack.shape)))
+    k1, v3, v1, k3, swapped = together(
+        shift_x(memory_keys, 1),
+        shift_x(memory_values, -1),
+        shift_x(memory_values, 1),
+        shift_x(memory_keys, -1),
+        swap_zy(cotangent),
+    )
+    both = jnp.concatenate([cotangent, swapped], axis=0)
+    k2, v2, pair = shift_x(k1, 1), shift_x(v3, -1), flip_tensor(both, 2)
+    quad = jnp.concatenate([both[:rows], pair[:rows], both[rows:], pair[rows:]], axis=0)
+
+    stored = q_all[:, rows, 0:16].astype(jnp.int32).reshape(8, 8)
     shards = z * NX + (x - jnp.arange(NX, dtype=jnp.int32)) % NX
     hit = (stored // SLOTS)[:, None, :] == shards[None, :, None]
     sel = (jnp.sum(jnp.where(hit, (stored % SLOTS)[:, None, :] + 1, 0), axis=2) - 1).reshape(-1)
-
-    both = jnp.concatenate([cotangent, swap_zy(cotangent)], axis=0)
-    pair = flip_tensor(both, 2)
-    quad = jnp.concatenate([both[:rows], pair[:rows], both[rows:], pair[rows:]], axis=0)
-    own = [quad] + [shift_y(quad, k) for k in (1, 2, 3)]
-    other = [flip_tensor(a, 1) for a in own]
 
     local_out = pl.pallas_call(
         local_kernel,
@@ -264,27 +299,39 @@
         name="local_attention",
     )(gate, segments.reshape(1, rows), queries, local_keys, local_values)
 
+    k2, v2, quad = together(k2, v2, quad)
     parts = pl.pallas_call(
         memory_kernel,
-        out_shape=[jax.ShapeDtypeStruct((rows + EXTRA, width), jnp.bfloat16)] * 4,
-        in_specs=[SM] + [VM] * 12,
-        out_specs=[VM] * 4,
+        out_shape=jax.ShapeDtypeStruct((NZ, rows + EXTRA, width), jnp.bfloat16),
+        in_specs=[SM] + [HB] * 9,
+        out_specs=VM,
+        scratch_shapes=[
+            pltpu.VMEM((NZ, rows + EXTRA, width), jnp.bfloat16),
+            pltpu.VMEM((NX, SLOTS * BLOCK, width), jnp.bfloat16),
+            pltpu.VMEM((NX, SLOTS * BLOCK, width), jnp.bfloat16),
+            pltpu.SemaphoreType.DMA((9,)),
+        ],
         compiler_params=params,
         name="memory_attention",
-    )(sel, *q_all, memory_keys, k1, k2, k3, memory_values, v1, v2, v3)
-
-    back = [parts[0]] + [shift_z(parts[j], -j) for j in (1, 2, 3)]
+    )(sel, q_all, memory_keys, k1, k2, k3, memory_values, v1, v2, v3)
+
+    back = exchange_z(parts)
     attention, att_t = pl.pallas_call(
         merge_kernel,
         out_shape=[
             jax.ShapeDtypeStruct((rows, width), jnp.bfloat16),
-            jax.ShapeDtypeStruct((width, rows), jnp.bfloat16),
+            jax.ShapeDtypeStruct((NZ, width, rows), jnp.bfloat16),
         ],
-        in_specs=[SM] + [VM] * 5,
+        in_specs=[SM] + [VM] * 2,
         out_specs=[VM] * 2,
         compiler_params=params,
         name="merge",
-    )(gate, local_out, *back)
+    )(gate, local_out, back)
+    att_all = exchange_z(att_t)
+
+    y1, y2, y3 = [shift_y(quad, k) for k in (1, 2, 3)]
+    c0, c1, c2, c3 = [flip_tensor(v, 1) for v in (quad, y1, y2, y3)]
+    own, other = [quad, y1, y2, y3], [c0, c1, c2, c3]
 
     attention_grad = pl.pallas_call(
         grad_kernel,
@@ -292,26 +339,34 @@
         grid_spec=pltpu.PrefetchScalarGridSpec(
             num_scalar_prefetch=1,
             grid=(NY,),
-            in_specs=[pl.BlockSpec((4 * rows, width), lambda g, ids: (0, 0))] * 8
+            in_specs=[
+                pl.BlockSpec(
+                    (4 * rows, width), lambda g, ids: (0, 0), pipeline_mode=pl.Buffered(1)
+                )
+            ]
+            * 8
             + [pl.BlockSpec((width, 4 * width), lambda g, ids: (0, (ids[2] - g) & 3))],
             out_specs=pl.BlockSpec((rows, width), lambda g, ids: (0, 0)),
             scratch_shapes=[pltpu.VMEM((rows, width), jnp.float32)],
         ),
         compiler_params=params,
         name="attention_grad",
-    )(ids, *own, *other, out_weight)
-
-    att_all = [att_t] + [shift_z(att_t, j) for j in (1, 2, 3)]
+    )(ids, *own, *other, *in_hbm([out_weight]))
+
     mine, *sent = pl.pallas_call(
         weight_kernel,
         out_shape=[jax.ShapeDtypeStruct((width, width), jnp.float32)]
         + [jax.ShapeDtypeStruct((width, width), jnp.bfloat16)] * 3,
-        in_specs=[SM] + [VM] * 12,
+        in_specs=[SM, VM] + [HB] * 8,
         out_specs=[VM] * 4,
-        scratch_shapes=[pltpu.VMEM((NZ, width, rows), jnp.bfloat16)],
+        scratch_shapes=[
+            pltpu.VMEM((width, NZ * rows), jnp.bfloat16),
+            pltpu.VMEM((4, NY * rows, width), jnp.bfloat16),
+            pltpu.SemaphoreType.DMA((16,)),
+        ],
         compiler_params=params,
         name="weight_partials",
-    )(ids, *att_all, *own, *other)
+    )(ids, att_all, *own, *other)
     got = [shift_x(sent[n - 1], n) for n in (1, 2, 3)]
     weight_grad = (mine + got[0].astype(jnp.float32)) + (
         got[1].astype(jnp.float32) + got[2].astype(jnp.float32)

time: 180 us -> 155 us (0.86)
  the two profiles are of different devices: /device:TPU:1 before, /device:TPU:56 now
where the time goes in v2:
time: 155 us
  waiting for transfers between devices  70.3 us (45%)
  starting transfers between devices  41 us (26%)
  Pallas kernels  25.6 us (17%)
  local copies, waits for them, and re-layouts  12.1 us (8%)
  other arithmetic  4.9 us (3%)
    ppermute x1, waiting for transfers between devices, swap_zy(): return lax.ppermute(value, ('mem', 'tensor'), pairs)  28 us
    all_to_all x3, waiting for transfers between devices, exchange_z(): lax.all_to_all(value, 'mem', split_axis=0, concat_axis=0, axis_index_grou...  19.7 us
    all_to_all x3, starting transfers between devices, exchange_z(): lax.all_to_all(value, 'mem', split_axis=0, concat_axis=0, axis_index_grou...  17.1 us
    ppermute x9, starting transfers between devices, shift_x(): return lax.ppermute(value, 'mem', pairs)  13.5 us
    ppermute x5, waiting for transfers between devices, flip_tensor(): return lax.ppermute(value, 'tensor', [(t, t ^ bit) for t in range(16)])  9.8 us
    pallas_call x1, Pallas kernels, per_device(): pl.pallas_call(memory_kernel, out_shape=jax.ShapeDtypeStruct((NZ, rows +...  9.42 us
    unnamed x36, local copies, waits for them, and re-layouts  8.97 us
    ppermute x3, waiting for transfers between devices, shift_y(): return lax.ppermute(value, 'tensor', pairs)  7.45 us
  transfers between devices with their start and end apart: 21, of which 7 were waited for; matrix products, arithmetic and copies ran while one was open for 4% of the time, Pallas kernels for 7%

profile of v2, /device:TPU:56, one launch (start us, length us, event | category | flops | bytes accessed | tf_op | source)
XLA Modules:
  0.0 154.8 jit_solution(14793131105990118939)
XLA Ops:
  0.6 2.8 %collective-permute-start.1 = (bf16[512,384]{1,0:T(8,128)(2,1)}, bf16[512,384]{1,0:T(8,128)(2,1)S(1)}, u32[]{:S(2)}, u32[]{:S(2)}) collective-permute-start(bf16[512,384]{1,0:T(8,128)(2,1)} %refs_5_.1), channel_id=1, source_target_pairs={{0,48},{16,0},{32,16},{48,32},{64,112},{80,64},{96,80},{112,96},{1... | collective-permute-start | bytes 1179656 | tf_op jit(solution)/shard_map/ppermute | solution.py:46
  3.5 0.0 collective-permute-start.2
  3.5 0.8 collective-permute-start
  4.2 2.5 %collective-permute-start.3 = (bf16[512,384]{1,0:T(8,128)(2,1)}, bf16[512,384]{1,0:T(8,128)(2,1)S(1)}, u32[]{:S(2)}, u32[]{:S(2)}) collective-permute-start(bf16[512,384]{1,0:T(8,128)(2,1)} %refs_1_.1), channel_id=1, source_target_pairs={{0,48},{16,0},{32,16},{48,32},{64,112},{80,64},{96,80},{112,96},{1... | collective-permute-start | bytes 1179656 | tf_op jit(solution)/shard_map/ppermute | solution.py:46
  6.7 0.8 eq.36
  7.5 0.8 select_reduce_fusion.1
  8.4 1.0 fusion.1
  9.3 1.0 broadcast_in_dim.38
  10.3 7.6 %all-to-all-start = ((bf16[4,272,384]{2,1,0:T(8,128)(2,1)}), bf16[4,272,384]{2,1,0:T(8,128)(2,1)S(1)}, u32[]{:S(2)}, u32[]{:S(2)}) async-start(bf16[4,272,384]{2,1,0:T(8,128)(2,1)} %broadcast_in_dim.38), calls=%async_computation | async-start | bytes 1671168 | tf_op jit(solution)/shard_map/all_to_all | solution.py:51
  17.9 5.8 %collective-permute-start.4 = (bf16[256,384]{1,0:T(8,128)(2,1)S(1)}, bf16[256,384]{1,0:T(8,128)(2,1)S(1)}, u32[]{:S(2)}, u32[]{:S(2)}) collective-permute-start(bf16[256,384]{1,0:T(8,128)(2,1)S(1)} %copy-done.15), channel_id=1, source_target_pairs={{0,0},{1,1},{2,2},{3,3},{4,64},{5,65},{6,66},{7,67},{8,128},{9,129... | collective-permute-start | bytes 589832 | tf_op jit(solution)/shard_map/ppermute | solution.py:72
  23.7 28.0 %collective-permute-done.4 = bf16[256,384]{1,0:T(8,128)(2,1)S(1)} collective-permute-done((bf16[256,384]{1,0:T(8,128)(2,1)S(1)}, bf16[256,384]{1,0:T(8,128)(2,1)S(1)}, u32[]{:S(2)}, u32[]{:S(2)}) %collective-permute-start.4) | collective-permute-done | bytes 196640 | tf_op jit(solution)/shard_map/ppermute | solution.py:72
  51.7 0.0 collective-permute-done.refs_2_
  51.7 0.0 collective-permute-done.2.refs_6_
  51.7 0.9 pad_maximum_fusion.1
  52.6 3.2 %collective-permute-start.6 = (bf16[512,384]{1,0:T(8,128)(2,1)S(1)}, bf16[512,384]{1,0:T(8,128)(2,1)S(1)}, u32[]{:S(2)}, u32[]{:S(2)}) collective-permute-start(bf16[512,384]{1,0:T(8,128)(2,1)S(1)} %collective-permute-done.1.refs_8_), channel_id=1, source_target_pairs={{0,48},{16,0},{32,16},{48,32},{64,112},{80,64},{96,80},{112,96},{1... | collective-permute-start | bytes 1179656 | tf_op jit(solution)/shard_map/ppermute | solution.py:46
  55.9 7.3 %collective-permute-done.7 = bf16[512,384]{1,0:T(8,128)(2,1)} collective-permute-done((bf16[512,384]{1,0:T(8,128)(2,1)}, bf16[512,384]{1,0:T(8,128)(2,1)}, u32[]{:S(2)}, u32[]{:S(2)}) %collective-permute-start.7) | collective-permute-done | bytes 393248 | tf_op jit(solution)/shard_map/ppermute | solution.py:62
  63.2 1.1 fusion.8
  64.2 1.0 pad_maximum_fusion.refs_0_.refs_1_
  65.3 0.0 collective-permute-done.5.refs_3_
  65.3 0.0 copy-start.8
  65.3 0.7 copy-done.8
  66.0 0.7 copy-done.10
  66.8 0.0 all-to-all-done.refs_0_
  66.8 0.1 reshape.107
  66.9 0.2 select_reduce_fusion
  67.1 0.1 copy.14
  67.2 0.1 sub.37.sel_ref
  67.3 0.0 copy-done.5
  67.3 1.0 copy-done.7
  68.3 1.0 copy-done.9
  69.3 1.0 copy-done.11
  70.3 9.4 %memory_attention.1 = bf16[4,272,384]{2,1,0:T(8,128)(2,1)} custom-call(s32[32]{0:T(128)S(1)} %sub.37.sel_ref, bf16[4,272,384]{2,1,0:T(8,128)(2,1)S(1)} %all-to-all-done.refs_0_, bf16[512,384]{1,0:T(8,128)(2,1)S(1)} %copy-done.4, bf16[512,384]{1,0:T(8,128)(2,1)} %collective-permute-done.refs_2_, bf16[512,384]{1,0:T(8,128)(2,1)S(1)} %copy-done.9, ...), custom_call_target="tpu_custom_call" | custom-call | tf_op jit(solution)/shard_map/memory_attention/pallas_call | solution.py:303
  79.7 0.0 copy-start.17
  79.7 0.0 copy-start.3
  79.7 0.0 copy-start.14
  79.7 4.2 %all-to-all-start.1 = ((bf16[4,272,384]{2,1,0:T(8,128)(2,1)}), bf16[4,272,384]{2,1,0:T(8,128)(2,1)S(1)}, u32[]{:S(2)}, u32[]{:S(2)}) async-start(bf16[4,272,384]{2,1,0:T(8,128)(2,1)} %memory_attention.1), calls=%async_computation.1 | async-start | bytes 1671168 | tf_op jit(solution)/shard_map/all_to_all | solution.py:51
  83.9 0.6 collective-permute-start.8
  84.5 3.2 %collective-permute-start.9 = (bf16[1024,384]{1,0:T(8,128)(2,1)S(1)}, bf16[1024,384]{1,0:T(8,128)(2,1)S(1)}, u32[]{:S(2)}, u32[]{:S(2)}) collective-permute-start(bf16[1024,384]{1,0:T(8,128)(2,1)S(1)} %pad_maximum_fusion.refs_0_.refs_1_), channel_id=1, source_target_pairs={{0,8},{1,9},{2,10},{3,11},{4,12},{5,13},{6,14},{7,15},{8,0},{9,1},... | collective-permute-start | bytes 2359304 | tf_op jit(solution)/shard_map/ppermute | solution.py:58
  87.7 0.1 collective-permute-start.10
  87.9 0.0 copy-start.12
  87.9 0.9 copy-done.12
  88.8 0.9 copy-done.13
  89.7 1.4 local_attention.1.local_ref
  91.1 0.0 copy-start
  91.1 0.7 copy-done
  91.8 11.1 %all-to-all-done.1.back_ref = bf16[4,272,384]{2,1,0:T(8,128)(2,1)S(1)} async-done(((bf16[4,272,384]{2,1,0:T(8,128)(2,1)}), bf16[4,272,384]{2,1,0:T(8,128)(2,1)S(1)}, u32[]{:S(2)}, u32[]{:S(2)}) %all-to-all-start.1) | async-done | bytes 835616 | tf_op jit(solution)/shard_map/all_to_all | solution.py:51
  103.0 1.0 copy-done.1
  103.9 2.1 %merge.1 = (bf16[256,384]{1,0:T(8,128)(2,1)}, bf16[4,384,256]{2,1,0:T(8,128)(2,1)S(1)}) custom-call(f32[3]{0:T(128)S(1)} %add_divide_fusion.gate_ref, f32[256,384]{1,0:T(8,128)S(1)} %copy-done.1, bf16[4,272,384]{2,1,0:T(8,128)(2,1)S(1)} %all-to-all-done.1.back_ref), custom_call_target="tpu_custom_call" | custom-call | tf_op jit(solution)/shard_map/merge/pallas_call | solution.py:319
  106.0 0.9 copy-done.2
  106.9 5.4 %all-to-all-start.2 = ((bf16[4,384,256]{2,1,0:T(8,128)(2,1)}), bf16[4,384,256]{2,1,0:T(8,128)(2,1)}, u32[]{:S(2)}, u32[]{:S(2)}) async-start(bf16[4,384,256]{2,1,0:T(8,128)(2,1)} %copy-done.2), calls=%async_computation.2 | async-start | bytes 1572864 | tf_op jit(solution)/shard_map/all_to_all | solution.py:51
  112.3 0.5 collective-permute-start.12
  112.8 0.1 collective-permute-start.13
  112.9 7.4 %collective-permute-done.10.refs_3_.refs_4_ = bf16[1024,384]{1,0:T(8,128)(2,1)} collective-permute-done((bf16[1024,384]{1,0:T(8,128)(2,1)S(1)}, bf16[1024,384]{1,0:T(8,128)(2,1)}, u32[]{:S(2)}, u32[]{:S(2)}) %collective-permute-start.10) | collective-permute-done | bytes 786464 | tf_op jit(solution)/shard_map/ppermute | solution.py:58
  120.4 0.0 collective-permute-start.14
  120.4 0.1 stack.23.ids_ref
  120.5 2.5 %collective-permute-done.14.refs_7_.refs_8_ = bf16[1024,384]{1,0:T(8,128)(2,1)} collective-permute-done((bf16[1024,384]{1,0:T(8,128)(2,1)}, bf16[1024,384]{1,0:T(8,128)(2,1)}, u32[]{:S(2)}, u32[]{:S(2)}) %collective-permute-start.14) | collective-permute-done | bytes 786464 | tf_op jit(solution)/shard_map/ppermute | solution.py:62
  123.0 8.6 %all-to-all-done.2.refs_0_ = bf16[4,384,256]{2,1,0:T(8,128)(2,1)} async-done(((bf16[4,384,256]{2,1,0:T(8,128)(2,1)}), bf16[4,384,256]{2,1,0:T(8,128)(2,1)}, u32[]{:S(2)}, u32[]{:S(2)}) %all-to-all-start.2) | async-done | bytes 786464 | tf_op jit(solution)/shard_map/all_to_all | solution.py:51
  131.6 5.9 %weight_partials.1 = (f32[384,384]{1,0:T(8,128)S(1)}, bf16[384,384]{1,0:T(8,128)(2,1)S(1)}, bf16[384,384]{1,0:T(8,128)(2,1)S(1)}, bf16[384,384]{1,0:T(8,128)(2,1)S(1)}) custom-call(s32[6]{0:T(128)S(1)} %stack.23.ids_ref, bf16[4,384,256]{2,1,0:T(8,128)(2,1)} %all-to-all-done.2.refs_0_, bf16[1024,384]{1,0:T(8,128)(2,1)S(1)} %pad_maximum_fusion.refs_0_.refs_1_, ...), custom_call_target="tpu_custom_call" | custom-call | tf_op jit(solution)/shard_map/weight_partials/pallas_call | solution.py:356
  137.4 0.1 collective-permute-start.15
  137.5 4.0 %collective-permute-start.16 = (bf16[384,384]{1,0:T(8,128)(2,1)S(1)}, bf16[384,384]{1,0:T(8,128)(2,1)S(1)}, u32[]{:S(2)}, u32[]{:S(2)}) collective-permute-start(bf16[384,384]{1,0:T(8,128)(2,1)S(1)} %get-tuple-element.41), channel_id=1, source_target_pairs={{0,32},{16,48},{32,0},{48,16},{64,96},{80,112},{96,64},{112,80},{1... | collective-permute-start | bytes 884744 | tf_op jit(solution)/shard_map/ppermute | solution.py:46
  141.5 0.0 collective-permute-start.17
  141.6 6.9 %attention_grad.1 = bf16[256,384]{1,0:T(8,128)(2,1)} custom-call(s32[6]{0:T(128)S(1)} %stack.23.ids_ref, bf16[1024,384]{1,0:T(8,128)(2,1)S(1)} %pad_maximum_fusion.refs_0_.refs_1_, bf16[1024,384]{1,0:T(8,128)(2,1)S(1)} %collective-permute-done.8.refs_1_.refs_2_, bf16[1024,384]{1,0:T(8,128)(2,1)S(1)} %collective-permute-done.9.refs_2_.refs_3_, ...), custom_call_target="tpu_custom_call" | custom-call | tf_op jit(solution)/shard_map/attention_grad/pallas_call | solution.py:336
  148.4 5.4 %collective-permute-done.16 = bf16[384,384]{1,0:T(8,128)(2,1)S(1)} collective-permute-done((bf16[384,384]{1,0:T(8,128)(2,1)S(1)}, bf16[384,384]{1,0:T(8,128)(2,1)S(1)}, u32[]{:S(2)}, u32[]{:S(2)}) %collective-permute-start.16) | collective-permute-done | bytes 294944 | tf_op jit(solution)/shard_map/ppermute | solution.py:46
  153.8 0.9 add_add_fusion
  (38 shorter events, 0.1 us)
Async XLA Ops:
  0.6 17.2 %copy-start.15 = (bf16[256,384]{1,0:T(8,128)(2,1)S(1)}, bf16[256,384]{1,0:T(8,128)(2,1)}, u32[]{:S(2)}) copy-start(bf16[256,384]{1,0:T(8,128)(2,1)} %param.23) | copy-start | bytes 589828
  0.6 51.1 %collective-permute-start.1 = (bf16[512,384]{1,0:T(8,128)(2,1)}, bf16[512,384]{1,0:T(8,128)(2,1)S(1)}, u32[]{:S(2)}, u32[]{:S(2)}) collective-permute-start(bf16[512,384]{1,0:T(8,128)(2,1)} %refs_5_.1), channel_id=1, source_target_pairs={{0,48},{16,0},{32,16},{48,32},{64,112},{80,64},{96,80},{112,96},{1... | collective-permute-start | bytes 1179656 | tf_op jit(solution)/shard_map/ppermute | solution.py:46
  3.5 48.2 %collective-permute-start.2 = (bf16[512,384]{1,0:T(8,128)(2,1)}, bf16[512,384]{1,0:T(8,128)(2,1)S(1)}, u32[]{:S(2)}, u32[]{:S(2)}) collective-permute-start(bf16[512,384]{1,0:T(8,128)(2,1)} %refs_5_.1), channel_id=1, source_target_pairs={{0,16},{16,32},{32,48},{48,0},{64,80},{80,96},{96,112},{112,64},{1... | collective-permute-start | bytes 1179656 | tf_op jit(solution)/shard_map/ppermute | solution.py:46
  3.5 48.2 %collective-permute-start = (bf16[512,384]{1,0:T(8,128)(2,1)}, bf16[512,384]{1,0:T(8,128)(2,1)}, u32[]{:S(2)}, u32[]{:S(2)}) collective-permute-start(bf16[512,384]{1,0:T(8,128)(2,1)} %refs_1_.1), channel_id=1, source_target_pairs={{0,16},{16,32},{32,48},{48,0},{64,80},{80,96},{96,112},{112,64},{1... | collective-permute-start | bytes 1179656 | tf_op jit(solution)/shard_map/ppermute | solution.py:46
  4.2 47.5 %collective-permute-start.3 = (bf16[512,384]{1,0:T(8,128)(2,1)}, bf16[512,384]{1,0:T(8,128)(2,1)S(1)}, u32[]{:S(2)}, u32[]{:S(2)}) collective-permute-start(bf16[512,384]{1,0:T(8,128)(2,1)} %refs_1_.1), channel_id=1, source_target_pairs={{0,48},{16,0},{32,16},{48,32},{64,112},{80,64},{96,80},{112,96},{1... | collective-permute-start | bytes 1179656 | tf_op jit(solution)/shard_map/ppermute | solution.py:46
  10.3 56.5 %all-to-all-start = ((bf16[4,272,384]{2,1,0:T(8,128)(2,1)}), bf16[4,272,384]{2,1,0:T(8,128)(2,1)S(1)}, u32[]{:S(2)}, u32[]{:S(2)}) async-start(bf16[4,272,384]{2,1,0:T(8,128)(2,1)} %broadcast_in_dim.38), calls=%async_computation | async-start | bytes 1671168 | tf_op jit(solution)/shard_map/all_to_all | solution.py:51
  17.9 49.4 %copy-start.4 = (bf16[512,384]{1,0:T(8,128)(2,1)S(1)}, bf16[512,384]{1,0:T(8,128)(2,1)}, u32[]{:S(2)}) copy-start(bf16[512,384]{1,0:T(8,128)(2,1)} %refs_1_.1) | copy-start | bytes 1179652
  17.9 49.4 %copy-start.5 = (bf16[512,384]{1,0:T(8,128)(2,1)S(1)}, bf16[512,384]{1,0:T(8,128)(2,1)}, u32[]{:S(2)}) copy-start(bf16[512,384]{1,0:T(8,128)(2,1)} %refs_5_.1) | copy-start | bytes 1179652
  17.9 33.8 %collective-permute-start.4 = (bf16[256,384]{1,0:T(8,128)(2,1)S(1)}, bf16[256,384]{1,0:T(8,128)(2,1)S(1)}, u32[]{:S(2)}, u32[]{:S(2)}) collective-permute-start(bf16[256,384]{1,0:T(8,128)(2,1)S(1)} %copy-done.15), channel_id=1, source_target_pairs={{0,0},{1,1},{2,2},{3,3},{4,64},{5,65},{6,66},{7,67},{8,128},{9,129... | collective-permute-start | bytes 589832 | tf_op jit(solution)/shard_map/ppermute | solution.py:72
  51.7 12.5 %copy-start.16 = (bf16[256,384]{1,0:T(8,128)(2,1)}, bf16[256,384]{1,0:T(8,128)(2,1)S(1)}, u32[]{:S(2)}) copy-start(bf16[256,384]{1,0:T(8,128)(2,1)S(1)} %collective-permute-done.4) | copy-start | bytes 589828
  51.7 12.5 %copy-start.6 = (bf16[512,384]{1,0:T(8,128)(2,1)}, bf16[512,384]{1,0:T(8,128)(2,1)S(1)}, u32[]{:S(2)}) copy-start(bf16[512,384]{1,0:T(8,128)(2,1)S(1)} %collective-permute-done.3.refs_4_) | copy-start | bytes 1179652
  52.6 10.5 %collective-permute-start.7 = (bf16[512,384]{1,0:T(8,128)(2,1)}, bf16[512,384]{1,0:T(8,128)(2,1)}, u32[]{:S(2)}, u32[]{:S(2)}) collective-permute-start(bf16[512,384]{1,0:T(8,128)(2,1)} %pad_maximum_fusion.1), channel_id=1, source_target_pairs={{0,2},{1,3},{2,0},{3,1},{4,6},{5,7},{6,4},{7,5},{8,10},{9,11},{10,... | collective-permute-start | bytes 1179656 | tf_op jit(solution)/shard_map/ppermute | solution.py:62
  52.6 12.6 %collective-permute-start.5 = (bf16[512,384]{1,0:T(8,128)(2,1)}, bf16[512,384]{1,0:T(8,128)(2,1)S(1)}, u32[]{:S(2)}, u32[]{:S(2)}) collective-permute-start(bf16[512,384]{1,0:T(8,128)(2,1)} %collective-permute-done.refs_2_), channel_id=1, source_target_pairs={{0,16},{16,32},{32,48},{48,0},{64,80},{80,96},{96,112},{112,64},{1... | collective-permute-start | bytes 1179656 | tf_op jit(solution)/shard_map/ppermute | solution.py:46
  52.6 13.4 %collective-permute-start.6 = (bf16[512,384]{1,0:T(8,128)(2,1)S(1)}, bf16[512,384]{1,0:T(8,128)(2,1)S(1)}, u32[]{:S(2)}, u32[]{:S(2)}) collective-permute-start(bf16[512,384]{1,0:T(8,128)(2,1)S(1)} %collective-permute-done.1.refs_8_), channel_id=1, source_target_pairs={{0,48},{16,0},{32,16},{48,32},{64,112},{80,64},{96,80},{112,96},{1... | collective-permute-start | bytes 1179656 | tf_op jit(solution)/shard_map/ppermute | solution.py:46
  65.3 0.7 copy-start.8
  66.0 0.8 copy-start.10
  67.3 1.0 copy-start.7
  68.3 1.0 copy-start.9
  69.3 1.0 copy-start.11
  79.7 8.1 %copy-start.17 = (f32[3]{0:T(128)S(1)}, f32[3]{0:T(128)}, u32[]{:S(2)}) copy-start(f32[3]{0:T(128)} %param.21) | copy-start | bytes 40
  79.7 8.1 %copy-start.3 = (bf16[256,384]{1,0:T(8,128)(2,1)S(1)}, bf16[256,384]{1,0:T(8,128)(2,1)}, u32[]{:S(2)}) copy-start(bf16[256,384]{1,0:T(8,128)(2,1)} %q_ref.1) | copy-start | bytes 589828
  79.7 8.1 %copy-start.14 = (s32[256]{0:T(256)S(1)}, s32[256]{0:T(256)}, u32[]{:S(2)}) copy-start(s32[256]{0:T(256)} %param.16) | copy-start | bytes 3076
  79.7 23.2 %all-to-all-start.1 = ((bf16[4,272,384]{2,1,0:T(8,128)(2,1)}), bf16[4,272,384]{2,1,0:T(8,128)(2,1)S(1)}, u32[]{:S(2)}, u32[]{:S(2)}) async-start(bf16[4,272,384]{2,1,0:T(8,128)(2,1)} %memory_attention.1), calls=%async_computation.1 | async-start | bytes 1671168 | tf_op jit(solution)/shard_map/all_to_all | solution.py:51
  83.9 28.4 %collective-permute-start.8 = (bf16[1024,384]{1,0:T(8,128)(2,1)S(1)}, bf16[1024,384]{1,0:T(8,128)(2,1)S(1)}, u32[]{:S(2)}, u32[]{:S(2)}) collective-permute-start(bf16[1024,384]{1,0:T(8,128)(2,1)S(1)} %pad_maximum_fusion.refs_0_.refs_1_), channel_id=1, source_target_pairs={{0,4},{1,5},{2,6},{3,7},{4,8},{5,9},{6,10},{7,11},{8,12},{9,13},{1... | collective-permute-start | bytes 2359304 | tf_op jit(solution)/shard_map/ppermute | solution.py:58
  84.5 28.3 %collective-permute-start.9 = (bf16[1024,384]{1,0:T(8,128)(2,1)S(1)}, bf16[1024,384]{1,0:T(8,128)(2,1)S(1)}, u32[]{:S(2)}, u32[]{:S(2)}) collective-permute-start(bf16[1024,384]{1,0:T(8,128)(2,1)S(1)} %pad_maximum_fusion.refs_0_.refs_1_), channel_id=1, source_target_pairs={{0,8},{1,9},{2,10},{3,11},{4,12},{5,13},{6,14},{7,15},{8,0},{9,1},... | collective-permute-start | bytes 2359304 | tf_op jit(solution)/shard_map/ppermute | solution.py:58
  87.7 32.7 %collective-permute-start.10 = (bf16[1024,384]{1,0:T(8,128)(2,1)S(1)}, bf16[1024,384]{1,0:T(8,128)(2,1)}, u32[]{:S(2)}, u32[]{:S(2)}) collective-permute-start(bf16[1024,384]{1,0:T(8,128)(2,1)S(1)} %pad_maximum_fusion.refs_0_.refs_1_), channel_id=1, source_target_pairs={{0,12},{1,13},{2,14},{3,15},{4,0},{5,1},{6,2},{7,3},{8,4},{9,5},{1... | collective-permute-start | bytes 2359304 | tf_op jit(solution)/shard_map/ppermute | solution.py:58
  87.9 0.9 copy-start.12
  88.8 0.9 copy-start.13
  91.1 0.7 copy-start
  103.0 1.0 copy-start.1
  106.0 0.9 copy-start.2
  106.9 24.7 %all-to-all-start.2 = ((bf16[4,384,256]{2,1,0:T(8,128)(2,1)}), bf16[4,384,256]{2,1,0:T(8,128)(2,1)}, u32[]{:S(2)}, u32[]{:S(2)}) async-start(bf16[4,384,256]{2,1,0:T(8,128)(2,1)} %copy-done.2), calls=%async_computation.2 | async-start | bytes 1572864 | tf_op jit(solution)/shard_map/all_to_all | solution.py:51
  112.3 8.2 %collective-permute-start.11 = (bf16[1024,384]{1,0:T(8,128)(2,1)S(1)}, bf16[1024,384]{1,0:T(8,128)(2,1)S(1)}, u32[]{:S(2)}, u32[]{:S(2)}) collective-permute-start(bf16[1024,384]{1,0:T(8,128)(2,1)S(1)} %pad_maximum_fusion.refs_0_.refs_1_), channel_id=1, source_target_pairs={{0,1},{1,0},{2,3},{3,2},{4,5},{5,4},{6,7},{7,6},{8,9},{9,8},{10,11... | collective-permute-start | bytes 2359304 | tf_op jit(solution)/shard_map/ppermute | solution.py:62
  112.3 8.2 %collective-permute-start.12 = (bf16[1024,384]{1,0:T(8,128)(2,1)S(1)}, bf16[1024,384]{1,0:T(8,128)(2,1)}, u32[]{:S(2)}, u32[]{:S(2)}) collective-permute-start(bf16[1024,384]{1,0:T(8,128)(2,1)S(1)} %collective-permute-done.8.refs_1_.refs_2_), channel_id=1, source_target_pairs={{0,1},{1,0},{2,3},{3,2},{4,5},{5,4},{6,7},{7,6},{8,9},{9,8},{10,11... | collective-permute-start | bytes 2359304 | tf_op jit(solution)/shard_map/ppermute | solution.py:62
  112.8 7.7 %collective-permute-start.13 = (bf16[1024,384]{1,0:T(8,128)(2,1)S(1)}, bf16[1024,384]{1,0:T(8,128)(2,1)}, u32[]{:S(2)}, u32[]{:S(2)}) collective-permute-start(bf16[1024,384]{1,0:T(8,128)(2,1)S(1)} %collective-permute-done.9.refs_2_.refs_3_), channel_id=1, source_target_pairs={{0,1},{1,0},{2,3},{3,2},{4,5},{5,4},{6,7},{7,6},{8,9},{9,8},{10,11... | collective-permute-start | bytes 2359304 | tf_op jit(solution)/shard_map/ppermute | solution.py:62
  120.4 2.6 %collective-permute-start.14 = (bf16[1024,384]{1,0:T(8,128)(2,1)}, bf16[1024,384]{1,0:T(8,128)(2,1)}, u32[]{:S(2)}, u32[]{:S(2)}) collective-permute-start(bf16[1024,384]{1,0:T(8,128)(2,1)} %collective-permute-done.10.refs_3_.refs_4_), channel_id=1, source_target_pairs={{0,1},{1,0},{2,3},{3,2},{4,5},{5,4},{6,7},{7,6},{8,9},{9,8},{10,11... | collective-permute-start | bytes 2359304 | tf_op jit(solution)/shard_map/ppermute | solution.py:62
  137.4 11.0 %collective-permute-start.15 = (bf16[384,384]{1,0:T(8,128)(2,1)S(1)}, bf16[384,384]{1,0:T(8,128)(2,1)S(1)}, u32[]{:S(2)}, u32[]{:S(2)}) collective-permute-start(bf16[384,384]{1,0:T(8,128)(2,1)S(1)} %get-tuple-element.40), channel_id=1, source_target_pairs={{0,16},{16,32},{32,48},{48,0},{64,80},{80,96},{96,112},{112,64},{1... | collective-permute-start | bytes 884744 | tf_op jit(solution)/shard_map/ppermute | solution.py:46
  137.5 16.3 %collective-permute-start.16 = (bf16[384,384]{1,0:T(8,128)(2,1)S(1)}, bf16[384,384]{1,0:T(8,128)(2,1)S(1)}, u32[]{:S(2)}, u32[]{:S(2)}) collective-permute-start(bf16[384,384]{1,0:T(8,128)(2,1)S(1)} %get-tuple-element.41), channel_id=1, source_target_pairs={{0,32},{16,48},{32,0},{48,16},{64,96},{80,112},{96,64},{112,80},{1... | collective-permute-start | bytes 884744 | tf_op jit(solution)/shard_map/ppermute | solution.py:46
  141.5 12.3 %collective-permute-start.17 = (bf16[384,384]{1,0:T(8,128)(2,1)S(1)}, bf16[384,384]{1,0:T(8,128)(2,1)S(1)}, u32[]{:S(2)}, u32[]{:S(2)}) collective-permute-start(bf16[384,384]{1,0:T(8,128)(2,1)S(1)} %get-tuple-element.42), channel_id=1, source_target_pairs={{0,48},{16,0},{32,16},{48,32},{64,112},{80,64},{96,80},{112,96},{1... | collective-permute-start | bytes 884744 | tf_op jit(solution)/shard_map/ppermute | solution.py:46

commit v3 on v2

--- a/solution.py
+++ b/solution.py
@@ -21,6 +21,12 @@
 HB = pl.BlockSpec(memory_space=pltpu.HBM)
 
 
+def cost(flops, transcendentals, bytes_accessed):
+    return pl.CostEstimate(
+        flops=flops, transcendentals=transcendentals, bytes_accessed=bytes_accessed
+    )
+
+
 def in_hbm(values):
     return [pltpu.with_memory_space_constraint(v, pltpu.HBM) for v in values]
 
@@ -43,6 +49,11 @@
 
 def shift_x(value, k):
     pairs = [(z * NX + x, z * NX + (x + k) % NX) for z in range(NZ) for x in range(NX)]
+    return lax.ppermute(value, "mem", pairs)
+
+
+def shift_z(value, k):
+    pairs = [(z * NX + x, (z + k) % NZ * NX + x) for z in range(NZ) for x in range(NX)]
     return lax.ppermute(value, "mem", pairs)
 
 
@@ -56,6 +67,10 @@
 def shift_y(value, k):
     pairs = [(y * 4 + r, (y + k) % NY * 4 + r) for y in range(NY) for r in range(4)]
     return lax.ppermute(value, "tensor", pairs)
+
+
+def gather_y(value):
+    return [value] + [shift_y(value, k) for k in (1, 2, 3)]
 
 
 def flip_tensor(value, bit):
@@ -90,23 +105,33 @@
         out_ref[:, cols] = out * ((1.0 - gate_ref[h]) / total)
 
 
-def memory_kernel(sel_ref, *refs):
-    sources, result_ref = refs[0:9], refs[9]
-    q_buf, k_buf, v_buf, sems = refs[10:14]
-    targets = [q_buf] + [buf.at[n] for buf in (k_buf, v_buf) for n in range(4)]
+def memory_kernel(ids_ref, stored_ref, *refs):
+    sources, result_ref = refs[0:12], refs[12]
+    q_buf, k_buf, v_buf, sel_ref, sems = refs[13:18]
+    targets = [buf.at[n] for buf in (q_buf, k_buf, v_buf) for n in range(4)]
     copies = [
         pltpu.make_async_copy(src, dst, sems.at[n])
         for n, (src, dst) in enumerate(zip(sources, targets))
     ]
     for copy in copies:
         copy.start()
+
+    z, x = ids_ref[0], ids_ref[1]
+    for n in range(2 * NZ * NX):
+        sel_ref[n] = -1
+    for n in range(2 * NZ * 8):
+        block = stored_ref[n]
+        shard = block // SLOTS
+        place = n // 8 * NX + ((x - shard) & 3)
+        sel_ref[jnp.where(shard // NX == z, place, 2 * NZ * NX)] = block % SLOTS
+
     for copy in copies:
         copy.wait()
     q_refs, k_refs, v_refs = [[buf.at[n] for n in range(4)] for buf in (q_buf, k_buf, v_buf)]
     heads = k_buf.shape[2] // HEAD
     lane = lax.broadcasted_iota(jnp.int32, (BLOCK, BLOCK), 1)
     for j in range(NZ):
-        q_ref, out_ref = q_refs[j], result_ref.at[j]
+        q_ref, out_ref = q_refs[j], result_ref.at[(z - j) & 3]
 
         for b in range(2):
             row = b * BLOCK
@@ -220,7 +245,7 @@
                 n = (2 * w + s) * NY + k
                 copies.append(
                     pltpu.make_async_copy(
-                        arrays[k].at[pl.ds((2 + s) * rows, rows)],
+                        arrays[k].at[pl.ds(s * rows, rows)],
                         cot_buf.at[2 * w + s, pl.ds(k * rows, rows)],
                         sems.at[n],
                     )
@@ -273,22 +298,19 @@
     extra = extra.at[0, 0 : storage.shape[0]].set(storage.astype(jnp.bfloat16))
     q_pack = jnp.concatenate([queries, extra], axis=0)
 
-    q_all = exchange_z(jnp.broadcast_to(q_pack[None], (NZ, *q_pack.shape)))
-    k1, v3, v1, k3, swapped = together(
-        shift_x(memory_keys, 1),
-        shift_x(memory_values, -1),
-        shift_x(memory_values, 1),
-        shift_x(memory_keys, -1),
-        swap_zy(cotangent),
-    )
-    both = jnp.concatenate([cotangent, swapped], axis=0)
-    k2, v2, pair = shift_x(k1, 1), shift_x(v3, -1), flip_tensor(both, 2)
-    quad = jnp.concatenate([both[:rows], pair[:rows], both[rows:], pair[rows:]], axis=0)
-
-    stored = q_all[:, rows, 0:16].astype(jnp.int32).reshape(8, 8)
-    shards = z * NX + (x - jnp.arange(NX, dtype=jnp.int32)) % NX
-    hit = (stored // SLOTS)[:, None, :] == shards[None, :, None]
-    sel = (jnp.sum(jnp.where(hit, (stored % SLOTS)[:, None, :] + 1, 0), axis=2) - 1).reshape(-1)
+    k1, v3 = shift_x(memory_keys, 1), shift_x(memory_values, -1)
+    q1, q3 = shift_z(q_pack, 1), shift_z(q_pack, 3)
+    near = flip_tensor(cotangent, 2)
+    k1, v3, q1, q3, near, own_keys, own_values, q_late = together(
+        k1, v3, q1, q3, near, memory_keys, memory_values, q_pack
+    )
+    k2, v2, q2 = shift_x(k1, 1), shift_x(v3, -1), shift_z(q_late, 2)
+    k3, v1 = shift_x(own_keys, -1), shift_x(own_values, 1)
+    k2, v2, k3, v1, q2, near = together(k2, v2, k3, v1, q2, near)
+    pair = jnp.concatenate([cotangent, near], axis=0)
+    w1, w3, swapped = shift_y(pair, 1), shift_y(pair, 3), swap_zy(pair[:rows])
+    q_all = [q_pack, q1, q2, q3]
+    stored = jnp.stack([q[rows, 0:16] for q in q_all]).reshape(-1).astype(jnp.int32)
 
     local_out = pl.pallas_call(
         local_kernel,
@@ -296,26 +318,34 @@
         in_specs=[SM] + [VM] * 4,
         out_specs=VM,
         compiler_params=params,
+        cost_estimate=cost(4 * heads * rows * rows * HEAD, heads * rows * rows, 6 * rows * width),
         name="local_attention",
     )(gate, segments.reshape(1, rows), queries, local_keys, local_values)
 
-    k2, v2, quad = together(k2, v2, quad)
     parts = pl.pallas_call(
         memory_kernel,
         out_shape=jax.ShapeDtypeStruct((NZ, rows + EXTRA, width), jnp.bfloat16),
-        in_specs=[SM] + [HB] * 9,
+        in_specs=[SM] * 2 + [HB] * 12,
         out_specs=VM,
         scratch_shapes=[
             pltpu.VMEM((NZ, rows + EXTRA, width), jnp.bfloat16),
             pltpu.VMEM((NX, SLOTS * BLOCK, width), jnp.bfloat16),
             pltpu.VMEM((NX, SLOTS * BLOCK, width), jnp.bfloat16),
-            pltpu.SemaphoreType.DMA((9,)),
+            pltpu.SMEM((2 * NZ * NX + 1,), jnp.int32),
+            pltpu.SemaphoreType.DMA((12,)),
         ],
         compiler_params=params,
+        cost_estimate=cost(
+            64 * heads * rows * rows * HEAD, 8 * heads * rows * rows, 24 * rows * width
+        ),
         name="memory_attention",
-    )(sel, q_all, memory_keys, k1, k2, k3, memory_values, v1, v2, v3)
-
+    )(ids, stored, *in_hbm([*q_all, memory_keys, k1, k2, k3, memory_values, v1, v2, v3]))
+
+    parts, swapped, w1, w3, pair = together(parts, swapped, w1, w3, pair)
     back = exchange_z(parts)
+    tall = jnp.concatenate([swapped, flip_tensor(swapped, 2)], axis=0)
+    w2, t1, t3 = shift_y(pair, 2), shift_y(tall, 1), shift_y(tall, 3)
+    back, w2, t1, t3, tall = together(back, w2, t1, t3, tall)
     attention, att_t = pl.pallas_call(
         merge_kernel,
         out_shape=[
@@ -325,13 +355,18 @@
         in_specs=[SM] + [VM] * 2,
         out_specs=[VM] * 2,
         compiler_params=params,
+        cost_estimate=cost(32 * rows * width, 4 * rows, 16 * rows * width),
         name="merge",
     )(gate, local_out, back)
+    att_t, tall, pair = together(att_t, tall, pair)
     att_all = exchange_z(att_t)
-
-    y1, y2, y3 = [shift_y(quad, k) for k in (1, 2, 3)]
-    c0, c1, c2, c3 = [flip_tensor(v, 1) for v in (quad, y1, y2, y3)]
-    own, other = [quad, y1, y2, y3], [c0, c1, c2, c3]
+    t2 = shift_y(tall, 2)
+    tall = [tall, t1, t2, t3]
+    tall = tall + [flip_tensor(v, 1) for v in tall]
+    wide = [pair, w1, w2, w3]
+    wide = wide + [flip_tensor(v, 1) for v in wide]
+    att_all, *flipped = together(att_all, *tall[4:], *wide[4:])
+    tall, wide = in_hbm(tall[:4] + flipped[:4]), in_hbm(wide[:4] + flipped[4:])
 
     attention_grad = pl.pallas_call(
         grad_kernel,
@@ -341,7 +376,7 @@
             grid=(NY,),
             in_specs=[
                 pl.BlockSpec(
-                    (4 * rows, width), lambda g, ids: (0, 0), pipeline_mode=pl.Buffered(1)
+                    (2 * rows, width), lambda g, ids: (0, 0), pipeline_mode=pl.Buffered(1)
                 )
             ]
             * 8
@@ -350,8 +385,9 @@
             scratch_shapes=[pltpu.VMEM((rows, width), jnp.float32)],
         ),
         compiler_params=params,
+        cost_estimate=cost(32 * rows * width * width, 0, 64 * rows * width),
         name="attention_grad",
-    )(ids, *own, *other, *in_hbm([out_weight]))
+    )(ids, *wide, *in_hbm([out_weight]))
 
     mine, *sent = pl.pallas_call(
         weight_kernel,
@@ -365,8 +401,9 @@
             pltpu.SemaphoreType.DMA((16,)),
         ],
         compiler_params=params,
+        cost_estimate=cost(32 * rows * width * width, 0, 48 * rows * width),
         name="weight_partials",
-    )(ids, att_all, *own, *other)
+    )(ids, att_all, *tall)
     got = [shift_x(sent[n - 1], n) for n in (1, 2, 3)]
     weight_grad = (mine + got[0].astype(jnp.float32)) + (
         got[1].astype(jnp.float32) + got[2].astype(jnp.float32)

time: 155 us -> 158 us (1.019)
  the two profiles are of different devices: /device:TPU:56 before, /device:TPU:1 now
where the time goes in v3:
time: 158 us; the launch traced here: 155 us
  waiting for transfers between devices  70.6 us (45%)
  starting transfers between devices  49.9 us (32%)
  Pallas kernels  25.1 us (16%)
  local copies, waits for them, and re-layouts  5.8 us (4%)
  other arithmetic  2.79 us (2%)
    ppermute x10, waiting for transfers between devices, flip_tensor(): return lax.ppermute(value, 'tensor', [(t, t ^ bit) for t in range(16)])  34.8 us
    ppermute x6, waiting for transfers between devices, shift_y(): return lax.ppermute(value, 'tensor', pairs)  17.2 us
    all_to_all x2, starting transfers between devices, exchange_z(): lax.all_to_all(value, 'mem', split_axis=0, concat_axis=0, axis_index_grou...  15.5 us
    ppermute x9, waiting for transfers between devices, shift_x(): return lax.ppermute(value, 'mem', pairs)  12.5 us
    ppermute x9, starting transfers between devices, shift_x(): return lax.ppermute(value, 'mem', pairs)  10.3 us
    pallas_call x1, Pallas kernels, per_device(): pl.pallas_call(memory_kernel, out_shape=jax.ShapeDtypeStruct((NZ, rows +...  10.2 us
    ppermute x3, starting transfers between devices, shift_z(): return lax.ppermute(value, 'mem', pairs)  10.2 us
    pallas_call x1, Pallas kernels, per_device(): pl.pallas_call(grad_kernel, out_shape=jax.ShapeDtypeStruct((rows, width),...  6.85 us
  transfers between devices with their start and end apart: 31, of which 10 were waited for; matrix products, arithmetic and copies ran while one was open for 4% of the time, Pallas kernels for 12%

profile of v3, /device:TPU:1, one launch (start us, length us, event | category | flops | bytes accessed | tf_op | source)
XLA Modules:
  0.0 155.2 jit_solution(5571791726895305767)
XLA Ops:
  0.6 2.1 %collective-permute-start = (bf16[512,384]{1,0:T(8,128)(2,1)}, bf16[512,384]{1,0:T(8,128)(2,1)S(1)}, u32[]{:S(2)}, u32[]{:S(2)}) collective-permute-start(bf16[512,384]{1,0:T(8,128)(2,1)} %refs_4_.1), channel_id=1, source_target_pairs={{0,16},{16,32},{32,48},{48,0},{64,80},{80,96},{96,112},{112,64},{1... | collective-permute-start | bytes 1179656 | tf_op jit(solution)/shard_map/ppermute | solution.py:52
  2.7 1.4 collective-permute-start.1
  4.1 0.8 eq.19
  4.9 0.8 select_reduce_fusion
  5.7 1.0 fusion.1.refs_0_
  6.7 0.0 copy-start.24
  6.7 0.0 copy-start
  6.7 0.0 copy-start.1
  6.7 0.0 copy-start.2
  6.7 0.0 copy-start.3
  6.7 3.2 %collective-permute-start.2 = (bf16[272,384]{1,0:T(8,128)(2,1)S(1)}, bf16[272,384]{1,0:T(8,128)(2,1)}, u32[]{:S(2)}, u32[]{:S(2)}) collective-permute-start(bf16[272,384]{1,0:T(8,128)(2,1)S(1)} %fusion.1.refs_0_), channel_id=1, source_target_pairs={{0,64},{16,80},{32,96},{48,112},{64,128},{80,144},{96,160},{112,17... | collective-permute-start | bytes 626696 | tf_op jit(solution)/shard_map/ppermute | solution.py:57
  9.9 3.1 %collective-permute-start.3 = (bf16[272,384]{1,0:T(8,128)(2,1)S(1)}, bf16[272,384]{1,0:T(8,128)(2,1)}, u32[]{:S(2)}, u32[]{:S(2)}) collective-permute-start(bf16[272,384]{1,0:T(8,128)(2,1)S(1)} %fusion.1.refs_0_), channel_id=1, source_target_pairs={{0,192},{16,208},{32,224},{48,240},{64,0},{80,16},{96,32},{112,48}... | collective-permute-start | bytes 626696 | tf_op jit(solution)/shard_map/ppermute | solution.py:57
  13.0 0.7 collective-permute-start.4
  13.8 13.2 %collective-permute-done.4 = bf16[256,384]{1,0:T(8,128)(2,1)S(1)} collective-permute-done((bf16[256,384]{1,0:T(8,128)(2,1)}, bf16[256,384]{1,0:T(8,128)(2,1)S(1)}, u32[]{:S(2)}, u32[]{:S(2)}) %collective-permute-start.4) | collective-permute-done | bytes 196640 | tf_op jit(solution)/shard_map/ppermute | solution.py:77
  27.0 0.0 copy-start.14
  27.0 0.1 collective-permute-start.5
  27.1 2.7 %collective-permute-start.6 = (bf16[512,384]{1,0:T(8,128)(2,1)S(1)}, bf16[512,384]{1,0:T(8,128)(2,1)S(1)}, u32[]{:S(2)}, u32[]{:S(2)}) collective-permute-start(bf16[512,384]{1,0:T(8,128)(2,1)S(1)} %collective-permute-done.1.refs_11_), channel_id=1, source_target_pairs={{0,48},{16,0},{32,16},{48,32},{64,112},{80,64},{96,80},{112,96},{1... | collective-permute-start | bytes 1179656 | tf_op jit(solution)/shard_map/ppermute | solution.py:52
  29.8 0.1 collective-permute-start.7
  29.8 1.4 collective-permute-start.8
  31.2 3.9 %collective-permute-start.9 = (bf16[272,384]{1,0:T(8,128)(2,1)S(1)}, bf16[272,384]{1,0:T(8,128)(2,1)S(1)}, u32[]{:S(2)}, u32[]{:S(2)}) collective-permute-start(bf16[272,384]{1,0:T(8,128)(2,1)S(1)} %fusion.1.refs_0_), channel_id=1, source_target_pairs={{0,128},{16,144},{32,160},{48,176},{64,192},{80,208},{96,224},{112... | collective-permute-start | bytes 626696 | tf_op jit(solution)/shard_map/ppermute | solution.py:57
  35.1 0.9 constant_dynamic-update-slice_fusion.1
  36.1 6.1 %collective-permute-done.9.refs_2_ = bf16[272,384]{1,0:T(8,128)(2,1)S(1)} collective-permute-done((bf16[272,384]{1,0:T(8,128)(2,1)S(1)}, bf16[272,384]{1,0:T(8,128)(2,1)S(1)}, u32[]{:S(2)}, u32[]{:S(2)}) %collective-permute-start.9) | collective-permute-done | bytes 208928 | tf_op jit(solution)/shard_map/ppermute | solution.py:57
  42.2 2.6 %collective-permute-done.7.refs_7_ = bf16[512,384]{1,0:T(8,128)(2,1)S(1)} collective-permute-done((bf16[512,384]{1,0:T(8,128)(2,1)}, bf16[512,384]{1,0:T(8,128)(2,1)S(1)}, u32[]{:S(2)}, u32[]{:S(2)}) %collective-permute-start.7) | collective-permute-done | bytes 393248 | tf_op jit(solution)/shard_map/ppermute | solution.py:52
  44.8 0.9 collective-permute-done.8.refs_9_
  45.8 1.4 collective-permute-start.11
  47.2 1.5 collective-permute-start.12
  48.7 1.6 %collective-permute-start.10 = (bf16[256,384]{1,0:T(8,128)(2,1)}, bf16[256,384]{1,0:T(8,128)(2,1)S(1)}, u32[]{:S(2)}, u32[]{:S(2)}) collective-permute-start(bf16[256,384]{1,0:T(8,128)(2,1)} %param.23), channel_id=1, source_target_pairs={{0,0},{1,1},{2,2},{3,3},{4,64},{5,65},{6,66},{7,67},{8,128},{9,129... | collective-permute-start | bytes 589832 | tf_op jit(solution)/shard_map/ppermute | solution.py:87
  50.3 0.1 stack.26.ids_ref
  50.4 0.7 slice.28
  51.0 0.7 slice.26
  51.7 0.7 slice.27
  52.4 0.1 reshape.49.stored_ref
  52.5 10.2 %memory_attention.1 = bf16[4,272,384]{2,1,0:T(8,128)(2,1)} custom-call(s32[6]{0:T(128)S(1)} %stack.26.ids_ref, s32[64]{0:T(128)S(1)} %reshape.49.stored_ref, bf16[272,384]{1,0:T(8,128)(2,1)} %copy-done.12, bf16[272,384]{1,0:T(8,128)(2,1)} %collective-permute-done.2.refs_1_, bf16[272,384]{1,0:T(8,128)(2,1)} %copy-done.23, ...), custom_call_target="tpu_custom_call" | custom-call | flops 1610612736 | bytes 2359296 | tf_op jit(solution)/shard_map/memory_attention/pallas_call | solution.py:325
  62.7 0.0 copy-start.5
  62.8 11.3 %all-to-all-start = ((bf16[4,272,384]{2,1,0:T(8,128)(2,1)}), bf16[4,272,384]{2,1,0:T(8,128)(2,1)S(1)}, u32[]{:S(2)}, u32[]{:S(2)}) async-start(bf16[4,272,384]{2,1,0:T(8,128)(2,1)} %memory_attention.1), calls=%async_computation | async-start | bytes 1671168 | tf_op jit(solution)/shard_map/all_to_all | solution.py:62
  74.1 21.4 %collective-permute-done.14 = bf16[256,384]{1,0:T(8,128)(2,1)S(1)} collective-permute-done((bf16[256,384]{1,0:T(8,128)(2,1)S(1)}, bf16[256,384]{1,0:T(8,128)(2,1)S(1)}, u32[]{:S(2)}, u32[]{:S(2)}) %collective-permute-start.14) | collective-permute-done | bytes 196640 | tf_op jit(solution)/shard_map/ppermute | solution.py:77
  95.5 0.1 collective-permute-start.15
  95.6 2.7 %collective-permute-start.16 = (bf16[512,384]{1,0:T(8,128)(2,1)S(1)}, bf16[512,384]{1,0:T(8,128)(2,1)}, u32[]{:S(2)}, u32[]{:S(2)}) collective-permute-start(bf16[512,384]{1,0:T(8,128)(2,1)S(1)} %constant_dynamic-update-slice_fusion.2.refs_1_), channel_id=1, source_target_pairs={{0,12},{1,13},{2,14},{3,15},{4,0},{5,1},{6,2},{7,3},{8,4},{9,5},{1... | collective-permute-start | bytes 1179656 | tf_op jit(solution)/shard_map/ppermute | solution.py:69
  98.3 1.4 local_attention.1.local_ref
  99.7 7.4 %collective-permute-done.15.refs_2_ = bf16[512,384]{1,0:T(8,128)(2,1)} collective-permute-done((bf16[512,384]{1,0:T(8,128)(2,1)S(1)}, bf16[512,384]{1,0:T(8,128)(2,1)}, u32[]{:S(2)}, u32[]{:S(2)}) %collective-permute-start.15) | collective-permute-done | bytes 393248 | tf_op jit(solution)/shard_map/ppermute | solution.py:69
  107.1 2.3 %merge.1 = (bf16[256,384]{1,0:T(8,128)(2,1)}, bf16[4,384,256]{2,1,0:T(8,128)(2,1)}) custom-call(f32[3]{0:T(128)S(1)} %add_divide_fusion.gate_ref, f32[256,384]{1,0:T(8,128)S(1)} %local_attention.1.local_ref, bf16[4,272,384]{2,1,0:T(8,128)(2,1)S(1)} %all-to-all-done.back_ref), custom_call_target="tpu_custom_call" | custom-call | flops 3145728 | bytes 1572864 | tf_op jit(solution)/shard_map/merge/pallas_call | solution.py:349
  109.5 4.2 %all-to-all-start.1 = ((bf16[4,384,256]{2,1,0:T(8,128)(2,1)}), bf16[4,384,256]{2,1,0:T(8,128)(2,1)S(1)}, u32[]{:S(2)}, u32[]{:S(2)}) async-start(bf16[4,384,256]{2,1,0:T(8,128)(2,1)} %get-tuple-element.82), calls=%async_computation.1 | async-start | bytes 1572864 | tf_op jit(solution)/shard_map/all_to_all | solution.py:62
  113.7 2.2 %collective-permute-start.23 = (bf16[512,384]{1,0:T(8,128)(2,1)S(1)}, bf16[512,384]{1,0:T(8,128)(2,1)S(1)}, u32[]{:S(2)}, u32[]{:S(2)}) collective-permute-start(bf16[512,384]{1,0:T(8,128)(2,1)S(1)} %collective-permute-done.11.refs_1_), channel_id=1, source_target_pairs={{0,1},{1,0},{2,3},{3,2},{4,5},{5,4},{6,7},{7,6},{8,9},{9,8},{10,11... | collective-permute-start | bytes 1179656 | tf_op jit(solution)/shard_map/ppermute | solution.py:77
  115.8 0.5 collective-permute-start.17
  116.4 1.2 collective-permute-start.19
  117.5 0.3 collective-permute-start.18
  117.8 0.3 collective-permute-start.21
  118.1 0.2 collective-permute-done.25.refs_7_
  118.3 0.4 collective-permute-start.22
  118.7 0.3 collective-permute-start.24
  119.0 9.8 %collective-permute-done.19.refs_3_ = bf16[512,384]{1,0:T(8,128)(2,1)S(1)} collective-permute-done((bf16[512,384]{1,0:T(8,128)(2,1)}, bf16[512,384]{1,0:T(8,128)(2,1)S(1)}, u32[]{:S(2)}, u32[]{:S(2)}) %collective-permute-start.19) | collective-permute-done | bytes 393248 | tf_op jit(solution)/shard_map/ppermute | solution.py:69
  128.8 0.8 collective-permute-start.20
  129.7 0.7 copy-done.21
  130.4 0.1 copy-done.22
  130.5 0.2 copy-done.10
  130.7 0.7 copy-done.11
  131.4 4.3 %weight_partials.1 = (f32[384,384]{1,0:T(8,128)S(1)}, bf16[384,384]{1,0:T(8,128)(2,1)S(1)}, bf16[384,384]{1,0:T(8,128)(2,1)S(1)}, bf16[384,384]{1,0:T(8,128)(2,1)S(1)}) custom-call(s32[6]{0:T(128)S(1)} %stack.26.ids_ref, bf16[4,384,256]{2,1,0:T(8,128)(2,1)S(1)} %all-to-all-done.1.refs_0_, bf16[512,384]{1,0:T(8,128)(2,1)} %copy-done.13, ...), custom_call_target="tpu_custom_call" | custom-call | flops 1207959552 | bytes 4718592 | tf_op jit(solution)/shard_map/weight_partials/pallas_call | solution.py:392
  135.8 1.9 %collective-permute-start.28 = (bf16[384,384]{1,0:T(8,128)(2,1)S(1)}, bf16[384,384]{1,0:T(8,128)(2,1)S(1)}, u32[]{:S(2)}, u32[]{:S(2)}) collective-permute-start(bf16[384,384]{1,0:T(8,128)(2,1)S(1)} %get-tuple-element.98), channel_id=1, source_target_pairs={{0,48},{16,0},{32,16},{48,32},{64,112},{80,64},{96,80},{112,96},{1... | collective-permute-start | bytes 884744 | tf_op jit(solution)/shard_map/ppermute | solution.py:52
  137.7 0.2 collective-permute-start.27
  137.9 0.5 collective-permute-start.26
  138.4 6.9 %attention_grad.1 = bf16[256,384]{1,0:T(8,128)(2,1)} custom-call(s32[6]{0:T(128)S(1)} %stack.26.ids_ref, bf16[512,384]{1,0:T(8,128)(2,1)} %copy-done.4, bf16[512,384]{1,0:T(8,128)(2,1)} %copy-done.5, bf16[512,384]{1,0:T(8,128)(2,1)} %copy-done.7, bf16[512,384]{1,0:T(8,128)(2,1)} %copy-done.6, bf16[512,384]{1,0:T(8,128)(2,1)} %copy-done.10, ...), custom_call_target="tpu_custom_call" | custom-call | flops 1207959552 | bytes 6291456 | tf_op jit(solution)/shard_map/attention_grad/pallas_call | solution.py:371
  145.3 1.8 %collective-permute-done.27 = bf16[384,384]{1,0:T(8,128)(2,1)S(1)} collective-permute-done((bf16[384,384]{1,0:T(8,128)(2,1)S(1)}, bf16[384,384]{1,0:T(8,128)(2,1)S(1)}, u32[]{:S(2)}, u32[]{:S(2)}) %collective-permute-start.27) | collective-permute-done | bytes 294944 | tf_op jit(solution)/shard_map/ppermute | solution.py:52
  147.0 7.2 %collective-permute-done.26 = bf16[384,384]{1,0:T(8,128)(2,1)S(1)} collective-permute-done((bf16[384,384]{1,0:T(8,128)(2,1)S(1)}, bf16[384,384]{1,0:T(8,128)(2,1)S(1)}, u32[]{:S(2)}, u32[]{:S(2)}) %collective-permute-start.26) | collective-permute-done | bytes 294944 | tf_op jit(solution)/shard_map/ppermute | solution.py:52
  154.2 1.0 add_add_fusion
  (69 shorter events, 0.3 us)
Async XLA Ops:
  0.6 26.3 %collective-permute-start = (bf16[512,384]{1,0:T(8,128)(2,1)}, bf16[512,384]{1,0:T(8,128)(2,1)S(1)}, u32[]{:S(2)}, u32[]{:S(2)}) collective-permute-start(bf16[512,384]{1,0:T(8,128)(2,1)} %refs_4_.1), channel_id=1, source_target_pairs={{0,16},{16,32},{32,48},{48,0},{64,80},{80,96},{96,112},{112,64},{1... | collective-permute-start | bytes 1179656 | tf_op jit(solution)/shard_map/ppermute | solution.py:52
  2.7 24.2 %collective-permute-start.1 = (bf16[512,384]{1,0:T(8,128)(2,1)}, bf16[512,384]{1,0:T(8,128)(2,1)S(1)}, u32[]{:S(2)}, u32[]{:S(2)}) collective-permute-start(bf16[512,384]{1,0:T(8,128)(2,1)} %refs_8_.2), channel_id=1, source_target_pairs={{0,48},{16,0},{32,16},{48,32},{64,112},{80,64},{96,80},{112,96},{1... | collective-permute-start | bytes 1179656 | tf_op jit(solution)/shard_map/ppermute | solution.py:52
  6.7 45.8 %copy-start.12 = (bf16[272,384]{1,0:T(8,128)(2,1)}, bf16[272,384]{1,0:T(8,128)(2,1)S(1)}, u32[]{:S(2)}) copy-start(bf16[272,384]{1,0:T(8,128)(2,1)S(1)} %fusion.1.refs_0_) | copy-start | bytes 626692
  6.7 91.6 %copy-start.24 = (f32[3]{0:T(128)S(1)}, f32[3]{0:T(128)}, u32[]{:S(2)}) copy-start(f32[3]{0:T(128)} %param.21) | copy-start | bytes 40
  6.7 91.6 %copy-start = (bf16[256,384]{1,0:T(8,128)(2,1)S(1)}, bf16[256,384]{1,0:T(8,128)(2,1)}, u32[]{:S(2)}) copy-start(bf16[256,384]{1,0:T(8,128)(2,1)} %q_ref.1) | copy-start | bytes 589828
  6.7 91.6 %copy-start.1 = (bf16[256,384]{1,0:T(8,128)(2,1)S(1)}, bf16[256,384]{1,0:T(8,128)(2,1)}, u32[]{:S(2)}) copy-start(bf16[256,384]{1,0:T(8,128)(2,1)} %k_ref.1) | copy-start | bytes 589828
  6.7 91.6 %copy-start.2 = (bf16[256,384]{1,0:T(8,128)(2,1)S(1)}, bf16[256,384]{1,0:T(8,128)(2,1)}, u32[]{:S(2)}) copy-start(bf16[256,384]{1,0:T(8,128)(2,1)} %v_ref.1) | copy-start | bytes 589828
  6.7 91.6 %copy-start.3 = (s32[256]{0:T(256)S(1)}, s32[256]{0:T(256)}, u32[]{:S(2)}) copy-start(s32[256]{0:T(256)} %param.16) | copy-start | bytes 3076
  6.7 20.2 %collective-permute-start.2 = (bf16[272,384]{1,0:T(8,128)(2,1)S(1)}, bf16[272,384]{1,0:T(8,128)(2,1)}, u32[]{:S(2)}, u32[]{:S(2)}) collective-permute-start(bf16[272,384]{1,0:T(8,128)(2,1)S(1)} %fusion.1.refs_0_), channel_id=1, source_target_pairs={{0,64},{16,80},{32,96},{48,112},{64,128},{80,144},{96,160},{112,17... | collective-permute-start | bytes 626696 | tf_op jit(solution)/shard_map/ppermute | solution.py:57
  9.9 17.1 %collective-permute-start.3 = (bf16[272,384]{1,0:T(8,128)(2,1)S(1)}, bf16[272,384]{1,0:T(8,128)(2,1)}, u32[]{:S(2)}, u32[]{:S(2)}) collective-permute-start(bf16[272,384]{1,0:T(8,128)(2,1)S(1)} %fusion.1.refs_0_), channel_id=1, source_target_pairs={{0,192},{16,208},{32,224},{48,240},{64,0},{80,16},{96,32},{112,48}... | collective-permute-start | bytes 626696 | tf_op jit(solution)/shard_map/ppermute | solution.py:57
  13.0 13.9 %collective-permute-start.4 = (bf16[256,384]{1,0:T(8,128)(2,1)}, bf16[256,384]{1,0:T(8,128)(2,1)S(1)}, u32[]{:S(2)}, u32[]{:S(2)}) collective-permute-start(bf16[256,384]{1,0:T(8,128)(2,1)} %param.23), channel_id=1, source_target_pairs={{0,2},{1,3},{2,0},{3,1},{4,6},{5,7},{6,4},{7,5},{8,10},{9,11},{10,... | collective-permute-start | bytes 589832 | tf_op jit(solution)/shard_map/ppermute | solution.py:77
  27.0 25.5 %copy-start.14 = (bf16[512,384]{1,0:T(8,128)(2,1)}, bf16[512,384]{1,0:T(8,128)(2,1)S(1)}, u32[]{:S(2)}) copy-start(bf16[512,384]{1,0:T(8,128)(2,1)S(1)} %collective-permute-done.refs_5_) | copy-start | bytes 1179652
  27.0 25.5 %copy-start.15 = (bf16[512,384]{1,0:T(8,128)(2,1)}, bf16[512,384]{1,0:T(8,128)(2,1)S(1)}, u32[]{:S(2)}) copy-start(bf16[512,384]{1,0:T(8,128)(2,1)S(1)} %collective-permute-done.1.refs_11_) | copy-start | bytes 1179652
  27.0 15.2 %collective-permute-start.5 = (bf16[512,384]{1,0:T(8,128)(2,1)S(1)}, bf16[512,384]{1,0:T(8,128)(2,1)S(1)}, u32[]{:S(2)}, u32[]{:S(2)}) collective-permute-start(bf16[512,384]{1,0:T(8,128)(2,1)S(1)} %collective-permute-done.refs_5_), channel_id=1, source_target_pairs={{0,16},{16,32},{32,48},{48,0},{64,80},{80,96},{96,112},{112,64},{1... | collective-permute-start | bytes 1179656 | tf_op jit(solution)/shard_map/ppermute | solution.py:52
  27.1 15.1 %collective-permute-start.6 = (bf16[512,384]{1,0:T(8,128)(2,1)S(1)}, bf16[512,384]{1,0:T(8,128)(2,1)S(1)}, u32[]{:S(2)}, u32[]{:S(2)}) collective-permute-start(bf16[512,384]{1,0:T(8,128)(2,1)S(1)} %collective-permute-done.1.refs_11_), channel_id=1, source_target_pairs={{0,48},{16,0},{32,16},{48,32},{64,112},{80,64},{96,80},{112,96},{1... | collective-permute-start | bytes 1179656 | tf_op jit(solution)/shard_map/ppermute | solution.py:52
  29.8 15.1 %collective-permute-start.7 = (bf16[512,384]{1,0:T(8,128)(2,1)}, bf16[512,384]{1,0:T(8,128)(2,1)S(1)}, u32[]{:S(2)}, u32[]{:S(2)}) collective-permute-start(bf16[512,384]{1,0:T(8,128)(2,1)} %refs_4_.1), channel_id=1, source_target_pairs={{0,48},{16,0},{32,16},{48,32},{64,112},{80,64},{96,80},{112,96},{1... | collective-permute-start | bytes 1179656 | tf_op jit(solution)/shard_map/ppermute | solution.py:52
  29.8 15.9 %collective-permute-start.8 = (bf16[512,384]{1,0:T(8,128)(2,1)}, bf16[512,384]{1,0:T(8,128)(2,1)S(1)}, u32[]{:S(2)}, u32[]{:S(2)}) collective-permute-start(bf16[512,384]{1,0:T(8,128)(2,1)} %refs_8_.2), channel_id=1, source_target_pairs={{0,16},{16,32},{32,48},{48,0},{64,80},{80,96},{96,112},{112,64},{1... | collective-permute-start | bytes 1179656 | tf_op jit(solution)/shard_map/ppermute | solution.py:52
  31.2 11.0 %collective-permute-start.9 = (bf16[272,384]{1,0:T(8,128)(2,1)S(1)}, bf16[272,384]{1,0:T(8,128)(2,1)S(1)}, u32[]{:S(2)}, u32[]{:S(2)}) collective-permute-start(bf16[272,384]{1,0:T(8,128)(2,1)S(1)} %fusion.1.refs_0_), channel_id=1, source_target_pairs={{0,128},{16,144},{32,160},{48,176},{64,192},{80,208},{96,224},{112... | collective-permute-start | bytes 626696 | tf_op jit(solution)/shard_map/ppermute | solution.py:57
  42.2 8.1 %copy-start.23 = (bf16[272,384]{1,0:T(8,128)(2,1)}, bf16[272,384]{1,0:T(8,128)(2,1)S(1)}, u32[]{:S(2)}) copy-start(bf16[272,384]{1,0:T(8,128)(2,1)S(1)} %collective-permute-done.9.refs_2_) | copy-start | bytes 626692
  42.2 5.0 %copy-start.16 = (bf16[512,384]{1,0:T(8,128)(2,1)}, bf16[512,384]{1,0:T(8,128)(2,1)S(1)}, u32[]{:S(2)}) copy-start(bf16[512,384]{1,0:T(8,128)(2,1)S(1)} %collective-permute-done.5.refs_6_) | copy-start | bytes 1179652
  42.2 3.5 %copy-start.17 = (bf16[512,384]{1,0:T(8,128)(2,1)}, bf16[512,384]{1,0:T(8,128)(2,1)S(1)}, u32[]{:S(2)}) copy-start(bf16[512,384]{1,0:T(8,128)(2,1)S(1)} %collective-permute-done.6.refs_10_) | copy-start | bytes 1179652
  44.8 1.0 copy-start.18
  45.7 3.0 %copy-start.19 = (bf16[512,384]{1,0:T(8,128)(2,1)}, bf16[512,384]{1,0:T(8,128)(2,1)S(1)}, u32[]{:S(2)}) copy-start(bf16[512,384]{1,0:T(8,128)(2,1)S(1)} %collective-permute-done.8.refs_9_) | copy-start | bytes 1179652
  45.8 72.5 %copy-start.4 = (bf16[512,384]{1,0:T(8,128)(2,1)}, bf16[512,384]{1,0:T(8,128)(2,1)S(1)}, u32[]{:S(2)}) copy-start(bf16[512,384]{1,0:T(8,128)(2,1)S(1)} %constant_dynamic-update-slice_fusion.refs_0_) | copy-start | bytes 1179652
  45.8 16.9 %collective-permute-start.11 = (bf16[512,384]{1,0:T(8,128)(2,1)S(1)}, bf16[512,384]{1,0:T(8,128)(2,1)S(1)}, u32[]{:S(2)}, u32[]{:S(2)}) collective-permute-start(bf16[512,384]{1,0:T(8,128)(2,1)S(1)} %constant_dynamic-update-slice_fusion.refs_0_), channel_id=1, source_target_pairs={{0,4},{1,5},{2,6},{3,7},{4,8},{5,9},{6,10},{7,11},{8,12},{9,13},{1... | collective-permute-start | bytes 1179656 | tf_op jit(solution)/shard_map/ppermute | solution.py:69
  47.2 15.6 %collective-permute-start.12 = (bf16[512,384]{1,0:T(8,128)(2,1)S(1)}, bf16[512,384]{1,0:T(8,128)(2,1)S(1)}, u32[]{:S(2)}, u32[]{:S(2)}) collective-permute-start(bf16[512,384]{1,0:T(8,128)(2,1)S(1)} %constant_dynamic-update-slice_fusion.refs_0_), channel_id=1, source_target_pairs={{0,12},{1,13},{2,14},{3,15},{4,0},{5,1},{6,2},{7,3},{8,4},{9,5},{1... | collective-permute-start | bytes 1179656 | tf_op jit(solution)/shard_map/ppermute | solution.py:69
  48.7 14.0 %collective-permute-start.10 = (bf16[256,384]{1,0:T(8,128)(2,1)}, bf16[256,384]{1,0:T(8,128)(2,1)S(1)}, u32[]{:S(2)}, u32[]{:S(2)}) collective-permute-start(bf16[256,384]{1,0:T(8,128)(2,1)} %param.23), channel_id=1, source_target_pairs={{0,0},{1,1},{2,2},{3,3},{4,64},{5,65},{6,66},{7,67},{8,128},{9,129... | collective-permute-start | bytes 589832 | tf_op jit(solution)/shard_map/ppermute | solution.py:87
  62.7 73.1 %copy-start.5 = (bf16[512,384]{1,0:T(8,128)(2,1)}, bf16[512,384]{1,0:T(8,128)(2,1)S(1)}, u32[]{:S(2)}) copy-start(bf16[512,384]{1,0:T(8,128)(2,1)S(1)} %collective-permute-done.11.refs_1_) | copy-start | bytes 1179652
  62.7 73.1 %copy-start.6 = (bf16[512,384]{1,0:T(8,128)(2,1)}, bf16[512,384]{1,0:T(8,128)(2,1)S(1)}, u32[]{:S(2)}) copy-start(bf16[512,384]{1,0:T(8,128)(2,1)S(1)} %collective-permute-done.12.refs_3_) | copy-start | bytes 1179652
  62.8 44.4 %all-to-all-start = ((bf16[4,272,384]{2,1,0:T(8,128)(2,1)}), bf16[4,272,384]{2,1,0:T(8,128)(2,1)S(1)}, u32[]{:S(2)}, u32[]{:S(2)}) async-start(bf16[4,272,384]{2,1,0:T(8,128)(2,1)} %memory_attention.1), calls=%async_computation | async-start | bytes 1671168 | tf_op jit(solution)/shard_map/all_to_all | solution.py:62
  74.0 21.5 %collective-permute-start.14 = (bf16[256,384]{1,0:T(8,128)(2,1)S(1)}, bf16[256,384]{1,0:T(8,128)(2,1)S(1)}, u32[]{:S(2)}, u32[]{:S(2)}) collective-permute-start(bf16[256,384]{1,0:T(8,128)(2,1)S(1)} %collective-permute-done.10), channel_id=1, source_target_pairs={{0,2},{1,3},{2,0},{3,1},{4,6},{5,7},{6,4},{7,5},{8,10},{9,11},{10,... | collective-permute-start | bytes 589832 | tf_op jit(solution)/shard_map/ppermute | solution.py:77
  74.0 25.7 %collective-permute-start.13 = (bf16[512,384]{1,0:T(8,128)(2,1)S(1)}, bf16[512,384]{1,0:T(8,128)(2,1)S(1)}, u32[]{:S(2)}, u32[]{:S(2)}) collective-permute-start(bf16[512,384]{1,0:T(8,128)(2,1)S(1)} %constant_dynamic-update-slice_fusion.refs_0_), channel_id=1, source_target_pairs={{0,8},{1,9},{2,10},{3,11},{4,12},{5,13},{6,14},{7,15},{8,0},{9,1},... | collective-permute-start | bytes 1179656 | tf_op jit(solution)/shard_map/ppermute | solution.py:69
  95.5 11.6 %copy-start.13 = (bf16[512,384]{1,0:T(8,128)(2,1)}, bf16[512,384]{1,0:T(8,128)(2,1)S(1)}, u32[]{:S(2)}) copy-start(bf16[512,384]{1,0:T(8,128)(2,1)S(1)} %constant_dynamic-update-slice_fusion.2.refs_1_) | copy-start | bytes 1179652
  95.5 11.6 %collective-permute-start.15 = (bf16[512,384]{1,0:T(8,128)(2,1)S(1)}, bf16[512,384]{1,0:T(8,128)(2,1)}, u32[]{:S(2)}, u32[]{:S(2)}) collective-permute-start(bf16[512,384]{1,0:T(8,128)(2,1)S(1)} %constant_dynamic-update-slice_fusion.2.refs_1_), channel_id=1, source_target_pairs={{0,4},{1,5},{2,6},{3,7},{4,8},{5,9},{6,10},{7,11},{8,12},{9,13},{1... | collective-permute-start | bytes 1179656 | tf_op jit(solution)/shard_map/ppermute | solution.py:69
  95.6 11.5 %collective-permute-start.16 = (bf16[512,384]{1,0:T(8,128)(2,1)S(1)}, bf16[512,384]{1,0:T(8,128)(2,1)}, u32[]{:S(2)}, u32[]{:S(2)}) collective-permute-start(bf16[512,384]{1,0:T(8,128)(2,1)S(1)} %constant_dynamic-update-slice_fusion.2.refs_1_), channel_id=1, source_target_pairs={{0,12},{1,13},{2,14},{3,15},{4,0},{5,1},{6,2},{7,3},{8,4},{9,5},{1... | collective-permute-start | bytes 1179656 | tf_op jit(solution)/shard_map/ppermute | solution.py:69
  99.7 38.7 %copy-start.7 = (bf16[512,384]{1,0:T(8,128)(2,1)}, bf16[512,384]{1,0:T(8,128)(2,1)S(1)}, u32[]{:S(2)}) copy-start(bf16[512,384]{1,0:T(8,128)(2,1)S(1)} %collective-permute-done.13.refs_2_) | copy-start | bytes 1179652
  109.5 22.0 %all-to-all-start.1 = ((bf16[4,384,256]{2,1,0:T(8,128)(2,1)}), bf16[4,384,256]{2,1,0:T(8,128)(2,1)S(1)}, u32[]{:S(2)}, u32[]{:S(2)}) async-start(bf16[4,384,256]{2,1,0:T(8,128)(2,1)} %get-tuple-element.82), calls=%async_computation.1 | async-start | bytes 1572864 | tf_op jit(solution)/shard_map/all_to_all | solution.py:62
  113.7 4.2 %collective-permute-start.23 = (bf16[512,384]{1,0:T(8,128)(2,1)S(1)}, bf16[512,384]{1,0:T(8,128)(2,1)S(1)}, u32[]{:S(2)}, u32[]{:S(2)}) collective-permute-start(bf16[512,384]{1,0:T(8,128)(2,1)S(1)} %collective-permute-done.11.refs_1_), channel_id=1, source_target_pairs={{0,1},{1,0},{2,3},{3,2},{4,5},{5,4},{6,7},{7,6},{8,9},{9,8},{10,11... | collective-permute-start | bytes 1179656 | tf_op jit(solution)/shard_map/ppermute | solution.py:77
  115.8 2.5 %collective-permute-start.25 = (bf16[512,384]{1,0:T(8,128)(2,1)S(1)}, bf16[512,384]{1,0:T(8,128)(2,1)S(1)}, u32[]{:S(2)}, u32[]{:S(2)}) collective-permute-start(bf16[512,384]{1,0:T(8,128)(2,1)S(1)} %collective-permute-done.12.refs_3_), channel_id=1, source_target_pairs={{0,1},{1,0},{2,3},{3,2},{4,5},{5,4},{6,7},{7,6},{8,9},{9,8},{10,11... | collective-permute-start | bytes 1179656 | tf_op jit(solution)/shard_map/ppermute | solution.py:77
  115.8 2.9 %collective-permute-start.17 = (bf16[512,384]{1,0:T(8,128)(2,1)}, bf16[512,384]{1,0:T(8,128)(2,1)}, u32[]{:S(2)}, u32[]{:S(2)}) collective-permute-start(bf16[512,384]{1,0:T(8,128)(2,1)} %copy-done.13), channel_id=1, source_target_pairs={{0,1},{1,0},{2,3},{3,2},{4,5},{5,4},{6,7},{7,6},{8,9},{9,8},{10,11... | collective-permute-start | bytes 1179656 | tf_op jit(solution)/shard_map/ppermute | solution.py:77
  116.4 12.5 %collective-permute-start.19 = (bf16[512,384]{1,0:T(8,128)(2,1)}, bf16[512,384]{1,0:T(8,128)(2,1)S(1)}, u32[]{:S(2)}, u32[]{:S(2)}) collective-permute-start(bf16[512,384]{1,0:T(8,128)(2,1)} %copy-done.13), channel_id=1, source_target_pairs={{0,8},{1,9},{2,10},{3,11},{4,12},{5,13},{6,14},{7,15},{8,0},{9,1},... | collective-permute-start | bytes 1179656 | tf_op jit(solution)/shard_map/ppermute | solution.py:69
  117.5 12.1 %collective-permute-start.18 = (bf16[512,384]{1,0:T(8,128)(2,1)}, bf16[512,384]{1,0:T(8,128)(2,1)S(1)}, u32[]{:S(2)}, u32[]{:S(2)}) collective-permute-start(bf16[512,384]{1,0:T(8,128)(2,1)} %collective-permute-done.15.refs_2_), channel_id=1, source_target_pairs={{0,1},{1,0},{2,3},{3,2},{4,5},{5,4},{6,7},{7,6},{8,9},{9,8},{10,11... | collective-permute-start | bytes 1179656 | tf_op jit(solution)/shard_map/ppermute | solution.py:77
  117.8 13.6 %copy-start.8 = (bf16[512,384]{1,0:T(8,128)(2,1)}, bf16[512,384]{1,0:T(8,128)(2,1)S(1)}, u32[]{:S(2)}) copy-start(bf16[512,384]{1,0:T(8,128)(2,1)S(1)} %collective-permute-done.23.refs_5_) | copy-start | bytes 1179652
  117.8 11.8 %collective-permute-start.21 = (bf16[512,384]{1,0:T(8,128)(2,1)}, bf16[512,384]{1,0:T(8,128)(2,1)S(1)}, u32[]{:S(2)}, u32[]{:S(2)}) collective-permute-start(bf16[512,384]{1,0:T(8,128)(2,1)} %collective-permute-done.16.refs_4_), channel_id=1, source_target_pairs={{0,1},{1,0},{2,3},{3,2},{4,5},{5,4},{6,7},{7,6},{8,9},{9,8},{10,11... | collective-permute-start | bytes 1179656 | tf_op jit(solution)/shard_map/ppermute | solution.py:77
  118.3 13.1 %copy-start.9 = (bf16[512,384]{1,0:T(8,128)(2,1)}, bf16[512,384]{1,0:T(8,128)(2,1)S(1)}, u32[]{:S(2)}) copy-start(bf16[512,384]{1,0:T(8,128)(2,1)S(1)} %collective-permute-done.25.refs_7_) | copy-start | bytes 1179652
  118.3 11.3 %collective-permute-start.22 = (bf16[512,384]{1,0:T(8,128)(2,1)S(1)}, bf16[512,384]{1,0:T(8,128)(2,1)S(1)}, u32[]{:S(2)}, u32[]{:S(2)}) collective-permute-start(bf16[512,384]{1,0:T(8,128)(2,1)S(1)} %constant_dynamic-update-slice_fusion.refs_0_), channel_id=1, source_target_pairs={{0,1},{1,0},{2,3},{3,2},{4,5},{5,4},{6,7},{7,6},{8,9},{9,8},{10,11... | collective-permute-start | bytes 1179656 | tf_op jit(solution)/shard_map/ppermute | solution.py:77
  118.7 10.9 %collective-permute-start.24 = (bf16[512,384]{1,0:T(8,128)(2,1)S(1)}, bf16[512,384]{1,0:T(8,128)(2,1)S(1)}, u32[]{:S(2)}, u32[]{:S(2)}) collective-permute-start(bf16[512,384]{1,0:T(8,128)(2,1)S(1)} %collective-permute-done.13.refs_2_), channel_id=1, source_target_pairs={{0,1},{1,0},{2,3},{3,2},{4,5},{5,4},{6,7},{7,6},{8,9},{9,8},{10,11... | collective-permute-start | bytes 1179656 | tf_op jit(solution)/shard_map/ppermute | solution.py:77
  128.8 0.8 copy-start.20
  128.8 2.6 %collective-permute-start.20 = (bf16[512,384]{1,0:T(8,128)(2,1)S(1)}, bf16[512,384]{1,0:T(8,128)(2,1)}, u32[]{:S(2)}, u32[]{:S(2)}) collective-permute-start(bf16[512,384]{1,0:T(8,128)(2,1)S(1)} %collective-permute-done.19.refs_3_), channel_id=1, source_target_pairs={{0,1},{1,0},{2,3},{3,2},{4,5},{5,4},{6,7},{7,6},{8,9},{9,8},{10,11... | collective-permute-start | bytes 1179656 | tf_op jit(solution)/shard_map/ppermute | solution.py:77
  129.6 0.8 copy-start.21
  129.6 0.9 copy-start.22
  129.6 1.0 copy-start.10
  130.7 0.7 copy-start.11
  135.8 9.5 %collective-permute-start.28 = (bf16[384,384]{1,0:T(8,128)(2,1)S(1)}, bf16[384,384]{1,0:T(8,128)(2,1)S(1)}, u32[]{:S(2)}, u32[]{:S(2)}) collective-permute-start(bf16[384,384]{1,0:T(8,128)(2,1)S(1)} %get-tuple-element.98), channel_id=1, source_target_pairs={{0,48},{16,0},{32,16},{48,32},{64,112},{80,64},{96,80},{112,96},{1... | collective-permute-start | bytes 884744 | tf_op jit(solution)/shard_map/ppermute | solution.py:52
  137.7 9.3 %collective-permute-start.27 = (bf16[384,384]{1,0:T(8,128)(2,1)S(1)}, bf16[384,384]{1,0:T(8,128)(2,1)S(1)}, u32[]{:S(2)}, u32[]{:S(2)}) collective-permute-start(bf16[384,384]{1,0:T(8,128)(2,1)S(1)} %get-tuple-element.97), channel_id=1, source_target_pairs={{0,32},{16,48},{32,0},{48,16},{64,96},{80,112},{96,64},{112,80},{1... | collective-permute-start | bytes 884744 | tf_op jit(solution)/shard_map/ppermute | solution.py:52
  137.9 16.3 %collective-permute-start.26 = (bf16[384,384]{1,0:T(8,128)(2,1)S(1)}, bf16[384,384]{1,0:T(8,128)(2,1)S(1)}, u32[]{:S(2)}, u32[]{:S(2)}) collective-permute-start(bf16[384,384]{1,0:T(8,128)(2,1)S(1)} %get-tuple-element.96), channel_id=1, source_target_pairs={{0,16},{16,32},{32,48},{48,0},{64,80},{80,96},{96,112},{112,64},{1... | collective-permute-start | bytes 884744 | tf_op jit(solution)/shard_map/ppermute | solution.py:52

commit v4 on v3

--- a/solution.py
+++ b/solution.py
@@ -125,7 +125,7 @@
         place = n // 8 * NX + ((x - shard) & 3)
         sel_ref[jnp.where(shard // NX == z, place, 2 * NZ * NX)] = block % SLOTS
 
-    for copy in copies:
+    for copy in copies[4:8] + copies[0:4]:
         copy.wait()
     q_refs, k_refs, v_refs = [[buf.at[n] for n in range(4)] for buf in (q_buf, k_buf, v_buf)]
     heads = k_buf.shape[2] // HEAD
@@ -148,13 +148,16 @@
                 cols = pl.ds(h * HEAD, HEAD)
                 query = q_ref[pl.ds(row, BLOCK), cols]
                 keys = jnp.concatenate([k_refs[i][pl.ds(starts[i], BLOCK), cols] for i in range(NX)])
-                values = jnp.concatenate(
-                    [v_refs[i][pl.ds(starts[i], BLOCK), cols] for i in range(NX)]
-                )
                 scores = dot_nt(query, keys) * SCALE2 + bias
                 top = jnp.max(scores, axis=1, keepdims=True)
                 weights = jnp.exp2(scores - top)
                 total = jnp.sum(weights, axis=1, keepdims=True)
+                if (j, b, h) == (0, 0, 0):
+                    for copy in copies[8:12]:
+                        copy.wait()
+                values = jnp.concatenate(
+                    [v_refs[i][pl.ds(starts[i], BLOCK), cols] for i in range(NX)]
+                )
                 acc = dot_nn(weights.astype(jnp.bfloat16), values)
                 out_ref[pl.ds(row, BLOCK), cols] = (acc / total).astype(jnp.bfloat16)
                 stat = jnp.where(lane == h, top + jnp.log2(total), stat)
@@ -206,31 +209,40 @@
 
 
 def grad_kernel(ids_ref, *refs):
-    own, other, w_ref, out_ref, acc_ref = refs[0:4], refs[4:8], refs[8], refs[9], refs[10]
-    step = pl.program_id(0)
-    zl, c = ids_ref[4], ids_ref[5]
-    width = own[0].shape[1]
-    rows = out_ref.shape[0]
-
-    @pl.when(step == 0)
-    def _():
-        acc_ref[...] = jnp.zeros_like(acc_ref)
-
+    tall, w_ref, out_ref = refs[0:8], refs[8], refs[9]
+    cot_buf, w_buf, sems = refs[10:13]
+    z, y, zl, c = ids_ref[0], ids_ref[2], ids_ref[4], ids_ref[5]
+    rows, width = out_ref.shape[1], out_ref.shape[2]
+    copies = []
+    for w in range(2):
+        for s in range(2):
+            column = (z * 4 + (zl ^ s) * 2 + (c ^ w)) * width
+            part = pl.ds((2 * w + s) * width, width)
+            copies.append(
+                pltpu.make_async_copy(
+                    w_ref.at[:, pl.ds(pl.multiple_of(column, 128), width)],
+                    w_buf.at[:, part],
+                    sems.at[2 * w + s],
+                )
+            )
     for k in range(NY):
-
-        @pl.when(step == k)
-        def _(k=k):
-            acc = acc_ref[...]
-            for w, arrays in enumerate((own, other)):
-                for s in range(2):
-                    place = (zl ^ s) * 2 + (c ^ w)
-                    cols = pl.ds(pl.multiple_of(place * width, 128), width)
-                    acc = acc + dot_nt(arrays[k][s * rows : (s + 1) * rows, :], w_ref[:, cols])
-            acc_ref[...] = acc
-
-    @pl.when(step == NY - 1)
-    def _():
-        out_ref[...] = acc_ref[...].astype(jnp.bfloat16)
+        for w in range(2):
+            for s in range(2):
+                copies.append(
+                    pltpu.make_async_copy(
+                        tall[NY * w + k].at[pl.ds(s * rows, rows)],
+                        cot_buf.at[k, :, pl.ds((2 * w + s) * width, width)],
+                        sems.at[4 * (k + 1) + 2 * w + s],
+                    )
+                )
+    for copy in copies:
+        copy.start()
+    for copy in copies[:4]:
+        copy.wait()
+    for k in range(NY):
+        for copy in copies[4 * (k + 1) : 4 * (k + 2)]:
+            copy.wait()
+        out_ref[(y - k) & 3] = dot_nt(cot_buf[k], w_buf[...]).astype(jnp.bfloat16)
 
 
 def weight_kernel(ids_ref, *refs):
@@ -298,17 +310,13 @@
     extra = extra.at[0, 0 : storage.shape[0]].set(storage.astype(jnp.bfloat16))
     q_pack = jnp.concatenate([queries, extra], axis=0)
 
+    swapped = swap_zy(cotangent)
     k1, v3 = shift_x(memory_keys, 1), shift_x(memory_values, -1)
     q1, q3 = shift_z(q_pack, 1), shift_z(q_pack, 3)
-    near = flip_tensor(cotangent, 2)
-    k1, v3, q1, q3, near, own_keys, own_values, q_late = together(
-        k1, v3, q1, q3, near, memory_keys, memory_values, q_pack
-    )
-    k2, v2, q2 = shift_x(k1, 1), shift_x(v3, -1), shift_z(q_late, 2)
-    k3, v1 = shift_x(own_keys, -1), shift_x(own_values, 1)
-    k2, v2, k3, v1, q2, near = together(k2, v2, k3, v1, q2, near)
-    pair = jnp.concatenate([cotangent, near], axis=0)
-    w1, w3, swapped = shift_y(pair, 1), shift_y(pair, 3), swap_zy(pair[:rows])
+    k2, v2 = shift_x(k1, 1), shift_x(v3, -1)
+    v1, k3 = shift_x(after(memory_values, swapped), 1), shift_x(after(memory_keys, q1), -1)
+    q2 = shift_z(after(q_pack, q3), 2)
+    near = flip_tensor(after(swapped, q2), 2)
     q_all = [q_pack, q1, q2, q3]
     stored = jnp.stack([q[rows, 0:16] for q in q_all]).reshape(-1).astype(jnp.int32)
 
@@ -341,11 +349,12 @@
         name="memory_attention",
     )(ids, stored, *in_hbm([*q_all, memory_keys, k1, k2, k3, memory_values, v1, v2, v3]))
 
-    parts, swapped, w1, w3, pair = together(parts, swapped, w1, w3, pair)
+    tall = jnp.concatenate([swapped, near], axis=0)
+    parts, tall = together(parts, tall)
     back = exchange_z(parts)
-    tall = jnp.concatenate([swapped, flip_tensor(swapped, 2)], axis=0)
-    w2, t1, t3 = shift_y(pair, 2), shift_y(tall, 1), shift_y(tall, 3)
-    back, w2, t1, t3, tall = together(back, w2, t1, t3, tall)
+    t1, t2, t3 = [shift_y(tall, k) for k in (1, 2, 3)]
+    c0 = flip_tensor(tall, 1)
+    back, c0, t1, t3 = together(back, c0, t1, t3)
     attention, att_t = pl.pallas_call(
         merge_kernel,
         out_shape=[
@@ -358,36 +367,24 @@
         cost_estimate=cost(32 * rows * width, 4 * rows, 16 * rows * width),
         name="merge",
     )(gate, local_out, back)
-    att_t, tall, pair = together(att_t, tall, pair)
+    att_t, t1, t2, t3 = together(att_t, t1, t2, t3)
     att_all = exchange_z(att_t)
-    t2 = shift_y(tall, 2)
-    tall = [tall, t1, t2, t3]
-    tall = tall + [flip_tensor(v, 1) for v in tall]
-    wide = [pair, w1, w2, w3]
-    wide = wide + [flip_tensor(v, 1) for v in wide]
-    att_all, *flipped = together(att_all, *tall[4:], *wide[4:])
-    tall, wide = in_hbm(tall[:4] + flipped[:4]), in_hbm(wide[:4] + flipped[4:])
-
-    attention_grad = pl.pallas_call(
+    tall = in_hbm([tall, t1, t2, t3, c0] + [flip_tensor(v, 1) for v in (t1, t2, t3)])
+    grads = pl.pallas_call(
         grad_kernel,
-        out_shape=jax.ShapeDtypeStruct((rows, width), jnp.bfloat16),
-        grid_spec=pltpu.PrefetchScalarGridSpec(
-            num_scalar_prefetch=1,
-            grid=(NY,),
-            in_specs=[
-                pl.BlockSpec(
-                    (2 * rows, width), lambda g, ids: (0, 0), pipeline_mode=pl.Buffered(1)
-                )
-            ]
-            * 8
-            + [pl.BlockSpec((width, 4 * width), lambda g, ids: (0, (ids[2] - g) & 3))],
-            out_specs=pl.BlockSpec((rows, width), lambda g, ids: (0, 0)),
-            scratch_shapes=[pltpu.VMEM((rows, width), jnp.float32)],
-        ),
+        out_shape=jax.ShapeDtypeStruct((NZ, rows, width), jnp.bfloat16),
+        in_specs=[SM] + [HB] * 9,
+        out_specs=VM,
+        scratch_shapes=[
+            pltpu.VMEM((NY, rows, 4 * width), jnp.bfloat16),
+            pltpu.VMEM((width, 4 * width), jnp.bfloat16),
+            pltpu.SemaphoreType.DMA((20,)),
+        ],
         compiler_params=params,
-        cost_estimate=cost(32 * rows * width * width, 0, 64 * rows * width),
+        cost_estimate=cost(32 * rows * width * width, 0, 48 * rows * width),
         name="attention_grad",
-    )(ids, *wide, *in_hbm([out_weight]))
+    )(ids, *tall, *in_hbm([out_weight]))
+    att_all, grads = together(att_all, grads)
 
     mine, *sent = pl.pallas_call(
         weight_kernel,
@@ -405,6 +402,7 @@
         name="weight_partials",
     )(ids, att_all, *tall)
     got = [shift_x(sent[n - 1], n) for n in (1, 2, 3)]
+    attention_grad = jnp.sum(exchange_z(after(grads, mine)).astype(jnp.float32), axis=0).astype(jnp.bfloat16)
     weight_grad = (mine + got[0].astype(jnp.float32)) + (
         got[1].astype(jnp.float32) + got[2].astype(jnp.float32)
     )

time: 158 us -> 163 us (1.032); the launches traced: 155 us -> 162 us
  starting transfers between devices: 49.9 us -> 65.8 us
  waiting for transfers between devices: 70.6 us -> 65.4 us
  local copies, waits for them, and re-layouts: 5.8 us -> 3.1 us
    ppermute x10 -> x5, waiting for transfers between devices: 34.8 us -> 10.6 us  [flip_tensor(): return lax.ppermute(value, 'tensor', [(t, t ^ bit) for t in range(16)])]
    all_to_all x2 -> x3, starting transfers between devices: 15.5 us -> 32.3 us  [exchange_z(): lax.all_to_all(value, 'mem', split_axis=0, concat_axis=0, axis_index_grou...]
    all_to_all x2 -> x3, waiting for transfers between devices: 0.01 us -> 9.54 us  [exchange_z(): lax.all_to_all(value, 'mem', split_axis=0, concat_axis=0, axis_index_grou...]
    ppermute x3, waiting for transfers between devices: 6.13 us -> 13.5 us  [shift_z(): return lax.ppermute(value, 'mem', pairs)]
    ppermute x6 -> x3, starting transfers between devices: 6.83 us -> 2.68 us  [shift_y(): return lax.ppermute(value, 'tensor', pairs)]
    ppermute x9, waiting for transfers between devices: 12.5 us -> 15.5 us  [shift_x(): return lax.ppermute(value, 'mem', pairs)]
    ppermute x3, starting transfers between devices: 10.2 us -> 12.6 us  [shift_z(): return lax.ppermute(value, 'mem', pairs)]
    slice x3, local copies, waits for them, and re-layouts: 1.99 us -> 0.01 us  [per_device(): q[rows, 0:16]]
  transfers between devices with their start and end apart: 31 -> 24, of which waited for: 10 -> 11; matrix products, arithmetic and copies ran while one was open for 4% -> 2% of each run, Pallas kernels for 12% -> 6%
where the time goes in v4:
time: 163 us; the launch traced here: 162 us
  starting transfers between devices  65.8 us (40%)
  waiting for transfers between devices  65.4 us (40%)
  Pallas kernels  23.5 us (14%)
  other arithmetic  3.61 us (2%)
  local copies, waits for them, and re-layouts  3.1 us (2%)
    all_to_all x3, starting transfers between devices, exchange_z(): lax.all_to_all(value, 'mem', split_axis=0, concat_axis=0, axis_index_grou...  32.3 us
    ppermute x3, waiting for transfers between devices, shift_y(): return lax.ppermute(value, 'tensor', pairs)  16.3 us
    ppermute x9, waiting for transfers between devices, shift_x(): return lax.ppermute(value, 'mem', pairs)  15.5 us
    ppermute x3, waiting for transfers between devices, shift_z(): return lax.ppermute(value, 'mem', pairs)  13.5 us
    ppermute x3, starting transfers between devices, shift_z(): return lax.ppermute(value, 'mem', pairs)  12.6 us
    ppermute x9, starting transfers between devices, shift_x(): return lax.ppermute(value, 'mem', pairs)  12.1 us
    ppermute x5, waiting for transfers between devices, flip_tensor(): return lax.ppermute(value, 'tensor', [(t, t ^ bit) for t in range(16)])  10.6 us
    pallas_call x1, Pallas kernels, per_device(): pl.pallas_call(memory_kernel, out_shape=jax.ShapeDtypeStruct((NZ, rows +...  9.96 us
  transfers between devices with their start and end apart: 24, of which 11 were waited for; matrix products, arithmetic and copies ran while one was open for 2% of the time, Pallas kernels for 6%

profile of v4, /device:TPU:1, one launch (start us, length us, event | category | flops | bytes accessed | tf_op | source)
XLA Modules:
  0.0 162.3 jit_solution(9965143371471276651)
XLA Ops:
  0.6 0.0 copy-start
  0.7 2.1 %collective-permute-start.3 = (bf16[512,384]{1,0:T(8,128)(2,1)}, bf16[512,384]{1,0:T(8,128)(2,1)S(1)}, u32[]{:S(2)}, u32[]{:S(2)}) collective-permute-start(bf16[512,384]{1,0:T(8,128)(2,1)} %refs_4_.1), channel_id=1, source_target_pairs={{0,16},{16,32},{32,48},{48,0},{64,80},{80,96},{96,112},{112,64},{1... | collective-permute-start | bytes 1179656 | tf_op jit(solution)/shard_map/ppermute | solution.py:52
  2.8 1.4 collective-permute-start.8
  4.2 0.8 eq.19
  4.9 0.8 select_reduce_fusion
  5.8 1.0 fusion.1.refs_0_
  6.7 6.2 %collective-permute-start.1 = (bf16[272,384]{1,0:T(8,128)(2,1)S(1)}, bf16[272,384]{1,0:T(8,128)(2,1)S(1)}, u32[]{:S(2)}, u32[]{:S(2)}) collective-permute-start(bf16[272,384]{1,0:T(8,128)(2,1)S(1)} %fusion.1.refs_0_), channel_id=1, source_target_pairs={{0,192},{16,208},{32,224},{48,240},{64,0},{80,16},{96,32},{112,48}... | collective-permute-start | bytes 626696 | tf_op jit(solution)/shard_map/ppermute | solution.py:57
  12.9 0.0 collective-permute-start
  12.9 1.6 collective-permute-start.6
  14.5 4.1 %collective-permute-done.1.refs_3_ = bf16[272,384]{1,0:T(8,128)(2,1)S(1)} collective-permute-done((bf16[272,384]{1,0:T(8,128)(2,1)S(1)}, bf16[272,384]{1,0:T(8,128)(2,1)S(1)}, u32[]{:S(2)}, u32[]{:S(2)}) %collective-permute-start.1) | collective-permute-done | bytes 208928 | tf_op jit(solution)/shard_map/ppermute | solution.py:57
  18.6 6.4 %collective-permute-start.2 = (bf16[272,384]{1,0:T(8,128)(2,1)S(1)}, bf16[272,384]{1,0:T(8,128)(2,1)S(1)}, u32[]{:S(2)}, u32[]{:S(2)}) collective-permute-start(bf16[272,384]{1,0:T(8,128)(2,1)S(1)} %fusion.1.refs_0_), channel_id=1, source_target_pairs={{0,128},{16,144},{32,160},{48,176},{64,192},{80,208},{96,224},{112... | collective-permute-start | bytes 626696 | tf_op jit(solution)/shard_map/ppermute | solution.py:57
  25.0 0.0 collective-permute-done.6
  25.0 0.0 collective-permute-start.7
  25.0 0.0 collective-permute-done.refs_1_
  25.1 2.7 %collective-permute-start.5 = (bf16[512,384]{1,0:T(8,128)(2,1)}, bf16[512,384]{1,0:T(8,128)(2,1)}, u32[]{:S(2)}, u32[]{:S(2)}) collective-permute-start(bf16[512,384]{1,0:T(8,128)(2,1)} %refs_4_.1), channel_id=1, source_target_pairs={{0,48},{16,0},{32,16},{48,32},{64,112},{80,64},{96,80},{112,96},{1... | collective-permute-start | bytes 1179656 | tf_op jit(solution)/shard_map/ppermute | solution.py:52
  27.7 0.0 collective-permute-done.3.refs_5_
  27.7 0.0 collective-permute-start.4
  27.7 0.0 collective-permute-done.8.refs_11_
  27.8 2.7 %collective-permute-start.9 = (bf16[512,384]{1,0:T(8,128)(2,1)S(1)}, bf16[512,384]{1,0:T(8,128)(2,1)}, u32[]{:S(2)}, u32[]{:S(2)}) collective-permute-start(bf16[512,384]{1,0:T(8,128)(2,1)S(1)} %collective-permute-done.8.refs_11_), channel_id=1, source_target_pairs={{0,48},{16,0},{32,16},{48,32},{64,112},{80,64},{96,80},{112,96},{1... | collective-permute-start | bytes 1179656 | tf_op jit(solution)/shard_map/ppermute | solution.py:52
  30.4 9.4 %collective-permute-done.2.refs_2_ = bf16[272,384]{1,0:T(8,128)(2,1)S(1)} collective-permute-done((bf16[272,384]{1,0:T(8,128)(2,1)S(1)}, bf16[272,384]{1,0:T(8,128)(2,1)S(1)}, u32[]{:S(2)}, u32[]{:S(2)}) %collective-permute-start.2) | collective-permute-done | bytes 208928 | tf_op jit(solution)/shard_map/ppermute | solution.py:57
  39.8 0.0 collective-permute-start.10
  39.8 0.1 stack.26.ids_ref
  39.9 0.1 reshape.49.stored_ref
  40.0 0.5 copy-done.16
  40.5 8.4 %collective-permute-done.10 = bf16[256,384]{1,0:T(8,128)(2,1)S(1)} collective-permute-done((bf16[256,384]{1,0:T(8,128)(2,1)S(1)}, bf16[256,384]{1,0:T(8,128)(2,1)S(1)}, u32[]{:S(2)}, u32[]{:S(2)}) %collective-permute-start.10) | collective-permute-done | bytes 196640 | tf_op jit(solution)/shard_map/ppermute | solution.py:77
  49.0 0.0 collective-permute-done.7.refs_9_
  49.0 0.0 collective-permute-done.5.refs_7_
  49.0 0.0 collective-permute-done.4.refs_6_
  49.0 0.0 collective-permute-done.9.refs_10_
  49.1 0.7 copy-done.13
  49.8 10.0 %memory_attention.1 = bf16[4,272,384]{2,1,0:T(8,128)(2,1)} custom-call(s32[6]{0:T(128)S(1)} %stack.26.ids_ref, s32[64]{0:T(128)S(1)} %reshape.49.stored_ref, bf16[272,384]{1,0:T(8,128)(2,1)} %copy-done.10, bf16[272,384]{1,0:T(8,128)(2,1)} %copy-done.15, bf16[272,384]{1,0:T(8,128)(2,1)} %copy-done.16, bf16[272,384]{1,0:T(8,128)(2,1)} %copy-done.14, ...), custom_call_target="tpu_custom_call" | custom-call | flops 1610612736 | bytes 2359296 | tf_op jit(solution)/shard_map/memory_attention/pallas_call | solution.py:333
  59.8 19.9 %all-to-all-start = ((bf16[4,272,384]{2,1,0:T(8,128)(2,1)}), bf16[4,272,384]{2,1,0:T(8,128)(2,1)S(1)}, u32[]{:S(2)}, u32[]{:S(2)}) async-start(bf16[4,272,384]{2,1,0:T(8,128)(2,1)} %memory_attention.1), calls=%async_computation | async-start | bytes 1671168 | tf_op jit(solution)/shard_map/all_to_all | solution.py:62
  79.7 2.9 %collective-permute-start.11 = (bf16[512,384]{1,0:T(8,128)(2,1)S(1)}, bf16[512,384]{1,0:T(8,128)(2,1)S(1)}, u32[]{:S(2)}, u32[]{:S(2)}) collective-permute-start(bf16[512,384]{1,0:T(8,128)(2,1)S(1)} %pad_maximum_fusion.refs_0_.refs_1_), channel_id=1, source_target_pairs={{0,1},{1,0},{2,3},{3,2},{4,5},{5,4},{6,7},{7,6},{8,9},{9,8},{10,11... | collective-permute-start | bytes 1179656 | tf_op jit(solution)/shard_map/ppermute | solution.py:77
  82.6 0.0 collective-permute-start.12
  82.6 2.7 %collective-permute-start.13 = (bf16[512,384]{1,0:T(8,128)(2,1)S(1)}, bf16[512,384]{1,0:T(8,128)(2,1)}, u32[]{:S(2)}, u32[]{:S(2)}) collective-permute-start(bf16[512,384]{1,0:T(8,128)(2,1)S(1)} %pad_maximum_fusion.refs_0_.refs_1_), channel_id=1, source_target_pairs={{0,12},{1,13},{2,14},{3,15},{4,0},{5,1},{6,2},{7,3},{8,4},{9,5},{1... | collective-permute-start | bytes 1179656 | tf_op jit(solution)/shard_map/ppermute | solution.py:69
  85.3 0.0 collective-permute-start.14
  85.3 1.4 local_attention.1.local_ref
  86.7 0.0 collective-permute-done.11.refs_4_.refs_5_
  86.7 16.3 %collective-permute-done.12.refs_1_.refs_2_ = bf16[512,384]{1,0:T(8,128)(2,1)S(1)} collective-permute-done((bf16[512,384]{1,0:T(8,128)(2,1)S(1)}, bf16[512,384]{1,0:T(8,128)(2,1)S(1)}, u32[]{:S(2)}, u32[]{:S(2)}) %collective-permute-start.12) | collective-permute-done | bytes 393248 | tf_op jit(solution)/shard_map/ppermute | solution.py:69
  103.0 0.0 collective-permute-done.13.refs_3_.refs_4_
  103.0 2.3 %merge.1 = (bf16[256,384]{1,0:T(8,128)(2,1)}, bf16[4,384,256]{2,1,0:T(8,128)(2,1)}) custom-call(f32[3]{0:T(128)S(1)} %add_divide_fusion.gate_ref, f32[256,384]{1,0:T(8,128)S(1)} %local_attention.1.local_ref, bf16[4,272,384]{2,1,0:T(8,128)(2,1)S(1)} %all-to-all-done.back_ref), custom_call_target="tpu_custom_call" | custom-call | flops 3145728 | bytes 1572864 | tf_op jit(solution)/shard_map/merge/pallas_call | solution.py:358
  105.3 0.0 collective-permute-done.14.refs_2_.refs_3_
  105.3 6.9 %all-to-all-start.1 = ((bf16[4,384,256]{2,1,0:T(8,128)(2,1)}), bf16[4,384,256]{2,1,0:T(8,128)(2,1)S(1)}, u32[]{:S(2)}, u32[]{:S(2)}) async-start(bf16[4,384,256]{2,1,0:T(8,128)(2,1)} %get-tuple-element.49), calls=%async_computation.1 | async-start | bytes 1572864 | tf_op jit(solution)/shard_map/all_to_all | solution.py:62
  112.3 1.1 collective-permute-start.15
  113.3 0.0 collective-permute-start.16
  113.3 0.5 collective-permute-start.17
  113.8 1.4 collective-permute-done.15.refs_5_.refs_6_
  115.2 0.2 collective-permute-done.16.refs_6_.refs_7_
  115.5 0.6 collective-permute-done.17.refs_7_.refs_8_
  116.0 0.2 copy-done.8
  116.2 0.7 copy-done.9
  116.9 5.5 %attention_grad.1 = bf16[4,256,384]{2,1,0:T(8,128)(2,1)} custom-call(s32[6]{0:T(128)S(1)} %stack.26.ids_ref, bf16[512,384]{1,0:T(8,128)(2,1)} %copy-done.4, bf16[512,384]{1,0:T(8,128)(2,1)} %copy-done.6, bf16[512,384]{1,0:T(8,128)(2,1)} %collective-permute-done.14.refs_2_.refs_3_, bf16[512,384]{1,0:T(8,128)(2,1)} %collective-permute-done.13.refs_3_.refs_4_, ...), custom_call_target="tpu_custom_call" | custom-call | flops 1207959552 | bytes 4718592 | tf_op jit(solution)/shard_map/attention_grad/pallas_call | solution.py:373
  122.4 9.5 %all-to-all-done.1.refs_0_ = bf16[4,384,256]{2,1,0:T(8,128)(2,1)S(1)} async-done(((bf16[4,384,256]{2,1,0:T(8,128)(2,1)}), bf16[4,384,256]{2,1,0:T(8,128)(2,1)S(1)}, u32[]{:S(2)}, u32[]{:S(2)}) %all-to-all-start.1) | async-done | bytes 786464 | tf_op jit(solution)/shard_map/all_to_all | solution.py:62
  132.0 4.3 %weight_partials.1 = (f32[384,384]{1,0:T(8,128)S(1)}, bf16[384,384]{1,0:T(8,128)(2,1)S(1)}, bf16[384,384]{1,0:T(8,128)(2,1)S(1)}, bf16[384,384]{1,0:T(8,128)(2,1)S(1)}) custom-call(s32[6]{0:T(128)S(1)} %stack.26.ids_ref, bf16[4,384,256]{2,1,0:T(8,128)(2,1)S(1)} %all-to-all-done.1.refs_0_, bf16[512,384]{1,0:T(8,128)(2,1)} %copy-done.4, ...), custom_call_target="tpu_custom_call" | custom-call | flops 1207959552 | bytes 4718592 | tf_op jit(solution)/shard_map/weight_partials/pallas_call | solution.py:389
  136.3 5.4 %all-to-all-start.2 = ((bf16[4,256,384]{2,1,0:T(8,128)(2,1)}), bf16[4,256,384]{2,1,0:T(8,128)(2,1)S(1)}, u32[]{:S(2)}, u32[]{:S(2)}) async-start(bf16[4,256,384]{2,1,0:T(8,128)(2,1)} %attention_grad.1), calls=%async_computation.2 | async-start | bytes 1572864 | tf_op jit(solution)/shard_map/all_to_all | solution.py:62
  141.8 2.7 %collective-permute-start.20 = (bf16[384,384]{1,0:T(8,128)(2,1)S(1)}, bf16[384,384]{1,0:T(8,128)(2,1)S(1)}, u32[]{:S(2)}, u32[]{:S(2)}) collective-permute-start(bf16[384,384]{1,0:T(8,128)(2,1)S(1)} %get-tuple-element.60), channel_id=1, source_target_pairs={{0,48},{16,0},{32,16},{48,32},{64,112},{80,64},{96,80},{112,96},{1... | collective-permute-start | bytes 884744 | tf_op jit(solution)/shard_map/ppermute | solution.py:52
  144.5 0.0 collective-permute-start.19
  144.5 0.6 collective-permute-start.18
  145.1 6.0 %collective-permute-done.20 = bf16[384,384]{1,0:T(8,128)(2,1)S(1)} collective-permute-done((bf16[384,384]{1,0:T(8,128)(2,1)S(1)}, bf16[384,384]{1,0:T(8,128)(2,1)S(1)}, u32[]{:S(2)}, u32[]{:S(2)}) %collective-permute-start.20) | collective-permute-done | bytes 294944 | tf_op jit(solution)/shard_map/ppermute | solution.py:52
  151.1 2.4 %collective-permute-done.19 = bf16[384,384]{1,0:T(8,128)(2,1)S(1)} collective-permute-done((bf16[384,384]{1,0:T(8,128)(2,1)S(1)}, bf16[384,384]{1,0:T(8,128)(2,1)S(1)}, u32[]{:S(2)}, u32[]{:S(2)}) %collective-permute-start.19) | collective-permute-done | bytes 294944 | tf_op jit(solution)/shard_map/ppermute | solution.py:52
  153.5 7.1 %collective-permute-done.18 = bf16[384,384]{1,0:T(8,128)(2,1)S(1)} collective-permute-done((bf16[384,384]{1,0:T(8,128)(2,1)S(1)}, bf16[384,384]{1,0:T(8,128)(2,1)S(1)}, u32[]{:S(2)}, u32[]{:S(2)}) %collective-permute-start.18) | collective-permute-done | bytes 294944 | tf_op jit(solution)/shard_map/ppermute | solution.py:52
  160.6 0.9 add_add_fusion
  161.5 0.0 all-to-all-done.2
  161.5 0.8 reduce_sum.22
  (39 shorter events, 0.1 us)
Async XLA Ops:
  0.6 84.7 %copy-start = (bf16[256,384]{1,0:T(8,128)(2,1)S(1)}, bf16[256,384]{1,0:T(8,128)(2,1)}, u32[]{:S(2)}) copy-start(bf16[256,384]{1,0:T(8,128)(2,1)} %q_ref.1) | copy-start | bytes 589828
  0.6 84.6 %copy-start.17 = (f32[3]{0:T(128)S(1)}, f32[3]{0:T(128)}, u32[]{:S(2)}) copy-start(f32[3]{0:T(128)} %param.21) | copy-start | bytes 40
  0.7 84.7 %copy-start.3 = (s32[256]{0:T(256)S(1)}, s32[256]{0:T(256)}, u32[]{:S(2)}) copy-start(s32[256]{0:T(256)} %param.16) | copy-start | bytes 3076
  0.7 84.7 %copy-start.1 = (bf16[256,384]{1,0:T(8,128)(2,1)S(1)}, bf16[256,384]{1,0:T(8,128)(2,1)}, u32[]{:S(2)}) copy-start(bf16[256,384]{1,0:T(8,128)(2,1)} %k_ref.1) | copy-start | bytes 589828
  0.7 84.7 %copy-start.2 = (bf16[256,384]{1,0:T(8,128)(2,1)S(1)}, bf16[256,384]{1,0:T(8,128)(2,1)}, u32[]{:S(2)}) copy-start(bf16[256,384]{1,0:T(8,128)(2,1)} %v_ref.1) | copy-start | bytes 589828
  0.7 27.0 %collective-permute-start.3 = (bf16[512,384]{1,0:T(8,128)(2,1)}, bf16[512,384]{1,0:T(8,128)(2,1)S(1)}, u32[]{:S(2)}, u32[]{:S(2)}) collective-permute-start(bf16[512,384]{1,0:T(8,128)(2,1)} %refs_4_.1), channel_id=1, source_target_pairs={{0,16},{16,32},{32,48},{48,0},{64,80},{80,96},{96,112},{112,64},{1... | collective-permute-start | bytes 1179656 | tf_op jit(solution)/shard_map/ppermute | solution.py:52
  2.8 24.9 %collective-permute-start.8 = (bf16[512,384]{1,0:T(8,128)(2,1)}, bf16[512,384]{1,0:T(8,128)(2,1)S(1)}, u32[]{:S(2)}, u32[]{:S(2)}) collective-permute-start(bf16[512,384]{1,0:T(8,128)(2,1)} %refs_8_.2), channel_id=1, source_target_pairs={{0,48},{16,0},{32,16},{48,32},{64,112},{80,64},{96,80},{112,96},{1... | collective-permute-start | bytes 1179656 | tf_op jit(solution)/shard_map/ppermute | solution.py:52
  6.7 42.3 %copy-start.10 = (bf16[272,384]{1,0:T(8,128)(2,1)}, bf16[272,384]{1,0:T(8,128)(2,1)S(1)}, u32[]{:S(2)}) copy-start(bf16[272,384]{1,0:T(8,128)(2,1)S(1)} %fusion.1.refs_0_) | copy-start | bytes 626692
  6.7 11.9 %collective-permute-start.1 = (bf16[272,384]{1,0:T(8,128)(2,1)S(1)}, bf16[272,384]{1,0:T(8,128)(2,1)S(1)}, u32[]{:S(2)}, u32[]{:S(2)}) collective-permute-start(bf16[272,384]{1,0:T(8,128)(2,1)S(1)} %fusion.1.refs_0_), channel_id=1, source_target_pairs={{0,192},{16,208},{32,224},{48,240},{64,0},{80,16},{96,32},{112,48}... | collective-permute-start | bytes 626696 | tf_op jit(solution)/shard_map/ppermute | solution.py:57
  12.9 12.1 %collective-permute-start = (bf16[272,384]{1,0:T(8,128)(2,1)S(1)}, bf16[272,384]{1,0:T(8,128)(2,1)S(1)}, u32[]{:S(2)}, u32[]{:S(2)}) collective-permute-start(bf16[272,384]{1,0:T(8,128)(2,1)S(1)} %fusion.1.refs_0_), channel_id=1, source_target_pairs={{0,64},{16,80},{32,96},{48,112},{64,128},{80,144},{96,160},{112,17... | collective-permute-start | bytes 626696 | tf_op jit(solution)/shard_map/ppermute | solution.py:57
  12.9 12.1 %collective-permute-start.6 = (bf16[256,384]{1,0:T(8,128)(2,1)}, bf16[256,384]{1,0:T(8,128)(2,1)S(1)}, u32[]{:S(2)}, u32[]{:S(2)}) collective-permute-start(bf16[256,384]{1,0:T(8,128)(2,1)} %param.23), channel_id=1, source_target_pairs={{0,0},{1,1},{2,2},{3,3},{4,64},{5,65},{6,66},{7,67},{8,128},{9,129... | collective-permute-start | bytes 589832 | tf_op jit(solution)/shard_map/ppermute | solution.py:87
  18.6 30.5 %copy-start.14 = (bf16[272,384]{1,0:T(8,128)(2,1)}, bf16[272,384]{1,0:T(8,128)(2,1)S(1)}, u32[]{:S(2)}) copy-start(bf16[272,384]{1,0:T(8,128)(2,1)S(1)} %collective-permute-done.1.refs_3_) | copy-start | bytes 626692
  18.6 21.2 %collective-permute-start.2 = (bf16[272,384]{1,0:T(8,128)(2,1)S(1)}, bf16[272,384]{1,0:T(8,128)(2,1)S(1)}, u32[]{:S(2)}, u32[]{:S(2)}) collective-permute-start(bf16[272,384]{1,0:T(8,128)(2,1)S(1)} %fusion.1.refs_0_), channel_id=1, source_target_pairs={{0,128},{16,144},{32,160},{48,176},{64,192},{80,208},{96,224},{112... | collective-permute-start | bytes 626696 | tf_op jit(solution)/shard_map/ppermute | solution.py:57
  25.0 24.0 %collective-permute-start.7 = (bf16[512,384]{1,0:T(8,128)(2,1)}, bf16[512,384]{1,0:T(8,128)(2,1)S(1)}, u32[]{:S(2)}, u32[]{:S(2)}) collective-permute-start(bf16[512,384]{1,0:T(8,128)(2,1)} %refs_8_.2), channel_id=1, source_target_pairs={{0,16},{16,32},{32,48},{48,0},{64,80},{80,96},{96,112},{112,64},{1... | collective-permute-start | bytes 1179656 | tf_op jit(solution)/shard_map/ppermute | solution.py:52
  25.1 24.0 %copy-start.15 = (bf16[272,384]{1,0:T(8,128)(2,1)}, bf16[272,384]{1,0:T(8,128)(2,1)S(1)}, u32[]{:S(2)}) copy-start(bf16[272,384]{1,0:T(8,128)(2,1)S(1)} %collective-permute-done.refs_1_) | copy-start | bytes 626692
  25.1 24.0 %collective-permute-start.5 = (bf16[512,384]{1,0:T(8,128)(2,1)}, bf16[512,384]{1,0:T(8,128)(2,1)}, u32[]{:S(2)}, u32[]{:S(2)}) collective-permute-start(bf16[512,384]{1,0:T(8,128)(2,1)} %refs_4_.1), channel_id=1, source_target_pairs={{0,48},{16,0},{32,16},{48,32},{64,112},{80,64},{96,80},{112,96},{1... | collective-permute-start | bytes 1179656 | tf_op jit(solution)/shard_map/ppermute | solution.py:52
  27.7 21.3 %copy-start.11 = (bf16[512,384]{1,0:T(8,128)(2,1)}, bf16[512,384]{1,0:T(8,128)(2,1)S(1)}, u32[]{:S(2)}) copy-start(bf16[512,384]{1,0:T(8,128)(2,1)S(1)} %collective-permute-done.3.refs_5_) | copy-start | bytes 1179652
  27.7 21.3 %collective-permute-start.4 = (bf16[512,384]{1,0:T(8,128)(2,1)S(1)}, bf16[512,384]{1,0:T(8,128)(2,1)}, u32[]{:S(2)}, u32[]{:S(2)}) collective-permute-start(bf16[512,384]{1,0:T(8,128)(2,1)S(1)} %collective-permute-done.3.refs_5_), channel_id=1, source_target_pairs={{0,16},{16,32},{32,48},{48,0},{64,80},{80,96},{96,112},{112,64},{1... | collective-permute-start | bytes 1179656 | tf_op jit(solution)/shard_map/ppermute | solution.py:52
  27.8 21.3 %copy-start.12 = (bf16[512,384]{1,0:T(8,128)(2,1)}, bf16[512,384]{1,0:T(8,128)(2,1)S(1)}, u32[]{:S(2)}) copy-start(bf16[512,384]{1,0:T(8,128)(2,1)S(1)} %collective-permute-done.8.refs_11_) | copy-start | bytes 1179652
  27.8 21.3 %collective-permute-start.9 = (bf16[512,384]{1,0:T(8,128)(2,1)S(1)}, bf16[512,384]{1,0:T(8,128)(2,1)}, u32[]{:S(2)}, u32[]{:S(2)}) collective-permute-start(bf16[512,384]{1,0:T(8,128)(2,1)S(1)} %collective-permute-done.8.refs_11_), channel_id=1, source_target_pairs={{0,48},{16,0},{32,16},{48,32},{64,112},{80,64},{96,80},{112,96},{1... | collective-permute-start | bytes 1179656 | tf_op jit(solution)/shard_map/ppermute | solution.py:52
  39.8 0.7 copy-start.16
  39.8 9.1 %collective-permute-start.10 = (bf16[256,384]{1,0:T(8,128)(2,1)S(1)}, bf16[256,384]{1,0:T(8,128)(2,1)S(1)}, u32[]{:S(2)}, u32[]{:S(2)}) collective-permute-start(bf16[256,384]{1,0:T(8,128)(2,1)S(1)} %collective-permute-done.6), channel_id=1, source_target_pairs={{0,2},{1,3},{2,0},{3,1},{4,6},{5,7},{6,4},{7,5},{8,10},{9,11},{10,... | collective-permute-start | bytes 589832 | tf_op jit(solution)/shard_map/ppermute | solution.py:77
  49.0 56.4 %copy-start.4 = (bf16[512,384]{1,0:T(8,128)(2,1)}, bf16[512,384]{1,0:T(8,128)(2,1)S(1)}, u32[]{:S(2)}) copy-start(bf16[512,384]{1,0:T(8,128)(2,1)S(1)} %pad_maximum_fusion.refs_0_.refs_1_) | copy-start | bytes 1179652
  49.0 0.8 copy-start.13
  59.8 43.2 %all-to-all-start = ((bf16[4,272,384]{2,1,0:T(8,128)(2,1)}), bf16[4,272,384]{2,1,0:T(8,128)(2,1)S(1)}, u32[]{:S(2)}, u32[]{:S(2)}) async-start(bf16[4,272,384]{2,1,0:T(8,128)(2,1)} %memory_attention.1), calls=%async_computation | async-start | bytes 1671168 | tf_op jit(solution)/shard_map/all_to_all | solution.py:62
  79.7 7.0 %collective-permute-start.11 = (bf16[512,384]{1,0:T(8,128)(2,1)S(1)}, bf16[512,384]{1,0:T(8,128)(2,1)S(1)}, u32[]{:S(2)}, u32[]{:S(2)}) collective-permute-start(bf16[512,384]{1,0:T(8,128)(2,1)S(1)} %pad_maximum_fusion.refs_0_.refs_1_), channel_id=1, source_target_pairs={{0,1},{1,0},{2,3},{3,2},{4,5},{5,4},{6,7},{7,6},{8,9},{9,8},{10,11... | collective-permute-start | bytes 1179656 | tf_op jit(solution)/shard_map/ppermute | solution.py:77
  82.6 20.4 %collective-permute-start.12 = (bf16[512,384]{1,0:T(8,128)(2,1)S(1)}, bf16[512,384]{1,0:T(8,128)(2,1)S(1)}, u32[]{:S(2)}, u32[]{:S(2)}) collective-permute-start(bf16[512,384]{1,0:T(8,128)(2,1)S(1)} %pad_maximum_fusion.refs_0_.refs_1_), channel_id=1, source_target_pairs={{0,4},{1,5},{2,6},{3,7},{4,8},{5,9},{6,10},{7,11},{8,12},{9,13},{1... | collective-permute-start | bytes 1179656 | tf_op jit(solution)/shard_map/ppermute | solution.py:69
  82.6 20.4 %collective-permute-start.13 = (bf16[512,384]{1,0:T(8,128)(2,1)S(1)}, bf16[512,384]{1,0:T(8,128)(2,1)}, u32[]{:S(2)}, u32[]{:S(2)}) collective-permute-start(bf16[512,384]{1,0:T(8,128)(2,1)S(1)} %pad_maximum_fusion.refs_0_.refs_1_), channel_id=1, source_target_pairs={{0,12},{1,13},{2,14},{3,15},{4,0},{5,1},{6,2},{7,3},{8,4},{9,5},{1... | collective-permute-start | bytes 1179656 | tf_op jit(solution)/shard_map/ppermute | solution.py:69
  85.3 20.1 %collective-permute-start.14 = (bf16[512,384]{1,0:T(8,128)(2,1)S(1)}, bf16[512,384]{1,0:T(8,128)(2,1)}, u32[]{:S(2)}, u32[]{:S(2)}) collective-permute-start(bf16[512,384]{1,0:T(8,128)(2,1)S(1)} %pad_maximum_fusion.refs_0_.refs_1_), channel_id=1, source_target_pairs={{0,8},{1,9},{2,10},{3,11},{4,12},{5,13},{6,14},{7,15},{8,0},{9,1},... | collective-permute-start | bytes 1179656 | tf_op jit(solution)/shard_map/ppermute | solution.py:69
  86.7 29.3 %copy-start.5 = (bf16[512,384]{1,0:T(8,128)(2,1)}, bf16[512,384]{1,0:T(8,128)(2,1)S(1)}, u32[]{:S(2)}) copy-start(bf16[512,384]{1,0:T(8,128)(2,1)S(1)} %collective-permute-done.11.refs_4_.refs_5_) | copy-start | bytes 1179652
  103.0 13.0 %copy-start.6 = (bf16[512,384]{1,0:T(8,128)(2,1)}, bf16[512,384]{1,0:T(8,128)(2,1)S(1)}, u32[]{:S(2)}) copy-start(bf16[512,384]{1,0:T(8,128)(2,1)S(1)} %collective-permute-done.12.refs_1_.refs_2_) | copy-start | bytes 1179652
  105.3 26.6 %all-to-all-start.1 = ((bf16[4,384,256]{2,1,0:T(8,128)(2,1)}), bf16[4,384,256]{2,1,0:T(8,128)(2,1)S(1)}, u32[]{:S(2)}, u32[]{:S(2)}) async-start(bf16[4,384,256]{2,1,0:T(8,128)(2,1)} %get-tuple-element.49), calls=%async_computation.1 | async-start | bytes 1572864 | tf_op jit(solution)/shard_map/all_to_all | solution.py:62
  112.3 2.9 %collective-permute-start.15 = (bf16[512,384]{1,0:T(8,128)(2,1)S(1)}, bf16[512,384]{1,0:T(8,128)(2,1)S(1)}, u32[]{:S(2)}, u32[]{:S(2)}) collective-permute-start(bf16[512,384]{1,0:T(8,128)(2,1)S(1)} %collective-permute-done.12.refs_1_.refs_2_), channel_id=1, source_target_pairs={{0,1},{1,0},{2,3},{3,2},{4,5},{5,4},{6,7},{7,6},{8,9},{9,8},{10,11... | collective-permute-start | bytes 1179656 | tf_op jit(solution)/shard_map/ppermute | solution.py:77
  113.3 2.1 %collective-permute-start.16 = (bf16[512,384]{1,0:T(8,128)(2,1)}, bf16[512,384]{1,0:T(8,128)(2,1)S(1)}, u32[]{:S(2)}, u32[]{:S(2)}) collective-permute-start(bf16[512,384]{1,0:T(8,128)(2,1)} %collective-permute-done.14.refs_2_.refs_3_), channel_id=1, source_target_pairs={{0,1},{1,0},{2,3},{3,2},{4,5},{5,4},{6,7},{7,6},{8,9},{9,8},{10,11... | collective-permute-start | bytes 1179656 | tf_op jit(solution)/shard_map/ppermute | solution.py:77
  113.3 2.7 %collective-permute-start.17 = (bf16[512,384]{1,0:T(8,128)(2,1)}, bf16[512,384]{1,0:T(8,128)(2,1)S(1)}, u32[]{:S(2)}, u32[]{:S(2)}) collective-permute-start(bf16[512,384]{1,0:T(8,128)(2,1)} %collective-permute-done.13.refs_3_.refs_4_), channel_id=1, source_target_pairs={{0,1},{1,0},{2,3},{3,2},{4,5},{5,4},{6,7},{7,6},{8,9},{9,8},{10,11... | collective-permute-start | bytes 1179656 | tf_op jit(solution)/shard_map/ppermute | solution.py:77
  115.2 0.8 copy-start.7
  115.5 0.7 copy-start.8
  116.2 0.7 copy-start.9
  136.3 25.2 %all-to-all-start.2 = ((bf16[4,256,384]{2,1,0:T(8,128)(2,1)}), bf16[4,256,384]{2,1,0:T(8,128)(2,1)S(1)}, u32[]{:S(2)}, u32[]{:S(2)}) async-start(bf16[4,256,384]{2,1,0:T(8,128)(2,1)} %attention_grad.1), calls=%async_computation.2 | async-start | bytes 1572864 | tf_op jit(solution)/shard_map/all_to_all | solution.py:62
  141.8 9.3 %collective-permute-start.20 = (bf16[384,384]{1,0:T(8,128)(2,1)S(1)}, bf16[384,384]{1,0:T(8,128)(2,1)S(1)}, u32[]{:S(2)}, u32[]{:S(2)}) collective-permute-start(bf16[384,384]{1,0:T(8,128)(2,1)S(1)} %get-tuple-element.60), channel_id=1, source_target_pairs={{0,48},{16,0},{32,16},{48,32},{64,112},{80,64},{96,80},{112,96},{1... | collective-permute-start | bytes 884744 | tf_op jit(solution)/shard_map/ppermute | solution.py:52
  144.5 9.0 %collective-permute-start.19 = (bf16[384,384]{1,0:T(8,128)(2,1)S(1)}, bf16[384,384]{1,0:T(8,128)(2,1)S(1)}, u32[]{:S(2)}, u32[]{:S(2)}) collective-permute-start(bf16[384,384]{1,0:T(8,128)(2,1)S(1)} %get-tuple-element.59), channel_id=1, source_target_pairs={{0,32},{16,48},{32,0},{48,16},{64,96},{80,112},{96,64},{112,80},{1... | collective-permute-start | bytes 884744 | tf_op jit(solution)/shard_map/ppermute | solution.py:52
  144.5 16.1 %collective-permute-start.18 = (bf16[384,384]{1,0:T(8,128)(2,1)S(1)}, bf16[384,384]{1,0:T(8,128)(2,1)S(1)}, u32[]{:S(2)}, u32[]{:S(2)}) collective-permute-start(bf16[384,384]{1,0:T(8,128)(2,1)S(1)} %get-tuple-element.58), channel_id=1, source_target_pairs={{0,16},{16,32},{32,48},{48,0},{64,80},{80,96},{96,112},{112,64},{1... | collective-permute-start | bytes 884744 | tf_op jit(solution)/shard_map/ppermute | solution.py:52

commit v5 on v3

--- a/solution.py
+++ b/solution.py
@@ -77,13 +77,20 @@
     return lax.ppermute(value, "tensor", [(t, t ^ bit) for t in range(16)])
 
 
-def swap_zy(value):
+def stored_in(*packs):
+    rows = packs[0].shape[0] - EXTRA
+    return jnp.concatenate([q[rows, 0:16] for q in packs]).astype(jnp.int32)
+
+
+def move_zy(value, target):
     pairs = []
     for z in range(NZ):
-        for x in range(NX):
-            for y in range(NY):
+        for y in range(NY):
+            to_z, to_y = target(z, y)
+            for x in range(NX):
                 for r in range(4):
-                    pairs.append(((z * NX + x) * 16 + y * 4 + r, (y * NX + x) * 16 + z * 4 + r))
+                    source = (z * NX + x) * 16 + y * 4 + r
+                    pairs.append((source, (to_z * NX + x) * 16 + to_y * 4 + r))
     return lax.ppermute(value, ("mem", "tensor"), pairs)
 
 
@@ -105,7 +112,7 @@
         out_ref[:, cols] = out * ((1.0 - gate_ref[h]) / total)
 
 
-def memory_kernel(ids_ref, stored_ref, *refs):
+def memory_kernel(ids_ref, early_ref, late_ref, *refs):
     sources, result_ref = refs[0:12], refs[12]
     q_buf, k_buf, v_buf, sel_ref, sems = refs[13:18]
     targets = [buf.at[n] for buf in (q_buf, k_buf, v_buf) for n in range(4)]
@@ -120,12 +127,13 @@
     for n in range(2 * NZ * NX):
         sel_ref[n] = -1
     for n in range(2 * NZ * 8):
-        block = stored_ref[n]
+        j = n // 16
+        block = late_ref[n % 16] if j == 2 else early_ref[min(j, 2) * 16 + n % 16]
         shard = block // SLOTS
         place = n // 8 * NX + ((x - shard) & 3)
         sel_ref[jnp.where(shard // NX == z, place, 2 * NZ * NX)] = block % SLOTS
 
-    for copy in copies:
+    for copy in copies[0:8]:
         copy.wait()
     q_refs, k_refs, v_refs = [[buf.at[n] for n in range(4)] for buf in (q_buf, k_buf, v_buf)]
     heads = k_buf.shape[2] // HEAD
@@ -148,13 +156,16 @@
                 cols = pl.ds(h * HEAD, HEAD)
                 query = q_ref[pl.ds(row, BLOCK), cols]
                 keys = jnp.concatenate([k_refs[i][pl.ds(starts[i], BLOCK), cols] for i in range(NX)])
-                values = jnp.concatenate(
-                    [v_refs[i][pl.ds(starts[i], BLOCK), cols] for i in range(NX)]
-                )
                 scores = dot_nt(query, keys) * SCALE2 + bias
                 top = jnp.max(scores, axis=1, keepdims=True)
                 weights = jnp.exp2(scores - top)
                 total = jnp.sum(weights, axis=1, keepdims=True)
+                if (j, b, h) == (0, 0, 0):
+                    for copy in copies[8:12]:
+                        copy.wait()
+                values = jnp.concatenate(
+                    [v_refs[i][pl.ds(starts[i], BLOCK), cols] for i in range(NX)]
+                )
                 acc = dot_nn(weights.astype(jnp.bfloat16), values)
                 out_ref[pl.ds(row, BLOCK), cols] = (acc / total).astype(jnp.bfloat16)
                 stat = jnp.where(lane == h, top + jnp.log2(total), stat)
@@ -236,7 +247,7 @@
 def weight_kernel(ids_ref, *refs):
     att_ref, own, other = refs[0], refs[1:5], refs[5:9]
     outs, att_scr, cot_buf, sems = refs[9:13], refs[13], refs[14], refs[15]
-    x, y, zl, c = ids_ref[1], ids_ref[2], ids_ref[4], ids_ref[5]
+    z, x, y, zl, c = ids_ref[0], ids_ref[1], ids_ref[2], ids_ref[4], ids_ref[5]
     rows = att_ref.shape[2]
     copies = []
     for w, arrays in enumerate((own, other)):
@@ -252,7 +263,7 @@
                 )
                 copies[-1].start()
     for j in range(NZ):
-        place = ((y - j) & 3) * rows
+        place = ((y - z - j) & 3) * rows
         att_scr[:, pl.ds(pl.multiple_of(place, 128), rows)] = att_ref[j]
     for w in range(2):
         for s in range(2):
@@ -298,19 +309,24 @@
     extra = extra.at[0, 0 : storage.shape[0]].set(storage.astype(jnp.bfloat16))
     q_pack = jnp.concatenate([queries, extra], axis=0)
 
-    k1, v3 = shift_x(memory_keys, 1), shift_x(memory_values, -1)
-    q1, q3 = shift_z(q_pack, 1), shift_z(q_pack, 3)
-    near = flip_tensor(cotangent, 2)
-    k1, v3, q1, q3, near, own_keys, own_values, q_late = together(
-        k1, v3, q1, q3, near, memory_keys, memory_values, q_pack
-    )
-    k2, v2, q2 = shift_x(k1, 1), shift_x(v3, -1), shift_z(q_late, 2)
-    k3, v1 = shift_x(own_keys, -1), shift_x(own_values, 1)
-    k2, v2, k3, v1, q2, near = together(k2, v2, k3, v1, q2, near)
-    pair = jnp.concatenate([cotangent, near], axis=0)
-    w1, w3, swapped = shift_y(pair, 1), shift_y(pair, 3), swap_zy(pair[:rows])
+    k1, v3, q1, q3, moved, own_keys, own_values, own_cot, q_pack = together(
+        shift_x(memory_keys, 1),
+        shift_x(memory_values, -1),
+        shift_z(q_pack, 1),
+        shift_z(q_pack, 3),
+        move_zy(cotangent, lambda z, y: (z, (y + z) % NY)),
+        memory_keys,
+        memory_values,
+        cotangent,
+        q_pack,
+    )
+    k2, v2, v1, q2 = shift_x(k1, 1), shift_x(v3, -1), shift_x(own_values, 1), shift_z(q_pack, 2)
+    swapped = move_zy(moved, lambda z, y: ((y - z) % NZ, y))
+    k3 = shift_x(after(own_keys, v2), -1)
+    early = stored_in(q_pack, q1, q3)
+    k2, v1, q2, k3, swapped, own_cot, early = together(k2, v1, q2, k3, swapped, own_cot, early)
+    near, near_own = flip_tensor(swapped, 2), flip_tensor(own_cot, 2)
     q_all = [q_pack, q1, q2, q3]
-    stored = jnp.stack([q[rows, 0:16] for q in q_all]).reshape(-1).astype(jnp.int32)
 
     local_out = pl.pallas_call(
         local_kernel,
@@ -325,7 +341,7 @@
     parts = pl.pallas_call(
         memory_kernel,
         out_shape=jax.ShapeDtypeStruct((NZ, rows + EXTRA, width), jnp.bfloat16),
-        in_specs=[SM] * 2 + [HB] * 12,
+        in_specs=[SM] * 3 + [HB] * 12,
         out_specs=VM,
         scratch_shapes=[
             pltpu.VMEM((NZ, rows + EXTRA, width), jnp.bfloat16),
@@ -339,13 +355,15 @@
             64 * heads * rows * rows * HEAD, 8 * heads * rows * rows, 24 * rows * width
         ),
         name="memory_attention",
-    )(ids, stored, *in_hbm([*q_all, memory_keys, k1, k2, k3, memory_values, v1, v2, v3]))
-
-    parts, swapped, w1, w3, pair = together(parts, swapped, w1, w3, pair)
+    )(ids, early, stored_in(q2), *in_hbm([*q_all, memory_keys, k1, k2, k3, memory_values, v1, v2, v3]))
+
+    tall = jnp.concatenate([swapped, near], axis=0)
+    wide = jnp.concatenate([cotangent, near_own], axis=0)
+    parts, tall, wide = together(parts, tall, wide)
     back = exchange_z(parts)
-    tall = jnp.concatenate([swapped, flip_tensor(swapped, 2)], axis=0)
-    w2, t1, t3 = shift_y(pair, 2), shift_y(tall, 1), shift_y(tall, 3)
-    back, w2, t1, t3, tall = together(back, w2, t1, t3, tall)
+    t1, t2, t3 = [shift_y(tall, k) for k in (1, 2, 3)]
+    c0 = flip_tensor(tall, 1)
+    back, c0, t1, t3 = together(back, c0, t1, t3)
     attention, att_t = pl.pallas_call(
         merge_kernel,
         out_shape=[
@@ -358,16 +376,28 @@
         cost_estimate=cost(32 * rows * width, 4 * rows, 16 * rows * width),
         name="merge",
     )(gate, local_out, back)
-    att_t, tall, pair = together(att_t, tall, pair)
+    att_t, t1, t2, t3, wide = together(att_t, t1, t2, t3, wide)
     att_all = exchange_z(att_t)
-    t2 = shift_y(tall, 2)
-    tall = [tall, t1, t2, t3]
-    tall = tall + [flip_tensor(v, 1) for v in tall]
-    wide = [pair, w1, w2, w3]
-    wide = wide + [flip_tensor(v, 1) for v in wide]
-    att_all, *flipped = together(att_all, *tall[4:], *wide[4:])
-    tall, wide = in_hbm(tall[:4] + flipped[:4]), in_hbm(wide[:4] + flipped[4:])
-
+    tall = in_hbm([tall, t1, t2, t3, c0] + [flip_tensor(v, 1) for v in (t1, t2, t3)])
+    w1, w2, w3 = [shift_y(wide, k) for k in (1, 2, 3)]
+    wide = [wide, w1, w2, w3] + [flip_tensor(v, 1) for v in (wide, w1, w2, w3)]
+
+    mine, *sent = pl.pallas_call(
+        weight_kernel,
+        out_shape=[jax.ShapeDtypeStruct((width, width), jnp.float32)]
+        + [jax.ShapeDtypeStruct((width, width), jnp.bfloat16)] * 3,
+        in_specs=[SM, VM] + [HB] * 8,
+        out_specs=[VM] * 4,
+        scratch_shapes=[
+            pltpu.VMEM((width, NZ * rows), jnp.bfloat16),
+            pltpu.VMEM((4, NY * rows, width), jnp.bfloat16),
+            pltpu.SemaphoreType.DMA((16,)),
+        ],
+        compiler_params=params,
+        cost_estimate=cost(32 * rows * width * width, 0, 48 * rows * width),
+        name="weight_partials",
+    )(ids, att_all, *tall)
+    got = [shift_x(sent[n - 1], n) for n in (1, 2, 3)]
     attention_grad = pl.pallas_call(
         grad_kernel,
         out_shape=jax.ShapeDtypeStruct((rows, width), jnp.bfloat16),
@@ -387,24 +417,8 @@
         compiler_params=params,
         cost_estimate=cost(32 * rows * width * width, 0, 64 * rows * width),
         name="attention_grad",
-    )(ids, *wide, *in_hbm([out_weight]))
-
-    mine, *sent = pl.pallas_call(
-        weight_kernel,
-        out_shape=[jax.ShapeDtypeStruct((width, width), jnp.float32)]
-        + [jax.ShapeDtypeStruct((width, width), jnp.bfloat16)] * 3,
-        in_specs=[SM, VM] + [HB] * 8,
-        out_specs=[VM] * 4,
-        scratch_shapes=[
-            pltpu.VMEM((width, NZ * rows), jnp.bfloat16),
-            pltpu.VMEM((4, NY * rows, width), jnp.bfloat16),
-            pltpu.SemaphoreType.DMA((16,)),
-        ],
-        compiler_params=params,
-        cost_estimate=cost(32 * rows * width * width, 0, 48 * rows * width),
-        name="weight_partials",
-    )(ids, att_all, *tall)
-    got = [shift_x(sent[n - 1], n) for n in (1, 2, 3)]
+    )(after(ids, mine), *wide, *in_hbm([out_weight]))
+
     weight_grad = (mine + got[0].astype(jnp.float32)) + (
         got[1].astype(jnp.float32) + got[2].astype(jnp.float32)
     )

time: 158 us -> 143 us (0.905); the launches traced: 155 us -> 142 us
  waiting for transfers between devices: 70.6 us -> 43.6 us
  starting transfers between devices: 49.9 us -> 69 us
  local copies, waits for them, and re-layouts: 5.8 us -> 1.68 us
    ppermute x10, waiting for transfers between devices: 34.8 us -> 0.03 us  [flip_tensor(): return lax.ppermute(value, 'tensor', [(t, t ^ bit) for t in range(16)])]
    ppermute x10, starting transfers between devices: 5.53 us -> 24.7 us  [flip_tensor(): return lax.ppermute(value, 'tensor', [(t, t ^ bit) for t in range(16)])]
    ppermute x9, waiting for transfers between devices: 12.5 us -> 20.9 us  [shift_x(): return lax.ppermute(value, 'mem', pairs)]
    ppermute x6, waiting for transfers between devices: 17.2 us -> 14 us  [shift_y(): return lax.ppermute(value, 'tensor', pairs)]
    all_to_all x2, starting transfers between devices: 15.5 us -> 12.9 us  [exchange_z(): lax.all_to_all(value, 'mem', split_axis=0, concat_axis=0, axis_index_grou...]
    ppermute x6, starting transfers between devices: 6.83 us -> 9.3 us  [shift_y(): return lax.ppermute(value, 'tensor', pairs)]
    ppermute x3, waiting for transfers between devices: 6.13 us -> 8.13 us  [shift_z(): return lax.ppermute(value, 'mem', pairs)]
    unnamed x52 -> x40, local copies, waits for them, and re-layouts: 2.82 us -> 0.83 us
  transfers between devices with their start and end apart: 31 -> 32, of which waited for: 10 -> 12; matrix products, arithmetic and copies ran while one was open for 4% -> 2% of each run, Pallas kernels for 12% -> 17%
where the time goes in v5:
time: 143 us; the launch traced here: 142 us
  starting transfers between devices  69 us (48%)
  waiting for transfers between devices  43.6 us (30%)
  Pallas kernels  24.2 us (17%)
  other arithmetic  2.94 us (2%)
  local copies, waits for them, and re-layouts  1.68 us (1%)
    ppermute x10, starting transfers between devices, flip_tensor(): return lax.ppermute(value, 'tensor', [(t, t ^ bit) for t in range(16)])  24.7 us
    ppermute x9, waiting for transfers between devices, shift_x(): return lax.ppermute(value, 'mem', pairs)  20.9 us
    ppermute x6, waiting for transfers between devices, shift_y(): return lax.ppermute(value, 'tensor', pairs)  14 us
    all_to_all x2, starting transfers between devices, exchange_z(): lax.all_to_all(value, 'mem', split_axis=0, concat_axis=0, axis_index_grou...  12.9 us
    ppermute x9, starting transfers between devices, shift_x(): return lax.ppermute(value, 'mem', pairs)  10.4 us
    pallas_call x1, Pallas kernels, per_device(): pl.pallas_call(memory_kernel, out_shape=jax.ShapeDtypeStruct((NZ, rows +...  10 us
    ppermute x3, starting transfers between devices, shift_z(): return lax.ppermute(value, 'mem', pairs)  9.54 us
    ppermute x6, starting transfers between devices, shift_y(): return lax.ppermute(value, 'tensor', pairs)  9.3 us
  transfers between devices with their start and end apart: 32, of which 12 were waited for; matrix products, arithmetic and copies ran while one was open for 2% of the time, Pallas kernels for 17%

profile of v5, /device:TPU:1, one launch (start us, length us, event | category | flops | bytes accessed | tf_op | source)
XLA Modules:
  0.0 142.3 jit_solution(426567274488690381)
XLA Ops:
  0.6 0.0 copy-start.6
  0.6 2.1 %collective-permute-start = (bf16[512,384]{1,0:T(8,128)(2,1)}, bf16[512,384]{1,0:T(8,128)(2,1)S(1)}, u32[]{:S(2)}, u32[]{:S(2)}) collective-permute-start(bf16[512,384]{1,0:T(8,128)(2,1)} %refs_4_.1), channel_id=1, source_target_pairs={{0,16},{16,32},{32,48},{48,0},{64,80},{80,96},{96,112},{112,64},{1... | collective-permute-start | bytes 1179656 | tf_op jit(solution)/shard_map/ppermute | solution.py:52
  2.8 1.4 collective-permute-start.1
  4.1 0.8 eq.19
  4.9 0.8 select_reduce_fusion
  5.7 1.0 fusion.1.refs_0_
  6.7 0.0 copy-start.19
  6.7 0.0 copy-start
  6.7 0.0 copy-start.1
  6.7 0.0 copy-start.2
  6.7 0.0 copy-start.3
  6.7 6.2 %collective-permute-start.3 = (bf16[272,384]{1,0:T(8,128)(2,1)S(1)}, bf16[272,384]{1,0:T(8,128)(2,1)S(1)}, u32[]{:S(2)}, u32[]{:S(2)}) collective-permute-start(bf16[272,384]{1,0:T(8,128)(2,1)S(1)} %fusion.1.refs_0_), channel_id=1, source_target_pairs={{0,192},{16,208},{32,224},{48,240},{64,0},{80,16},{96,32},{112,48}... | collective-permute-start | bytes 626696 | tf_op jit(solution)/shard_map/ppermute | solution.py:57
  13.0 0.0 collective-permute-start.2
  13.0 1.6 %collective-permute-start.4 = (bf16[256,384]{1,0:T(8,128)(2,1)}, bf16[256,384]{1,0:T(8,128)(2,1)S(1)}, u32[]{:S(2)}, u32[]{:S(2)}) collective-permute-start(bf16[256,384]{1,0:T(8,128)(2,1)} %param.23), channel_id=1, source_target_pairs={{0,0},{1,1},{2,2},{3,3},{16,16},{17,17},{18,18},{19,19},{32,32},{3... | collective-permute-start | bytes 589832 | tf_op jit(solution)/shard_map/ppermute | solution.py:94
  14.5 4.1 %collective-permute-done.3.refs_3_ = bf16[272,384]{1,0:T(8,128)(2,1)S(1)} collective-permute-done((bf16[272,384]{1,0:T(8,128)(2,1)S(1)}, bf16[272,384]{1,0:T(8,128)(2,1)S(1)}, u32[]{:S(2)}, u32[]{:S(2)}) %collective-permute-start.3) | collective-permute-done | bytes 208928 | tf_op jit(solution)/shard_map/ppermute | solution.py:57
  18.6 3.2 %collective-permute-done.2.refs_1_ = bf16[272,384]{1,0:T(8,128)(2,1)S(1)} collective-permute-done((bf16[272,384]{1,0:T(8,128)(2,1)S(1)}, bf16[272,384]{1,0:T(8,128)(2,1)S(1)}, u32[]{:S(2)}, u32[]{:S(2)}) %collective-permute-start.2) | collective-permute-done | bytes 208928 | tf_op jit(solution)/shard_map/ppermute | solution.py:57
  21.8 0.0 collective-permute-done.refs_5_
  21.8 0.0 collective-permute-done.1.refs_11_
  21.9 1.3 collective-permute-start.8
  23.2 0.1 stack.23.ids_ref
  23.3 0.7 collective-permute-start.10
  24.0 3.3 %collective-permute-start.7 = (bf16[272,384]{1,0:T(8,128)(2,1)S(1)}, bf16[272,384]{1,0:T(8,128)(2,1)S(1)}, u32[]{:S(2)}, u32[]{:S(2)}) collective-permute-start(bf16[272,384]{1,0:T(8,128)(2,1)S(1)} %fusion.1.refs_0_), channel_id=1, source_target_pairs={{0,128},{16,144},{32,160},{48,176},{64,192},{80,208},{96,224},{112... | collective-permute-start | bytes 626696 | tf_op jit(solution)/shard_map/ppermute | solution.py:57
  27.3 0.2 collective-permute-start.6
  27.5 0.0 collective-permute-start.5
  27.5 1.0 collective-permute-done.8.refs_10_
  28.6 0.7 copy-done.11
  29.3 2.5 %collective-permute-start.9 = (bf16[512,384]{1,0:T(8,128)(2,1)}, bf16[512,384]{1,0:T(8,128)(2,1)S(1)}, u32[]{:S(2)}, u32[]{:S(2)}) collective-permute-start(bf16[512,384]{1,0:T(8,128)(2,1)} %refs_4_.1), channel_id=1, source_target_pairs={{0,48},{16,0},{32,16},{48,32},{64,112},{80,64},{96,80},{112,96},{1... | collective-permute-start | bytes 1179656 | tf_op jit(solution)/shard_map/ppermute | solution.py:52
  31.8 0.1 maximum_convert_fusion.early_ref
  31.9 0.0 collective-permute-done.10
  31.9 0.8 collective-permute-done.7.refs_2_
  32.7 3.8 %collective-permute-done.6.refs_9_ = bf16[512,384]{1,0:T(8,128)(2,1)S(1)} collective-permute-done((bf16[512,384]{1,0:T(8,128)(2,1)}, bf16[512,384]{1,0:T(8,128)(2,1)S(1)}, u32[]{:S(2)}, u32[]{:S(2)}) %collective-permute-start.6) | collective-permute-done | bytes 393248 | tf_op jit(solution)/shard_map/ppermute | solution.py:52
  36.5 8.4 %collective-permute-done.5.refs_6_ = bf16[512,384]{1,0:T(8,128)(2,1)S(1)} collective-permute-done((bf16[512,384]{1,0:T(8,128)(2,1)S(1)}, bf16[512,384]{1,0:T(8,128)(2,1)S(1)}, u32[]{:S(2)}, u32[]{:S(2)}) %collective-permute-start.5) | collective-permute-done | bytes 393248 | tf_op jit(solution)/shard_map/ppermute | solution.py:52
  45.0 3.7 %collective-permute-start.12 = (bf16[256,384]{1,0:T(8,128)(2,1)}, bf16[256,384]{1,0:T(8,128)(2,1)S(1)}, u32[]{:S(2)}, u32[]{:S(2)}) collective-permute-start(bf16[256,384]{1,0:T(8,128)(2,1)} %param.23), channel_id=1, source_target_pairs={{0,2},{1,3},{2,0},{3,1},{4,6},{5,7},{6,4},{7,5},{8,10},{9,11},{10,... | collective-permute-start | bytes 589832 | tf_op jit(solution)/shard_map/ppermute | solution.py:77
  48.7 0.3 collective-permute-start.11
  49.0 10.0 %memory_attention.1 = bf16[4,272,384]{2,1,0:T(8,128)(2,1)} custom-call(s32[6]{0:T(128)S(1)} %stack.23.ids_ref, s32[48]{0:T(128)S(1)} %maximum_convert_fusion.early_ref, s32[16]{0:T(128)S(1)} %bitcast_convert_fusion.late_ref, bf16[272,384]{1,0:T(8,128)(2,1)} %copy-done.5, bf16[272,384]{1,0:T(8,128)(2,1)} %copy-done.8, bf16[272,384]{1,0:T(8,128)(2,1)} %copy-done.18, ...), custom_call_target="tpu_custom_call" | custom-call | flops 1610612736 | bytes 2359296 | tf_op jit(solution)/shard_map/memory_attention/pallas_call | solution.py:341
  59.2 0.0 copy-start.4
  59.2 6.4 %all-to-all-start = ((bf16[4,272,384]{2,1,0:T(8,128)(2,1)}), bf16[4,272,384]{2,1,0:T(8,128)(2,1)S(1)}, u32[]{:S(2)}, u32[]{:S(2)}) async-start(bf16[4,272,384]{2,1,0:T(8,128)(2,1)} %memory_attention.1), calls=%async_computation | async-start | bytes 1671168 | tf_op jit(solution)/shard_map/all_to_all | solution.py:62
  65.6 2.5 %collective-permute-start.15 = (bf16[512,384]{1,0:T(8,128)(2,1)S(1)}, bf16[512,384]{1,0:T(8,128)(2,1)}, u32[]{:S(2)}, u32[]{:S(2)}) collective-permute-start(bf16[512,384]{1,0:T(8,128)(2,1)S(1)} %pad_maximum_fusion.refs_1_), channel_id=1, source_target_pairs={{0,12},{1,13},{2,14},{3,15},{4,0},{5,1},{6,2},{7,3},{8,4},{9,5},{1... | collective-permute-start | bytes 1179656 | tf_op jit(solution)/shard_map/ppermute | solution.py:69
  68.1 4.1 %collective-permute-start.13 = (bf16[512,384]{1,0:T(8,128)(2,1)S(1)}, bf16[512,384]{1,0:T(8,128)(2,1)}, u32[]{:S(2)}, u32[]{:S(2)}) collective-permute-start(bf16[512,384]{1,0:T(8,128)(2,1)S(1)} %pad_maximum_fusion.refs_1_), channel_id=1, source_target_pairs={{0,1},{1,0},{2,3},{3,2},{4,5},{5,4},{6,7},{7,6},{8,9},{9,8},{10,11... | collective-permute-start | bytes 1179656 | tf_op jit(solution)/shard_map/ppermute | solution.py:77
  72.2 3.6 %collective-permute-start.16 = (bf16[512,384]{1,0:T(8,128)(2,1)S(1)}, bf16[512,384]{1,0:T(8,128)(2,1)}, u32[]{:S(2)}, u32[]{:S(2)}) collective-permute-start(bf16[512,384]{1,0:T(8,128)(2,1)S(1)} %pad_maximum_fusion.refs_1_), channel_id=1, source_target_pairs={{0,8},{1,9},{2,10},{3,11},{4,12},{5,13},{6,14},{7,15},{8,0},{9,1},... | collective-permute-start | bytes 1179656 | tf_op jit(solution)/shard_map/ppermute | solution.py:69
  75.9 1.4 local_attention.1.local_ref
  77.3 0.6 all-to-all-done.back_ref
  77.9 2.3 %merge.1 = (bf16[256,384]{1,0:T(8,128)(2,1)}, bf16[4,384,256]{2,1,0:T(8,128)(2,1)}) custom-call(f32[3]{0:T(128)S(1)} %add_divide_fusion.gate_ref, f32[256,384]{1,0:T(8,128)S(1)} %local_attention.1.local_ref, bf16[4,272,384]{2,1,0:T(8,128)(2,1)S(1)} %all-to-all-done.back_ref), custom_call_target="tpu_custom_call" | custom-call | flops 3145728 | bytes 1572864 | tf_op jit(solution)/shard_map/merge/pallas_call | solution.py:367
  80.2 5.2 %collective-permute-done.16.refs_3_ = bf16[512,384]{1,0:T(8,128)(2,1)} collective-permute-done((bf16[512,384]{1,0:T(8,128)(2,1)S(1)}, bf16[512,384]{1,0:T(8,128)(2,1)}, u32[]{:S(2)}, u32[]{:S(2)}) %collective-permute-start.16) | collective-permute-done | bytes 393248 | tf_op jit(solution)/shard_map/ppermute | solution.py:69
  85.4 6.5 %all-to-all-start.1 = ((bf16[4,384,256]{2,1,0:T(8,128)(2,1)}), bf16[4,384,256]{2,1,0:T(8,128)(2,1)S(1)}, u32[]{:S(2)}, u32[]{:S(2)}) async-start(bf16[4,384,256]{2,1,0:T(8,128)(2,1)} %get-tuple-element.76), calls=%async_computation.1 | async-start | bytes 1572864 | tf_op jit(solution)/shard_map/all_to_all | solution.py:62
  91.9 5.4 %collective-permute-start.17 = (bf16[512,384]{1,0:T(8,128)(2,1)S(1)}, bf16[512,384]{1,0:T(8,128)(2,1)S(1)}, u32[]{:S(2)}, u32[]{:S(2)}) collective-permute-start(bf16[512,384]{1,0:T(8,128)(2,1)S(1)} %collective-permute-done.14.refs_2_), channel_id=1, source_target_pairs={{0,1},{1,0},{2,3},{3,2},{4,5},{5,4},{6,7},{7,6},{8,9},{9,8},{10,11... | collective-permute-start | bytes 1179656 | tf_op jit(solution)/shard_map/ppermute | solution.py:77
  97.3 1.7 %collective-permute-start.22 = (bf16[512,384]{1,0:T(8,128)(2,1)S(1)}, bf16[512,384]{1,0:T(8,128)(2,1)S(1)}, u32[]{:S(2)}, u32[]{:S(2)}) collective-permute-start(bf16[512,384]{1,0:T(8,128)(2,1)S(1)} %pad_maximum_fusion.1.refs_0_), channel_id=1, source_target_pairs={{0,12},{1,13},{2,14},{3,15},{4,0},{5,1},{6,2},{7,3},{8,4},{9,5},{1... | collective-permute-start | bytes 1179656 | tf_op jit(solution)/shard_map/ppermute | solution.py:69
  99.0 0.7 collective-permute-start.21
  99.6 0.8 collective-permute-start.20
  100.4 1.3 collective-permute-start.19
  101.8 0.1 collective-permute-start.23
  101.9 5.6 %collective-permute-done.22.refs_3_ = bf16[512,384]{1,0:T(8,128)(2,1)S(1)} collective-permute-done((bf16[512,384]{1,0:T(8,128)(2,1)S(1)}, bf16[512,384]{1,0:T(8,128)(2,1)S(1)}, u32[]{:S(2)}, u32[]{:S(2)}) %collective-permute-start.22) | collective-permute-done | bytes 393248 | tf_op jit(solution)/shard_map/ppermute | solution.py:69
  107.5 9.3 %collective-permute-start.26 = (bf16[512,384]{1,0:T(8,128)(2,1)S(1)}, bf16[512,384]{1,0:T(8,128)(2,1)S(1)}, u32[]{:S(2)}, u32[]{:S(2)}) collective-permute-start(bf16[512,384]{1,0:T(8,128)(2,1)S(1)} %collective-permute-done.22.refs_3_), channel_id=1, source_target_pairs={{0,1},{1,0},{2,3},{3,2},{4,5},{5,4},{6,7},{7,6},{8,9},{9,8},{10,11... | collective-permute-start | bytes 1179656 | tf_op jit(solution)/shard_map/ppermute | solution.py:77
  116.8 0.0 collective-permute-start.25
  116.8 3.2 %collective-permute-done.20.refs_1_ = bf16[512,384]{1,0:T(8,128)(2,1)S(1)} collective-permute-done((bf16[512,384]{1,0:T(8,128)(2,1)S(1)}, bf16[512,384]{1,0:T(8,128)(2,1)S(1)}, u32[]{:S(2)}, u32[]{:S(2)}) %collective-permute-start.20) | collective-permute-done | bytes 393248 | tf_op jit(solution)/shard_map/ppermute | solution.py:69
  120.0 0.5 collective-permute-start.24
  120.5 4.3 %weight_partials.1 = (f32[384,384]{1,0:T(8,128)S(1)}, bf16[384,384]{1,0:T(8,128)(2,1)S(1)}, bf16[384,384]{1,0:T(8,128)(2,1)S(1)}, bf16[384,384]{1,0:T(8,128)(2,1)S(1)}) custom-call(s32[6]{0:T(128)S(1)} %stack.23.ids_ref, bf16[4,384,256]{2,1,0:T(8,128)(2,1)S(1)} %all-to-all-done.1.refs_0_, bf16[512,384]{1,0:T(8,128)(2,1)} %copy-done.4, ...), custom_call_target="tpu_custom_call" | custom-call | flops 1207959552 | bytes 4718592 | tf_op jit(solution)/shard_map/weight_partials/pallas_call | solution.py:385
  124.8 0.1 collective-permute-start.27
  124.9 0.5 collective-permute-start.28
  125.4 2.2 %collective-permute-start.29 = (bf16[384,384]{1,0:T(8,128)(2,1)S(1)}, bf16[384,384]{1,0:T(8,128)(2,1)S(1)}, u32[]{:S(2)}, u32[]{:S(2)}) collective-permute-start(bf16[384,384]{1,0:T(8,128)(2,1)S(1)} %get-tuple-element.86), channel_id=1, source_target_pairs={{0,48},{16,0},{32,16},{48,32},{64,112},{80,64},{96,80},{112,96},{1... | collective-permute-start | bytes 884744 | tf_op jit(solution)/shard_map/ppermute | solution.py:52
  127.7 6.1 %attention_grad.1 = bf16[256,384]{1,0:T(8,128)(2,1)} custom-call(s32[6]{0:T(128)S(1)} %stack.23.ids_ref, bf16[512,384]{1,0:T(8,128)(2,1)S(1)} %pad_maximum_fusion.1.refs_0_, bf16[512,384]{1,0:T(8,128)(2,1)S(1)} %collective-permute-done.20.refs_1_, bf16[512,384]{1,0:T(8,128)(2,1)S(1)} %collective-permute-done.21.refs_2_, ...), custom_call_target="tpu_custom_call" | custom-call | flops 1207959552 | bytes 6291456 | tf_op jit(solution)/shard_map/attention_grad/pallas_call | solution.py:401
  133.8 7.3 %collective-permute-done.27 = bf16[384,384]{1,0:T(8,128)(2,1)S(1)} collective-permute-done((bf16[384,384]{1,0:T(8,128)(2,1)S(1)}, bf16[384,384]{1,0:T(8,128)(2,1)S(1)}, u32[]{:S(2)}, u32[]{:S(2)}) %collective-permute-start.27) | collective-permute-done | bytes 294944 | tf_op jit(solution)/shard_map/ppermute | solution.py:52
  141.1 0.3 collective-permute-done.29
  141.4 1.0 add_add_fusion
  (58 shorter events, 0.2 us)
Async XLA Ops:
  0.6 58.4 %copy-start.6 = (bf16[256,384]{1,0:T(8,128)(2,1)S(1)}, bf16[256,384]{1,0:T(8,128)(2,1)}, u32[]{:S(2)}) copy-start(bf16[256,384]{1,0:T(8,128)(2,1)} %param.23) | copy-start | bytes 589828
  0.6 21.2 %collective-permute-start = (bf16[512,384]{1,0:T(8,128)(2,1)}, bf16[512,384]{1,0:T(8,128)(2,1)S(1)}, u32[]{:S(2)}, u32[]{:S(2)}) collective-permute-start(bf16[512,384]{1,0:T(8,128)(2,1)} %refs_4_.1), channel_id=1, source_target_pairs={{0,16},{16,32},{32,48},{48,0},{64,80},{80,96},{96,112},{112,64},{1... | collective-permute-start | bytes 1179656 | tf_op jit(solution)/shard_map/ppermute | solution.py:52
  2.8 19.1 %collective-permute-start.1 = (bf16[512,384]{1,0:T(8,128)(2,1)}, bf16[512,384]{1,0:T(8,128)(2,1)S(1)}, u32[]{:S(2)}, u32[]{:S(2)}) collective-permute-start(bf16[512,384]{1,0:T(8,128)(2,1)} %refs_8_.2), channel_id=1, source_target_pairs={{0,48},{16,0},{32,16},{48,32},{64,112},{80,64},{96,80},{112,96},{1... | collective-permute-start | bytes 1179656 | tf_op jit(solution)/shard_map/ppermute | solution.py:52
  6.7 42.3 %copy-start.5 = (bf16[272,384]{1,0:T(8,128)(2,1)}, bf16[272,384]{1,0:T(8,128)(2,1)S(1)}, u32[]{:S(2)}) copy-start(bf16[272,384]{1,0:T(8,128)(2,1)S(1)} %fusion.1.refs_0_) | copy-start | bytes 626692
  6.7 69.1 %copy-start.19 = (f32[3]{0:T(128)S(1)}, f32[3]{0:T(128)}, u32[]{:S(2)}) copy-start(f32[3]{0:T(128)} %param.21) | copy-start | bytes 40
  6.7 69.1 %copy-start = (bf16[256,384]{1,0:T(8,128)(2,1)S(1)}, bf16[256,384]{1,0:T(8,128)(2,1)}, u32[]{:S(2)}) copy-start(bf16[256,384]{1,0:T(8,128)(2,1)} %q_ref.1) | copy-start | bytes 589828
  6.7 69.1 %copy-start.1 = (bf16[256,384]{1,0:T(8,128)(2,1)S(1)}, bf16[256,384]{1,0:T(8,128)(2,1)}, u32[]{:S(2)}) copy-start(bf16[256,384]{1,0:T(8,128)(2,1)} %k_ref.1) | copy-start | bytes 589828
  6.7 69.1 %copy-start.2 = (bf16[256,384]{1,0:T(8,128)(2,1)S(1)}, bf16[256,384]{1,0:T(8,128)(2,1)}, u32[]{:S(2)}) copy-start(bf16[256,384]{1,0:T(8,128)(2,1)} %v_ref.1) | copy-start | bytes 589828
  6.7 69.1 %copy-start.3 = (s32[256]{0:T(256)S(1)}, s32[256]{0:T(256)}, u32[]{:S(2)}) copy-start(s32[256]{0:T(256)} %param.16) | copy-start | bytes 3076
  6.7 11.9 %collective-permute-start.3 = (bf16[272,384]{1,0:T(8,128)(2,1)S(1)}, bf16[272,384]{1,0:T(8,128)(2,1)S(1)}, u32[]{:S(2)}, u32[]{:S(2)}) collective-permute-start(bf16[272,384]{1,0:T(8,128)(2,1)S(1)} %fusion.1.refs_0_), channel_id=1, source_target_pairs={{0,192},{16,208},{32,224},{48,240},{64,0},{80,16},{96,32},{112,48}... | collective-permute-start | bytes 626696 | tf_op jit(solution)/shard_map/ppermute | solution.py:57
  13.0 8.9 %collective-permute-start.2 = (bf16[272,384]{1,0:T(8,128)(2,1)S(1)}, bf16[272,384]{1,0:T(8,128)(2,1)S(1)}, u32[]{:S(2)}, u32[]{:S(2)}) collective-permute-start(bf16[272,384]{1,0:T(8,128)(2,1)S(1)} %fusion.1.refs_0_), channel_id=1, source_target_pairs={{0,64},{16,80},{32,96},{48,112},{64,128},{80,144},{96,160},{112,17... | collective-permute-start | bytes 626696 | tf_op jit(solution)/shard_map/ppermute | solution.py:57
  13.0 1.6 %collective-permute-start.4 = (bf16[256,384]{1,0:T(8,128)(2,1)}, bf16[256,384]{1,0:T(8,128)(2,1)S(1)}, u32[]{:S(2)}, u32[]{:S(2)}) collective-permute-start(bf16[256,384]{1,0:T(8,128)(2,1)} %param.23), channel_id=1, source_target_pairs={{0,0},{1,1},{2,2},{3,3},{16,16},{17,17},{18,18},{19,19},{32,32},{3... | collective-permute-start | bytes 589832 | tf_op jit(solution)/shard_map/ppermute | solution.py:94
  18.6 30.3 %copy-start.7 = (bf16[272,384]{1,0:T(8,128)(2,1)}, bf16[272,384]{1,0:T(8,128)(2,1)S(1)}, u32[]{:S(2)}) copy-start(bf16[272,384]{1,0:T(8,128)(2,1)S(1)} %collective-permute-done.3.refs_3_) | copy-start | bytes 626692
  21.8 27.1 %copy-start.8 = (bf16[272,384]{1,0:T(8,128)(2,1)}, bf16[272,384]{1,0:T(8,128)(2,1)S(1)}, u32[]{:S(2)}) copy-start(bf16[272,384]{1,0:T(8,128)(2,1)S(1)} %collective-permute-done.2.refs_1_) | copy-start | bytes 626692
  21.8 27.1 %copy-start.9 = (bf16[512,384]{1,0:T(8,128)(2,1)}, bf16[512,384]{1,0:T(8,128)(2,1)S(1)}, u32[]{:S(2)}) copy-start(bf16[512,384]{1,0:T(8,128)(2,1)S(1)} %collective-permute-done.refs_5_) | copy-start | bytes 1179652
  21.8 27.1 %copy-start.10 = (bf16[512,384]{1,0:T(8,128)(2,1)}, bf16[512,384]{1,0:T(8,128)(2,1)S(1)}, u32[]{:S(2)}) copy-start(bf16[512,384]{1,0:T(8,128)(2,1)S(1)} %collective-permute-done.1.refs_11_) | copy-start | bytes 1179652
  21.9 6.7 %collective-permute-start.8 = (bf16[512,384]{1,0:T(8,128)(2,1)S(1)}, bf16[512,384]{1,0:T(8,128)(2,1)S(1)}, u32[]{:S(2)}, u32[]{:S(2)}) collective-permute-start(bf16[512,384]{1,0:T(8,128)(2,1)S(1)} %collective-permute-done.1.refs_11_), channel_id=1, source_target_pairs={{0,48},{16,0},{32,16},{48,32},{64,112},{80,64},{96,80},{112,96},{1... | collective-permute-start | bytes 1179656 | tf_op jit(solution)/shard_map/ppermute | solution.py:52
  23.3 8.6 %collective-permute-start.10 = (bf16[256,384]{1,0:T(8,128)(2,1)S(1)}, bf16[256,384]{1,0:T(8,128)(2,1)S(1)}, u32[]{:S(2)}, u32[]{:S(2)}) collective-permute-start(bf16[256,384]{1,0:T(8,128)(2,1)S(1)} %collective-permute-done.4), channel_id=1, source_target_pairs={{0,0},{1,1},{2,2},{3,3},{16,16},{17,17},{18,18},{19,19},{32,32},{3... | collective-permute-start | bytes 589832 | tf_op jit(solution)/shard_map/ppermute | solution.py:94
  24.0 8.7 %collective-permute-start.7 = (bf16[272,384]{1,0:T(8,128)(2,1)S(1)}, bf16[272,384]{1,0:T(8,128)(2,1)S(1)}, u32[]{:S(2)}, u32[]{:S(2)}) collective-permute-start(bf16[272,384]{1,0:T(8,128)(2,1)S(1)} %fusion.1.refs_0_), channel_id=1, source_target_pairs={{0,128},{16,144},{32,160},{48,176},{64,192},{80,208},{96,224},{112... | collective-permute-start | bytes 626696 | tf_op jit(solution)/shard_map/ppermute | solution.py:57
  27.3 9.2 %collective-permute-start.6 = (bf16[512,384]{1,0:T(8,128)(2,1)}, bf16[512,384]{1,0:T(8,128)(2,1)S(1)}, u32[]{:S(2)}, u32[]{:S(2)}) collective-permute-start(bf16[512,384]{1,0:T(8,128)(2,1)} %refs_8_.2), channel_id=1, source_target_pairs={{0,16},{16,32},{32,48},{48,0},{64,80},{80,96},{96,112},{112,64},{1... | collective-permute-start | bytes 1179656 | tf_op jit(solution)/shard_map/ppermute | solution.py:52
  27.5 17.5 %collective-permute-start.5 = (bf16[512,384]{1,0:T(8,128)(2,1)S(1)}, bf16[512,384]{1,0:T(8,128)(2,1)S(1)}, u32[]{:S(2)}, u32[]{:S(2)}) collective-permute-start(bf16[512,384]{1,0:T(8,128)(2,1)S(1)} %collective-permute-done.refs_5_), channel_id=1, source_target_pairs={{0,16},{16,32},{32,48},{48,0},{64,80},{80,96},{96,112},{112,64},{1... | collective-permute-start | bytes 1179656 | tf_op jit(solution)/shard_map/ppermute | solution.py:52
  28.6 0.7 copy-start.11
  29.3 15.7 %collective-permute-start.9 = (bf16[512,384]{1,0:T(8,128)(2,1)}, bf16[512,384]{1,0:T(8,128)(2,1)S(1)}, u32[]{:S(2)}, u32[]{:S(2)}) collective-permute-start(bf16[512,384]{1,0:T(8,128)(2,1)} %refs_4_.1), channel_id=1, source_target_pairs={{0,48},{16,0},{32,16},{48,32},{64,112},{80,64},{96,80},{112,96},{1... | collective-permute-start | bytes 1179656 | tf_op jit(solution)/shard_map/ppermute | solution.py:52
  32.7 16.3 %copy-start.18 = (bf16[272,384]{1,0:T(8,128)(2,1)}, bf16[272,384]{1,0:T(8,128)(2,1)S(1)}, u32[]{:S(2)}) copy-start(bf16[272,384]{1,0:T(8,128)(2,1)S(1)} %collective-permute-done.7.refs_2_) | copy-start | bytes 626692
  36.5 12.5 %copy-start.15 = (bf16[512,384]{1,0:T(8,128)(2,1)}, bf16[512,384]{1,0:T(8,128)(2,1)S(1)}, u32[]{:S(2)}) copy-start(bf16[512,384]{1,0:T(8,128)(2,1)S(1)} %collective-permute-done.6.refs_9_) | copy-start | bytes 1179652
  45.0 4.0 %copy-start.16 = (bf16[512,384]{1,0:T(8,128)(2,1)}, bf16[512,384]{1,0:T(8,128)(2,1)S(1)}, u32[]{:S(2)}) copy-start(bf16[512,384]{1,0:T(8,128)(2,1)S(1)} %collective-permute-done.5.refs_6_) | copy-start | bytes 1179652
  45.0 4.0 %copy-start.17 = (bf16[512,384]{1,0:T(8,128)(2,1)}, bf16[512,384]{1,0:T(8,128)(2,1)S(1)}, u32[]{:S(2)}) copy-start(bf16[512,384]{1,0:T(8,128)(2,1)S(1)} %collective-permute-done.9.refs_7_) | copy-start | bytes 1179652
  45.0 14.1 %collective-permute-start.12 = (bf16[256,384]{1,0:T(8,128)(2,1)}, bf16[256,384]{1,0:T(8,128)(2,1)S(1)}, u32[]{:S(2)}, u32[]{:S(2)}) collective-permute-start(bf16[256,384]{1,0:T(8,128)(2,1)} %param.23), channel_id=1, source_target_pairs={{0,2},{1,3},{2,0},{3,1},{4,6},{5,7},{6,4},{7,5},{8,10},{9,11},{10,... | collective-permute-start | bytes 589832 | tf_op jit(solution)/shard_map/ppermute | solution.py:77
  48.7 10.4 %collective-permute-start.11 = (bf16[256,384]{1,0:T(8,128)(2,1)S(1)}, bf16[256,384]{1,0:T(8,128)(2,1)S(1)}, u32[]{:S(2)}, u32[]{:S(2)}) collective-permute-start(bf16[256,384]{1,0:T(8,128)(2,1)S(1)} %collective-permute-done.10), channel_id=1, source_target_pairs={{0,2},{1,3},{2,0},{3,1},{4,6},{5,7},{6,4},{7,5},{8,10},{9,11},{10,... | collective-permute-start | bytes 589832 | tf_op jit(solution)/shard_map/ppermute | solution.py:77
  59.2 39.8 %copy-start.4 = (bf16[512,384]{1,0:T(8,128)(2,1)}, bf16[512,384]{1,0:T(8,128)(2,1)S(1)}, u32[]{:S(2)}) copy-start(bf16[512,384]{1,0:T(8,128)(2,1)S(1)} %pad_maximum_fusion.refs_1_) | copy-start | bytes 1179652
  59.2 18.7 %all-to-all-start = ((bf16[4,272,384]{2,1,0:T(8,128)(2,1)}), bf16[4,272,384]{2,1,0:T(8,128)(2,1)S(1)}, u32[]{:S(2)}, u32[]{:S(2)}) async-start(bf16[4,272,384]{2,1,0:T(8,128)(2,1)} %memory_attention.1), calls=%async_computation | async-start | bytes 1671168 | tf_op jit(solution)/shard_map/all_to_all | solution.py:62
  65.6 11.7 %collective-permute-start.15 = (bf16[512,384]{1,0:T(8,128)(2,1)S(1)}, bf16[512,384]{1,0:T(8,128)(2,1)}, u32[]{:S(2)}, u32[]{:S(2)}) collective-permute-start(bf16[512,384]{1,0:T(8,128)(2,1)S(1)} %pad_maximum_fusion.refs_1_), channel_id=1, source_target_pairs={{0,12},{1,13},{2,14},{3,15},{4,0},{5,1},{6,2},{7,3},{8,4},{9,5},{1... | collective-permute-start | bytes 1179656 | tf_op jit(solution)/shard_map/ppermute | solution.py:69
  68.1 9.2 %collective-permute-start.14 = (bf16[512,384]{1,0:T(8,128)(2,1)S(1)}, bf16[512,384]{1,0:T(8,128)(2,1)S(1)}, u32[]{:S(2)}, u32[]{:S(2)}) collective-permute-start(bf16[512,384]{1,0:T(8,128)(2,1)S(1)} %pad_maximum_fusion.refs_1_), channel_id=1, source_target_pairs={{0,4},{1,5},{2,6},{3,7},{4,8},{5,9},{6,10},{7,11},{8,12},{9,13},{1... | collective-permute-start | bytes 1179656 | tf_op jit(solution)/shard_map/ppermute | solution.py:69
  68.1 9.2 %collective-permute-start.13 = (bf16[512,384]{1,0:T(8,128)(2,1)S(1)}, bf16[512,384]{1,0:T(8,128)(2,1)}, u32[]{:S(2)}, u32[]{:S(2)}) collective-permute-start(bf16[512,384]{1,0:T(8,128)(2,1)S(1)} %pad_maximum_fusion.refs_1_), channel_id=1, source_target_pairs={{0,1},{1,0},{2,3},{3,2},{4,5},{5,4},{6,7},{7,6},{8,9},{9,8},{10,11... | collective-permute-start | bytes 1179656 | tf_op jit(solution)/shard_map/ppermute | solution.py:77
  72.2 13.2 %collective-permute-start.16 = (bf16[512,384]{1,0:T(8,128)(2,1)S(1)}, bf16[512,384]{1,0:T(8,128)(2,1)}, u32[]{:S(2)}, u32[]{:S(2)}) collective-permute-start(bf16[512,384]{1,0:T(8,128)(2,1)S(1)} %pad_maximum_fusion.refs_1_), channel_id=1, source_target_pairs={{0,8},{1,9},{2,10},{3,11},{4,12},{5,13},{6,14},{7,15},{8,0},{9,1},... | collective-permute-start | bytes 1179656 | tf_op jit(solution)/shard_map/ppermute | solution.py:69
  77.3 24.5 %copy-start.12 = (bf16[512,384]{1,0:T(8,128)(2,1)}, bf16[512,384]{1,0:T(8,128)(2,1)S(1)}, u32[]{:S(2)}) copy-start(bf16[512,384]{1,0:T(8,128)(2,1)S(1)} %collective-permute-done.14.refs_2_) | copy-start | bytes 1179652
  85.4 35.0 %all-to-all-start.1 = ((bf16[4,384,256]{2,1,0:T(8,128)(2,1)}), bf16[4,384,256]{2,1,0:T(8,128)(2,1)S(1)}, u32[]{:S(2)}, u32[]{:S(2)}) async-start(bf16[4,384,256]{2,1,0:T(8,128)(2,1)} %get-tuple-element.76), calls=%async_computation.1 | async-start | bytes 1572864 | tf_op jit(solution)/shard_map/all_to_all | solution.py:62
  91.9 8.5 %collective-permute-start.17 = (bf16[512,384]{1,0:T(8,128)(2,1)S(1)}, bf16[512,384]{1,0:T(8,128)(2,1)S(1)}, u32[]{:S(2)}, u32[]{:S(2)}) collective-permute-start(bf16[512,384]{1,0:T(8,128)(2,1)S(1)} %collective-permute-done.14.refs_2_), channel_id=1, source_target_pairs={{0,1},{1,0},{2,3},{3,2},{4,5},{5,4},{6,7},{7,6},{8,9},{9,8},{10,11... | collective-permute-start | bytes 1179656 | tf_op jit(solution)/shard_map/ppermute | solution.py:77
  97.3 4.5 %collective-permute-start.18 = (bf16[512,384]{1,0:T(8,128)(2,1)}, bf16[512,384]{1,0:T(8,128)(2,1)S(1)}, u32[]{:S(2)}, u32[]{:S(2)}) collective-permute-start(bf16[512,384]{1,0:T(8,128)(2,1)} %collective-permute-done.16.refs_3_), channel_id=1, source_target_pairs={{0,1},{1,0},{2,3},{3,2},{4,5},{5,4},{6,7},{7,6},{8,9},{9,8},{10,11... | collective-permute-start | bytes 1179656 | tf_op jit(solution)/shard_map/ppermute | solution.py:77
  97.3 10.2 %collective-permute-start.22 = (bf16[512,384]{1,0:T(8,128)(2,1)S(1)}, bf16[512,384]{1,0:T(8,128)(2,1)S(1)}, u32[]{:S(2)}, u32[]{:S(2)}) collective-permute-start(bf16[512,384]{1,0:T(8,128)(2,1)S(1)} %pad_maximum_fusion.1.refs_0_), channel_id=1, source_target_pairs={{0,12},{1,13},{2,14},{3,15},{4,0},{5,1},{6,2},{7,3},{8,4},{9,5},{1... | collective-permute-start | bytes 1179656 | tf_op jit(solution)/shard_map/ppermute | solution.py:69
  99.0 17.8 %collective-permute-start.21 = (bf16[512,384]{1,0:T(8,128)(2,1)S(1)}, bf16[512,384]{1,0:T(8,128)(2,1)S(1)}, u32[]{:S(2)}, u32[]{:S(2)}) collective-permute-start(bf16[512,384]{1,0:T(8,128)(2,1)S(1)} %pad_maximum_fusion.1.refs_0_), channel_id=1, source_target_pairs={{0,8},{1,9},{2,10},{3,11},{4,12},{5,13},{6,14},{7,15},{8,0},{9,1},... | collective-permute-start | bytes 1179656 | tf_op jit(solution)/shard_map/ppermute | solution.py:69
  99.6 20.3 %collective-permute-start.20 = (bf16[512,384]{1,0:T(8,128)(2,1)S(1)}, bf16[512,384]{1,0:T(8,128)(2,1)S(1)}, u32[]{:S(2)}, u32[]{:S(2)}) collective-permute-start(bf16[512,384]{1,0:T(8,128)(2,1)S(1)} %pad_maximum_fusion.1.refs_0_), channel_id=1, source_target_pairs={{0,4},{1,5},{2,6},{3,7},{4,8},{5,9},{6,10},{7,11},{8,12},{9,13},{1... | collective-permute-start | bytes 1179656 | tf_op jit(solution)/shard_map/ppermute | solution.py:69
  100.4 20.0 %copy-start.13 = (bf16[512,384]{1,0:T(8,128)(2,1)}, bf16[512,384]{1,0:T(8,128)(2,1)S(1)}, u32[]{:S(2)}) copy-start(bf16[512,384]{1,0:T(8,128)(2,1)S(1)} %collective-permute-done.17.refs_6_) | copy-start | bytes 1179652
  100.4 20.0 %collective-permute-start.19 = (bf16[512,384]{1,0:T(8,128)(2,1)}, bf16[512,384]{1,0:T(8,128)(2,1)}, u32[]{:S(2)}, u32[]{:S(2)}) collective-permute-start(bf16[512,384]{1,0:T(8,128)(2,1)} %collective-permute-done.15.refs_4_), channel_id=1, source_target_pairs={{0,1},{1,0},{2,3},{3,2},{4,5},{5,4},{6,7},{7,6},{8,9},{9,8},{10,11... | collective-permute-start | bytes 1179656 | tf_op jit(solution)/shard_map/ppermute | solution.py:77
  101.8 18.7 %copy-start.14 = (bf16[512,384]{1,0:T(8,128)(2,1)}, bf16[512,384]{1,0:T(8,128)(2,1)S(1)}, u32[]{:S(2)}) copy-start(bf16[512,384]{1,0:T(8,128)(2,1)S(1)} %collective-permute-done.18.refs_7_) | copy-start | bytes 1179652
  101.8 23.1 %collective-permute-start.23 = (bf16[512,384]{1,0:T(8,128)(2,1)S(1)}, bf16[512,384]{1,0:T(8,128)(2,1)S(1)}, u32[]{:S(2)}, u32[]{:S(2)}) collective-permute-start(bf16[512,384]{1,0:T(8,128)(2,1)S(1)} %pad_maximum_fusion.1.refs_0_), channel_id=1, source_target_pairs={{0,1},{1,0},{2,3},{3,2},{4,5},{5,4},{6,7},{7,6},{8,9},{9,8},{10,11... | collective-permute-start | bytes 1179656 | tf_op jit(solution)/shard_map/ppermute | solution.py:77
  107.5 18.0 %collective-permute-start.26 = (bf16[512,384]{1,0:T(8,128)(2,1)S(1)}, bf16[512,384]{1,0:T(8,128)(2,1)S(1)}, u32[]{:S(2)}, u32[]{:S(2)}) collective-permute-start(bf16[512,384]{1,0:T(8,128)(2,1)S(1)} %collective-permute-done.22.refs_3_), channel_id=1, source_target_pairs={{0,1},{1,0},{2,3},{3,2},{4,5},{5,4},{6,7},{7,6},{8,9},{9,8},{10,11... | collective-permute-start | bytes 1179656 | tf_op jit(solution)/shard_map/ppermute | solution.py:77
  116.8 10.9 %collective-permute-start.25 = (bf16[512,384]{1,0:T(8,128)(2,1)S(1)}, bf16[512,384]{1,0:T(8,128)(2,1)}, u32[]{:S(2)}, u32[]{:S(2)}) collective-permute-start(bf16[512,384]{1,0:T(8,128)(2,1)S(1)} %collective-permute-done.21.refs_2_), channel_id=1, source_target_pairs={{0,1},{1,0},{2,3},{3,2},{4,5},{5,4},{6,7},{7,6},{8,9},{9,8},{10,11... | collective-permute-start | bytes 1179656 | tf_op jit(solution)/shard_map/ppermute | solution.py:77
  120.0 7.7 %collective-permute-start.24 = (bf16[512,384]{1,0:T(8,128)(2,1)S(1)}, bf16[512,384]{1,0:T(8,128)(2,1)}, u32[]{:S(2)}, u32[]{:S(2)}) collective-permute-start(bf16[512,384]{1,0:T(8,128)(2,1)S(1)} %collective-permute-done.20.refs_1_), channel_id=1, source_target_pairs={{0,1},{1,0},{2,3},{3,2},{4,5},{5,4},{6,7},{7,6},{8,9},{9,8},{10,11... | collective-permute-start | bytes 1179656 | tf_op jit(solution)/shard_map/ppermute | solution.py:77
  124.8 16.2 %collective-permute-start.27 = (bf16[384,384]{1,0:T(8,128)(2,1)S(1)}, bf16[384,384]{1,0:T(8,128)(2,1)S(1)}, u32[]{:S(2)}, u32[]{:S(2)}) collective-permute-start(bf16[384,384]{1,0:T(8,128)(2,1)S(1)} %get-tuple-element.84), channel_id=1, source_target_pairs={{0,16},{16,32},{32,48},{48,0},{64,80},{80,96},{96,112},{112,64},{1... | collective-permute-start | bytes 884744 | tf_op jit(solution)/shard_map/ppermute | solution.py:52
  124.9 16.1 %collective-permute-start.28 = (bf16[384,384]{1,0:T(8,128)(2,1)S(1)}, bf16[384,384]{1,0:T(8,128)(2,1)S(1)}, u32[]{:S(2)}, u32[]{:S(2)}) collective-permute-start(bf16[384,384]{1,0:T(8,128)(2,1)S(1)} %get-tuple-element.85), channel_id=1, source_target_pairs={{0,32},{16,48},{32,0},{48,16},{64,96},{80,112},{96,64},{112,80},{1... | collective-permute-start | bytes 884744 | tf_op jit(solution)/shard_map/ppermute | solution.py:52
  125.4 15.9 %collective-permute-start.29 = (bf16[384,384]{1,0:T(8,128)(2,1)S(1)}, bf16[384,384]{1,0:T(8,128)(2,1)S(1)}, u32[]{:S(2)}, u32[]{:S(2)}) collective-permute-start(bf16[384,384]{1,0:T(8,128)(2,1)S(1)} %get-tuple-element.86), channel_id=1, source_target_pairs={{0,48},{16,0},{32,16},{48,32},{64,112},{80,64},{96,80},{112,96},{1... | collective-permute-start | bytes 884744 | tf_op jit(solution)/shard_map/ppermute | solution.py:52

commit v6 on v5

--- a/solution.py
+++ b/solution.py
@@ -116,12 +116,18 @@
     sources, result_ref = refs[0:12], refs[12]
     q_buf, k_buf, v_buf, sel_ref, sems = refs[13:18]
     targets = [buf.at[n] for buf in (q_buf, k_buf, v_buf) for n in range(4)]
-    copies = [
-        pltpu.make_async_copy(src, dst, sems.at[n])
-        for n, (src, dst) in enumerate(zip(sources, targets))
-    ]
-    for copy in copies:
-        copy.start()
+    heads = k_buf.shape[2] // HEAD
+    copies = []
+    for h in range(heads):
+        cols = pl.ds(h * HEAD, HEAD)
+        copies.append(
+            [
+                pltpu.make_async_copy(src.at[:, cols], dst.at[:, cols], sems.at[12 * h + n])
+                for n, (src, dst) in enumerate(zip(sources, targets))
+            ]
+        )
+        for copy in copies[h]:
+            copy.start()
 
     z, x = ids_ref[0], ids_ref[1]
     for n in range(2 * NZ * NX):
@@ -133,59 +139,54 @@
         place = n // 8 * NX + ((x - shard) & 3)
         sel_ref[jnp.where(shard // NX == z, place, 2 * NZ * NX)] = block % SLOTS
 
-    for copy in copies[0:8]:
-        copy.wait()
-    q_refs, k_refs, v_refs = [[buf.at[n] for n in range(4)] for buf in (q_buf, k_buf, v_buf)]
-    heads = k_buf.shape[2] // HEAD
-    lane = lax.broadcasted_iota(jnp.int32, (BLOCK, BLOCK), 1)
+    sub = lax.broadcasted_iota(jnp.int32, (8, BLOCK), 0)
+    stats = [jnp.zeros((8, BLOCK), jnp.float32) for _ in range(2 * NZ)]
+    for h in range(heads):
+        cols = pl.ds(h * HEAD, HEAD)
+        for copy in copies[h]:
+            copy.wait()
+        for n in range(2 * NZ):
+            j, b = n // 2, n % 2
+            rows = pl.ds(b * BLOCK, BLOCK)
+            slots = [sel_ref[n * NX + i] for i in range(NX)]
+            places = [
+                pl.ds(pl.multiple_of(jnp.maximum(slot, 0) * BLOCK, BLOCK), BLOCK) for slot in slots
+            ]
+            keys = jnp.concatenate([k_buf[i, places[i], cols] for i in range(NX)])
+            values = jnp.concatenate([v_buf[i, places[i], cols] for i in range(NX)])
+            products = dot_nt(keys, q_buf[j, rows, cols])
+            scores = [
+                products[i * BLOCK : (i + 1) * BLOCK] * SCALE2 + jnp.where(slots[i] >= 0, 0.0, NEG)
+                for i in range(NX)
+            ]
+            peak = jnp.maximum(jnp.maximum(scores[0], scores[1]), jnp.maximum(scores[2], scores[3]))
+            top = jnp.max(peak, axis=0, keepdims=True)
+            weights = [jnp.exp2(s - top) for s in scores]
+            total = jnp.sum(
+                (weights[0] + weights[1]) + (weights[2] + weights[3]), axis=0, keepdims=True
+            )
+            inverse = 1.0 / total
+            weights = jnp.concatenate([(w * inverse).astype(jnp.bfloat16) for w in weights])
+            out = lax.dot_general(
+                weights, values, (((0,), (0,)), ((), ())), preferred_element_type=jnp.float32
+            )
+            result_ref[(z - j) & 3, rows, cols] = out.astype(jnp.bfloat16)
+            stats[n] = jnp.where(sub == h, top + jnp.log2(total), stats[n])
+    for n in range(2 * NZ):
+        stat = stats[n]
+        high = stat.astype(jnp.bfloat16).astype(jnp.float32)
+        mid = (stat - high).astype(jnp.bfloat16).astype(jnp.float32)
+        low = (stat - high) - mid
+        packed = jnp.concatenate(
+            [high[0:4], mid[0:4], low[0:4], jnp.zeros((4, BLOCK), jnp.float32)], axis=0
+        )
+        target = result_ref.at[(z - n // 2) & 3]
+        target[2 * BLOCK : 2 * BLOCK + EXTRA, pl.ds(n % 2 * BLOCK, BLOCK)] = packed.astype(
+            jnp.bfloat16
+        )
     for j in range(NZ):
-        q_ref, out_ref = q_refs[j], result_ref.at[(z - j) & 3]
-
-        for b in range(2):
-            row = b * BLOCK
-            stat = jnp.zeros((BLOCK, BLOCK), jnp.float32)
-            starts, biases = [], []
-            for i in range(NX):
-                slot = sel_ref[(2 * j + b) * NX + i]
-                starts.append(pl.multiple_of(jnp.maximum(slot, 0) * BLOCK, BLOCK))
-                biases.append(
-                    jnp.full((1, BLOCK), jnp.where(slot >= 0, 0.0, NEG), jnp.float32)
-                )
-            bias = jnp.concatenate(biases, axis=1)
-            for h in range(heads):
-                cols = pl.ds(h * HEAD, HEAD)
-                query = q_ref[pl.ds(row, BLOCK), cols]
-                keys = jnp.concatenate([k_refs[i][pl.ds(starts[i], BLOCK), cols] for i in range(NX)])
-                scores = dot_nt(query, keys) * SCALE2 + bias
-                top = jnp.max(scores, axis=1, keepdims=True)
-                weights = jnp.exp2(scores - top)
-                total = jnp.sum(weights, axis=1, keepdims=True)
-                if (j, b, h) == (0, 0, 0):
-                    for copy in copies[8:12]:
-                        copy.wait()
-                values = jnp.concatenate(
-                    [v_refs[i][pl.ds(starts[i], BLOCK), cols] for i in range(NX)]
-                )
-                acc = dot_nn(weights.astype(jnp.bfloat16), values)
-                out_ref[pl.ds(row, BLOCK), cols] = (acc / total).astype(jnp.bfloat16)
-                stat = jnp.where(lane == h, top + jnp.log2(total), stat)
-            stat = stat.T[0:8]
-            high = stat.astype(jnp.bfloat16)
-            rest = stat - high.astype(jnp.float32)
-            mid = rest.astype(jnp.bfloat16)
-            low = rest - mid.astype(jnp.float32)
-            packed = jnp.concatenate(
-                [
-                    high[0:4].astype(jnp.float32),
-                    mid[0:4].astype(jnp.float32),
-                    low[0:4],
-                    jnp.zeros((4, BLOCK), jnp.float32),
-                ],
-                axis=0,
-            )
-            out_ref[2 * BLOCK : 2 * BLOCK + EXTRA, pl.ds(row, BLOCK)] = packed.astype(jnp.bfloat16)
-        out_ref[2 * BLOCK : 2 * BLOCK + EXTRA, 2 * BLOCK :] = jnp.zeros(
-            (EXTRA, out_ref.shape[1] - 2 * BLOCK), jnp.bfloat16
+        result_ref[j, 2 * BLOCK : 2 * BLOCK + EXTRA, 2 * BLOCK :] = jnp.zeros(
+            (EXTRA, result_ref.shape[2] - 2 * BLOCK), jnp.bfloat16
         )
 
 
@@ -320,8 +321,9 @@
         cotangent,
         q_pack,
     )
-    k2, v2, v1, q2 = shift_x(k1, 1), shift_x(v3, -1), shift_x(own_values, 1), shift_z(q_pack, 2)
+    q2 = shift_z(q_pack, 2)
     swapped = move_zy(moved, lambda z, y: ((y - z) % NZ, y))
+    v1, k2, v2 = shift_x(own_values, 1), shift_x(k1, 1), shift_x(v3, -1)
     k3 = shift_x(after(own_keys, v2), -1)
     early = stored_in(q_pack, q1, q3)
     k2, v1, q2, k3, swapped, own_cot, early = together(k2, v1, q2, k3, swapped, own_cot, early)
@@ -348,7 +350,7 @@
             pltpu.VMEM((NX, SLOTS * BLOCK, width), jnp.bfloat16),
             pltpu.VMEM((NX, SLOTS * BLOCK, width), jnp.bfloat16),
             pltpu.SMEM((2 * NZ * NX + 1,), jnp.int32),
-            pltpu.SemaphoreType.DMA((12,)),
+            pltpu.SemaphoreType.DMA((12 * heads,)),
         ],
         compiler_params=params,
         cost_estimate=cost(
@@ -361,9 +363,8 @@
     wide = jnp.concatenate([cotangent, near_own], axis=0)
     parts, tall, wide = together(parts, tall, wide)
     back = exchange_z(parts)
-    t1, t2, t3 = [shift_y(tall, k) for k in (1, 2, 3)]
-    c0 = flip_tensor(tall, 1)
-    back, c0, t1, t3 = together(back, c0, t1, t3)
+    t1, t3, w1, w3 = [shift_y(v, k) for v in (tall, wide) for k in (1, 3)]
+    back, t1, t3, w1, w3 = together(back, t1, t3, w1, w3)
     attention, att_t = pl.pallas_call(
         merge_kernel,
         out_shape=[
@@ -376,11 +377,13 @@
         cost_estimate=cost(32 * rows * width, 4 * rows, 16 * rows * width),
         name="merge",
     )(gate, local_out, back)
-    att_t, t1, t2, t3, wide = together(att_t, t1, t2, t3, wide)
+    att_t, tall, wide, t1, t3, w1, w3 = together(att_t, tall, wide, t1, t3, w1, w3)
     att_all = exchange_z(att_t)
-    tall = in_hbm([tall, t1, t2, t3, c0] + [flip_tensor(v, 1) for v in (t1, t2, t3)])
-    w1, w2, w3 = [shift_y(wide, k) for k in (1, 2, 3)]
-    wide = [wide, w1, w2, w3] + [flip_tensor(v, 1) for v in (wide, w1, w2, w3)]
+    tall = [tall, t1, shift_y(tall, 2), t3]
+    wide = [wide, w1, shift_y(wide, 2), w3]
+    flipped = [flip_tensor(v, 1) for v in tall + [wide[0], wide[1], wide[3]]]
+    att_all, *flipped = together(att_all, *flipped)
+    tall = in_hbm(tall + flipped[:4])
 
     mine, *sent = pl.pallas_call(
         weight_kernel,
@@ -397,7 +400,8 @@
         cost_estimate=cost(32 * rows * width * width, 0, 48 * rows * width),
         name="weight_partials",
     )(ids, att_all, *tall)
-    got = [shift_x(sent[n - 1], n) for n in (1, 2, 3)]
+    got = [shift_x(sent[n - 1], n) for n in (1, 3, 2)]
+    wide = wide + flipped[4:6] + [flip_tensor(after(wide[2], mine), 1), flipped[6]]
     attention_grad = pl.pallas_call(
         grad_kernel,
         out_shape=jax.ShapeDtypeStruct((rows, width), jnp.bfloat16),
@@ -417,8 +421,9 @@
         compiler_params=params,
         cost_estimate=cost(32 * rows * width * width, 0, 64 * rows * width),
         name="attention_grad",
-    )(after(ids, mine), *wide, *in_hbm([out_weight]))
-
+    )(ids, *wide, *in_hbm([out_weight]))
+
+    attention_grad, *got = together(attention_grad, *got)
     weight_grad = (mine + got[0].astype(jnp.float32)) + (
         got[1].astype(jnp.float32) + got[2].astype(jnp.float32)
     )

time: 143 us -> 136 us (0.951)
  starting transfers between devices: 69 us -> 55.9 us
  waiting for transfers between devices: 43.6 us -> 52.7 us
  Pallas kernels: 24.2 us -> 21.1 us
    ppermute x10, starting transfers between devices: 24.7 us -> 10.2 us  [flip_tensor(): return lax.ppermute(value, 'tensor', [(t, t ^ bit) for t in range(16)])]
    ppermute x6, waiting for transfers between devices: 14 us -> 21.9 us  [shift_y(): return lax.ppermute(value, 'tensor', pairs)]
    ppermute x6, starting transfers between devices: 9.3 us -> 13 us  [shift_y(): return lax.ppermute(value, 'tensor', pairs)]
    pallas_call x1, Pallas kernels: 10 us -> 6.98 us  [per_device(): pl.pallas_call(memory_kernel, out_shape=jax.ShapeDtypeStruct((NZ, rows +...]
    all_to_all x2, starting transfers between devices: 12.9 us -> 11.2 us  [exchange_z(): lax.all_to_all(value, 'mem', split_axis=0, concat_axis=0, axis_index_grou...]
  transfers between devices with their start and end apart: 32 -> 32, of which waited for: 12 -> 10; matrix products, arithmetic and copies ran while one was open for 2% -> 3% of each run, Pallas kernels for 17% -> 14%
where the time goes in v6:
time: 136 us; the launch traced here: 135 us
  starting transfers between devices  55.9 us (41%)
  waiting for transfers between devices  52.7 us (39%)
  Pallas kernels  21.1 us (16%)
  other arithmetic  3.65 us (3%)
    ppermute x6, waiting for transfers between devices, shift_y(): return lax.ppermute(value, 'tensor', pairs)  21.9 us
    ppermute x9, waiting for transfers between devices, shift_x(): return lax.ppermute(value, 'mem', pairs)  21.6 us
    ppermute x6, starting transfers between devices, shift_y(): return lax.ppermute(value, 'tensor', pairs)  13 us
    all_to_all x2, starting transfers between devices, exchange_z(): lax.all_to_all(value, 'mem', split_axis=0, concat_axis=0, axis_index_grou...  11.2 us
    ppermute x9, starting transfers between devices, shift_x(): return lax.ppermute(value, 'mem', pairs)  10.2 us
    ppermute x10, starting transfers between devices, flip_tensor(): return lax.ppermute(value, 'tensor', [(t, t ^ bit) for t in range(16)])  10.2 us
    ppermute x3, waiting for transfers between devices, shift_z(): return lax.ppermute(value, 'mem', pairs)  9.08 us
    ppermute x3, starting transfers between devices, shift_z(): return lax.ppermute(value, 'mem', pairs)  9.07 us
  transfers between devices with their start and end apart: 32, of which 10 were waited for; matrix products, arithmetic and copies ran while one was open for 3% of the time, Pallas kernels for 14%

profile of v6, /device:TPU:1, one launch (start us, length us, event | category | flops | bytes accessed | tf_op | source)
XLA Modules:
  0.0 135.1 jit_solution(18193738900125661184)
XLA Ops:
  0.6 0.0 copy-start.5
  0.6 2.1 %collective-permute-start = (bf16[512,384]{1,0:T(8,128)(2,1)}, bf16[512,384]{1,0:T(8,128)(2,1)S(1)}, u32[]{:S(2)}, u32[]{:S(2)}) collective-permute-start(bf16[512,384]{1,0:T(8,128)(2,1)} %refs_4_.1), channel_id=1, source_target_pairs={{0,16},{16,32},{32,48},{48,0},{64,80},{80,96},{96,112},{112,64},{1... | collective-permute-start | bytes 1179656 | tf_op jit(solution)/shard_map/ppermute | solution.py:52
  2.8 1.4 %collective-permute-start.1 = (bf16[512,384]{1,0:T(8,128)(2,1)}, bf16[512,384]{1,0:T(8,128)(2,1)S(1)}, u32[]{:S(2)}, u32[]{:S(2)}) collective-permute-start(bf16[512,384]{1,0:T(8,128)(2,1)} %refs_8_.2), channel_id=1, source_target_pairs={{0,48},{16,0},{32,16},{48,32},{64,112},{80,64},{96,80},{112,96},{1... | collective-permute-start | bytes 1179656 | tf_op jit(solution)/shard_map/ppermute | solution.py:52
  4.1 0.8 eq.19
  4.9 0.8 select_reduce_fusion
  5.7 1.0 fusion.1.refs_0_
  6.7 0.0 copy-start.19
  6.7 0.0 copy-start
  6.7 0.0 copy-start.1
  6.7 0.0 copy-start.2
  6.7 0.0 copy-start.3
  6.7 3.2 %collective-permute-start.2 = (bf16[272,384]{1,0:T(8,128)(2,1)S(1)}, bf16[272,384]{1,0:T(8,128)(2,1)S(1)}, u32[]{:S(2)}, u32[]{:S(2)}) collective-permute-start(bf16[272,384]{1,0:T(8,128)(2,1)S(1)} %fusion.1.refs_0_), channel_id=1, source_target_pairs={{0,64},{16,80},{32,96},{48,112},{64,128},{80,144},{96,160},{112,17... | collective-permute-start | bytes 626696 | tf_op jit(solution)/shard_map/ppermute | solution.py:57
  9.9 3.1 %collective-permute-start.3 = (bf16[272,384]{1,0:T(8,128)(2,1)S(1)}, bf16[272,384]{1,0:T(8,128)(2,1)S(1)}, u32[]{:S(2)}, u32[]{:S(2)}) collective-permute-start(bf16[272,384]{1,0:T(8,128)(2,1)S(1)} %fusion.1.refs_0_), channel_id=1, source_target_pairs={{0,192},{16,208},{32,224},{48,240},{64,0},{80,16},{96,32},{112,48}... | collective-permute-start | bytes 626696 | tf_op jit(solution)/shard_map/ppermute | solution.py:57
  13.0 1.6 %collective-permute-start.4 = (bf16[256,384]{1,0:T(8,128)(2,1)}, bf16[256,384]{1,0:T(8,128)(2,1)S(1)}, u32[]{:S(2)}, u32[]{:S(2)}) collective-permute-start(bf16[256,384]{1,0:T(8,128)(2,1)} %param.23), channel_id=1, source_target_pairs={{0,0},{1,1},{2,2},{3,3},{16,16},{17,17},{18,18},{19,19},{32,32},{3... | collective-permute-start | bytes 589832 | tf_op jit(solution)/shard_map/ppermute | solution.py:94
  14.6 0.0 collective-permute-done.4
  14.6 3.2 %collective-permute-done.2.refs_1_ = bf16[272,384]{1,0:T(8,128)(2,1)S(1)} collective-permute-done((bf16[272,384]{1,0:T(8,128)(2,1)S(1)}, bf16[272,384]{1,0:T(8,128)(2,1)S(1)}, u32[]{:S(2)}, u32[]{:S(2)}) %collective-permute-start.2) | collective-permute-done | bytes 208928 | tf_op jit(solution)/shard_map/ppermute | solution.py:57
  17.8 5.9 %collective-permute-done.3.refs_3_ = bf16[272,384]{1,0:T(8,128)(2,1)S(1)} collective-permute-done((bf16[272,384]{1,0:T(8,128)(2,1)S(1)}, bf16[272,384]{1,0:T(8,128)(2,1)S(1)}, u32[]{:S(2)}, u32[]{:S(2)}) %collective-permute-start.3) | collective-permute-done | bytes 208928 | tf_op jit(solution)/shard_map/ppermute | solution.py:57
  23.7 0.0 collective-permute-done.refs_5_
  23.7 0.0 collective-permute-done.1.refs_11_
  23.7 1.3 collective-permute-start.8
  25.1 0.1 stack.23.ids_ref
  25.2 2.8 %collective-permute-start.7 = (bf16[272,384]{1,0:T(8,128)(2,1)S(1)}, bf16[272,384]{1,0:T(8,128)(2,1)S(1)}, u32[]{:S(2)}, u32[]{:S(2)}) collective-permute-start(bf16[272,384]{1,0:T(8,128)(2,1)S(1)} %fusion.1.refs_0_), channel_id=1, source_target_pairs={{0,128},{16,144},{32,160},{48,176},{64,192},{80,208},{96,224},{112... | collective-permute-start | bytes 626696 | tf_op jit(solution)/shard_map/ppermute | solution.py:57
  27.9 0.2 collective-permute-start.5
  28.1 0.0 collective-permute-start.6
  28.2 0.7 collective-permute-start.10
  28.8 4.6 %collective-permute-done.8.refs_10_ = bf16[512,384]{1,0:T(8,128)(2,1)S(1)} collective-permute-done((bf16[512,384]{1,0:T(8,128)(2,1)S(1)}, bf16[512,384]{1,0:T(8,128)(2,1)S(1)}, u32[]{:S(2)}, u32[]{:S(2)}) %collective-permute-start.8) | collective-permute-done | bytes 393248 | tf_op jit(solution)/shard_map/ppermute | solution.py:52
  33.4 2.5 %collective-permute-start.9 = (bf16[512,384]{1,0:T(8,128)(2,1)}, bf16[512,384]{1,0:T(8,128)(2,1)S(1)}, u32[]{:S(2)}, u32[]{:S(2)}) collective-permute-start(bf16[512,384]{1,0:T(8,128)(2,1)} %refs_4_.1), channel_id=1, source_target_pairs={{0,48},{16,0},{32,16},{48,32},{64,112},{80,64},{96,80},{112,96},{1... | collective-permute-start | bytes 1179656 | tf_op jit(solution)/shard_map/ppermute | solution.py:52
  35.9 0.1 maximum_convert_fusion.early_ref
  36.0 0.0 collective-permute-done.10
  36.0 0.0 collective-permute-done.7.refs_2_
  36.0 1.1 collective-permute-done.5.refs_6_
  37.1 8.4 %collective-permute-done.6.refs_9_ = bf16[512,384]{1,0:T(8,128)(2,1)S(1)} collective-permute-done((bf16[512,384]{1,0:T(8,128)(2,1)}, bf16[512,384]{1,0:T(8,128)(2,1)S(1)}, u32[]{:S(2)}, u32[]{:S(2)}) %collective-permute-start.6) | collective-permute-done | bytes 393248 | tf_op jit(solution)/shard_map/ppermute | solution.py:52
  45.6 0.0 collective-permute-done.9.refs_7_
  45.6 0.1 collective-permute-start.11
  45.7 1.4 %collective-permute-start.12 = (bf16[256,384]{1,0:T(8,128)(2,1)}, bf16[256,384]{1,0:T(8,128)(2,1)S(1)}, u32[]{:S(2)}, u32[]{:S(2)}) collective-permute-start(bf16[256,384]{1,0:T(8,128)(2,1)} %param.23), channel_id=1, source_target_pairs={{0,2},{1,3},{2,0},{3,1},{4,6},{5,7},{6,4},{7,5},{8,10},{9,11},{10,... | collective-permute-start | bytes 589832 | tf_op jit(solution)/shard_map/ppermute | solution.py:77
  47.2 7.0 %memory_attention.1 = bf16[4,272,384]{2,1,0:T(8,128)(2,1)} custom-call(s32[6]{0:T(128)S(1)} %stack.23.ids_ref, s32[48]{0:T(128)S(1)} %maximum_convert_fusion.early_ref, s32[16]{0:T(128)S(1)} %bitcast_convert_fusion.late_ref, bf16[272,384]{1,0:T(8,128)(2,1)} %copy-done.4, bf16[272,384]{1,0:T(8,128)(2,1)} %copy-done.6, bf16[272,384]{1,0:T(8,128)(2,1)} %copy-done.18, ...), custom_call_target="tpu_custom_call" | custom-call | flops 1610612736 | bytes 2359296 | tf_op jit(solution)/shard_map/memory_attention/pallas_call | solution.py:343
  54.2 0.0 collective-permute-done.11
  54.2 0.8 pad_maximum_fusion.refs_1_
  55.0 0.0 collective-permute-done.12
  55.0 5.1 %all-to-all-start = ((bf16[4,272,384]{2,1,0:T(8,128)(2,1)}), bf16[4,272,384]{2,1,0:T(8,128)(2,1)S(1)}, u32[]{:S(2)}, u32[]{:S(2)}) async-start(bf16[4,272,384]{2,1,0:T(8,128)(2,1)} %memory_attention.1), calls=%async_computation | async-start | bytes 1671168 | tf_op jit(solution)/shard_map/all_to_all | solution.py:62
  60.1 1.8 %collective-permute-start.13 = (bf16[512,384]{1,0:T(8,128)(2,1)}, bf16[512,384]{1,0:T(8,128)(2,1)S(1)}, u32[]{:S(2)}, u32[]{:S(2)}) collective-permute-start(bf16[512,384]{1,0:T(8,128)(2,1)} %pad_maximum_fusion.refs_1_), channel_id=1, source_target_pairs={{0,4},{1,5},{2,6},{3,7},{4,8},{5,9},{6,10},{7,11},{8,12},{9,13},{1... | collective-permute-start | bytes 1179656 | tf_op jit(solution)/shard_map/ppermute | solution.py:69
  62.0 3.9 %collective-permute-start.14 = (bf16[512,384]{1,0:T(8,128)(2,1)}, bf16[512,384]{1,0:T(8,128)(2,1)}, u32[]{:S(2)}, u32[]{:S(2)}) collective-permute-start(bf16[512,384]{1,0:T(8,128)(2,1)} %pad_maximum_fusion.refs_1_), channel_id=1, source_target_pairs={{0,12},{1,13},{2,14},{3,15},{4,0},{5,1},{6,2},{7,3},{8,4},{9,5},{1... | collective-permute-start | bytes 1179656 | tf_op jit(solution)/shard_map/ppermute | solution.py:69
  65.9 2.7 %collective-permute-start.16 = (bf16[512,384]{1,0:T(8,128)(2,1)S(1)}, bf16[512,384]{1,0:T(8,128)(2,1)S(1)}, u32[]{:S(2)}, u32[]{:S(2)}) collective-permute-start(bf16[512,384]{1,0:T(8,128)(2,1)S(1)} %pad_maximum_fusion.1.refs_0_), channel_id=1, source_target_pairs={{0,12},{1,13},{2,14},{3,15},{4,0},{5,1},{6,2},{7,3},{8,4},{9,5},{1... | collective-permute-start | bytes 1179656 | tf_op jit(solution)/shard_map/ppermute | solution.py:69
  68.6 1.4 %local_attention.1.local_ref = f32[256,384]{1,0:T(8,128)S(1)} custom-call(f32[3]{0:T(128)S(1)} %add_divide_fusion.gate_ref, s32[1,256]{1,0:T(1,128)S(1)} %bitcast.17, bf16[256,384]{1,0:T(8,128)(2,1)S(1)} %copy-done, bf16[256,384]{1,0:T(8,128)(2,1)S(1)} %copy-done.1, bf16[256,384]{1,0:T(8,128)(2,1)S(1)} %copy-done.2), custom_call_target="tpu_custom_call" | custom-call | flops 100663296 | bytes 589824 | tf_op jit(solution)/shard_map/local_attention/pallas_call | solution.py:333
  70.0 4.2 %collective-permute-done.13.refs_2_ = bf16[512,384]{1,0:T(8,128)(2,1)S(1)} collective-permute-done((bf16[512,384]{1,0:T(8,128)(2,1)}, bf16[512,384]{1,0:T(8,128)(2,1)S(1)}, u32[]{:S(2)}, u32[]{:S(2)}) %collective-permute-start.13) | collective-permute-done | bytes 393248 | tf_op jit(solution)/shard_map/ppermute | solution.py:69
  74.2 8.4 %collective-permute-done.15.refs_1_ = bf16[512,384]{1,0:T(8,128)(2,1)S(1)} collective-permute-done((bf16[512,384]{1,0:T(8,128)(2,1)S(1)}, bf16[512,384]{1,0:T(8,128)(2,1)S(1)}, u32[]{:S(2)}, u32[]{:S(2)}) %collective-permute-start.15) | collective-permute-done | bytes 393248 | tf_op jit(solution)/shard_map/ppermute | solution.py:69
  82.6 2.4 %merge.1 = (bf16[256,384]{1,0:T(8,128)(2,1)}, bf16[4,384,256]{2,1,0:T(8,128)(2,1)}) custom-call(f32[3]{0:T(128)S(1)} %add_divide_fusion.gate_ref, f32[256,384]{1,0:T(8,128)S(1)} %local_attention.1.local_ref, bf16[4,272,384]{2,1,0:T(8,128)(2,1)S(1)} %all-to-all-done.back_ref), custom_call_target="tpu_custom_call" | custom-call | flops 3145728 | bytes 1572864 | tf_op jit(solution)/shard_map/merge/pallas_call | solution.py:368
  85.0 6.1 %all-to-all-start.1 = ((bf16[4,384,256]{2,1,0:T(8,128)(2,1)}), bf16[4,384,256]{2,1,0:T(8,128)(2,1)S(1)}, u32[]{:S(2)}, u32[]{:S(2)}) async-start(bf16[4,384,256]{2,1,0:T(8,128)(2,1)} %get-tuple-element.96), calls=%async_computation.1 | async-start | bytes 1572864 | tf_op jit(solution)/shard_map/all_to_all | solution.py:62
  91.1 2.3 %collective-permute-start.20 = (bf16[512,384]{1,0:T(8,128)(2,1)}, bf16[512,384]{1,0:T(8,128)(2,1)S(1)}, u32[]{:S(2)}, u32[]{:S(2)}) collective-permute-start(bf16[512,384]{1,0:T(8,128)(2,1)} %pad_maximum_fusion.refs_1_), channel_id=1, source_target_pairs={{0,8},{1,9},{2,10},{3,11},{4,12},{5,13},{6,14},{7,15},{8,0},{9,1},... | collective-permute-start | bytes 1179656 | tf_op jit(solution)/shard_map/ppermute | solution.py:69
  93.4 3.2 %collective-permute-start.18 = (bf16[512,384]{1,0:T(8,128)(2,1)}, bf16[512,384]{1,0:T(8,128)(2,1)}, u32[]{:S(2)}, u32[]{:S(2)}) collective-permute-start(bf16[512,384]{1,0:T(8,128)(2,1)} %pad_maximum_fusion.refs_1_), channel_id=1, source_target_pairs={{0,1},{1,0},{2,3},{3,2},{4,5},{5,4},{6,7},{7,6},{8,9},{9,8},{10,11... | collective-permute-start | bytes 1179656 | tf_op jit(solution)/shard_map/ppermute | solution.py:77
  96.6 0.5 collective-permute-start.22
  97.1 3.7 %collective-permute-done.20.refs_3_ = bf16[512,384]{1,0:T(8,128)(2,1)S(1)} collective-permute-done((bf16[512,384]{1,0:T(8,128)(2,1)}, bf16[512,384]{1,0:T(8,128)(2,1)S(1)}, u32[]{:S(2)}, u32[]{:S(2)}) %collective-permute-start.20) | collective-permute-done | bytes 393248 | tf_op jit(solution)/shard_map/ppermute | solution.py:69
  100.8 3.5 %collective-permute-start.24 = (bf16[512,384]{1,0:T(8,128)(2,1)S(1)}, bf16[512,384]{1,0:T(8,128)(2,1)S(1)}, u32[]{:S(2)}, u32[]{:S(2)}) collective-permute-start(bf16[512,384]{1,0:T(8,128)(2,1)S(1)} %collective-permute-done.15.refs_1_), channel_id=1, source_target_pairs={{0,1},{1,0},{2,3},{3,2},{4,5},{5,4},{6,7},{7,6},{8,9},{9,8},{10,11... | collective-permute-start | bytes 1179656 | tf_op jit(solution)/shard_map/ppermute | solution.py:77
  104.3 0.1 collective-permute-start.25
  104.4 0.4 collective-permute-start.21
  104.9 2.3 %collective-permute-start.17 = (bf16[512,384]{1,0:T(8,128)(2,1)S(1)}, bf16[512,384]{1,0:T(8,128)(2,1)}, u32[]{:S(2)}, u32[]{:S(2)}) collective-permute-start(bf16[512,384]{1,0:T(8,128)(2,1)S(1)} %pad_maximum_fusion.1.refs_0_), channel_id=1, source_target_pairs={{0,8},{1,9},{2,10},{3,11},{4,12},{5,13},{6,14},{7,15},{8,0},{9,1},... | collective-permute-start | bytes 1179656 | tf_op jit(solution)/shard_map/ppermute | solution.py:69
  107.2 4.3 %weight_partials.1 = (f32[384,384]{1,0:T(8,128)S(1)}, bf16[384,384]{1,0:T(8,128)(2,1)S(1)}, bf16[384,384]{1,0:T(8,128)(2,1)S(1)}, bf16[384,384]{1,0:T(8,128)(2,1)S(1)}) custom-call(s32[6]{0:T(128)S(1)} %stack.23.ids_ref, bf16[4,384,256]{2,1,0:T(8,128)(2,1)S(1)} %all-to-all-done.1.refs_0_, bf16[512,384]{1,0:T(8,128)(2,1)} %pad_maximum_fusion.refs_1_, ...), custom_call_target="tpu_custom_call" | custom-call | flops 1207959552 | bytes 4718592 | tf_op jit(solution)/shard_map/weight_partials/pallas_call | solution.py:388
  111.6 5.6 %collective-permute-done.17.refs_2_ = bf16[512,384]{1,0:T(8,128)(2,1)} collective-permute-done((bf16[512,384]{1,0:T(8,128)(2,1)S(1)}, bf16[512,384]{1,0:T(8,128)(2,1)}, u32[]{:S(2)}, u32[]{:S(2)}) %collective-permute-start.17) | collective-permute-done | bytes 393248 | tf_op jit(solution)/shard_map/ppermute | solution.py:69
  117.2 0.9 collective-permute-start.26
  118.0 0.5 collective-permute-start.27
  118.5 2.2 %collective-permute-start.28 = (bf16[384,384]{1,0:T(8,128)(2,1)S(1)}, bf16[384,384]{1,0:T(8,128)(2,1)S(1)}, u32[]{:S(2)}, u32[]{:S(2)}) collective-permute-start(bf16[384,384]{1,0:T(8,128)(2,1)S(1)} %get-tuple-element.111), channel_id=1, source_target_pairs={{0,48},{16,0},{32,16},{48,32},{64,112},{80,64},{96,80},{112,96},{1... | collective-permute-start | bytes 884744 | tf_op jit(solution)/shard_map/ppermute | solution.py:52
  120.7 6.0 %attention_grad.1 = bf16[256,384]{1,0:T(8,128)(2,1)} custom-call(s32[6]{0:T(128)S(1)} %stack.23.ids_ref, bf16[512,384]{1,0:T(8,128)(2,1)S(1)} %pad_maximum_fusion.1.refs_0_, bf16[512,384]{1,0:T(8,128)(2,1)S(1)} %collective-permute-done.15.refs_1_, bf16[512,384]{1,0:T(8,128)(2,1)} %collective-permute-done.17.refs_2_, ...), custom_call_target="tpu_custom_call" | custom-call | flops 1207959552 | bytes 6291456 | tf_op jit(solution)/shard_map/attention_grad/pallas_call | solution.py:405
  126.7 7.5 %collective-permute-done.27 = bf16[384,384]{1,0:T(8,128)(2,1)S(1)} collective-permute-done((bf16[384,384]{1,0:T(8,128)(2,1)S(1)}, bf16[384,384]{1,0:T(8,128)(2,1)S(1)}, u32[]{:S(2)}, u32[]{:S(2)}) %collective-permute-start.27) | collective-permute-done | bytes 294944 | tf_op jit(solution)/shard_map/ppermute | solution.py:52
  134.2 0.9 add_add_fusion
  (58 shorter events, 0.2 us)
Async XLA Ops:
  0.6 54.4 %copy-start.5 = (bf16[256,384]{1,0:T(8,128)(2,1)S(1)}, bf16[256,384]{1,0:T(8,128)(2,1)}, u32[]{:S(2)}) copy-start(bf16[256,384]{1,0:T(8,128)(2,1)} %param.23) | copy-start | bytes 589828
  0.6 23.1 %collective-permute-start = (bf16[512,384]{1,0:T(8,128)(2,1)}, bf16[512,384]{1,0:T(8,128)(2,1)S(1)}, u32[]{:S(2)}, u32[]{:S(2)}) collective-permute-start(bf16[512,384]{1,0:T(8,128)(2,1)} %refs_4_.1), channel_id=1, source_target_pairs={{0,16},{16,32},{32,48},{48,0},{64,80},{80,96},{96,112},{112,64},{1... | collective-permute-start | bytes 1179656 | tf_op jit(solution)/shard_map/ppermute | solution.py:52
  2.8 21.0 %collective-permute-start.1 = (bf16[512,384]{1,0:T(8,128)(2,1)}, bf16[512,384]{1,0:T(8,128)(2,1)S(1)}, u32[]{:S(2)}, u32[]{:S(2)}) collective-permute-start(bf16[512,384]{1,0:T(8,128)(2,1)} %refs_8_.2), channel_id=1, source_target_pairs={{0,48},{16,0},{32,16},{48,32},{64,112},{80,64},{96,80},{112,96},{1... | collective-permute-start | bytes 1179656 | tf_op jit(solution)/shard_map/ppermute | solution.py:52
  6.7 40.5 %copy-start.4 = (bf16[272,384]{1,0:T(8,128)(2,1)}, bf16[272,384]{1,0:T(8,128)(2,1)S(1)}, u32[]{:S(2)}) copy-start(bf16[272,384]{1,0:T(8,128)(2,1)S(1)} %fusion.1.refs_0_) | copy-start | bytes 626692
  6.7 61.9 %copy-start.19 = (f32[3]{0:T(128)S(1)}, f32[3]{0:T(128)}, u32[]{:S(2)}) copy-start(f32[3]{0:T(128)} %param.21) | copy-start | bytes 40
  6.7 61.9 %copy-start = (bf16[256,384]{1,0:T(8,128)(2,1)S(1)}, bf16[256,384]{1,0:T(8,128)(2,1)}, u32[]{:S(2)}) copy-start(bf16[256,384]{1,0:T(8,128)(2,1)} %q_ref.1) | copy-start | bytes 589828
  6.7 61.9 %copy-start.1 = (bf16[256,384]{1,0:T(8,128)(2,1)S(1)}, bf16[256,384]{1,0:T(8,128)(2,1)}, u32[]{:S(2)}) copy-start(bf16[256,384]{1,0:T(8,128)(2,1)} %k_ref.1) | copy-start | bytes 589828
  6.7 61.9 %copy-start.2 = (bf16[256,384]{1,0:T(8,128)(2,1)S(1)}, bf16[256,384]{1,0:T(8,128)(2,1)}, u32[]{:S(2)}) copy-start(bf16[256,384]{1,0:T(8,128)(2,1)} %v_ref.1) | copy-start | bytes 589828
  6.7 61.9 %copy-start.3 = (s32[256]{0:T(256)S(1)}, s32[256]{0:T(256)}, u32[]{:S(2)}) copy-start(s32[256]{0:T(256)} %param.16) | copy-start | bytes 3076
  6.7 11.1 %collective-permute-start.2 = (bf16[272,384]{1,0:T(8,128)(2,1)S(1)}, bf16[272,384]{1,0:T(8,128)(2,1)S(1)}, u32[]{:S(2)}, u32[]{:S(2)}) collective-permute-start(bf16[272,384]{1,0:T(8,128)(2,1)S(1)} %fusion.1.refs_0_), channel_id=1, source_target_pairs={{0,64},{16,80},{32,96},{48,112},{64,128},{80,144},{96,160},{112,17... | collective-permute-start | bytes 626696 | tf_op jit(solution)/shard_map/ppermute | solution.py:57
  9.9 13.8 %collective-permute-start.3 = (bf16[272,384]{1,0:T(8,128)(2,1)S(1)}, bf16[272,384]{1,0:T(8,128)(2,1)S(1)}, u32[]{:S(2)}, u32[]{:S(2)}) collective-permute-start(bf16[272,384]{1,0:T(8,128)(2,1)S(1)} %fusion.1.refs_0_), channel_id=1, source_target_pairs={{0,192},{16,208},{32,224},{48,240},{64,0},{80,16},{96,32},{112,48}... | collective-permute-start | bytes 626696 | tf_op jit(solution)/shard_map/ppermute | solution.py:57
  13.0 1.6 %collective-permute-start.4 = (bf16[256,384]{1,0:T(8,128)(2,1)}, bf16[256,384]{1,0:T(8,128)(2,1)S(1)}, u32[]{:S(2)}, u32[]{:S(2)}) collective-permute-start(bf16[256,384]{1,0:T(8,128)(2,1)} %param.23), channel_id=1, source_target_pairs={{0,0},{1,1},{2,2},{3,3},{16,16},{17,17},{18,18},{19,19},{32,32},{3... | collective-permute-start | bytes 589832 | tf_op jit(solution)/shard_map/ppermute | solution.py:94
  17.8 29.3 %copy-start.6 = (bf16[272,384]{1,0:T(8,128)(2,1)}, bf16[272,384]{1,0:T(8,128)(2,1)S(1)}, u32[]{:S(2)}) copy-start(bf16[272,384]{1,0:T(8,128)(2,1)S(1)} %collective-permute-done.2.refs_1_) | copy-start | bytes 626692
  23.7 23.4 %copy-start.7 = (bf16[272,384]{1,0:T(8,128)(2,1)}, bf16[272,384]{1,0:T(8,128)(2,1)S(1)}, u32[]{:S(2)}) copy-start(bf16[272,384]{1,0:T(8,128)(2,1)S(1)} %collective-permute-done.3.refs_3_) | copy-start | bytes 626692
  23.7 23.4 %copy-start.8 = (bf16[512,384]{1,0:T(8,128)(2,1)}, bf16[512,384]{1,0:T(8,128)(2,1)S(1)}, u32[]{:S(2)}) copy-start(bf16[512,384]{1,0:T(8,128)(2,1)S(1)} %collective-permute-done.refs_5_) | copy-start | bytes 1179652
  23.7 23.4 %copy-start.9 = (bf16[512,384]{1,0:T(8,128)(2,1)}, bf16[512,384]{1,0:T(8,128)(2,1)S(1)}, u32[]{:S(2)}) copy-start(bf16[512,384]{1,0:T(8,128)(2,1)S(1)} %collective-permute-done.1.refs_11_) | copy-start | bytes 1179652
  23.7 9.7 %collective-permute-start.8 = (bf16[512,384]{1,0:T(8,128)(2,1)S(1)}, bf16[512,384]{1,0:T(8,128)(2,1)S(1)}, u32[]{:S(2)}, u32[]{:S(2)}) collective-permute-start(bf16[512,384]{1,0:T(8,128)(2,1)S(1)} %collective-permute-done.1.refs_11_), channel_id=1, source_target_pairs={{0,48},{16,0},{32,16},{48,32},{64,112},{80,64},{96,80},{112,96},{1... | collective-permute-start | bytes 1179656 | tf_op jit(solution)/shard_map/ppermute | solution.py:52
  25.2 10.8 %collective-permute-start.7 = (bf16[272,384]{1,0:T(8,128)(2,1)S(1)}, bf16[272,384]{1,0:T(8,128)(2,1)S(1)}, u32[]{:S(2)}, u32[]{:S(2)}) collective-permute-start(bf16[272,384]{1,0:T(8,128)(2,1)S(1)} %fusion.1.refs_0_), channel_id=1, source_target_pairs={{0,128},{16,144},{32,160},{48,176},{64,192},{80,208},{96,224},{112... | collective-permute-start | bytes 626696 | tf_op jit(solution)/shard_map/ppermute | solution.py:57
  27.9 9.2 %collective-permute-start.5 = (bf16[512,384]{1,0:T(8,128)(2,1)S(1)}, bf16[512,384]{1,0:T(8,128)(2,1)S(1)}, u32[]{:S(2)}, u32[]{:S(2)}) collective-permute-start(bf16[512,384]{1,0:T(8,128)(2,1)S(1)} %collective-permute-done.refs_5_), channel_id=1, source_target_pairs={{0,16},{16,32},{32,48},{48,0},{64,80},{80,96},{96,112},{112,64},{1... | collective-permute-start | bytes 1179656 | tf_op jit(solution)/shard_map/ppermute | solution.py:52
  28.1 17.4 %collective-permute-start.6 = (bf16[512,384]{1,0:T(8,128)(2,1)}, bf16[512,384]{1,0:T(8,128)(2,1)S(1)}, u32[]{:S(2)}, u32[]{:S(2)}) collective-permute-start(bf16[512,384]{1,0:T(8,128)(2,1)} %refs_8_.2), channel_id=1, source_target_pairs={{0,16},{16,32},{32,48},{48,0},{64,80},{80,96},{96,112},{112,64},{1... | collective-permute-start | bytes 1179656 | tf_op jit(solution)/shard_map/ppermute | solution.py:52
  28.2 7.8 %collective-permute-start.10 = (bf16[256,384]{1,0:T(8,128)(2,1)S(1)}, bf16[256,384]{1,0:T(8,128)(2,1)S(1)}, u32[]{:S(2)}, u32[]{:S(2)}) collective-permute-start(bf16[256,384]{1,0:T(8,128)(2,1)S(1)} %collective-permute-done.4), channel_id=1, source_target_pairs={{0,0},{1,1},{2,2},{3,3},{16,16},{17,17},{18,18},{19,19},{32,32},{3... | collective-permute-start | bytes 589832 | tf_op jit(solution)/shard_map/ppermute | solution.py:94
  33.4 12.2 %copy-start.10 = (bf16[512,384]{1,0:T(8,128)(2,1)}, bf16[512,384]{1,0:T(8,128)(2,1)S(1)}, u32[]{:S(2)}) copy-start(bf16[512,384]{1,0:T(8,128)(2,1)S(1)} %collective-permute-done.8.refs_10_) | copy-start | bytes 1179652
  33.4 12.2 %collective-permute-start.9 = (bf16[512,384]{1,0:T(8,128)(2,1)}, bf16[512,384]{1,0:T(8,128)(2,1)S(1)}, u32[]{:S(2)}, u32[]{:S(2)}) collective-permute-start(bf16[512,384]{1,0:T(8,128)(2,1)} %refs_4_.1), channel_id=1, source_target_pairs={{0,48},{16,0},{32,16},{48,32},{64,112},{80,64},{96,80},{112,96},{1... | collective-permute-start | bytes 1179656 | tf_op jit(solution)/shard_map/ppermute | solution.py:52
  36.0 11.2 %copy-start.18 = (bf16[272,384]{1,0:T(8,128)(2,1)}, bf16[272,384]{1,0:T(8,128)(2,1)S(1)}, u32[]{:S(2)}) copy-start(bf16[272,384]{1,0:T(8,128)(2,1)S(1)} %collective-permute-done.7.refs_2_) | copy-start | bytes 626692
  37.1 10.0 %copy-start.15 = (bf16[512,384]{1,0:T(8,128)(2,1)}, bf16[512,384]{1,0:T(8,128)(2,1)S(1)}, u32[]{:S(2)}) copy-start(bf16[512,384]{1,0:T(8,128)(2,1)S(1)} %collective-permute-done.5.refs_6_) | copy-start | bytes 1179652
  45.6 1.6 %copy-start.16 = (bf16[512,384]{1,0:T(8,128)(2,1)}, bf16[512,384]{1,0:T(8,128)(2,1)S(1)}, u32[]{:S(2)}) copy-start(bf16[512,384]{1,0:T(8,128)(2,1)S(1)} %collective-permute-done.6.refs_9_) | copy-start | bytes 1179652
  45.6 1.6 %copy-start.17 = (bf16[512,384]{1,0:T(8,128)(2,1)}, bf16[512,384]{1,0:T(8,128)(2,1)S(1)}, u32[]{:S(2)}) copy-start(bf16[512,384]{1,0:T(8,128)(2,1)S(1)} %collective-permute-done.9.refs_7_) | copy-start | bytes 1179652
  45.6 8.6 %collective-permute-start.11 = (bf16[256,384]{1,0:T(8,128)(2,1)S(1)}, bf16[256,384]{1,0:T(8,128)(2,1)S(1)}, u32[]{:S(2)}, u32[]{:S(2)}) collective-permute-start(bf16[256,384]{1,0:T(8,128)(2,1)S(1)} %collective-permute-done.10), channel_id=1, source_target_pairs={{0,2},{1,3},{2,0},{3,1},{4,6},{5,7},{6,4},{7,5},{8,10},{9,11},{10,... | collective-permute-start | bytes 589832 | tf_op jit(solution)/shard_map/ppermute | solution.py:77
  45.7 9.3 %collective-permute-start.12 = (bf16[256,384]{1,0:T(8,128)(2,1)}, bf16[256,384]{1,0:T(8,128)(2,1)S(1)}, u32[]{:S(2)}, u32[]{:S(2)}) collective-permute-start(bf16[256,384]{1,0:T(8,128)(2,1)} %param.23), channel_id=1, source_target_pairs={{0,2},{1,3},{2,0},{3,1},{4,6},{5,7},{6,4},{7,5},{8,10},{9,11},{10,... | collective-permute-start | bytes 589832 | tf_op jit(solution)/shard_map/ppermute | solution.py:77
  55.0 27.6 %all-to-all-start = ((bf16[4,272,384]{2,1,0:T(8,128)(2,1)}), bf16[4,272,384]{2,1,0:T(8,128)(2,1)S(1)}, u32[]{:S(2)}, u32[]{:S(2)}) async-start(bf16[4,272,384]{2,1,0:T(8,128)(2,1)} %memory_attention.1), calls=%async_computation | async-start | bytes 1671168 | tf_op jit(solution)/shard_map/all_to_all | solution.py:62
  60.1 14.0 %collective-permute-start.13 = (bf16[512,384]{1,0:T(8,128)(2,1)}, bf16[512,384]{1,0:T(8,128)(2,1)S(1)}, u32[]{:S(2)}, u32[]{:S(2)}) collective-permute-start(bf16[512,384]{1,0:T(8,128)(2,1)} %pad_maximum_fusion.refs_1_), channel_id=1, source_target_pairs={{0,4},{1,5},{2,6},{3,7},{4,8},{5,9},{6,10},{7,11},{8,12},{9,13},{1... | collective-permute-start | bytes 1179656 | tf_op jit(solution)/shard_map/ppermute | solution.py:69
  62.0 12.2 %collective-permute-start.14 = (bf16[512,384]{1,0:T(8,128)(2,1)}, bf16[512,384]{1,0:T(8,128)(2,1)}, u32[]{:S(2)}, u32[]{:S(2)}) collective-permute-start(bf16[512,384]{1,0:T(8,128)(2,1)} %pad_maximum_fusion.refs_1_), channel_id=1, source_target_pairs={{0,12},{1,13},{2,14},{3,15},{4,0},{5,1},{6,2},{7,3},{8,4},{9,5},{1... | collective-permute-start | bytes 1179656 | tf_op jit(solution)/shard_map/ppermute | solution.py:69
  65.9 16.7 %collective-permute-start.15 = (bf16[512,384]{1,0:T(8,128)(2,1)S(1)}, bf16[512,384]{1,0:T(8,128)(2,1)S(1)}, u32[]{:S(2)}, u32[]{:S(2)}) collective-permute-start(bf16[512,384]{1,0:T(8,128)(2,1)S(1)} %pad_maximum_fusion.1.refs_0_), channel_id=1, source_target_pairs={{0,4},{1,5},{2,6},{3,7},{4,8},{5,9},{6,10},{7,11},{8,12},{9,13},{1... | collective-permute-start | bytes 1179656 | tf_op jit(solution)/shard_map/ppermute | solution.py:69
  65.9 16.7 %collective-permute-start.16 = (bf16[512,384]{1,0:T(8,128)(2,1)S(1)}, bf16[512,384]{1,0:T(8,128)(2,1)S(1)}, u32[]{:S(2)}, u32[]{:S(2)}) collective-permute-start(bf16[512,384]{1,0:T(8,128)(2,1)S(1)} %pad_maximum_fusion.1.refs_0_), channel_id=1, source_target_pairs={{0,12},{1,13},{2,14},{3,15},{4,0},{5,1},{6,2},{7,3},{8,4},{9,5},{1... | collective-permute-start | bytes 1179656 | tf_op jit(solution)/shard_map/ppermute | solution.py:69
  74.2 8.4 %copy-start.11 = (bf16[512,384]{1,0:T(8,128)(2,1)}, bf16[512,384]{1,0:T(8,128)(2,1)S(1)}, u32[]{:S(2)}) copy-start(bf16[512,384]{1,0:T(8,128)(2,1)S(1)} %collective-permute-done.13.refs_2_) | copy-start | bytes 1179652
  85.0 22.2 %all-to-all-start.1 = ((bf16[4,384,256]{2,1,0:T(8,128)(2,1)}), bf16[4,384,256]{2,1,0:T(8,128)(2,1)S(1)}, u32[]{:S(2)}, u32[]{:S(2)}) async-start(bf16[4,384,256]{2,1,0:T(8,128)(2,1)} %get-tuple-element.96), calls=%async_computation.1 | async-start | bytes 1572864 | tf_op jit(solution)/shard_map/all_to_all | solution.py:62
  91.1 9.7 %collective-permute-start.20 = (bf16[512,384]{1,0:T(8,128)(2,1)}, bf16[512,384]{1,0:T(8,128)(2,1)S(1)}, u32[]{:S(2)}, u32[]{:S(2)}) collective-permute-start(bf16[512,384]{1,0:T(8,128)(2,1)} %pad_maximum_fusion.refs_1_), channel_id=1, source_target_pairs={{0,8},{1,9},{2,10},{3,11},{4,12},{5,13},{6,14},{7,15},{8,0},{9,1},... | collective-permute-start | bytes 1179656 | tf_op jit(solution)/shard_map/ppermute | solution.py:69
  93.4 11.0 %collective-permute-start.18 = (bf16[512,384]{1,0:T(8,128)(2,1)}, bf16[512,384]{1,0:T(8,128)(2,1)}, u32[]{:S(2)}, u32[]{:S(2)}) collective-permute-start(bf16[512,384]{1,0:T(8,128)(2,1)} %pad_maximum_fusion.refs_1_), channel_id=1, source_target_pairs={{0,1},{1,0},{2,3},{3,2},{4,5},{5,4},{6,7},{7,6},{8,9},{9,8},{10,11... | collective-permute-start | bytes 1179656 | tf_op jit(solution)/shard_map/ppermute | solution.py:77
  96.6 7.9 %collective-permute-start.19 = (bf16[512,384]{1,0:T(8,128)(2,1)}, bf16[512,384]{1,0:T(8,128)(2,1)S(1)}, u32[]{:S(2)}, u32[]{:S(2)}) collective-permute-start(bf16[512,384]{1,0:T(8,128)(2,1)} %copy-done.11), channel_id=1, source_target_pairs={{0,1},{1,0},{2,3},{3,2},{4,5},{5,4},{6,7},{7,6},{8,9},{9,8},{10,11... | collective-permute-start | bytes 1179656 | tf_op jit(solution)/shard_map/ppermute | solution.py:77
  96.6 8.3 %collective-permute-start.22 = (bf16[512,384]{1,0:T(8,128)(2,1)}, bf16[512,384]{1,0:T(8,128)(2,1)S(1)}, u32[]{:S(2)}, u32[]{:S(2)}) collective-permute-start(bf16[512,384]{1,0:T(8,128)(2,1)} %collective-permute-done.14.refs_4_), channel_id=1, source_target_pairs={{0,1},{1,0},{2,3},{3,2},{4,5},{5,4},{6,7},{7,6},{8,9},{9,8},{10,11... | collective-permute-start | bytes 1179656 | tf_op jit(solution)/shard_map/ppermute | solution.py:77
  97.1 10.1 %collective-permute-start.23 = (bf16[512,384]{1,0:T(8,128)(2,1)S(1)}, bf16[512,384]{1,0:T(8,128)(2,1)S(1)}, u32[]{:S(2)}, u32[]{:S(2)}) collective-permute-start(bf16[512,384]{1,0:T(8,128)(2,1)S(1)} %pad_maximum_fusion.1.refs_0_), channel_id=1, source_target_pairs={{0,1},{1,0},{2,3},{3,2},{4,5},{5,4},{6,7},{7,6},{8,9},{9,8},{10,11... | collective-permute-start | bytes 1179656 | tf_op jit(solution)/shard_map/ppermute | solution.py:77
  100.8 6.3 %copy-start.12 = (bf16[512,384]{1,0:T(8,128)(2,1)}, bf16[512,384]{1,0:T(8,128)(2,1)S(1)}, u32[]{:S(2)}) copy-start(bf16[512,384]{1,0:T(8,128)(2,1)S(1)} %collective-permute-done.20.refs_3_) | copy-start | bytes 1179652
  100.8 6.3 %collective-permute-start.24 = (bf16[512,384]{1,0:T(8,128)(2,1)S(1)}, bf16[512,384]{1,0:T(8,128)(2,1)S(1)}, u32[]{:S(2)}, u32[]{:S(2)}) collective-permute-start(bf16[512,384]{1,0:T(8,128)(2,1)S(1)} %collective-permute-done.15.refs_1_), channel_id=1, source_target_pairs={{0,1},{1,0},{2,3},{3,2},{4,5},{5,4},{6,7},{7,6},{8,9},{9,8},{10,11... | collective-permute-start | bytes 1179656 | tf_op jit(solution)/shard_map/ppermute | solution.py:77
  104.3 2.8 %collective-permute-start.25 = (bf16[512,384]{1,0:T(8,128)(2,1)S(1)}, bf16[512,384]{1,0:T(8,128)(2,1)S(1)}, u32[]{:S(2)}, u32[]{:S(2)}) collective-permute-start(bf16[512,384]{1,0:T(8,128)(2,1)S(1)} %collective-permute-done.16.refs_3_), channel_id=1, source_target_pairs={{0,1},{1,0},{2,3},{3,2},{4,5},{5,4},{6,7},{7,6},{8,9},{9,8},{10,11... | collective-permute-start | bytes 1179656 | tf_op jit(solution)/shard_map/ppermute | solution.py:77
  104.4 2.7 %copy-start.13 = (bf16[512,384]{1,0:T(8,128)(2,1)}, bf16[512,384]{1,0:T(8,128)(2,1)S(1)}, u32[]{:S(2)}) copy-start(bf16[512,384]{1,0:T(8,128)(2,1)S(1)} %collective-permute-done.19.refs_6_) | copy-start | bytes 1179652
  104.4 2.8 %collective-permute-start.21 = (bf16[512,384]{1,0:T(8,128)(2,1)S(1)}, bf16[512,384]{1,0:T(8,128)(2,1)}, u32[]{:S(2)}, u32[]{:S(2)}) collective-permute-start(bf16[512,384]{1,0:T(8,128)(2,1)S(1)} %collective-permute-done.20.refs_3_), channel_id=1, source_target_pairs={{0,1},{1,0},{2,3},{3,2},{4,5},{5,4},{6,7},{7,6},{8,9},{9,8},{10,11... | collective-permute-start | bytes 1179656 | tf_op jit(solution)/shard_map/ppermute | solution.py:77
  104.9 2.3 %copy-start.14 = (bf16[512,384]{1,0:T(8,128)(2,1)}, bf16[512,384]{1,0:T(8,128)(2,1)S(1)}, u32[]{:S(2)}) copy-start(bf16[512,384]{1,0:T(8,128)(2,1)S(1)} %collective-permute-done.22.refs_8_) | copy-start | bytes 1179652
  104.9 12.3 %collective-permute-start.17 = (bf16[512,384]{1,0:T(8,128)(2,1)S(1)}, bf16[512,384]{1,0:T(8,128)(2,1)}, u32[]{:S(2)}, u32[]{:S(2)}) collective-permute-start(bf16[512,384]{1,0:T(8,128)(2,1)S(1)} %pad_maximum_fusion.1.refs_0_), channel_id=1, source_target_pairs={{0,8},{1,9},{2,10},{3,11},{4,12},{5,13},{6,14},{7,15},{8,0},{9,1},... | collective-permute-start | bytes 1179656 | tf_op jit(solution)/shard_map/ppermute | solution.py:69
  117.2 3.6 %collective-permute-start.26 = (bf16[512,384]{1,0:T(8,128)(2,1)}, bf16[512,384]{1,0:T(8,128)(2,1)S(1)}, u32[]{:S(2)}, u32[]{:S(2)}) collective-permute-start(bf16[512,384]{1,0:T(8,128)(2,1)} %collective-permute-done.17.refs_2_), channel_id=1, source_target_pairs={{0,1},{1,0},{2,3},{3,2},{4,5},{5,4},{6,7},{7,6},{8,9},{9,8},{10,11... | collective-permute-start | bytes 1179656 | tf_op jit(solution)/shard_map/ppermute | solution.py:77
  118.0 16.2 %collective-permute-start.27 = (bf16[384,384]{1,0:T(8,128)(2,1)S(1)}, bf16[384,384]{1,0:T(8,128)(2,1)S(1)}, u32[]{:S(2)}, u32[]{:S(2)}) collective-permute-start(bf16[384,384]{1,0:T(8,128)(2,1)S(1)} %get-tuple-element.110), channel_id=1, source_target_pairs={{0,16},{16,32},{32,48},{48,0},{64,80},{80,96},{96,112},{112,64},{1... | collective-permute-start | bytes 884744 | tf_op jit(solution)/shard_map/ppermute | solution.py:52
  118.5 15.7 %collective-permute-start.28 = (bf16[384,384]{1,0:T(8,128)(2,1)S(1)}, bf16[384,384]{1,0:T(8,128)(2,1)S(1)}, u32[]{:S(2)}, u32[]{:S(2)}) collective-permute-start(bf16[384,384]{1,0:T(8,128)(2,1)S(1)} %get-tuple-element.111), channel_id=1, source_target_pairs={{0,48},{16,0},{32,16},{48,32},{64,112},{80,64},{96,80},{112,96},{1... | collective-permute-start | bytes 884744 | tf_op jit(solution)/shard_map/ppermute | solution.py:52
  120.7 13.5 %collective-permute-start.29 = (bf16[384,384]{1,0:T(8,128)(2,1)S(1)}, bf16[384,384]{1,0:T(8,128)(2,1)S(1)}, u32[]{:S(2)}, u32[]{:S(2)}) collective-permute-start(bf16[384,384]{1,0:T(8,128)(2,1)S(1)} %get-tuple-element.112), channel_id=1, source_target_pairs={{0,32},{16,48},{32,0},{48,16},{64,96},{80,112},{96,64},{112,80},{1... | collective-permute-start | bytes 884744 | tf_op jit(solution)/shard_map/ppermute | solution.py:52

commit v7 on v6

--- a/solution.py
+++ b/solution.py
@@ -326,7 +326,7 @@
     v1, k2, v2 = shift_x(own_values, 1), shift_x(k1, 1), shift_x(v3, -1)
     k3 = shift_x(after(own_keys, v2), -1)
     early = stored_in(q_pack, q1, q3)
-    k2, v1, q2, k3, swapped, own_cot, early = together(k2, v1, q2, k3, swapped, own_cot, early)
+    q2, k2, v1, k3, swapped, own_cot, early = together(q2, k2, v1, k3, swapped, own_cot, early)
     near, near_own = flip_tensor(swapped, 2), flip_tensor(own_cot, 2)
     q_all = [q_pack, q1, q2, q3]
 
@@ -364,7 +364,9 @@
     parts, tall, wide = together(parts, tall, wide)
     back = exchange_z(parts)
     t1, t3, w1, w3 = [shift_y(v, k) for v in (tall, wide) for k in (1, 3)]
-    back, t1, t3, w1, w3 = together(back, t1, t3, w1, w3)
+    back, t1, t3, w1, w3, tall, wide = together(back, t1, t3, w1, w3, tall, wide)
+    t2 = shift_y(tall, 2)
+    w2 = shift_y(after(wide, t2), 2)
     attention, att_t = pl.pallas_call(
         merge_kernel,
         out_shape=[
@@ -379,11 +381,10 @@
     )(gate, local_out, back)
     att_t, tall, wide, t1, t3, w1, w3 = together(att_t, tall, wide, t1, t3, w1, w3)
     att_all = exchange_z(att_t)
-    tall = [tall, t1, shift_y(tall, 2), t3]
-    wide = [wide, w1, shift_y(wide, 2), w3]
-    flipped = [flip_tensor(v, 1) for v in tall + [wide[0], wide[1], wide[3]]]
+    tall, wide = [tall, t1, t2, t3], [wide, w1, w2, w3]
+    flipped = [flip_tensor(v, 1) for v in tall + wide]
     att_all, *flipped = together(att_all, *flipped)
-    tall = in_hbm(tall + flipped[:4])
+    tall, wide = in_hbm(tall + flipped[:4]), wide + flipped[4:]
 
     mine, *sent = pl.pallas_call(
         weight_kernel,
@@ -401,7 +402,6 @@
         name="weight_partials",
     )(ids, att_all, *tall)
     got = [shift_x(sent[n - 1], n) for n in (1, 3, 2)]
-    wide = wide + flipped[4:6] + [flip_tensor(after(wide[2], mine), 1), flipped[6]]
     attention_grad = pl.pallas_call(
         grad_kernel,
         out_shape=jax.ShapeDtypeStruct((rows, width), jnp.bfloat16),

time: 136 us -> 135 us (level)
  the two profiles are of different devices: /device:TPU:1 before, /device:TPU:46 now
where the time goes in v7:
time: 135 us
  waiting for transfers between devices  55.8 us (41%)
  starting transfers between devices  51.9 us (38%)
  Pallas kernels  21.1 us (16%)
  other arithmetic  3.65 us (3%)
  local copies, waits for them, and re-layouts  1.68 us (1%)
    ppermute x6, waiting for transfers between devices, shift_y(): return lax.ppermute(value, 'tensor', pairs)  23.5 us
    ppermute x6, starting transfers between devices, shift_y(): return lax.ppermute(value, 'tensor', pairs)  13.5 us
    ppermute x9, starting transfers between devices, shift_x(): return lax.ppermute(value, 'mem', pairs)  11.2 us
    ppermute x3, starting transfers between devices, shift_z(): return lax.ppermute(value, 'mem', pairs)  10.8 us
    ppermute x2, waiting for transfers between devices, move_zy(): return lax.ppermute(value, ('mem', 'tensor'), pairs)  10.1 us
    all_to_all x2, starting transfers between devices, exchange_z(): lax.all_to_all(value, 'mem', split_axis=0, concat_axis=0, axis_index_grou...  9.14 us
    ppermute x9, waiting for transfers between devices, shift_x(): return lax.ppermute(value, 'mem', pairs)  7.79 us
    ppermute x3, waiting for transfers between devices, shift_z(): return lax.ppermute(value, 'mem', pairs)  7.42 us
  transfers between devices with their start and end apart: 32, of which 13 were waited for; matrix products, arithmetic and copies ran while one was open for 3% of the time, Pallas kernels for 12%

profile of v7, /device:TPU:46, one launch (start us, length us, event | category | flops | bytes accessed | tf_op | source)
XLA Modules:
  0.0 135.0 jit_solution(17673648706692869811)
XLA Ops:
  0.6 0.0 copy-start.7
  0.6 0.6 collective-permute-start
  1.2 1.5 %collective-permute-start.1 = (bf16[512,384]{1,0:T(8,128)(2,1)}, bf16[512,384]{1,0:T(8,128)(2,1)S(1)}, u32[]{:S(2)}, u32[]{:S(2)}) collective-permute-start(bf16[512,384]{1,0:T(8,128)(2,1)} %refs_8_.2), channel_id=1, source_target_pairs={{0,48},{16,0},{32,16},{48,32},{64,112},{80,64},{96,80},{112,96},{1... | collective-permute-start | bytes 1179656 | tf_op jit(solution)/shard_map/ppermute | solution.py:52
  2.7 0.8 eq.19
  3.5 0.8 select_reduce_fusion
  4.3 1.0 fusion.1.refs_0_
  5.3 0.0 copy-start.19
  5.3 0.0 copy-start
  5.3 0.0 copy-start.3
  5.3 0.0 copy-start.4
  5.4 0.0 copy-start.5
  5.4 3.3 %collective-permute-start.2 = (bf16[272,384]{1,0:T(8,128)(2,1)S(1)}, bf16[272,384]{1,0:T(8,128)(2,1)S(1)}, u32[]{:S(2)}, u32[]{:S(2)}) collective-permute-start(bf16[272,384]{1,0:T(8,128)(2,1)S(1)} %fusion.1.refs_0_), channel_id=1, source_target_pairs={{0,64},{16,80},{32,96},{48,112},{64,128},{80,144},{96,160},{112,17... | collective-permute-start | bytes 626696 | tf_op jit(solution)/shard_map/ppermute | solution.py:57
  8.7 2.2 %collective-permute-start.3 = (bf16[272,384]{1,0:T(8,128)(2,1)S(1)}, bf16[272,384]{1,0:T(8,128)(2,1)S(1)}, u32[]{:S(2)}, u32[]{:S(2)}) collective-permute-start(bf16[272,384]{1,0:T(8,128)(2,1)S(1)} %fusion.1.refs_0_), channel_id=1, source_target_pairs={{0,192},{16,208},{32,224},{48,240},{64,0},{80,16},{96,32},{112,48}... | collective-permute-start | bytes 626696 | tf_op jit(solution)/shard_map/ppermute | solution.py:57
  10.9 1.6 %collective-permute-start.4 = (bf16[256,384]{1,0:T(8,128)(2,1)}, bf16[256,384]{1,0:T(8,128)(2,1)S(1)}, u32[]{:S(2)}, u32[]{:S(2)}) collective-permute-start(bf16[256,384]{1,0:T(8,128)(2,1)} %param.23), channel_id=1, source_target_pairs={{0,0},{1,1},{2,2},{3,3},{16,16},{17,17},{18,18},{19,19},{32,32},{3... | collective-permute-start | bytes 589832 | tf_op jit(solution)/shard_map/ppermute | solution.py:94
  12.5 7.4 %collective-permute-done.2.refs_1_ = bf16[272,384]{1,0:T(8,128)(2,1)S(1)} collective-permute-done((bf16[272,384]{1,0:T(8,128)(2,1)S(1)}, bf16[272,384]{1,0:T(8,128)(2,1)S(1)}, u32[]{:S(2)}, u32[]{:S(2)}) %collective-permute-start.2) | collective-permute-done | bytes 208928 | tf_op jit(solution)/shard_map/ppermute | solution.py:57
  19.9 0.0 collective-permute-done.3.refs_3_
  19.9 0.0 collective-permute-done.refs_5_
  19.9 0.0 copy-start.10
  20.0 0.9 collective-permute-start.8
  20.9 0.1 stack.23.ids_ref
  21.0 5.2 %collective-permute-start.5 = (bf16[272,384]{1,0:T(8,128)(2,1)S(1)}, bf16[272,384]{1,0:T(8,128)(2,1)S(1)}, u32[]{:S(2)}, u32[]{:S(2)}) collective-permute-start(bf16[272,384]{1,0:T(8,128)(2,1)S(1)} %fusion.1.refs_0_), channel_id=1, source_target_pairs={{0,128},{16,144},{32,160},{48,176},{64,192},{80,208},{96,224},{112... | collective-permute-start | bytes 626696 | tf_op jit(solution)/shard_map/ppermute | solution.py:57
  26.2 2.4 %collective-permute-start.6 = (bf16[512,384]{1,0:T(8,128)(2,1)S(1)}, bf16[512,384]{1,0:T(8,128)(2,1)S(1)}, u32[]{:S(2)}, u32[]{:S(2)}) collective-permute-start(bf16[512,384]{1,0:T(8,128)(2,1)S(1)} %collective-permute-done.refs_5_), channel_id=1, source_target_pairs={{0,16},{16,32},{32,48},{48,0},{64,80},{80,96},{96,112},{112,64},{1... | collective-permute-start | bytes 1179656 | tf_op jit(solution)/shard_map/ppermute | solution.py:52
  28.6 0.5 collective-permute-start.7
  29.1 1.9 %collective-permute-start.10 = (bf16[256,384]{1,0:T(8,128)(2,1)S(1)}, bf16[256,384]{1,0:T(8,128)(2,1)S(1)}, u32[]{:S(2)}, u32[]{:S(2)}) collective-permute-start(bf16[256,384]{1,0:T(8,128)(2,1)S(1)} %collective-permute-done.4), channel_id=1, source_target_pairs={{0,0},{1,1},{2,2},{3,3},{16,16},{17,17},{18,18},{19,19},{32,32},{3... | collective-permute-start | bytes 589832 | tf_op jit(solution)/shard_map/ppermute | solution.py:94
  31.0 0.8 collective-permute-done.8.refs_10_
  31.8 0.9 collective-permute-start.9
  32.7 0.1 maximum_convert_fusion.early_ref
  32.8 10.1 %collective-permute-done.10 = bf16[256,384]{1,0:T(8,128)(2,1)S(1)} collective-permute-done((bf16[256,384]{1,0:T(8,128)(2,1)S(1)}, bf16[256,384]{1,0:T(8,128)(2,1)S(1)}, u32[]{:S(2)}, u32[]{:S(2)}) %collective-permute-start.10) | collective-permute-done | bytes 196640 | tf_op jit(solution)/shard_map/ppermute | solution.py:94
  43.0 2.0 %collective-permute-start.11 = (bf16[256,384]{1,0:T(8,128)(2,1)S(1)}, bf16[256,384]{1,0:T(8,128)(2,1)S(1)}, u32[]{:S(2)}, u32[]{:S(2)}) collective-permute-start(bf16[256,384]{1,0:T(8,128)(2,1)S(1)} %collective-permute-done.10), channel_id=1, source_target_pairs={{0,2},{1,3},{2,0},{3,1},{4,6},{5,7},{6,4},{7,5},{8,10},{9,11},{10,... | collective-permute-start | bytes 589832 | tf_op jit(solution)/shard_map/ppermute | solution.py:77
  45.0 0.3 collective-permute-start.12
  45.3 7.0 %memory_attention.1 = bf16[4,272,384]{2,1,0:T(8,128)(2,1)} custom-call(s32[6]{0:T(128)S(1)} %stack.23.ids_ref, s32[48]{0:T(128)S(1)} %maximum_convert_fusion.early_ref, s32[16]{0:T(128)S(1)} %bitcast_convert_fusion.late_ref, bf16[272,384]{1,0:T(8,128)(2,1)} %copy-done.6, bf16[272,384]{1,0:T(8,128)(2,1)} %copy-done.8, bf16[272,384]{1,0:T(8,128)(2,1)} %copy-done.18, ...), custom_call_target="tpu_custom_call" | custom-call | flops 1610612736 | bytes 2359296 | tf_op jit(solution)/shard_map/memory_attention/pallas_call | solution.py:343
  52.3 0.8 pad_maximum_fusion.refs_1_
  53.1 1.0 collective-permute-done.12
  54.1 5.1 %all-to-all-start = ((bf16[4,272,384]{2,1,0:T(8,128)(2,1)}), bf16[4,272,384]{2,1,0:T(8,128)(2,1)S(1)}, u32[]{:S(2)}, u32[]{:S(2)}) async-start(bf16[4,272,384]{2,1,0:T(8,128)(2,1)} %memory_attention.1), calls=%async_computation | async-start | bytes 1671168 | tf_op jit(solution)/shard_map/all_to_all | solution.py:62
  59.2 0.2 collective-permute-start.13
  59.4 1.8 %collective-permute-start.14 = (bf16[512,384]{1,0:T(8,128)(2,1)}, bf16[512,384]{1,0:T(8,128)(2,1)}, u32[]{:S(2)}, u32[]{:S(2)}) collective-permute-start(bf16[512,384]{1,0:T(8,128)(2,1)} %pad_maximum_fusion.refs_1_), channel_id=1, source_target_pairs={{0,12},{1,13},{2,14},{3,15},{4,0},{5,1},{6,2},{7,3},{8,4},{9,5},{1... | collective-permute-start | bytes 1179656 | tf_op jit(solution)/shard_map/ppermute | solution.py:69
  61.3 2.1 %collective-permute-start.15 = (bf16[512,384]{1,0:T(8,128)(2,1)S(1)}, bf16[512,384]{1,0:T(8,128)(2,1)S(1)}, u32[]{:S(2)}, u32[]{:S(2)}) collective-permute-start(bf16[512,384]{1,0:T(8,128)(2,1)S(1)} %pad_maximum_fusion.1.refs_0_), channel_id=1, source_target_pairs={{0,4},{1,5},{2,6},{3,7},{4,8},{5,9},{6,10},{7,11},{8,12},{9,13},{1... | collective-permute-start | bytes 1179656 | tf_op jit(solution)/shard_map/ppermute | solution.py:69
  63.4 0.7 collective-permute-start.16
  64.1 1.4 %local_attention.1.local_ref = f32[256,384]{1,0:T(8,128)S(1)} custom-call(f32[3]{0:T(128)S(1)} %add_divide_fusion.gate_ref, s32[1,256]{1,0:T(1,128)S(1)} %bitcast.17, bf16[256,384]{1,0:T(8,128)(2,1)S(1)} %copy-done, bf16[256,384]{1,0:T(8,128)(2,1)S(1)} %copy-done.3, bf16[256,384]{1,0:T(8,128)(2,1)S(1)} %copy-done.4), custom_call_target="tpu_custom_call" | custom-call | flops 100663296 | bytes 589824 | tf_op jit(solution)/shard_map/local_attention/pallas_call | solution.py:333
  65.5 6.0 %collective-permute-done.13.refs_2_ = bf16[512,384]{1,0:T(8,128)(2,1)S(1)} collective-permute-done((bf16[512,384]{1,0:T(8,128)(2,1)}, bf16[512,384]{1,0:T(8,128)(2,1)S(1)}, u32[]{:S(2)}, u32[]{:S(2)}) %collective-permute-start.13) | collective-permute-done | bytes 393248 | tf_op jit(solution)/shard_map/ppermute | solution.py:69
  71.5 2.2 %collective-permute-done.14.refs_4_ = bf16[512,384]{1,0:T(8,128)(2,1)} collective-permute-done((bf16[512,384]{1,0:T(8,128)(2,1)}, bf16[512,384]{1,0:T(8,128)(2,1)}, u32[]{:S(2)}, u32[]{:S(2)}) %collective-permute-start.14) | collective-permute-done | bytes 393248 | tf_op jit(solution)/shard_map/ppermute | solution.py:69
  73.8 4.4 %collective-permute-done.15.refs_1_ = bf16[512,384]{1,0:T(8,128)(2,1)S(1)} collective-permute-done((bf16[512,384]{1,0:T(8,128)(2,1)S(1)}, bf16[512,384]{1,0:T(8,128)(2,1)S(1)}, u32[]{:S(2)}, u32[]{:S(2)}) %collective-permute-start.15) | collective-permute-done | bytes 393248 | tf_op jit(solution)/shard_map/ppermute | solution.py:69
  78.1 2.1 %collective-permute-done.16.refs_3_ = bf16[512,384]{1,0:T(8,128)(2,1)S(1)} collective-permute-done((bf16[512,384]{1,0:T(8,128)(2,1)S(1)}, bf16[512,384]{1,0:T(8,128)(2,1)S(1)}, u32[]{:S(2)}, u32[]{:S(2)}) %collective-permute-start.16) | collective-permute-done | bytes 393248 | tf_op jit(solution)/shard_map/ppermute | solution.py:69
  80.2 5.4 %collective-permute-start.17 = (bf16[512,384]{1,0:T(8,128)(2,1)}, bf16[512,384]{1,0:T(8,128)(2,1)}, u32[]{:S(2)}, u32[]{:S(2)}) collective-permute-start(bf16[512,384]{1,0:T(8,128)(2,1)} %pad_maximum_fusion.refs_1_), channel_id=1, source_target_pairs={{0,8},{1,9},{2,10},{3,11},{4,12},{5,13},{6,14},{7,15},{8,0},{9,1},... | collective-permute-start | bytes 1179656 | tf_op jit(solution)/shard_map/ppermute | solution.py:69
  85.6 2.4 %merge.1 = (bf16[256,384]{1,0:T(8,128)(2,1)}, bf16[4,384,256]{2,1,0:T(8,128)(2,1)}) custom-call(f32[3]{0:T(128)S(1)} %add_divide_fusion.gate_ref, f32[256,384]{1,0:T(8,128)S(1)} %local_attention.1.local_ref, bf16[4,272,384]{2,1,0:T(8,128)(2,1)S(1)} %all-to-all-done.back_ref), custom_call_target="tpu_custom_call" | custom-call | flops 3145728 | bytes 1572864 | tf_op jit(solution)/shard_map/merge/pallas_call | solution.py:370
  88.0 4.0 %all-to-all-start.1 = ((bf16[4,384,256]{2,1,0:T(8,128)(2,1)}), bf16[4,384,256]{2,1,0:T(8,128)(2,1)S(1)}, u32[]{:S(2)}, u32[]{:S(2)}) async-start(bf16[4,384,256]{2,1,0:T(8,128)(2,1)} %get-tuple-element.102), calls=%async_computation.1 | async-start | bytes 1572864 | tf_op jit(solution)/shard_map/all_to_all | solution.py:62
  92.0 0.5 collective-permute-start.20
  92.5 1.7 %collective-permute-done.17.refs_3_ = bf16[512,384]{1,0:T(8,128)(2,1)} collective-permute-done((bf16[512,384]{1,0:T(8,128)(2,1)}, bf16[512,384]{1,0:T(8,128)(2,1)}, u32[]{:S(2)}, u32[]{:S(2)}) %collective-permute-start.17) | collective-permute-done | bytes 393248 | tf_op jit(solution)/shard_map/ppermute | solution.py:69
  94.3 3.2 %collective-permute-start.18 = (bf16[512,384]{1,0:T(8,128)(2,1)S(1)}, bf16[512,384]{1,0:T(8,128)(2,1)S(1)}, u32[]{:S(2)}, u32[]{:S(2)}) collective-permute-start(bf16[512,384]{1,0:T(8,128)(2,1)S(1)} %pad_maximum_fusion.1.refs_0_), channel_id=1, source_target_pairs={{0,8},{1,9},{2,10},{3,11},{4,12},{5,13},{6,14},{7,15},{8,0},{9,1},... | collective-permute-start | bytes 1179656 | tf_op jit(solution)/shard_map/ppermute | solution.py:69
  97.5 0.0 collective-permute-start.23
  97.5 0.5 collective-permute-start.24
  98.0 0.1 collective-permute-start.26
  98.1 0.4 collective-permute-start.21
  98.5 7.0 %collective-permute-done.18.refs_2_ = bf16[512,384]{1,0:T(8,128)(2,1)S(1)} collective-permute-done((bf16[512,384]{1,0:T(8,128)(2,1)S(1)}, bf16[512,384]{1,0:T(8,128)(2,1)S(1)}, u32[]{:S(2)}, u32[]{:S(2)}) %collective-permute-start.18) | collective-permute-done | bytes 393248 | tf_op jit(solution)/shard_map/ppermute | solution.py:69
  105.6 0.0 copy-start.1
  105.6 0.7 copy-done.1
  106.4 6.0 %all-to-all-done.1.refs_0_ = bf16[4,384,256]{2,1,0:T(8,128)(2,1)S(1)} async-done(((bf16[4,384,256]{2,1,0:T(8,128)(2,1)}), bf16[4,384,256]{2,1,0:T(8,128)(2,1)S(1)}, u32[]{:S(2)}, u32[]{:S(2)}) %all-to-all-start.1) | async-done | bytes 786464 | tf_op jit(solution)/shard_map/all_to_all | solution.py:62
  112.3 4.3 %weight_partials.1 = (f32[384,384]{1,0:T(8,128)S(1)}, bf16[384,384]{1,0:T(8,128)(2,1)S(1)}, bf16[384,384]{1,0:T(8,128)(2,1)S(1)}, bf16[384,384]{1,0:T(8,128)(2,1)S(1)}) custom-call(s32[6]{0:T(128)S(1)} %stack.23.ids_ref, bf16[4,384,256]{2,1,0:T(8,128)(2,1)S(1)} %all-to-all-done.1.refs_0_, bf16[512,384]{1,0:T(8,128)(2,1)} %pad_maximum_fusion.refs_1_, ...), custom_call_target="tpu_custom_call" | custom-call | flops 1207959552 | bytes 4718592 | tf_op jit(solution)/shard_map/weight_partials/pallas_call | solution.py:389
  116.7 2.2 %collective-permute-start.27 = (bf16[384,384]{1,0:T(8,128)(2,1)S(1)}, bf16[384,384]{1,0:T(8,128)(2,1)S(1)}, u32[]{:S(2)}, u32[]{:S(2)}) collective-permute-start(bf16[384,384]{1,0:T(8,128)(2,1)S(1)} %get-tuple-element.115), channel_id=1, source_target_pairs={{0,16},{16,32},{32,48},{48,0},{64,80},{80,96},{96,112},{112,64},{1... | collective-permute-start | bytes 884744 | tf_op jit(solution)/shard_map/ppermute | solution.py:52
  118.9 2.2 %collective-permute-start.29 = (bf16[384,384]{1,0:T(8,128)(2,1)S(1)}, bf16[384,384]{1,0:T(8,128)(2,1)S(1)}, u32[]{:S(2)}, u32[]{:S(2)}) collective-permute-start(bf16[384,384]{1,0:T(8,128)(2,1)S(1)} %get-tuple-element.117), channel_id=1, source_target_pairs={{0,32},{16,48},{32,0},{48,16},{64,96},{80,112},{96,64},{112,80},{1... | collective-permute-start | bytes 884744 | tf_op jit(solution)/shard_map/ppermute | solution.py:52
  121.1 6.0 %attention_grad.1 = bf16[256,384]{1,0:T(8,128)(2,1)} custom-call(s32[6]{0:T(128)S(1)} %stack.23.ids_ref, bf16[512,384]{1,0:T(8,128)(2,1)S(1)} %pad_maximum_fusion.1.refs_0_, bf16[512,384]{1,0:T(8,128)(2,1)S(1)} %collective-permute-done.15.refs_1_, bf16[512,384]{1,0:T(8,128)(2,1)S(1)} %collective-permute-done.18.refs_2_, ...), custom_call_target="tpu_custom_call" | custom-call | flops 1207959552 | bytes 6291456 | tf_op jit(solution)/shard_map/attention_grad/pallas_call | solution.py:405
  127.1 3.6 %collective-permute-done.27 = bf16[384,384]{1,0:T(8,128)(2,1)S(1)} collective-permute-done((bf16[384,384]{1,0:T(8,128)(2,1)S(1)}, bf16[384,384]{1,0:T(8,128)(2,1)S(1)}, u32[]{:S(2)}, u32[]{:S(2)}) %collective-permute-start.27) | collective-permute-done | bytes 294944 | tf_op jit(solution)/shard_map/ppermute | solution.py:52
  130.7 3.4 %collective-permute-done.28 = bf16[384,384]{1,0:T(8,128)(2,1)S(1)} collective-permute-done((bf16[384,384]{1,0:T(8,128)(2,1)S(1)}, bf16[384,384]{1,0:T(8,128)(2,1)S(1)}, u32[]{:S(2)}, u32[]{:S(2)}) %collective-permute-start.28) | collective-permute-done | bytes 294944 | tf_op jit(solution)/shard_map/ppermute | solution.py:52
  134.1 0.9 add_add_fusion
  (58 shorter events, 0.2 us)
Async XLA Ops:
  0.6 53.5 %copy-start.7 = (bf16[256,384]{1,0:T(8,128)(2,1)S(1)}, bf16[256,384]{1,0:T(8,128)(2,1)}, u32[]{:S(2)}) copy-start(bf16[256,384]{1,0:T(8,128)(2,1)} %param.23) | copy-start | bytes 589828
  0.6 19.3 %collective-permute-start = (bf16[512,384]{1,0:T(8,128)(2,1)}, bf16[512,384]{1,0:T(8,128)(2,1)S(1)}, u32[]{:S(2)}, u32[]{:S(2)}) collective-permute-start(bf16[512,384]{1,0:T(8,128)(2,1)} %refs_4_.1), channel_id=1, source_target_pairs={{0,16},{16,32},{32,48},{48,0},{64,80},{80,96},{96,112},{112,64},{1... | collective-permute-start | bytes 1179656 | tf_op jit(solution)/shard_map/ppermute | solution.py:52
  1.2 18.8 %collective-permute-start.1 = (bf16[512,384]{1,0:T(8,128)(2,1)}, bf16[512,384]{1,0:T(8,128)(2,1)S(1)}, u32[]{:S(2)}, u32[]{:S(2)}) collective-permute-start(bf16[512,384]{1,0:T(8,128)(2,1)} %refs_8_.2), channel_id=1, source_target_pairs={{0,48},{16,0},{32,16},{48,32},{64,112},{80,64},{96,80},{112,96},{1... | collective-permute-start | bytes 1179656 | tf_op jit(solution)/shard_map/ppermute | solution.py:52
  5.3 39.9 %copy-start.6 = (bf16[272,384]{1,0:T(8,128)(2,1)}, bf16[272,384]{1,0:T(8,128)(2,1)S(1)}, u32[]{:S(2)}) copy-start(bf16[272,384]{1,0:T(8,128)(2,1)S(1)} %fusion.1.refs_0_) | copy-start | bytes 626692
  5.3 58.8 %copy-start.19 = (f32[3]{0:T(128)S(1)}, f32[3]{0:T(128)}, u32[]{:S(2)}) copy-start(f32[3]{0:T(128)} %param.21) | copy-start | bytes 40
  5.3 58.8 %copy-start = (bf16[256,384]{1,0:T(8,128)(2,1)S(1)}, bf16[256,384]{1,0:T(8,128)(2,1)}, u32[]{:S(2)}) copy-start(bf16[256,384]{1,0:T(8,128)(2,1)} %q_ref.1) | copy-start | bytes 589828
  5.3 58.8 %copy-start.3 = (bf16[256,384]{1,0:T(8,128)(2,1)S(1)}, bf16[256,384]{1,0:T(8,128)(2,1)}, u32[]{:S(2)}) copy-start(bf16[256,384]{1,0:T(8,128)(2,1)} %k_ref.1) | copy-start | bytes 589828
  5.3 58.7 %copy-start.4 = (bf16[256,384]{1,0:T(8,128)(2,1)S(1)}, bf16[256,384]{1,0:T(8,128)(2,1)}, u32[]{:S(2)}) copy-start(bf16[256,384]{1,0:T(8,128)(2,1)} %v_ref.1) | copy-start | bytes 589828
  5.4 58.7 %copy-start.5 = (s32[256]{0:T(256)S(1)}, s32[256]{0:T(256)}, u32[]{:S(2)}) copy-start(s32[256]{0:T(256)} %param.16) | copy-start | bytes 3076
  5.4 14.6 %collective-permute-start.2 = (bf16[272,384]{1,0:T(8,128)(2,1)S(1)}, bf16[272,384]{1,0:T(8,128)(2,1)S(1)}, u32[]{:S(2)}, u32[]{:S(2)}) collective-permute-start(bf16[272,384]{1,0:T(8,128)(2,1)S(1)} %fusion.1.refs_0_), channel_id=1, source_target_pairs={{0,64},{16,80},{32,96},{48,112},{64,128},{80,144},{96,160},{112,17... | collective-permute-start | bytes 626696 | tf_op jit(solution)/shard_map/ppermute | solution.py:57
  8.7 11.2 %collective-permute-start.3 = (bf16[272,384]{1,0:T(8,128)(2,1)S(1)}, bf16[272,384]{1,0:T(8,128)(2,1)S(1)}, u32[]{:S(2)}, u32[]{:S(2)}) collective-permute-start(bf16[272,384]{1,0:T(8,128)(2,1)S(1)} %fusion.1.refs_0_), channel_id=1, source_target_pairs={{0,192},{16,208},{32,224},{48,240},{64,0},{80,16},{96,32},{112,48}... | collective-permute-start | bytes 626696 | tf_op jit(solution)/shard_map/ppermute | solution.py:57
  10.9 1.6 %collective-permute-start.4 = (bf16[256,384]{1,0:T(8,128)(2,1)}, bf16[256,384]{1,0:T(8,128)(2,1)S(1)}, u32[]{:S(2)}, u32[]{:S(2)}) collective-permute-start(bf16[256,384]{1,0:T(8,128)(2,1)} %param.23), channel_id=1, source_target_pairs={{0,0},{1,1},{2,2},{3,3},{16,16},{17,17},{18,18},{19,19},{32,32},{3... | collective-permute-start | bytes 589832 | tf_op jit(solution)/shard_map/ppermute | solution.py:94
  19.9 25.3 %copy-start.8 = (bf16[272,384]{1,0:T(8,128)(2,1)}, bf16[272,384]{1,0:T(8,128)(2,1)S(1)}, u32[]{:S(2)}) copy-start(bf16[272,384]{1,0:T(8,128)(2,1)S(1)} %collective-permute-done.2.refs_1_) | copy-start | bytes 626692
  19.9 25.3 %copy-start.9 = (bf16[272,384]{1,0:T(8,128)(2,1)}, bf16[272,384]{1,0:T(8,128)(2,1)S(1)}, u32[]{:S(2)}) copy-start(bf16[272,384]{1,0:T(8,128)(2,1)S(1)} %collective-permute-done.3.refs_3_) | copy-start | bytes 626692
  19.9 25.3 %copy-start.10 = (bf16[512,384]{1,0:T(8,128)(2,1)}, bf16[512,384]{1,0:T(8,128)(2,1)S(1)}, u32[]{:S(2)}) copy-start(bf16[512,384]{1,0:T(8,128)(2,1)S(1)} %collective-permute-done.refs_5_) | copy-start | bytes 1179652
  20.0 25.3 %copy-start.11 = (bf16[512,384]{1,0:T(8,128)(2,1)}, bf16[512,384]{1,0:T(8,128)(2,1)S(1)}, u32[]{:S(2)}) copy-start(bf16[512,384]{1,0:T(8,128)(2,1)S(1)} %collective-permute-done.1.refs_11_) | copy-start | bytes 1179652
  20.0 11.8 %collective-permute-start.8 = (bf16[512,384]{1,0:T(8,128)(2,1)S(1)}, bf16[512,384]{1,0:T(8,128)(2,1)S(1)}, u32[]{:S(2)}, u32[]{:S(2)}) collective-permute-start(bf16[512,384]{1,0:T(8,128)(2,1)S(1)} %collective-permute-done.1.refs_11_), channel_id=1, source_target_pairs={{0,48},{16,0},{32,16},{48,32},{64,112},{80,64},{96,80},{112,96},{1... | collective-permute-start | bytes 1179656 | tf_op jit(solution)/shard_map/ppermute | solution.py:52
  21.0 21.9 %collective-permute-start.5 = (bf16[272,384]{1,0:T(8,128)(2,1)S(1)}, bf16[272,384]{1,0:T(8,128)(2,1)S(1)}, u32[]{:S(2)}, u32[]{:S(2)}) collective-permute-start(bf16[272,384]{1,0:T(8,128)(2,1)S(1)} %fusion.1.refs_0_), channel_id=1, source_target_pairs={{0,128},{16,144},{32,160},{48,176},{64,192},{80,208},{96,224},{112... | collective-permute-start | bytes 626696 | tf_op jit(solution)/shard_map/ppermute | solution.py:57
  26.2 16.7 %collective-permute-start.6 = (bf16[512,384]{1,0:T(8,128)(2,1)S(1)}, bf16[512,384]{1,0:T(8,128)(2,1)S(1)}, u32[]{:S(2)}, u32[]{:S(2)}) collective-permute-start(bf16[512,384]{1,0:T(8,128)(2,1)S(1)} %collective-permute-done.refs_5_), channel_id=1, source_target_pairs={{0,16},{16,32},{32,48},{48,0},{64,80},{80,96},{96,112},{112,64},{1... | collective-permute-start | bytes 1179656 | tf_op jit(solution)/shard_map/ppermute | solution.py:52
  28.6 14.3 %collective-permute-start.7 = (bf16[512,384]{1,0:T(8,128)(2,1)}, bf16[512,384]{1,0:T(8,128)(2,1)S(1)}, u32[]{:S(2)}, u32[]{:S(2)}) collective-permute-start(bf16[512,384]{1,0:T(8,128)(2,1)} %refs_8_.2), channel_id=1, source_target_pairs={{0,16},{16,32},{32,48},{48,0},{64,80},{80,96},{96,112},{112,64},{1... | collective-permute-start | bytes 1179656 | tf_op jit(solution)/shard_map/ppermute | solution.py:52
  29.1 13.8 %collective-permute-start.10 = (bf16[256,384]{1,0:T(8,128)(2,1)S(1)}, bf16[256,384]{1,0:T(8,128)(2,1)S(1)}, u32[]{:S(2)}, u32[]{:S(2)}) collective-permute-start(bf16[256,384]{1,0:T(8,128)(2,1)S(1)} %collective-permute-done.4), channel_id=1, source_target_pairs={{0,0},{1,1},{2,2},{3,3},{16,16},{17,17},{18,18},{19,19},{32,32},{3... | collective-permute-start | bytes 589832 | tf_op jit(solution)/shard_map/ppermute | solution.py:94
  31.8 11.1 %copy-start.12 = (bf16[512,384]{1,0:T(8,128)(2,1)}, bf16[512,384]{1,0:T(8,128)(2,1)S(1)}, u32[]{:S(2)}) copy-start(bf16[512,384]{1,0:T(8,128)(2,1)S(1)} %collective-permute-done.8.refs_10_) | copy-start | bytes 1179652
  31.8 11.1 %collective-permute-start.9 = (bf16[512,384]{1,0:T(8,128)(2,1)}, bf16[512,384]{1,0:T(8,128)(2,1)S(1)}, u32[]{:S(2)}, u32[]{:S(2)}) collective-permute-start(bf16[512,384]{1,0:T(8,128)(2,1)} %refs_4_.1), channel_id=1, source_target_pairs={{0,48},{16,0},{32,16},{48,32},{64,112},{80,64},{96,80},{112,96},{1... | collective-permute-start | bytes 1179656 | tf_op jit(solution)/shard_map/ppermute | solution.py:52
  42.9 2.4 %copy-start.18 = (bf16[272,384]{1,0:T(8,128)(2,1)}, bf16[272,384]{1,0:T(8,128)(2,1)S(1)}, u32[]{:S(2)}) copy-start(bf16[272,384]{1,0:T(8,128)(2,1)S(1)} %collective-permute-done.5.refs_2_) | copy-start | bytes 626692
  42.9 2.4 %copy-start.15 = (bf16[512,384]{1,0:T(8,128)(2,1)}, bf16[512,384]{1,0:T(8,128)(2,1)S(1)}, u32[]{:S(2)}) copy-start(bf16[512,384]{1,0:T(8,128)(2,1)S(1)} %collective-permute-done.6.refs_6_) | copy-start | bytes 1179652
  42.9 2.4 %copy-start.16 = (bf16[512,384]{1,0:T(8,128)(2,1)}, bf16[512,384]{1,0:T(8,128)(2,1)S(1)}, u32[]{:S(2)}) copy-start(bf16[512,384]{1,0:T(8,128)(2,1)S(1)} %collective-permute-done.7.refs_9_) | copy-start | bytes 1179652
  42.9 2.3 %copy-start.17 = (bf16[512,384]{1,0:T(8,128)(2,1)}, bf16[512,384]{1,0:T(8,128)(2,1)S(1)}, u32[]{:S(2)}) copy-start(bf16[512,384]{1,0:T(8,128)(2,1)S(1)} %collective-permute-done.9.refs_7_) | copy-start | bytes 1179652
  43.0 9.4 %collective-permute-start.11 = (bf16[256,384]{1,0:T(8,128)(2,1)S(1)}, bf16[256,384]{1,0:T(8,128)(2,1)S(1)}, u32[]{:S(2)}, u32[]{:S(2)}) collective-permute-start(bf16[256,384]{1,0:T(8,128)(2,1)S(1)} %collective-permute-done.10), channel_id=1, source_target_pairs={{0,2},{1,3},{2,0},{3,1},{4,6},{5,7},{6,4},{7,5},{8,10},{9,11},{10,... | collective-permute-start | bytes 589832 | tf_op jit(solution)/shard_map/ppermute | solution.py:77
  45.0 9.1 %collective-permute-start.12 = (bf16[256,384]{1,0:T(8,128)(2,1)}, bf16[256,384]{1,0:T(8,128)(2,1)S(1)}, u32[]{:S(2)}, u32[]{:S(2)}) collective-permute-start(bf16[256,384]{1,0:T(8,128)(2,1)} %param.23), channel_id=1, source_target_pairs={{0,2},{1,3},{2,0},{3,1},{4,6},{5,7},{6,4},{7,5},{8,10},{9,11},{10,... | collective-permute-start | bytes 589832 | tf_op jit(solution)/shard_map/ppermute | solution.py:77
  54.1 26.1 %all-to-all-start = ((bf16[4,272,384]{2,1,0:T(8,128)(2,1)}), bf16[4,272,384]{2,1,0:T(8,128)(2,1)S(1)}, u32[]{:S(2)}, u32[]{:S(2)}) async-start(bf16[4,272,384]{2,1,0:T(8,128)(2,1)} %memory_attention.1), calls=%async_computation | async-start | bytes 1671168 | tf_op jit(solution)/shard_map/all_to_all | solution.py:62
  59.2 12.3 %collective-permute-start.13 = (bf16[512,384]{1,0:T(8,128)(2,1)}, bf16[512,384]{1,0:T(8,128)(2,1)S(1)}, u32[]{:S(2)}, u32[]{:S(2)}) collective-permute-start(bf16[512,384]{1,0:T(8,128)(2,1)} %pad_maximum_fusion.refs_1_), channel_id=1, source_target_pairs={{0,4},{1,5},{2,6},{3,7},{4,8},{5,9},{6,10},{7,11},{8,12},{9,13},{1... | collective-permute-start | bytes 1179656 | tf_op jit(solution)/shard_map/ppermute | solution.py:69
  59.4 14.3 %collective-permute-start.14 = (bf16[512,384]{1,0:T(8,128)(2,1)}, bf16[512,384]{1,0:T(8,128)(2,1)}, u32[]{:S(2)}, u32[]{:S(2)}) collective-permute-start(bf16[512,384]{1,0:T(8,128)(2,1)} %pad_maximum_fusion.refs_1_), channel_id=1, source_target_pairs={{0,12},{1,13},{2,14},{3,15},{4,0},{5,1},{6,2},{7,3},{8,4},{9,5},{1... | collective-permute-start | bytes 1179656 | tf_op jit(solution)/shard_map/ppermute | solution.py:69
  61.3 16.8 %collective-permute-start.15 = (bf16[512,384]{1,0:T(8,128)(2,1)S(1)}, bf16[512,384]{1,0:T(8,128)(2,1)S(1)}, u32[]{:S(2)}, u32[]{:S(2)}) collective-permute-start(bf16[512,384]{1,0:T(8,128)(2,1)S(1)} %pad_maximum_fusion.1.refs_0_), channel_id=1, source_target_pairs={{0,4},{1,5},{2,6},{3,7},{4,8},{5,9},{6,10},{7,11},{8,12},{9,13},{1... | collective-permute-start | bytes 1179656 | tf_op jit(solution)/shard_map/ppermute | solution.py:69
  63.4 16.8 %collective-permute-start.16 = (bf16[512,384]{1,0:T(8,128)(2,1)S(1)}, bf16[512,384]{1,0:T(8,128)(2,1)S(1)}, u32[]{:S(2)}, u32[]{:S(2)}) collective-permute-start(bf16[512,384]{1,0:T(8,128)(2,1)S(1)} %pad_maximum_fusion.1.refs_0_), channel_id=1, source_target_pairs={{0,12},{1,13},{2,14},{3,15},{4,0},{5,1},{6,2},{7,3},{8,4},{9,5},{1... | collective-permute-start | bytes 1179656 | tf_op jit(solution)/shard_map/ppermute | solution.py:69
  71.5 6.6 %copy-start.13 = (bf16[512,384]{1,0:T(8,128)(2,1)}, bf16[512,384]{1,0:T(8,128)(2,1)S(1)}, u32[]{:S(2)}) copy-start(bf16[512,384]{1,0:T(8,128)(2,1)S(1)} %collective-permute-done.13.refs_2_) | copy-start | bytes 1179652
  80.2 14.0 %collective-permute-start.17 = (bf16[512,384]{1,0:T(8,128)(2,1)}, bf16[512,384]{1,0:T(8,128)(2,1)}, u32[]{:S(2)}, u32[]{:S(2)}) collective-permute-start(bf16[512,384]{1,0:T(8,128)(2,1)} %pad_maximum_fusion.refs_1_), channel_id=1, source_target_pairs={{0,8},{1,9},{2,10},{3,11},{4,12},{5,13},{6,14},{7,15},{8,0},{9,1},... | collective-permute-start | bytes 1179656 | tf_op jit(solution)/shard_map/ppermute | solution.py:69
  88.0 24.4 %all-to-all-start.1 = ((bf16[4,384,256]{2,1,0:T(8,128)(2,1)}), bf16[4,384,256]{2,1,0:T(8,128)(2,1)S(1)}, u32[]{:S(2)}, u32[]{:S(2)}) async-start(bf16[4,384,256]{2,1,0:T(8,128)(2,1)} %get-tuple-element.102), calls=%async_computation.1 | async-start | bytes 1572864 | tf_op jit(solution)/shard_map/all_to_all | solution.py:62
  92.0 5.5 %collective-permute-start.19 = (bf16[512,384]{1,0:T(8,128)(2,1)}, bf16[512,384]{1,0:T(8,128)(2,1)}, u32[]{:S(2)}, u32[]{:S(2)}) collective-permute-start(bf16[512,384]{1,0:T(8,128)(2,1)} %pad_maximum_fusion.refs_1_), channel_id=1, source_target_pairs={{0,1},{1,0},{2,3},{3,2},{4,5},{5,4},{6,7},{7,6},{8,9},{9,8},{10,11... | collective-permute-start | bytes 1179656 | tf_op jit(solution)/shard_map/ppermute | solution.py:77
  92.0 6.0 %collective-permute-start.20 = (bf16[512,384]{1,0:T(8,128)(2,1)}, bf16[512,384]{1,0:T(8,128)(2,1)}, u32[]{:S(2)}, u32[]{:S(2)}) collective-permute-start(bf16[512,384]{1,0:T(8,128)(2,1)} %copy-done.13), channel_id=1, source_target_pairs={{0,1},{1,0},{2,3},{3,2},{4,5},{5,4},{6,7},{7,6},{8,9},{9,8},{10,11... | collective-permute-start | bytes 1179656 | tf_op jit(solution)/shard_map/ppermute | solution.py:77
  92.5 5.6 %collective-permute-start.22 = (bf16[512,384]{1,0:T(8,128)(2,1)}, bf16[512,384]{1,0:T(8,128)(2,1)S(1)}, u32[]{:S(2)}, u32[]{:S(2)}) collective-permute-start(bf16[512,384]{1,0:T(8,128)(2,1)} %collective-permute-done.14.refs_4_), channel_id=1, source_target_pairs={{0,1},{1,0},{2,3},{3,2},{4,5},{5,4},{6,7},{7,6},{8,9},{9,8},{10,11... | collective-permute-start | bytes 1179656 | tf_op jit(solution)/shard_map/ppermute | solution.py:77
  94.3 11.3 %collective-permute-start.18 = (bf16[512,384]{1,0:T(8,128)(2,1)S(1)}, bf16[512,384]{1,0:T(8,128)(2,1)S(1)}, u32[]{:S(2)}, u32[]{:S(2)}) collective-permute-start(bf16[512,384]{1,0:T(8,128)(2,1)S(1)} %pad_maximum_fusion.1.refs_0_), channel_id=1, source_target_pairs={{0,8},{1,9},{2,10},{3,11},{4,12},{5,13},{6,14},{7,15},{8,0},{9,1},... | collective-permute-start | bytes 1179656 | tf_op jit(solution)/shard_map/ppermute | solution.py:69
  97.5 8.1 %collective-permute-start.23 = (bf16[512,384]{1,0:T(8,128)(2,1)S(1)}, bf16[512,384]{1,0:T(8,128)(2,1)S(1)}, u32[]{:S(2)}, u32[]{:S(2)}) collective-permute-start(bf16[512,384]{1,0:T(8,128)(2,1)S(1)} %pad_maximum_fusion.1.refs_0_), channel_id=1, source_target_pairs={{0,1},{1,0},{2,3},{3,2},{4,5},{5,4},{6,7},{7,6},{8,9},{9,8},{10,11... | collective-permute-start | bytes 1179656 | tf_op jit(solution)/shard_map/ppermute | solution.py:77
  97.5 8.1 %collective-permute-start.24 = (bf16[512,384]{1,0:T(8,128)(2,1)S(1)}, bf16[512,384]{1,0:T(8,128)(2,1)S(1)}, u32[]{:S(2)}, u32[]{:S(2)}) collective-permute-start(bf16[512,384]{1,0:T(8,128)(2,1)S(1)} %collective-permute-done.15.refs_1_), channel_id=1, source_target_pairs={{0,1},{1,0},{2,3},{3,2},{4,5},{5,4},{6,7},{7,6},{8,9},{9,8},{10,11... | collective-permute-start | bytes 1179656 | tf_op jit(solution)/shard_map/ppermute | solution.py:77
  98.0 7.6 %collective-permute-start.26 = (bf16[512,384]{1,0:T(8,128)(2,1)S(1)}, bf16[512,384]{1,0:T(8,128)(2,1)S(1)}, u32[]{:S(2)}, u32[]{:S(2)}) collective-permute-start(bf16[512,384]{1,0:T(8,128)(2,1)S(1)} %collective-permute-done.16.refs_3_), channel_id=1, source_target_pairs={{0,1},{1,0},{2,3},{3,2},{4,5},{5,4},{6,7},{7,6},{8,9},{9,8},{10,11... | collective-permute-start | bytes 1179656 | tf_op jit(solution)/shard_map/ppermute | solution.py:77
  98.1 7.5 %copy-start.14 = (bf16[512,384]{1,0:T(8,128)(2,1)}, bf16[512,384]{1,0:T(8,128)(2,1)S(1)}, u32[]{:S(2)}) copy-start(bf16[512,384]{1,0:T(8,128)(2,1)S(1)} %collective-permute-done.22.refs_8_) | copy-start | bytes 1179652
  98.1 8.2 %collective-permute-start.21 = (bf16[512,384]{1,0:T(8,128)(2,1)}, bf16[512,384]{1,0:T(8,128)(2,1)}, u32[]{:S(2)}, u32[]{:S(2)}) collective-permute-start(bf16[512,384]{1,0:T(8,128)(2,1)} %collective-permute-done.17.refs_3_), channel_id=1, source_target_pairs={{0,1},{1,0},{2,3},{3,2},{4,5},{5,4},{6,7},{7,6},{8,9},{9,8},{10,11... | collective-permute-start | bytes 1179656 | tf_op jit(solution)/shard_map/ppermute | solution.py:77
  105.6 6.8 %collective-permute-start.25 = (bf16[512,384]{1,0:T(8,128)(2,1)S(1)}, bf16[512,384]{1,0:T(8,128)(2,1)}, u32[]{:S(2)}, u32[]{:S(2)}) collective-permute-start(bf16[512,384]{1,0:T(8,128)(2,1)S(1)} %collective-permute-done.18.refs_2_), channel_id=1, source_target_pairs={{0,1},{1,0},{2,3},{3,2},{4,5},{5,4},{6,7},{7,6},{8,9},{9,8},{10,11... | collective-permute-start | bytes 1179656 | tf_op jit(solution)/shard_map/ppermute | solution.py:77
  105.6 0.7 copy-start.1
  112.3 8.8 %copy-start.2 = (bf16[512,384]{1,0:T(8,128)(2,1)S(1)}, bf16[512,384]{1,0:T(8,128)(2,1)}, u32[]{:S(2)}) copy-start(bf16[512,384]{1,0:T(8,128)(2,1)} %copy-done.1) | copy-start | bytes 1179652
  116.7 14.0 %collective-permute-start.27 = (bf16[384,384]{1,0:T(8,128)(2,1)S(1)}, bf16[384,384]{1,0:T(8,128)(2,1)S(1)}, u32[]{:S(2)}, u32[]{:S(2)}) collective-permute-start(bf16[384,384]{1,0:T(8,128)(2,1)S(1)} %get-tuple-element.115), channel_id=1, source_target_pairs={{0,16},{16,32},{32,48},{48,0},{64,80},{80,96},{96,112},{112,64},{1... | collective-permute-start | bytes 884744 | tf_op jit(solution)/shard_map/ppermute | solution.py:52
  118.9 15.2 %collective-permute-start.28 = (bf16[384,384]{1,0:T(8,128)(2,1)S(1)}, bf16[384,384]{1,0:T(8,128)(2,1)S(1)}, u32[]{:S(2)}, u32[]{:S(2)}) collective-permute-start(bf16[384,384]{1,0:T(8,128)(2,1)S(1)} %get-tuple-element.116), channel_id=1, source_target_pairs={{0,48},{16,0},{32,16},{48,32},{64,112},{80,64},{96,80},{112,96},{1... | collective-permute-start | bytes 884744 | tf_op jit(solution)/shard_map/ppermute | solution.py:52
  118.9 15.2 %collective-permute-start.29 = (bf16[384,384]{1,0:T(8,128)(2,1)S(1)}, bf16[384,384]{1,0:T(8,128)(2,1)S(1)}, u32[]{:S(2)}, u32[]{:S(2)}) collective-permute-start(bf16[384,384]{1,0:T(8,128)(2,1)S(1)} %get-tuple-element.117), channel_id=1, source_target_pairs={{0,32},{16,48},{32,0},{48,16},{64,96},{80,112},{96,64},{112,80},{1... | collective-permute-start | bytes 884744 | tf_op jit(solution)/shard_map/ppermute | solution.py:52

commit v8 on v7

--- a/solution.py
+++ b/solution.py
@@ -359,9 +359,9 @@
         name="memory_attention",
     )(ids, early, stored_in(q2), *in_hbm([*q_all, memory_keys, k1, k2, k3, memory_values, v1, v2, v3]))
 
+    parts, near, near_own = together(parts, near, near_own)
     tall = jnp.concatenate([swapped, near], axis=0)
     wide = jnp.concatenate([cotangent, near_own], axis=0)
-    parts, tall, wide = together(parts, tall, wide)
     back = exchange_z(parts)
     t1, t3, w1, w3 = [shift_y(v, k) for v in (tall, wide) for k in (1, 3)]
     back, t1, t3, w1, w3, tall, wide = together(back, t1, t3, w1, w3, tall, wide)
@@ -401,7 +401,7 @@
         cost_estimate=cost(32 * rows * width * width, 0, 48 * rows * width),
         name="weight_partials",
     )(ids, att_all, *tall)
-    got = [shift_x(sent[n - 1], n) for n in (1, 3, 2)]
+    got = [shift_x(sent[n - 1], n) for n in (2, 1, 3)]
     attention_grad = pl.pallas_call(
         grad_kernel,
         out_shape=jax.ShapeDtypeStruct((rows, width), jnp.bfloat16),

time: 135 us -> 136 us (level)
  the two profiles are of different devices: /device:TPU:46 before, /device:TPU:1 now
where the time goes in v8:
time: 136 us; the launch traced here: 134 us
  waiting for transfers between devices  53.6 us (39%)
  starting transfers between devices  52.9 us (39%)
  Pallas kernels  21 us (15%)
  other arithmetic  2.87 us (2%)
  local copies, waits for them, and re-layouts  2.4 us (2%)
    ppermute x6, waiting for transfers between devices, shift_y(): return lax.ppermute(value, 'tensor', pairs)  22.2 us
    ppermute x9, waiting for transfers between devices, shift_x(): return lax.ppermute(value, 'mem', pairs)  21.7 us
    ppermute x6, starting transfers between devices, shift_y(): return lax.ppermute(value, 'tensor', pairs)  11.8 us
    all_to_all x2, starting transfers between devices, exchange_z(): lax.all_to_all(value, 'mem', split_axis=0, concat_axis=0, axis_index_grou...  11.3 us
    ppermute x9, starting transfers between devices, shift_x(): return lax.ppermute(value, 'mem', pairs)  10.9 us
    ppermute x3, waiting for transfers between devices, shift_z(): return lax.ppermute(value, 'mem', pairs)  9.08 us
    ppermute x3, starting transfers between devices, shift_z(): return lax.ppermute(value, 'mem', pairs)  9.07 us
    ppermute x10, starting transfers between devices, flip_tensor(): return lax.ppermute(value, 'tensor', [(t, t ^ bit) for t in range(16)])  7.57 us
  transfers between devices with their start and end apart: 32, of which 10 were waited for; matrix products, arithmetic and copies ran while one was open for 2% of the time, Pallas kernels for 12%

profile of v8, /device:TPU:1, one launch (start us, length us, event | category | flops | bytes accessed | tf_op | source)
XLA Modules:
  0.0 133.7 jit_solution(8323673509174982361)
XLA Ops:
  0.6 0.0 copy-start.7
  0.6 2.1 %collective-permute-start = (bf16[512,384]{1,0:T(8,128)(2,1)}, bf16[512,384]{1,0:T(8,128)(2,1)S(1)}, u32[]{:S(2)}, u32[]{:S(2)}) collective-permute-start(bf16[512,384]{1,0:T(8,128)(2,1)} %refs_4_.1), channel_id=1, source_target_pairs={{0,16},{16,32},{32,48},{48,0},{64,80},{80,96},{96,112},{112,64},{1... | collective-permute-start | bytes 1179656 | tf_op jit(solution)/shard_map/ppermute | solution.py:52
  2.8 1.4 %collective-permute-start.1 = (bf16[512,384]{1,0:T(8,128)(2,1)}, bf16[512,384]{1,0:T(8,128)(2,1)S(1)}, u32[]{:S(2)}, u32[]{:S(2)}) collective-permute-start(bf16[512,384]{1,0:T(8,128)(2,1)} %refs_8_.2), channel_id=1, source_target_pairs={{0,48},{16,0},{32,16},{48,32},{64,112},{80,64},{96,80},{112,96},{1... | collective-permute-start | bytes 1179656 | tf_op jit(solution)/shard_map/ppermute | solution.py:52
  4.1 0.8 eq.19
  4.9 0.8 select_reduce_fusion
  5.7 1.0 fusion.1.refs_0_
  6.7 0.0 copy-start.21
  6.7 0.0 copy-start
  6.7 0.0 copy-start.3
  6.7 0.0 copy-start.4
  6.7 0.0 copy-start.5
  6.7 3.2 %collective-permute-start.2 = (bf16[272,384]{1,0:T(8,128)(2,1)S(1)}, bf16[272,384]{1,0:T(8,128)(2,1)S(1)}, u32[]{:S(2)}, u32[]{:S(2)}) collective-permute-start(bf16[272,384]{1,0:T(8,128)(2,1)S(1)} %fusion.1.refs_0_), channel_id=1, source_target_pairs={{0,64},{16,80},{32,96},{48,112},{64,128},{80,144},{96,160},{112,17... | collective-permute-start | bytes 626696 | tf_op jit(solution)/shard_map/ppermute | solution.py:57
  9.9 3.1 %collective-permute-start.3 = (bf16[272,384]{1,0:T(8,128)(2,1)S(1)}, bf16[272,384]{1,0:T(8,128)(2,1)S(1)}, u32[]{:S(2)}, u32[]{:S(2)}) collective-permute-start(bf16[272,384]{1,0:T(8,128)(2,1)S(1)} %fusion.1.refs_0_), channel_id=1, source_target_pairs={{0,192},{16,208},{32,224},{48,240},{64,0},{80,16},{96,32},{112,48}... | collective-permute-start | bytes 626696 | tf_op jit(solution)/shard_map/ppermute | solution.py:57
  13.0 1.6 %collective-permute-start.4 = (bf16[256,384]{1,0:T(8,128)(2,1)}, bf16[256,384]{1,0:T(8,128)(2,1)S(1)}, u32[]{:S(2)}, u32[]{:S(2)}) collective-permute-start(bf16[256,384]{1,0:T(8,128)(2,1)} %param.23), channel_id=1, source_target_pairs={{0,0},{1,1},{2,2},{3,3},{16,16},{17,17},{18,18},{19,19},{32,32},{3... | collective-permute-start | bytes 589832 | tf_op jit(solution)/shard_map/ppermute | solution.py:94
  14.6 0.0 collective-permute-done.4
  14.6 3.2 %collective-permute-done.2.refs_1_ = bf16[272,384]{1,0:T(8,128)(2,1)S(1)} collective-permute-done((bf16[272,384]{1,0:T(8,128)(2,1)S(1)}, bf16[272,384]{1,0:T(8,128)(2,1)S(1)}, u32[]{:S(2)}, u32[]{:S(2)}) %collective-permute-start.2) | collective-permute-done | bytes 208928 | tf_op jit(solution)/shard_map/ppermute | solution.py:57
  17.8 5.9 %collective-permute-done.3.refs_3_ = bf16[272,384]{1,0:T(8,128)(2,1)S(1)} collective-permute-done((bf16[272,384]{1,0:T(8,128)(2,1)S(1)}, bf16[272,384]{1,0:T(8,128)(2,1)S(1)}, u32[]{:S(2)}, u32[]{:S(2)}) %collective-permute-start.3) | collective-permute-done | bytes 208928 | tf_op jit(solution)/shard_map/ppermute | solution.py:57
  23.7 0.0 collective-permute-done.1.refs_11_
  23.7 1.3 %collective-permute-start.8 = (bf16[512,384]{1,0:T(8,128)(2,1)S(1)}, bf16[512,384]{1,0:T(8,128)(2,1)S(1)}, u32[]{:S(2)}, u32[]{:S(2)}) collective-permute-start(bf16[512,384]{1,0:T(8,128)(2,1)S(1)} %collective-permute-done.1.refs_11_), channel_id=1, source_target_pairs={{0,48},{16,0},{32,16},{48,32},{64,112},{80,64},{96,80},{112,96},{1... | collective-permute-start | bytes 1179656 | tf_op jit(solution)/shard_map/ppermute | solution.py:52
  25.1 0.1 stack.23.ids_ref
  25.2 2.8 %collective-permute-start.5 = (bf16[272,384]{1,0:T(8,128)(2,1)S(1)}, bf16[272,384]{1,0:T(8,128)(2,1)S(1)}, u32[]{:S(2)}, u32[]{:S(2)}) collective-permute-start(bf16[272,384]{1,0:T(8,128)(2,1)S(1)} %fusion.1.refs_0_), channel_id=1, source_target_pairs={{0,128},{16,144},{32,160},{48,176},{64,192},{80,208},{96,224},{112... | collective-permute-start | bytes 626696 | tf_op jit(solution)/shard_map/ppermute | solution.py:57
  27.9 0.2 collective-permute-start.6
  28.1 0.0 collective-permute-start.7
  28.2 0.7 collective-permute-start.10
  28.8 4.6 %collective-permute-done.8.refs_10_ = bf16[512,384]{1,0:T(8,128)(2,1)S(1)} collective-permute-done((bf16[512,384]{1,0:T(8,128)(2,1)S(1)}, bf16[512,384]{1,0:T(8,128)(2,1)S(1)}, u32[]{:S(2)}, u32[]{:S(2)}) %collective-permute-start.8) | collective-permute-done | bytes 393248 | tf_op jit(solution)/shard_map/ppermute | solution.py:52
  33.4 2.5 %collective-permute-start.9 = (bf16[512,384]{1,0:T(8,128)(2,1)}, bf16[512,384]{1,0:T(8,128)(2,1)S(1)}, u32[]{:S(2)}, u32[]{:S(2)}) collective-permute-start(bf16[512,384]{1,0:T(8,128)(2,1)} %refs_4_.1), channel_id=1, source_target_pairs={{0,48},{16,0},{32,16},{48,32},{64,112},{80,64},{96,80},{112,96},{1... | collective-permute-start | bytes 1179656 | tf_op jit(solution)/shard_map/ppermute | solution.py:52
  35.9 0.1 maximum_convert_fusion.early_ref
  36.0 1.1 collective-permute-done.6.refs_6_
  37.1 8.4 %collective-permute-done.7.refs_9_ = bf16[512,384]{1,0:T(8,128)(2,1)S(1)} collective-permute-done((bf16[512,384]{1,0:T(8,128)(2,1)}, bf16[512,384]{1,0:T(8,128)(2,1)S(1)}, u32[]{:S(2)}, u32[]{:S(2)}) %collective-permute-start.7) | collective-permute-done | bytes 393248 | tf_op jit(solution)/shard_map/ppermute | solution.py:52
  45.6 0.0 collective-permute-done.9.refs_7_
  45.6 0.1 collective-permute-start.11
  45.7 1.5 %collective-permute-start.12 = (bf16[256,384]{1,0:T(8,128)(2,1)}, bf16[256,384]{1,0:T(8,128)(2,1)S(1)}, u32[]{:S(2)}, u32[]{:S(2)}) collective-permute-start(bf16[256,384]{1,0:T(8,128)(2,1)} %param.23), channel_id=1, source_target_pairs={{0,2},{1,3},{2,0},{3,1},{4,6},{5,7},{6,4},{7,5},{8,10},{9,11},{10,... | collective-permute-start | bytes 589832 | tf_op jit(solution)/shard_map/ppermute | solution.py:77
  47.2 6.9 %memory_attention.1 = bf16[4,272,384]{2,1,0:T(8,128)(2,1)} custom-call(s32[6]{0:T(128)S(1)} %stack.23.ids_ref, s32[48]{0:T(128)S(1)} %maximum_convert_fusion.early_ref, s32[16]{0:T(128)S(1)} %bitcast_convert_fusion.late_ref, bf16[272,384]{1,0:T(8,128)(2,1)} %copy-done.6, bf16[272,384]{1,0:T(8,128)(2,1)} %copy-done.9, bf16[272,384]{1,0:T(8,128)(2,1)} %copy-done.20, ...), custom_call_target="tpu_custom_call" | custom-call | flops 1610612736 | bytes 2359296 | tf_op jit(solution)/shard_map/memory_attention/pallas_call | solution.py:343
  54.1 5.1 %all-to-all-start = ((bf16[4,272,384]{2,1,0:T(8,128)(2,1)}), bf16[4,272,384]{2,1,0:T(8,128)(2,1)S(1)}, u32[]{:S(2)}, u32[]{:S(2)}) async-start(bf16[4,272,384]{2,1,0:T(8,128)(2,1)} %memory_attention.1), calls=%async_computation | async-start | bytes 1671168 | tf_op jit(solution)/shard_map/all_to_all | solution.py:62
  59.3 2.2 %collective-permute-start.13 = (bf16[512,384]{1,0:T(8,128)(2,1)S(1)}, bf16[512,384]{1,0:T(8,128)(2,1)}, u32[]{:S(2)}, u32[]{:S(2)}) collective-permute-start(bf16[512,384]{1,0:T(8,128)(2,1)S(1)} %constant_dynamic-update-slice_fusion.refs_1_), channel_id=1, source_target_pairs={{0,4},{1,5},{2,6},{3,7},{4,8},{5,9},{6,10},{7,11},{8,12},{9,13},{1... | collective-permute-start | bytes 1179656 | tf_op jit(solution)/shard_map/ppermute | solution.py:69
  61.6 4.4 %collective-permute-start.14 = (bf16[512,384]{1,0:T(8,128)(2,1)S(1)}, bf16[512,384]{1,0:T(8,128)(2,1)}, u32[]{:S(2)}, u32[]{:S(2)}) collective-permute-start(bf16[512,384]{1,0:T(8,128)(2,1)S(1)} %constant_dynamic-update-slice_fusion.refs_1_), channel_id=1, source_target_pairs={{0,12},{1,13},{2,14},{3,15},{4,0},{5,1},{6,2},{7,3},{8,4},{9,5},{1... | collective-permute-start | bytes 1179656 | tf_op jit(solution)/shard_map/ppermute | solution.py:69
  66.0 0.1 collective-permute-start.15
  66.1 2.7 %collective-permute-start.16 = (bf16[512,384]{1,0:T(8,128)(2,1)S(1)}, bf16[512,384]{1,0:T(8,128)(2,1)S(1)}, u32[]{:S(2)}, u32[]{:S(2)}) collective-permute-start(bf16[512,384]{1,0:T(8,128)(2,1)S(1)} %constant_dynamic-update-slice_fusion.2.refs_0_), channel_id=1, source_target_pairs={{0,12},{1,13},{2,14},{3,15},{4,0},{5,1},{6,2},{7,3},{8,4},{9,5},{1... | collective-permute-start | bytes 1179656 | tf_op jit(solution)/shard_map/ppermute | solution.py:69
  68.8 1.4 %local_attention.1.local_ref = f32[256,384]{1,0:T(8,128)S(1)} custom-call(f32[3]{0:T(128)S(1)} %add_divide_fusion.gate_ref, s32[1,256]{1,0:T(1,128)S(1)} %bitcast.17, bf16[256,384]{1,0:T(8,128)(2,1)S(1)} %copy-done, bf16[256,384]{1,0:T(8,128)(2,1)S(1)} %copy-done.3, bf16[256,384]{1,0:T(8,128)(2,1)S(1)} %copy-done.4), custom_call_target="tpu_custom_call" | custom-call | flops 100663296 | bytes 589824 | tf_op jit(solution)/shard_map/local_attention/pallas_call | solution.py:333
  70.2 4.1 %collective-permute-done.13.refs_2_ = bf16[512,384]{1,0:T(8,128)(2,1)} collective-permute-done((bf16[512,384]{1,0:T(8,128)(2,1)S(1)}, bf16[512,384]{1,0:T(8,128)(2,1)}, u32[]{:S(2)}, u32[]{:S(2)}) %collective-permute-start.13) | collective-permute-done | bytes 393248 | tf_op jit(solution)/shard_map/ppermute | solution.py:69
  74.3 8.3 %collective-permute-done.15.refs_1_ = bf16[512,384]{1,0:T(8,128)(2,1)S(1)} collective-permute-done((bf16[512,384]{1,0:T(8,128)(2,1)S(1)}, bf16[512,384]{1,0:T(8,128)(2,1)S(1)}, u32[]{:S(2)}, u32[]{:S(2)}) %collective-permute-start.15) | collective-permute-done | bytes 393248 | tf_op jit(solution)/shard_map/ppermute | solution.py:69
  82.6 2.0 %collective-permute-start.17 = (bf16[512,384]{1,0:T(8,128)(2,1)}, bf16[512,384]{1,0:T(8,128)(2,1)}, u32[]{:S(2)}, u32[]{:S(2)}) collective-permute-start(bf16[512,384]{1,0:T(8,128)(2,1)} %copy-done.8), channel_id=1, source_target_pairs={{0,8},{1,9},{2,10},{3,11},{4,12},{5,13},{6,14},{7,15},{8,0},{9,1},... | collective-permute-start | bytes 1179656 | tf_op jit(solution)/shard_map/ppermute | solution.py:69
  84.7 2.4 %merge.1 = (bf16[256,384]{1,0:T(8,128)(2,1)}, bf16[4,384,256]{2,1,0:T(8,128)(2,1)}) custom-call(f32[3]{0:T(128)S(1)} %add_divide_fusion.gate_ref, f32[256,384]{1,0:T(8,128)S(1)} %local_attention.1.local_ref, bf16[4,272,384]{2,1,0:T(8,128)(2,1)S(1)} %all-to-all-done.back_ref), custom_call_target="tpu_custom_call" | custom-call | flops 3145728 | bytes 1572864 | tf_op jit(solution)/shard_map/merge/pallas_call | solution.py:370
  87.0 6.2 %all-to-all-start.1 = ((bf16[4,384,256]{2,1,0:T(8,128)(2,1)}), bf16[4,384,256]{2,1,0:T(8,128)(2,1)S(1)}, u32[]{:S(2)}, u32[]{:S(2)}) async-start(bf16[4,384,256]{2,1,0:T(8,128)(2,1)} %get-tuple-element.102), calls=%async_computation.1 | async-start | bytes 1572864 | tf_op jit(solution)/shard_map/all_to_all | solution.py:62
  93.3 3.2 %collective-permute-start.19 = (bf16[512,384]{1,0:T(8,128)(2,1)}, bf16[512,384]{1,0:T(8,128)(2,1)S(1)}, u32[]{:S(2)}, u32[]{:S(2)}) collective-permute-start(bf16[512,384]{1,0:T(8,128)(2,1)} %copy-done.8), channel_id=1, source_target_pairs={{0,1},{1,0},{2,3},{3,2},{4,5},{5,4},{6,7},{7,6},{8,9},{9,8},{10,11... | collective-permute-start | bytes 1179656 | tf_op jit(solution)/shard_map/ppermute | solution.py:77
  96.5 0.5 collective-permute-start.22
  97.0 0.4 collective-permute-start.18
  97.4 0.9 collective-permute-start.23
  98.3 0.1 collective-permute-start.24
  98.4 0.6 copy-done.14
  99.1 0.1 collective-permute-start.26
  99.2 0.4 collective-permute-start.21
  99.6 9.7 %collective-permute-done.18.refs_2_ = bf16[512,384]{1,0:T(8,128)(2,1)S(1)} collective-permute-done((bf16[512,384]{1,0:T(8,128)(2,1)S(1)}, bf16[512,384]{1,0:T(8,128)(2,1)S(1)}, u32[]{:S(2)}, u32[]{:S(2)}) %collective-permute-start.18) | collective-permute-done | bytes 393248 | tf_op jit(solution)/shard_map/ppermute | solution.py:69
  109.3 0.8 collective-permute-start.25
  110.1 0.0 copy-start.1
  110.1 0.7 copy-done.1
  110.9 0.7 collective-permute-done.25.refs_6_
  111.5 4.3 %weight_partials.1 = (f32[384,384]{1,0:T(8,128)S(1)}, bf16[384,384]{1,0:T(8,128)(2,1)S(1)}, bf16[384,384]{1,0:T(8,128)(2,1)S(1)}, bf16[384,384]{1,0:T(8,128)(2,1)S(1)}) custom-call(s32[6]{0:T(128)S(1)} %stack.23.ids_ref, bf16[4,384,256]{2,1,0:T(8,128)(2,1)S(1)} %all-to-all-done.1.refs_0_, bf16[512,384]{1,0:T(8,128)(2,1)} %copy-done.8, ...), custom_call_target="tpu_custom_call" | custom-call | flops 1207959552 | bytes 4718592 | tf_op jit(solution)/shard_map/weight_partials/pallas_call | solution.py:389
  115.9 0.6 collective-permute-start.27
  116.5 0.6 collective-permute-start.28
  117.1 2.1 %collective-permute-start.29 = (bf16[384,384]{1,0:T(8,128)(2,1)S(1)}, bf16[384,384]{1,0:T(8,128)(2,1)S(1)}, u32[]{:S(2)}, u32[]{:S(2)}) collective-permute-start(bf16[384,384]{1,0:T(8,128)(2,1)S(1)} %get-tuple-element.117), channel_id=1, source_target_pairs={{0,48},{16,0},{32,16},{48,32},{64,112},{80,64},{96,80},{112,96},{1... | collective-permute-start | bytes 884744 | tf_op jit(solution)/shard_map/ppermute | solution.py:52
  119.2 6.0 %attention_grad.1 = bf16[256,384]{1,0:T(8,128)(2,1)} custom-call(s32[6]{0:T(128)S(1)} %stack.23.ids_ref, bf16[512,384]{1,0:T(8,128)(2,1)S(1)} %constant_dynamic-update-slice_fusion.2.refs_0_, bf16[512,384]{1,0:T(8,128)(2,1)S(1)} %collective-permute-done.15.refs_1_, bf16[512,384]{1,0:T(8,128)(2,1)S(1)} %collective-permute-done.18.refs_2_, ...), custom_call_target="tpu_custom_call" | custom-call | flops 1207959552 | bytes 6291456 | tf_op jit(solution)/shard_map/attention_grad/pallas_call | solution.py:405
  125.2 7.5 %collective-permute-done.28 = bf16[384,384]{1,0:T(8,128)(2,1)S(1)} collective-permute-done((bf16[384,384]{1,0:T(8,128)(2,1)S(1)}, bf16[384,384]{1,0:T(8,128)(2,1)S(1)}, u32[]{:S(2)}, u32[]{:S(2)}) %collective-permute-start.28) | collective-permute-done | bytes 294944 | tf_op jit(solution)/shard_map/ppermute | solution.py:52
  132.7 1.0 add_add_fusion
  (64 shorter events, 0.3 us)
Async XLA Ops:
  0.6 58.6 %copy-start.7 = (bf16[256,384]{1,0:T(8,128)(2,1)S(1)}, bf16[256,384]{1,0:T(8,128)(2,1)}, u32[]{:S(2)}) copy-start(bf16[256,384]{1,0:T(8,128)(2,1)} %param.23) | copy-start | bytes 589828
  0.6 23.1 %collective-permute-start = (bf16[512,384]{1,0:T(8,128)(2,1)}, bf16[512,384]{1,0:T(8,128)(2,1)S(1)}, u32[]{:S(2)}, u32[]{:S(2)}) collective-permute-start(bf16[512,384]{1,0:T(8,128)(2,1)} %refs_4_.1), channel_id=1, source_target_pairs={{0,16},{16,32},{32,48},{48,0},{64,80},{80,96},{96,112},{112,64},{1... | collective-permute-start | bytes 1179656 | tf_op jit(solution)/shard_map/ppermute | solution.py:52
  2.8 21.0 %collective-permute-start.1 = (bf16[512,384]{1,0:T(8,128)(2,1)}, bf16[512,384]{1,0:T(8,128)(2,1)S(1)}, u32[]{:S(2)}, u32[]{:S(2)}) collective-permute-start(bf16[512,384]{1,0:T(8,128)(2,1)} %refs_8_.2), channel_id=1, source_target_pairs={{0,48},{16,0},{32,16},{48,32},{64,112},{80,64},{96,80},{112,96},{1... | collective-permute-start | bytes 1179656 | tf_op jit(solution)/shard_map/ppermute | solution.py:52
  6.7 40.4 %copy-start.6 = (bf16[272,384]{1,0:T(8,128)(2,1)}, bf16[272,384]{1,0:T(8,128)(2,1)S(1)}, u32[]{:S(2)}) copy-start(bf16[272,384]{1,0:T(8,128)(2,1)S(1)} %fusion.1.refs_0_) | copy-start | bytes 626692
  6.7 62.0 %copy-start.21 = (f32[3]{0:T(128)S(1)}, f32[3]{0:T(128)}, u32[]{:S(2)}) copy-start(f32[3]{0:T(128)} %param.21) | copy-start | bytes 40
  6.7 62.0 %copy-start = (bf16[256,384]{1,0:T(8,128)(2,1)S(1)}, bf16[256,384]{1,0:T(8,128)(2,1)}, u32[]{:S(2)}) copy-start(bf16[256,384]{1,0:T(8,128)(2,1)} %q_ref.1) | copy-start | bytes 589828
  6.7 62.0 %copy-start.3 = (bf16[256,384]{1,0:T(8,128)(2,1)S(1)}, bf16[256,384]{1,0:T(8,128)(2,1)}, u32[]{:S(2)}) copy-start(bf16[256,384]{1,0:T(8,128)(2,1)} %k_ref.1) | copy-start | bytes 589828
  6.7 62.0 %copy-start.4 = (bf16[256,384]{1,0:T(8,128)(2,1)S(1)}, bf16[256,384]{1,0:T(8,128)(2,1)}, u32[]{:S(2)}) copy-start(bf16[256,384]{1,0:T(8,128)(2,1)} %v_ref.1) | copy-start | bytes 589828
  6.7 62.0 %copy-start.5 = (s32[256]{0:T(256)S(1)}, s32[256]{0:T(256)}, u32[]{:S(2)}) copy-start(s32[256]{0:T(256)} %param.16) | copy-start | bytes 3076
  6.7 11.1 %collective-permute-start.2 = (bf16[272,384]{1,0:T(8,128)(2,1)S(1)}, bf16[272,384]{1,0:T(8,128)(2,1)S(1)}, u32[]{:S(2)}, u32[]{:S(2)}) collective-permute-start(bf16[272,384]{1,0:T(8,128)(2,1)S(1)} %fusion.1.refs_0_), channel_id=1, source_target_pairs={{0,64},{16,80},{32,96},{48,112},{64,128},{80,144},{96,160},{112,17... | collective-permute-start | bytes 626696 | tf_op jit(solution)/shard_map/ppermute | solution.py:57
  9.9 13.8 %collective-permute-start.3 = (bf16[272,384]{1,0:T(8,128)(2,1)S(1)}, bf16[272,384]{1,0:T(8,128)(2,1)S(1)}, u32[]{:S(2)}, u32[]{:S(2)}) collective-permute-start(bf16[272,384]{1,0:T(8,128)(2,1)S(1)} %fusion.1.refs_0_), channel_id=1, source_target_pairs={{0,192},{16,208},{32,224},{48,240},{64,0},{80,16},{96,32},{112,48}... | collective-permute-start | bytes 626696 | tf_op jit(solution)/shard_map/ppermute | solution.py:57
  13.0 1.6 %collective-permute-start.4 = (bf16[256,384]{1,0:T(8,128)(2,1)}, bf16[256,384]{1,0:T(8,128)(2,1)S(1)}, u32[]{:S(2)}, u32[]{:S(2)}) collective-permute-start(bf16[256,384]{1,0:T(8,128)(2,1)} %param.23), channel_id=1, source_target_pairs={{0,0},{1,1},{2,2},{3,3},{16,16},{17,17},{18,18},{19,19},{32,32},{3... | collective-permute-start | bytes 589832 | tf_op jit(solution)/shard_map/ppermute | solution.py:94
  17.8 29.3 %copy-start.9 = (bf16[272,384]{1,0:T(8,128)(2,1)}, bf16[272,384]{1,0:T(8,128)(2,1)S(1)}, u32[]{:S(2)}) copy-start(bf16[272,384]{1,0:T(8,128)(2,1)S(1)} %collective-permute-done.2.refs_1_) | copy-start | bytes 626692
  23.7 23.4 %copy-start.10 = (bf16[272,384]{1,0:T(8,128)(2,1)}, bf16[272,384]{1,0:T(8,128)(2,1)S(1)}, u32[]{:S(2)}) copy-start(bf16[272,384]{1,0:T(8,128)(2,1)S(1)} %collective-permute-done.3.refs_3_) | copy-start | bytes 626692
  23.7 23.4 %copy-start.11 = (bf16[512,384]{1,0:T(8,128)(2,1)}, bf16[512,384]{1,0:T(8,128)(2,1)S(1)}, u32[]{:S(2)}) copy-start(bf16[512,384]{1,0:T(8,128)(2,1)S(1)} %collective-permute-done.refs_5_) | copy-start | bytes 1179652
  23.7 23.4 %copy-start.12 = (bf16[512,384]{1,0:T(8,128)(2,1)}, bf16[512,384]{1,0:T(8,128)(2,1)S(1)}, u32[]{:S(2)}) copy-start(bf16[512,384]{1,0:T(8,128)(2,1)S(1)} %collective-permute-done.1.refs_11_) | copy-start | bytes 1179652
  23.7 9.7 %collective-permute-start.8 = (bf16[512,384]{1,0:T(8,128)(2,1)S(1)}, bf16[512,384]{1,0:T(8,128)(2,1)S(1)}, u32[]{:S(2)}, u32[]{:S(2)}) collective-permute-start(bf16[512,384]{1,0:T(8,128)(2,1)S(1)} %collective-permute-done.1.refs_11_), channel_id=1, source_target_pairs={{0,48},{16,0},{32,16},{48,32},{64,112},{80,64},{96,80},{112,96},{1... | collective-permute-start | bytes 1179656 | tf_op jit(solution)/shard_map/ppermute | solution.py:52
  25.2 10.8 %collective-permute-start.5 = (bf16[272,384]{1,0:T(8,128)(2,1)S(1)}, bf16[272,384]{1,0:T(8,128)(2,1)S(1)}, u32[]{:S(2)}, u32[]{:S(2)}) collective-permute-start(bf16[272,384]{1,0:T(8,128)(2,1)S(1)} %fusion.1.refs_0_), channel_id=1, source_target_pairs={{0,128},{16,144},{32,160},{48,176},{64,192},{80,208},{96,224},{112... | collective-permute-start | bytes 626696 | tf_op jit(solution)/shard_map/ppermute | solution.py:57
  27.9 9.2 %collective-permute-start.6 = (bf16[512,384]{1,0:T(8,128)(2,1)S(1)}, bf16[512,384]{1,0:T(8,128)(2,1)S(1)}, u32[]{:S(2)}, u32[]{:S(2)}) collective-permute-start(bf16[512,384]{1,0:T(8,128)(2,1)S(1)} %collective-permute-done.refs_5_), channel_id=1, source_target_pairs={{0,16},{16,32},{32,48},{48,0},{64,80},{80,96},{96,112},{112,64},{1... | collective-permute-start | bytes 1179656 | tf_op jit(solution)/shard_map/ppermute | solution.py:52
  28.1 17.4 %collective-permute-start.7 = (bf16[512,384]{1,0:T(8,128)(2,1)}, bf16[512,384]{1,0:T(8,128)(2,1)S(1)}, u32[]{:S(2)}, u32[]{:S(2)}) collective-permute-start(bf16[512,384]{1,0:T(8,128)(2,1)} %refs_8_.2), channel_id=1, source_target_pairs={{0,16},{16,32},{32,48},{48,0},{64,80},{80,96},{96,112},{112,64},{1... | collective-permute-start | bytes 1179656 | tf_op jit(solution)/shard_map/ppermute | solution.py:52
  28.2 7.8 %collective-permute-start.10 = (bf16[256,384]{1,0:T(8,128)(2,1)S(1)}, bf16[256,384]{1,0:T(8,128)(2,1)S(1)}, u32[]{:S(2)}, u32[]{:S(2)}) collective-permute-start(bf16[256,384]{1,0:T(8,128)(2,1)S(1)} %collective-permute-done.4), channel_id=1, source_target_pairs={{0,0},{1,1},{2,2},{3,3},{16,16},{17,17},{18,18},{19,19},{32,32},{3... | collective-permute-start | bytes 589832 | tf_op jit(solution)/shard_map/ppermute | solution.py:94
  33.4 13.8 %copy-start.13 = (bf16[512,384]{1,0:T(8,128)(2,1)}, bf16[512,384]{1,0:T(8,128)(2,1)S(1)}, u32[]{:S(2)}) copy-start(bf16[512,384]{1,0:T(8,128)(2,1)S(1)} %collective-permute-done.8.refs_10_) | copy-start | bytes 1179652
  33.4 12.2 %collective-permute-start.9 = (bf16[512,384]{1,0:T(8,128)(2,1)}, bf16[512,384]{1,0:T(8,128)(2,1)S(1)}, u32[]{:S(2)}, u32[]{:S(2)}) collective-permute-start(bf16[512,384]{1,0:T(8,128)(2,1)} %refs_4_.1), channel_id=1, source_target_pairs={{0,48},{16,0},{32,16},{48,32},{64,112},{80,64},{96,80},{112,96},{1... | collective-permute-start | bytes 1179656 | tf_op jit(solution)/shard_map/ppermute | solution.py:52
  36.0 11.2 %copy-start.20 = (bf16[272,384]{1,0:T(8,128)(2,1)}, bf16[272,384]{1,0:T(8,128)(2,1)S(1)}, u32[]{:S(2)}) copy-start(bf16[272,384]{1,0:T(8,128)(2,1)S(1)} %collective-permute-done.5.refs_2_) | copy-start | bytes 626692
  37.1 10.0 %copy-start.17 = (bf16[512,384]{1,0:T(8,128)(2,1)}, bf16[512,384]{1,0:T(8,128)(2,1)S(1)}, u32[]{:S(2)}) copy-start(bf16[512,384]{1,0:T(8,128)(2,1)S(1)} %collective-permute-done.6.refs_6_) | copy-start | bytes 1179652
  45.6 1.6 %copy-start.18 = (bf16[512,384]{1,0:T(8,128)(2,1)}, bf16[512,384]{1,0:T(8,128)(2,1)S(1)}, u32[]{:S(2)}) copy-start(bf16[512,384]{1,0:T(8,128)(2,1)S(1)} %collective-permute-done.7.refs_9_) | copy-start | bytes 1179652
  45.6 1.6 %copy-start.19 = (bf16[512,384]{1,0:T(8,128)(2,1)}, bf16[512,384]{1,0:T(8,128)(2,1)S(1)}, u32[]{:S(2)}) copy-start(bf16[512,384]{1,0:T(8,128)(2,1)S(1)} %collective-permute-done.9.refs_7_) | copy-start | bytes 1179652
  45.6 8.6 %collective-permute-start.11 = (bf16[256,384]{1,0:T(8,128)(2,1)S(1)}, bf16[256,384]{1,0:T(8,128)(2,1)S(1)}, u32[]{:S(2)}, u32[]{:S(2)}) collective-permute-start(bf16[256,384]{1,0:T(8,128)(2,1)S(1)} %collective-permute-done.10), channel_id=1, source_target_pairs={{0,2},{1,3},{2,0},{3,1},{4,6},{5,7},{6,4},{7,5},{8,10},{9,11},{10,... | collective-permute-start | bytes 589832 | tf_op jit(solution)/shard_map/ppermute | solution.py:77
  45.7 8.5 %collective-permute-start.12 = (bf16[256,384]{1,0:T(8,128)(2,1)}, bf16[256,384]{1,0:T(8,128)(2,1)S(1)}, u32[]{:S(2)}, u32[]{:S(2)}) collective-permute-start(bf16[256,384]{1,0:T(8,128)(2,1)} %param.23), channel_id=1, source_target_pairs={{0,2},{1,3},{2,0},{3,1},{4,6},{5,7},{6,4},{7,5},{8,10},{9,11},{10,... | collective-permute-start | bytes 589832 | tf_op jit(solution)/shard_map/ppermute | solution.py:77
  54.1 28.5 %all-to-all-start = ((bf16[4,272,384]{2,1,0:T(8,128)(2,1)}), bf16[4,272,384]{2,1,0:T(8,128)(2,1)S(1)}, u32[]{:S(2)}, u32[]{:S(2)}) async-start(bf16[4,272,384]{2,1,0:T(8,128)(2,1)} %memory_attention.1), calls=%async_computation | async-start | bytes 1671168 | tf_op jit(solution)/shard_map/all_to_all | solution.py:62
  59.3 23.3 %copy-start.8 = (bf16[512,384]{1,0:T(8,128)(2,1)}, bf16[512,384]{1,0:T(8,128)(2,1)S(1)}, u32[]{:S(2)}) copy-start(bf16[512,384]{1,0:T(8,128)(2,1)S(1)} %constant_dynamic-update-slice_fusion.refs_1_) | copy-start | bytes 1179652
  59.3 14.9 %collective-permute-start.13 = (bf16[512,384]{1,0:T(8,128)(2,1)S(1)}, bf16[512,384]{1,0:T(8,128)(2,1)}, u32[]{:S(2)}, u32[]{:S(2)}) collective-permute-start(bf16[512,384]{1,0:T(8,128)(2,1)S(1)} %constant_dynamic-update-slice_fusion.refs_1_), channel_id=1, source_target_pairs={{0,4},{1,5},{2,6},{3,7},{4,8},{5,9},{6,10},{7,11},{8,12},{9,13},{1... | collective-permute-start | bytes 1179656 | tf_op jit(solution)/shard_map/ppermute | solution.py:69
  61.6 12.7 %collective-permute-start.14 = (bf16[512,384]{1,0:T(8,128)(2,1)S(1)}, bf16[512,384]{1,0:T(8,128)(2,1)}, u32[]{:S(2)}, u32[]{:S(2)}) collective-permute-start(bf16[512,384]{1,0:T(8,128)(2,1)S(1)} %constant_dynamic-update-slice_fusion.refs_1_), channel_id=1, source_target_pairs={{0,12},{1,13},{2,14},{3,15},{4,0},{5,1},{6,2},{7,3},{8,4},{9,5},{1... | collective-permute-start | bytes 1179656 | tf_op jit(solution)/shard_map/ppermute | solution.py:69
  66.0 16.6 %collective-permute-start.15 = (bf16[512,384]{1,0:T(8,128)(2,1)S(1)}, bf16[512,384]{1,0:T(8,128)(2,1)S(1)}, u32[]{:S(2)}, u32[]{:S(2)}) collective-permute-start(bf16[512,384]{1,0:T(8,128)(2,1)S(1)} %constant_dynamic-update-slice_fusion.2.refs_0_), channel_id=1, source_target_pairs={{0,4},{1,5},{2,6},{3,7},{4,8},{5,9},{6,10},{7,11},{8,12},{9,13},{1... | collective-permute-start | bytes 1179656 | tf_op jit(solution)/shard_map/ppermute | solution.py:69
  66.1 16.5 %collective-permute-start.16 = (bf16[512,384]{1,0:T(8,128)(2,1)S(1)}, bf16[512,384]{1,0:T(8,128)(2,1)S(1)}, u32[]{:S(2)}, u32[]{:S(2)}) collective-permute-start(bf16[512,384]{1,0:T(8,128)(2,1)S(1)} %constant_dynamic-update-slice_fusion.2.refs_0_), channel_id=1, source_target_pairs={{0,12},{1,13},{2,14},{3,15},{4,0},{5,1},{6,2},{7,3},{8,4},{9,5},{1... | collective-permute-start | bytes 1179656 | tf_op jit(solution)/shard_map/ppermute | solution.py:69
  82.6 14.4 %collective-permute-start.17 = (bf16[512,384]{1,0:T(8,128)(2,1)}, bf16[512,384]{1,0:T(8,128)(2,1)}, u32[]{:S(2)}, u32[]{:S(2)}) collective-permute-start(bf16[512,384]{1,0:T(8,128)(2,1)} %copy-done.8), channel_id=1, source_target_pairs={{0,8},{1,9},{2,10},{3,11},{4,12},{5,13},{6,14},{7,15},{8,0},{9,1},... | collective-permute-start | bytes 1179656 | tf_op jit(solution)/shard_map/ppermute | solution.py:69
  87.0 23.8 %all-to-all-start.1 = ((bf16[4,384,256]{2,1,0:T(8,128)(2,1)}), bf16[4,384,256]{2,1,0:T(8,128)(2,1)S(1)}, u32[]{:S(2)}, u32[]{:S(2)}) async-start(bf16[4,384,256]{2,1,0:T(8,128)(2,1)} %get-tuple-element.102), calls=%async_computation.1 | async-start | bytes 1572864 | tf_op jit(solution)/shard_map/all_to_all | solution.py:62
  93.3 5.0 %collective-permute-start.19 = (bf16[512,384]{1,0:T(8,128)(2,1)}, bf16[512,384]{1,0:T(8,128)(2,1)S(1)}, u32[]{:S(2)}, u32[]{:S(2)}) collective-permute-start(bf16[512,384]{1,0:T(8,128)(2,1)} %copy-done.8), channel_id=1, source_target_pairs={{0,1},{1,0},{2,3},{3,2},{4,5},{5,4},{6,7},{7,6},{8,9},{9,8},{10,11... | collective-permute-start | bytes 1179656 | tf_op jit(solution)/shard_map/ppermute | solution.py:77
  96.5 2.6 %collective-permute-start.20 = (bf16[512,384]{1,0:T(8,128)(2,1)}, bf16[512,384]{1,0:T(8,128)(2,1)S(1)}, u32[]{:S(2)}, u32[]{:S(2)}) collective-permute-start(bf16[512,384]{1,0:T(8,128)(2,1)} %collective-permute-done.13.refs_2_), channel_id=1, source_target_pairs={{0,1},{1,0},{2,3},{3,2},{4,5},{5,4},{6,7},{7,6},{8,9},{9,8},{10,11... | collective-permute-start | bytes 1179656 | tf_op jit(solution)/shard_map/ppermute | solution.py:77
  96.5 2.7 %collective-permute-start.22 = (bf16[512,384]{1,0:T(8,128)(2,1)}, bf16[512,384]{1,0:T(8,128)(2,1)S(1)}, u32[]{:S(2)}, u32[]{:S(2)}) collective-permute-start(bf16[512,384]{1,0:T(8,128)(2,1)} %collective-permute-done.14.refs_4_), channel_id=1, source_target_pairs={{0,1},{1,0},{2,3},{3,2},{4,5},{5,4},{6,7},{7,6},{8,9},{9,8},{10,11... | collective-permute-start | bytes 1179656 | tf_op jit(solution)/shard_map/ppermute | solution.py:77
  97.0 12.3 %collective-permute-start.18 = (bf16[512,384]{1,0:T(8,128)(2,1)S(1)}, bf16[512,384]{1,0:T(8,128)(2,1)S(1)}, u32[]{:S(2)}, u32[]{:S(2)}) collective-permute-start(bf16[512,384]{1,0:T(8,128)(2,1)S(1)} %constant_dynamic-update-slice_fusion.2.refs_0_), channel_id=1, source_target_pairs={{0,8},{1,9},{2,10},{3,11},{4,12},{5,13},{6,14},{7,15},{8,0},{9,1},... | collective-permute-start | bytes 1179656 | tf_op jit(solution)/shard_map/ppermute | solution.py:69
  97.4 12.6 %collective-permute-start.23 = (bf16[512,384]{1,0:T(8,128)(2,1)S(1)}, bf16[512,384]{1,0:T(8,128)(2,1)S(1)}, u32[]{:S(2)}, u32[]{:S(2)}) collective-permute-start(bf16[512,384]{1,0:T(8,128)(2,1)S(1)} %constant_dynamic-update-slice_fusion.2.refs_0_), channel_id=1, source_target_pairs={{0,1},{1,0},{2,3},{3,2},{4,5},{5,4},{6,7},{7,6},{8,9},{9,8},{10,11... | collective-permute-start | bytes 1179656 | tf_op jit(solution)/shard_map/ppermute | solution.py:77
  98.3 0.8 copy-start.14
  98.3 11.8 %collective-permute-start.24 = (bf16[512,384]{1,0:T(8,128)(2,1)S(1)}, bf16[512,384]{1,0:T(8,128)(2,1)S(1)}, u32[]{:S(2)}, u32[]{:S(2)}) collective-permute-start(bf16[512,384]{1,0:T(8,128)(2,1)S(1)} %collective-permute-done.15.refs_1_), channel_id=1, source_target_pairs={{0,1},{1,0},{2,3},{3,2},{4,5},{5,4},{6,7},{7,6},{8,9},{9,8},{10,11... | collective-permute-start | bytes 1179656 | tf_op jit(solution)/shard_map/ppermute | solution.py:77
  99.1 11.0 %copy-start.15 = (bf16[512,384]{1,0:T(8,128)(2,1)}, bf16[512,384]{1,0:T(8,128)(2,1)S(1)}, u32[]{:S(2)}) copy-start(bf16[512,384]{1,0:T(8,128)(2,1)S(1)} %collective-permute-done.20.refs_6_) | copy-start | bytes 1179652
  99.1 11.0 %collective-permute-start.26 = (bf16[512,384]{1,0:T(8,128)(2,1)S(1)}, bf16[512,384]{1,0:T(8,128)(2,1)S(1)}, u32[]{:S(2)}, u32[]{:S(2)}) collective-permute-start(bf16[512,384]{1,0:T(8,128)(2,1)S(1)} %collective-permute-done.16.refs_3_), channel_id=1, source_target_pairs={{0,1},{1,0},{2,3},{3,2},{4,5},{5,4},{6,7},{7,6},{8,9},{9,8},{10,11... | collective-permute-start | bytes 1179656 | tf_op jit(solution)/shard_map/ppermute | solution.py:77
  99.2 10.9 %copy-start.16 = (bf16[512,384]{1,0:T(8,128)(2,1)}, bf16[512,384]{1,0:T(8,128)(2,1)S(1)}, u32[]{:S(2)}) copy-start(bf16[512,384]{1,0:T(8,128)(2,1)S(1)} %collective-permute-done.22.refs_8_) | copy-start | bytes 1179652
  99.2 11.6 %collective-permute-start.21 = (bf16[512,384]{1,0:T(8,128)(2,1)}, bf16[512,384]{1,0:T(8,128)(2,1)}, u32[]{:S(2)}, u32[]{:S(2)}) collective-permute-start(bf16[512,384]{1,0:T(8,128)(2,1)} %collective-permute-done.17.refs_3_), channel_id=1, source_target_pairs={{0,1},{1,0},{2,3},{3,2},{4,5},{5,4},{6,7},{7,6},{8,9},{9,8},{10,11... | collective-permute-start | bytes 1179656 | tf_op jit(solution)/shard_map/ppermute | solution.py:77
  109.3 2.3 %collective-permute-start.25 = (bf16[512,384]{1,0:T(8,128)(2,1)S(1)}, bf16[512,384]{1,0:T(8,128)(2,1)}, u32[]{:S(2)}, u32[]{:S(2)}) collective-permute-start(bf16[512,384]{1,0:T(8,128)(2,1)S(1)} %collective-permute-done.18.refs_2_), channel_id=1, source_target_pairs={{0,1},{1,0},{2,3},{3,2},{4,5},{5,4},{6,7},{7,6},{8,9},{9,8},{10,11... | collective-permute-start | bytes 1179656 | tf_op jit(solution)/shard_map/ppermute | solution.py:77
  110.1 0.7 copy-start.1
  110.8 8.4 %copy-start.2 = (bf16[512,384]{1,0:T(8,128)(2,1)S(1)}, bf16[512,384]{1,0:T(8,128)(2,1)}, u32[]{:S(2)}) copy-start(bf16[512,384]{1,0:T(8,128)(2,1)} %copy-done.1) | copy-start | bytes 1179652
  115.9 9.3 %collective-permute-start.27 = (bf16[384,384]{1,0:T(8,128)(2,1)S(1)}, bf16[384,384]{1,0:T(8,128)(2,1)S(1)}, u32[]{:S(2)}, u32[]{:S(2)}) collective-permute-start(bf16[384,384]{1,0:T(8,128)(2,1)S(1)} %get-tuple-element.115), channel_id=1, source_target_pairs={{0,32},{16,48},{32,0},{48,16},{64,96},{80,112},{96,64},{112,80},{1... | collective-permute-start | bytes 884744 | tf_op jit(solution)/shard_map/ppermute | solution.py:52
  116.5 16.2 %collective-permute-start.28 = (bf16[384,384]{1,0:T(8,128)(2,1)S(1)}, bf16[384,384]{1,0:T(8,128)(2,1)S(1)}, u32[]{:S(2)}, u32[]{:S(2)}) collective-permute-start(bf16[384,384]{1,0:T(8,128)(2,1)S(1)} %get-tuple-element.116), channel_id=1, source_target_pairs={{0,16},{16,32},{32,48},{48,0},{64,80},{80,96},{96,112},{112,64},{1... | collective-permute-start | bytes 884744 | tf_op jit(solution)/shard_map/ppermute | solution.py:52
  117.1 15.6 %collective-permute-start.29 = (bf16[384,384]{1,0:T(8,128)(2,1)S(1)}, bf16[384,384]{1,0:T(8,128)(2,1)S(1)}, u32[]{:S(2)}, u32[]{:S(2)}) collective-permute-start(bf16[384,384]{1,0:T(8,128)(2,1)S(1)} %get-tuple-element.117), channel_id=1, source_target_pairs={{0,48},{16,0},{32,16},{48,32},{64,112},{80,64},{96,80},{112,96},{1... | collective-permute-start | bytes 884744 | tf_op jit(solution)/shard_map/ppermute | solution.py:52
